TPU v7x, 128 devices: a whole 4x4x4 slice. The times are simulated.
128 devices in a mesh: row: 16 (over z, y), col: 8 (over x, core).
Axes of the slice: x: 4, y: 4, z: 4, core: 2. Of those that a mesh axis runs over, the one named last changes fastest.
Arguments:
- trailing: bfloat16 [24576, 24576], P('row', 'col'), may hold values from -6 to 6
- rows_a: int32 [16, 12], replicated, may hold values from 0 to 11, as said below
- counts_a: int32 [16], replicated, may hold values from 1 to 12, as said below
- factor_a: bfloat16 [24576, 512], P('row'), may hold values from -0.0390625 to 0.0390625
- rows_b: int32 [16, 12], replicated, may hold values from 0 to 11, as said below
- counts_b: int32 [16], replicated, may hold values from 1 to 12, as said below
- factor_b: bfloat16 [24576, 512], P('row'), may hold values from -0.0390625 to 0.0390625
- factor_top: bfloat16 [512, 512], replicated, may hold values from -0.25 to 0.25
- base_a: float32 [512, 512], P('col'), may hold values from -3 to 3
- base_b: float32 [512, 512], P('col'), may hold values from -3 to 3
Outputs:
- column_a: bfloat16 [24576, 512], P('row')
- diag_a: float32 [512, 512], P('col')
- column_b: bfloat16 [24576, 512], P('row')
- top_b: bfloat16 [512, 512], P('col')
- diag_b: float32 [512, 512], P('col')
Inputs may be any that keep to these rules, and one draw needn't show every extreme that they name: `rows_a`: the first counts_a[r] entries of row r are distinct; the rest of the row is padding. `counts_a`: some owner uses all 12 slots in every draw. `rows_b`: the first counts_b[r] entries of row r are distinct and lie among the first counts_a[r] entries of row r of rows_a; the rest is padding. counts_b[r] <= counts_a[r]; some owner uses all 12 slots in every draw.
All inputs are finite; a program needn't handle non-finite values.
Results may differ from a plain program's by a relative error of at most 0.007.
Values may be sent and summed in bfloat16 or wider, within the bound.
No kernel may reach another device: no remote copies, remote signals or barrier semaphores. Data moves between devices by JAX's collectives and lax.ppermute only.
A program may use at most 128 MiB of HBM per device.

v0:
```python
import jax
import jax.numpy as jnp
from jax import lax
from jax.sharding import PartitionSpec as P

BS = 128
W = 512
RBD = 12
PAD = 12


def spread_2(value, axis, source):
    kept = jnp.where(lax.axis_index(axis) == source, value, 0).astype(value.dtype)
    return lax.psum(kept, axis)


def contract_rows(former, latter):
    return lax.dot_general(
        former, latter, (((0,), (0,)), ((), ())), preferred_element_type=jnp.float32
    )


def slot_live(counts, owner_idx):
    live_count = lax.dynamic_index_in_dim(counts, owner_idx, 0, keepdims=False)
    return jnp.arange(PAD, dtype=jnp.int32) < live_count


def on_device(
    trailing, rows_a, counts_a, factor_a, rows_b, counts_b, factor_b, factor_top, base_a, base_b
):
    row_count = lax.axis_size("row")
    col_count = lax.axis_size("col")
    fanout = row_count // col_count
    row_index = lax.axis_index("row")
    col_index = lax.axis_index("col")
    col_blocks = trailing.shape[1] // BS
    part_width = W // col_count
    slot_rows = PAD * BS
    width_start = col_index * part_width
    slab_blocks = trailing.reshape(RBD, BS, trailing.shape[1])

    def row_gate(live_rows):
        return jnp.repeat(live_rows.astype(jnp.float32), BS)[:, None]

    def partial_product(rows, counts, factor):
        own_rows = lax.dynamic_index_in_dim(rows, row_index, 0, keepdims=False)
        row_slab = jnp.take(slab_blocks, own_rows, axis=0).reshape(slot_rows, trailing.shape[1])
        pieces = []
        targets = []
        flags = []
        for offset in range(fanout):
            source = col_index + offset * col_count
            pieces.append(spread_2(factor, "row", source))
            src_rows = lax.dynamic_index_in_dim(rows, source, 0, keepdims=False)
            targets.append(src_rows * fanout + offset)
            flags.append(slot_live(counts, source))
        received = jnp.stack(pieces).reshape(fanout * PAD, BS * W)
        target = jnp.concatenate(targets)
        live_src = jnp.concatenate(flags)
        selector = (
            (jnp.arange(col_blocks, dtype=jnp.int32)[:, None] == target[None, :])
            & live_src[None, :]
        ).astype(jnp.bfloat16)
        spread = jnp.dot(selector, received, preferred_element_type=jnp.float32).astype(
            jnp.bfloat16
        )
        return jnp.dot(
            row_slab, spread.reshape(col_blocks * BS, W), preferred_element_type=jnp.float32
        )

    def finish(partial_value, live_rows, addend):
        gate = row_gate(live_rows)
        summed = lax.psum(partial_value, "col")
        if addend is not None:
            summed = summed + addend(0, slot_rows)
        return (-summed * gate).astype(jnp.bfloat16)

    def row_sums(pieces_in):
        return lax.psum(pieces_in, "row")

    live_a = slot_live(counts_a, row_index)
    live_b = slot_live(counts_b, row_index)
    column_a = finish(partial_product(rows_a, counts_a, factor_a), live_a, None)
    own_rows_a = lax.dynamic_index_in_dim(rows_a, row_index, 0, keepdims=False)
    own_rows_b = lax.dynamic_index_in_dim(rows_b, row_index, 0, keepdims=False)
    pairing = (
        (own_rows_b[:, None] == own_rows_a[None, :]) & live_a[None, :] & live_b[:, None]
    ).astype(jnp.bfloat16)
    carried = (
        jnp.dot(pairing, column_a.reshape(PAD, BS * W), preferred_element_type=jnp.float32)
        .astype(jnp.bfloat16)
        .reshape(slot_rows, W)
    )
    width_a = lax.dynamic_slice_in_dim(column_a, width_start, part_width, 1)
    width_c = lax.dynamic_slice_in_dim(carried, width_start, part_width, 1)
    sums_a = row_sums((contract_rows(width_a, factor_a), contract_rows(width_c, factor_b)))
    diag_a = base_a - sums_a[0]
    top_b = (-(sums_a[1] + jnp.dot(diag_a, factor_top.astype(jnp.float32)))).astype(jnp.bfloat16)

    def cross_rows(first_row, row_total):
        return jnp.dot(carried, factor_top, preferred_element_type=jnp.float32)

    column_b = finish(partial_product(rows_b, counts_b, factor_b), live_b, cross_rows)
    width_b = lax.dynamic_slice_in_dim(column_b, width_start, part_width, 1)
    sums_b = row_sums((contract_rows(width_b, factor_b),))
    top_whole = lax.all_gather(top_b, "col", axis=0, tiled=True)
    top_cols = lax.dynamic_slice_in_dim(top_whole, width_start, part_width, 1)
    diag_b = base_b - sums_b[0] - contract_rows(top_cols, factor_top)
    return (column_a, diag_a, column_b, top_b, diag_b)


def solution(mesh):
    in_specs = (
        P("row", "col"),
        P(),
        P(),
        P("row", None),
        P(),
        P(),
        P("row", None),
        P(),
        P("col", None),
        P("col", None),
    )
    out_specs = (P("row", None), P("col", None), P("row", None), P("col", None), P("col", None))
    return jax.shard_map(
        on_device, mesh=mesh, in_specs=in_specs, out_specs=out_specs, check_vma=False
    )
```

profile of v0, /device:TPU:1, one launch (start us, length us, event | category | flops | bytes accessed | tf_op | source)
XLA Modules:
  0.0 408.7 jit_solution(16539790048383573170)
XLA Ops:
  7.2 0.0 copy-start
  7.2 0.0 all-reduce.11.cloned.1.call-start
  7.2 4.8 %select_bitcast_fusion.1 = (bf16[1,1536,512]{2,1,0:T(8,128)(2,1)}, bf16[1,1536,512]{2,1,0:T(8,128)(2,1)}, bf16[1,1536,512]{2,1,0:T(8,128)(2,1)}, bf16[1,1536,512]{2,1,0:T(8,128)(2,1)}) fusion(bf16[1536,512]{1,0:T(8,128)(2,1)} %param.18, pred[]{:T(512)S(6)} %eq.50, pred[]{:T(512)S(6)} %eq.51, bf16[1536,512]{1,0:T(8,128)(2,1)} %param.15), kind=kLoop, calls=%fused_computation.15 | loop fusion | flops 3145728 | bytes 9437186 | tf_op jit(solution)/shard_map/stack | solution.py:57
  12.0 0.0 all-reduce.11.cloned.1.call-update
  12.0 0.0 all-reduce.9.cloned.1.call-start
  12.1 0.7 compare_and_fusion
  12.8 0.7 compare_and_fusion.1
  13.5 9.3 %gather_fusion.1 = bf16[12,128,3072]{2,1,0:T(8,128)(2,1)} fusion(bf16[12,128,3072]{2,1,0:T(8,128)(2,1)} %bitcast.50, s32[1024]{0:T(1024)S(1)} %pad_clamp_fusion), kind=kCustom, calls=%fused_computation.1.clone | custom fusion | bytes 18874416 | tf_op jit(solution)/shard_map/jit(_take)/gather | solution.py:47
  22.8 0.0 copy-start.11
  22.8 10.6 %gather_fusion = bf16[12,128,3072]{2,1,0:T(8,128)(2,1)} fusion(bf16[12,128,3072]{2,1,0:T(8,128)(2,1)} %bitcast.51, s32[1024]{0:T(1024)S(1)} %pad_clamp_fusion.1), kind=kCustom, calls=%fused_computation.clone | custom fusion | bytes 18874416 | tf_op jit(solution)/shard_map/jit(_take)/gather | solution.py:47
  33.4 0.0 copy-done.11
  33.4 0.7 fusion.47
  34.0 0.6 iota_compare_fusion.3
  34.7 0.7 iota_compare_fusion.4
  35.4 0.6 iota_compare_fusion.6
  36.0 0.6 iota_compare_fusion.7
  36.6 0.1 pad_add_fusion.1
  36.6 0.1 pad_add_fusion
  36.7 0.7 fusion.38
  37.4 0.7 fusion.33
  38.1 0.1 pad_add_fusion.2
  38.2 8.5 %broadcast_select_fusion = bf16[12,128,3072]{2,1,0:T(8,128)(2,1)} fusion(bf16[12,128,3072]{2,1,0:T(8,128)(2,1)} %gather_fusion.1, pred[12]{0:T(512)(128)(4,1)S(1)} %get-tuple-element.15), kind=kLoop, calls=%fused_computation.5 | loop fusion | flops 4718592 | bytes 18874380 | tf_op jit(solution)/shard_map/jit(_take)/select_n | solution.py:47
  46.7 8.6 %broadcast_select_fusion.1 = bf16[12,128,3072]{2,1,0:T(8,128)(2,1)} fusion(bf16[12,128,3072]{2,1,0:T(8,128)(2,1)} %gather_fusion, pred[12]{0:T(512)(128)(4,1)S(1)} %get-tuple-element.17), kind=kLoop, calls=%fused_computation.6 | loop fusion | flops 4718592 | bytes 18874380 | tf_op jit(solution)/shard_map/jit(_take)/select_n | solution.py:47
  55.3 83.3 %all-reduce.11.cloned.1.call-done = (bf16[1,1536,512]{2,1,0:T(8,128)(2,1)}, bf16[1,1536,512]{2,1,0:T(8,128)(2,1)}, bf16[1,1536,512]{2,1,0:T(8,128)(2,1)}, bf16[1,1536,512]{2,1,0:T(8,128)(2,1)}) async-done(((bf16[1,1536,512]{2,1,0:T(8,128)(2,1)}, bf16[1,1536,512]{2,1,0:T(8,128)(2,1)}, bf16[1,1536,512]{2,1,0:T(8,128)(2,1)}, bf16[1,1536,512]{2,1,0:T(8,128)(2,1)}), (bf16[1,1536,512]{2,1,0:T(8,128)(2,1)}, ...) | async-done | bytes 6291472 | tf_op jit(solution)/shard_map/psum | solution.py:14
  138.6 3.9 pad_maximum_fusion.1
  142.5 5.2 %reshape.75 = bf16[24,65536]{1,0:T(8,128)(2,1)} reshape(bf16[2,1536,512]{2,1,0:T(8,128)(2,1)} %pad_maximum_fusion.1) | data formatting | bytes 6291456 | tf_op jit(solution)/shard_map/reshape | solution.py:57
  147.7 4.5 %convolution_convert_fusion = bf16[24,65536]{1,0:T(8,128)(2,1)} fusion(bf16[24,65536]{1,0:T(8,128)(2,1)} %reshape.75, s32[24]{0:T(128)S(1)} %get-tuple-element.36, pred[24]{0:T(512)(128)(4,1)S(1)} %pad_add_fusion.1), kind=kOutput, calls=%fused_computation.2 | convolution fusion | flops 77071488 | bytes 6291576 | tf_op jit(solution)/shard_map/dot_general | solution.py:64
  152.2 5.3 %reshape.76 = bf16[3072,512]{1,0:T(8,128)(2,1)} reshape(bf16[24,65536]{1,0:T(8,128)(2,1)} %convolution_convert_fusion) | data formatting | bytes 6291456 | tf_op jit(solution)/shard_map/reshape | solution.py:68
  157.5 3.4 pad_maximum_fusion
  160.9 5.2 %reshape.72 = bf16[24,65536]{1,0:T(8,128)(2,1)} reshape(bf16[2,1536,512]{2,1,0:T(8,128)(2,1)} %pad_maximum_fusion) | data formatting | bytes 6291456 | tf_op jit(solution)/shard_map/reshape | solution.py:57
  166.1 4.5 %convolution_convert_fusion.1 = bf16[24,65536]{1,0:T(8,128)(2,1)} fusion(bf16[24,65536]{1,0:T(8,128)(2,1)} %reshape.72, s32[24]{0:T(128)S(1)} %get-tuple-element.35, pred[24]{0:T(512)(128)(4,1)S(1)} %pad_add_fusion), kind=kOutput, calls=%fused_computation.3 | convolution fusion | flops 77071488 | bytes 6291576 | tf_op jit(solution)/shard_map/dot_general | solution.py:64
  170.6 5.2 %reshape.73 = bf16[3072,512]{1,0:T(8,128)(2,1)} reshape(bf16[24,65536]{1,0:T(8,128)(2,1)} %convolution_convert_fusion.1) | data formatting | bytes 6291456 | tf_op jit(solution)/shard_map/reshape | solution.py:68
  175.9 10.8 %fusion.50 = f32[1536,512]{1,0:T(8,128)} fusion(bf16[1536,3072]{1,0:T(8,128)(2,1)} %bitcast.52, bf16[3072,512]{1,0:T(8,128)(2,1)} %reshape.76), kind=kOutput, calls=%fused_computation.89 | convolution fusion | flops 4831838208 | bytes 15728640 | tf_op jit(solution)/shard_map/dot_general | solution.py:67
  186.7 0.0 slice-done.1
  186.7 6.8 %fusion.49 = f32[1536,512]{1,0:T(8,128)} fusion(bf16[1536,3072]{1,0:T(8,128)(2,1)S(1)} %bitcast.55, bf16[3072,512]{1,0:T(8,128)(2,1)S(1)} %copy-done.3), kind=kOutput, calls=%fused_computation.88 | convolution fusion | flops 4831838208 | bytes 15728640 | tf_op jit(solution)/shard_map/dot_general | solution.py:67
  193.5 0.0 all-reduce.9.cloned.1.call-update
  193.5 0.0 all-reduce.7.cloned.1.call-start
  193.6 0.6 fusion.43
  194.2 0.6 iota_compare_fusion.5
  194.8 0.7 iota_compare_fusion.2
  195.5 0.7 fusion.44
  196.2 0.1 broadcast_bitcast_fusion.1
  196.2 0.1 broadcast_bitcast_fusion
  196.3 81.0 %all-reduce.9.cloned.1.call-done = (f32[1536,512]{1,0:T(8,128)}, f32[1536,512]{1,0:T(8,128)}) async-done(((f32[1536,512]{1,0:T(8,128)}, f32[1536,512]{1,0:T(8,128)}), (f32[1536,512]{1,0:T(8,128)}, f32[1536,512]{1,0:T(8,128)})) %all-reduce.9.cloned.1.call-update) | async-done | bytes 6291472 | tf_op jit(solution)/shard_map/psum | solution.py:73
  277.3 3.5 multiply_convert_fusion
  280.8 2.2 reshape.77
  283.0 2.1 convolution_convert_fusion.2
  285.1 3.4 reshape.78
  288.5 2.9 fusion.9
  291.4 2.2 fusion.7
  293.6 0.0 copy-done
  293.6 2.9 fusion.2
  296.5 0.0 copy-start.4
  296.5 1.1 copy-done.4
  297.7 1.2 fusion.5
  298.9 0.0 all-reduce.7.cloned.1.call-update
  298.9 83.9 %all-reduce.7.cloned.1.call-done = (f32[64,512]{1,0:T(8,128)}, f32[64,512]{1,0:T(8,128)}, f32[64,512]{1,0:T(8,128)}) async-done(((f32[64,512]{1,0:T(8,128)}, f32[64,512]{1,0:T(8,128)}, f32[64,512]{1,0:T(8,128)}), (f32[64,512]{1,0:T(8,128)}, f32[64,512]{1,0:T(8,128)}, f32[64,512]{1,0:T(8,128)})) %all-reduce.7.cloned.1.call-update) | async-done | bytes 393232 | tf_op jit(solution)/shard_map/psum | solution.py:79
  382.8 0.9 sub.9
  383.8 0.0 copy-start.6
  383.8 1.2 fusion.4
  384.9 0.0 copy-start.7
  385.0 15.4 %all_gather.3 = bf16[512,512]{1,0:T(8,128)(2,1)S(1)} all-gather(bf16[64,512]{1,0:T(8,128)(2,1)S(1)} %fusion.4), channel_id=1, replica_groups=mesh['row'=16,'col'=8] {'col'}, dimensions={0}, use_global_device_ids=true | all-gather | bytes 589824 | tf_op jit(solution)/shard_map/all_gather | solution.py:106
  400.3 0.0 copy-done.9
  400.3 1.9 convolution_subtract_fusion
  (24 shorter events, 0.1 us)
Async XLA Ops:
  7.2 286.4 %copy-start = (bf16[512,512]{1,0:T(8,128)(2,1)S(1)}, bf16[512,512]{1,0:T(8,128)(2,1)}, u32[]{:S(2)}) copy-start(bf16[512,512]{1,0:T(8,128)(2,1)} %param.19) | copy-start | bytes 1572868
  7.2 131.4 %all-reduce.11.cloned.1.call-start = ((), (), s32[]{:S(2)}) async-start(), calls=%async_computation.2 | async-start | bytes 12582912 | tf_op jit(solution)/shard_map/psum | solution.py:14
  12.0 265.3 %all-reduce.9.cloned.1.call-start = ((), (), s32[]{:S(2)}) async-start(), calls=%async_computation.1 | async-start | bytes 12582912 | tf_op jit(solution)/shard_map/psum | solution.py:73
  22.8 10.6 %copy-start.10 = (s32[16]{0:T(128)S(1)}, s32[16]{0:T(128)}, u32[]{:S(2)}) copy-start(s32[16]{0:T(128)} %param.17) | copy-start | bytes 196
  22.8 10.6 %copy-start.11 = (s32[16]{0:T(128)S(1)}, s32[16]{0:T(128)}, u32[]{:S(2)}) copy-start(s32[16]{0:T(128)} %param.14) | copy-start | bytes 196
  152.2 5.3 %copy-start.5 = (bf16[1,1536,512]{2,1,0:T(8,128)(2,1)S(1)}, bf16[1,1536,512]{2,1,0:T(8,128)(2,1)}, u32[]{:S(2)}) copy-start(bf16[1,1536,512]{2,1,0:T(8,128)(2,1)} %get-tuple-element.11) | copy-start | bytes 4718596
  170.6 16.0 %slice-start = ((s8[9437184]{0:T(1024)(128)(4,1)}), s8[1048576]{0:T(1024)(128)(4,1)S(1)}, s32[]{:S(2)}) async-start(s8[9437184]{0:T(1024)(128)(4,1)} %bitcast.53), calls=%async_computation.3 | async-start | bytes 2097152
  175.9 10.8 %slice-start.1 = ((s8[9437184]{0:T(1024)(128)(4,1)}), s8[4194304]{0:T(1024)(128)(4,1)S(1)}, s32[]{:S(2)}) async-start(s8[9437184]{0:T(1024)(128)(4,1)} %bitcast.53), calls=%async_computation.4 | async-start | bytes 8388608
  175.9 10.8 %slice-start.2 = ((s8[9437184]{0:T(1024)(128)(4,1)}), s8[4194304]{0:T(1024)(128)(4,1)S(1)}, s32[]{:S(2)}) async-start(s8[9437184]{0:T(1024)(128)(4,1)} %bitcast.53), calls=%async_computation.5 | async-start | bytes 8388608
  175.9 10.8 %copy-start.3 = (bf16[3072,512]{1,0:T(8,128)(2,1)S(1)}, bf16[3072,512]{1,0:T(8,128)(2,1)}, u32[]{:S(2)}) copy-start(bf16[3072,512]{1,0:T(8,128)(2,1)} %reshape.73) | copy-start | bytes 9437188
  193.5 189.3 %all-reduce.7.cloned.1.call-start = ((), (), s32[]{:S(2)}) async-start(), calls=%async_computation | async-start | bytes 786432 | tf_op jit(solution)/shard_map/psum | solution.py:79
  285.1 6.3 %copy-start.1 = (bf16[1536,512]{1,0:T(8,128)(2,1)S(1)}, bf16[1536,512]{1,0:T(8,128)(2,1)}, u32[]{:S(2)}) copy-start(bf16[1536,512]{1,0:T(8,128)(2,1)} %param.18) | copy-start | bytes 4718596
  288.5 5.1 %copy-start.2 = (bf16[1536,512]{1,0:T(8,128)(2,1)S(1)}, bf16[1536,512]{1,0:T(8,128)(2,1)}, u32[]{:S(2)}) copy-start(bf16[1536,512]{1,0:T(8,128)(2,1)} %reshape.78) | copy-start | bytes 4718596
  293.6 89.2 %copy-start.8 = (f32[64,512]{1,0:T(8,128)S(1)}, f32[64,512]{1,0:T(8,128)}, u32[]{:S(2)}) copy-start(f32[64,512]{1,0:T(8,128)} %param.20) | copy-start | bytes 393220
  296.5 1.1 copy-start.4
  297.7 102.7 %copy-start.9 = (f32[64,512]{1,0:T(8,128)S(1)}, f32[64,512]{1,0:T(8,128)}, u32[]{:S(2)}) copy-start(f32[64,512]{1,0:T(8,128)} %param.21) | copy-start | bytes 393220
  383.8 18.4 %copy-start.6 = (f32[64,512]{1,0:T(8,128)}, f32[64,512]{1,0:T(8,128)S(1)}, u32[]{:S(2)}) copy-start(f32[64,512]{1,0:T(8,128)S(1)} %sub.9) | copy-start | bytes 393220
  384.9 17.3 %copy-start.7 = (bf16[64,512]{1,0:T(8,128)(2,1)}, bf16[64,512]{1,0:T(8,128)(2,1)S(1)}, u32[]{:S(2)}) copy-start(bf16[64,512]{1,0:T(8,128)(2,1)S(1)} %fusion.4) | copy-start | bytes 196612
Sparse Core Ops, SparseCore 0:
  12.3 126.2 all-reduce.10
  193.6 83.6 all-reduce.8
  299.0 83.7 all-reduce.6
where the time goes:
time: 410 us; the launch traced here: 409 us
  waiting for transfers between devices  248 us (60%)
  local copies, waits for them, and re-layouts  48.5 us (12%)
  other arithmetic  41.6 us (10%)
  matrix products  41 us (10%)
  blocking collectives  15.4 us (4%)
  between operations  13.9 us (3%)
    psum x1, waiting for transfers between devices, row_sums(): return lax.psum(pieces_in, 'row')  83.9 us
    psum x1, waiting for transfers between devices, spread_2(): return lax.psum(kept, axis)  83.3 us
    psum x1, waiting for transfers between devices, finish(): summed = lax.psum(partial_value, 'col')  81 us
    gather x2, local copies, waits for them, and re-layouts, partial_product(): jnp.take(slab_blocks, own_rows, axis=0)  19.9 us
    dot_general x2, matrix products, partial_product(): jnp.dot(row_slab, spread.reshape(col_blocks * BS, W), preferred_element_t...  17.6 us
    select_n x3, other arithmetic, partial_product(): jnp.take(slab_blocks, own_rows, axis=0)  17.1 us
    all_gather x1, blocking collectives, on_device(): top_whole = lax.all_gather(top_b, 'col', axis=0, tiled=True)  15.4 us
    another operation x3, other arithmetic, partial_product(): received = jnp.stack(pieces).reshape(fanout * PAD, BS * W)  12 us
  transfers between devices with their start and end apart: 3, of which 3 were waited for; matrix products, arithmetic and copies ran while one was open for 11% of the time, Pallas kernels for 0%

commit v1 on v0

v1 whole, which is shorter than its diff:
```python
import functools

import jax
import jax.numpy as jnp
from jax import lax
from jax.experimental import pallas as pl
from jax.experimental.pallas import tpu as pltpu
from jax.sharding import PartitionSpec as P

BS = 128
W = 512
NB = 12
HALF = NB // 2
ROWS = NB * BS
SIDE = 4
PART = 64
BOTH = ("row", "col")
VMEM_LIMIT = 56 * 1024 * 1024
BF = jnp.bfloat16
F32 = jnp.float32


def device(z, y, x, core):
    return ((z % SIDE) * SIDE + y % SIDE) * 8 + (x % SIDE) * 2 + core % 2


def all_places():
    return [
        (z, y, x, core)
        for z in range(SIDE)
        for y in range(SIDE)
        for x in range(SIDE)
        for core in range(2)
    ]


def shifted(dz=0, dy=0, dx=0, dc=0):
    return [
        (device(z, y, x, c), device(z + dz, y + dy, x + dx, c + dc))
        for z, y, x, c in all_places()
    ]


def spread_pairs(along_z):
    pairs = []
    for z, y, x, core in all_places():
        owner = z * SIDE + y
        plane, second = owner % 8, owner // 8
        far = (2 - (x - plane // 2)) % SIDE
        if along_z:
            to_z, to_y = z + core, y + far
        else:
            to_z, to_y = z + far, y + 2 * second + core
        pairs.append((device(z, y, x, core), device(to_z, to_y, plane // 2, plane % 2)))
    return pairs


def params(**more):
    return pltpu.CompilerParams(vmem_limit_bytes=VMEM_LIMIT, **more)


def cost(flops, moved):
    return pl.CostEstimate(flops=flops, bytes_accessed=moved, transcendentals=0)


def whole(shape):
    return pl.BlockSpec(shape, lambda *_: (0,) * len(shape))


def find_slot(rows, counts, owner, block):
    slot = jnp.int32(0)
    live = jnp.int32(0)
    for k in range(NB):
        hit = (rows[owner, k] == block) & (k < counts[owner])
        slot = jnp.where(hit, k, slot)
        live = jnp.where(hit, 1, live)
    return slot, live


def prep_body(place, rows_a, counts_a, rows_b, counts_b, fa, fb, top, a_lo, a_hi, b_lo, b_hi, top_t):
    owner = place[0]
    for rows, counts, factor, low, high in (
        (rows_a, counts_a, fa, a_lo, a_hi),
        (rows_b, counts_b, fb, b_lo, b_hi),
    ):
        for block in range(NB):
            slot, live = find_slot(rows, counts, owner, block)
            piece = factor[pl.ds(pl.multiple_of(slot * BS, BS), BS), :]
            piece = jnp.where(live > 0, piece, jnp.zeros_like(piece))
            target = low if block < HALF else high
            target[block % HALF] = piece.T
    top_t[...] = top[...].T


def prep(place, lists, factor_a, factor_b, factor_top):
    quarter = jax.ShapeDtypeStruct((HALF, 2 * BS, BS), BF)
    half_width = pl.BlockSpec((ROWS, W // 2), lambda i, place, *_: (0, place[1] % 2))
    return pl.pallas_call(
        prep_body,
        name="prep",
        grid_spec=pltpu.PrefetchScalarGridSpec(
            num_scalar_prefetch=5,
            grid=(1,),
            in_specs=[half_width, half_width, whole((W, W))],
            out_specs=[whole((HALF, 2 * BS, BS))] * 4 + [whole((W, W))],
        ),
        out_shape=[quarter] * 4 + [jax.ShapeDtypeStruct((W, W), BF)],
        compiler_params=params(),
        cost_estimate=cost(0, 4 * ROWS * W),
    )(place, *lists, factor_a, factor_b, factor_top)


def product_body(corrected, place, *refs):
    bufs = refs[:8]
    if corrected:
        tile, top_t, before, full, give, spread, sems = refs[8:]
    else:
        tile, full, give, spread, sems = refs[8:]
    core = place[1] % 2
    zc, yc = (place[1] // SIDE) % SIDE, place[1] % SIDE
    z, y = place[0] // SIDE, place[0] % SIDE

    @pl.when(pl.program_id(0) == 0)
    def _():
        copies = []
        for i in range(8):
            steps = i % 4
            q = ((z - zc) if i < 4 else (y - yc)) - steps + 2 * SIDE
            q = q % SIDE
            first = 0 if i < 4 else HALF
            copies.append(
                pltpu.make_async_copy(
                    bufs[i],
                    spread.at[
                        pl.ds(first, HALF),
                        q // 2,
                        pl.ds(pl.multiple_of((q % 2) * 2 * BS, 2 * BS), 2 * BS),
                        :,
                    ],
                    sems.at[i],
                )
            )
        for copy in copies:
            copy.start()
        for copy in copies:
            copy.wait()

    for part in range(2):
        at = slice(part * 2 * BS, (part + 1) * 2 * BS)
        left = jnp.concatenate(
            [spread[n, h, at, :] for n in range(NB) for h in range(2)], axis=1
        )
        value = lax.dot_general(
            left, tile[...], (((1,), (1,)), ((), ())), preferred_element_type=F32
        )
        if corrected:
            value = value - jnp.dot(
                top_t[at, :], before[...], preferred_element_type=F32
            )
        full[at, :] = value.astype(BF)
    for xs in range(SIDE):
        give[xs] = full[pl.ds(pl.multiple_of(xs * BS + (1 - core) * PART, PART), PART), :]


def product(place, bufs, trailing, correction=None):
    width = 2 * BS
    steps = ROWS // width
    in_specs = [pl.BlockSpec(memory_space=pl.ANY)] * 8 + [
        pl.BlockSpec((width, trailing.shape[1]), lambda i, *_: (i, 0))
    ]
    operands = [*bufs, trailing]
    if correction is not None:
        in_specs += [whole((W, W)), pl.BlockSpec((W, width), lambda i, *_: (0, i))]
        operands += list(correction)
    return pl.pallas_call(
        functools.partial(product_body, correction is not None),
        name="product",
        grid_spec=pltpu.PrefetchScalarGridSpec(
            num_scalar_prefetch=1,
            grid=(steps,),
            in_specs=in_specs,
            out_specs=[
                pl.BlockSpec((W, width), lambda i, *_: (0, i)),
                pl.BlockSpec((SIDE, PART, width), lambda i, *_: (0, 0, i)),
            ],
            scratch_shapes=[
                pltpu.VMEM((NB, 2, W, BS), BF),
                pltpu.SemaphoreType.DMA((8,)),
            ],
        ),
        out_shape=[
            jax.ShapeDtypeStruct((W, ROWS), BF),
            jax.ShapeDtypeStruct((SIDE, PART, ROWS), BF),
        ],
        compiler_params=params(dimension_semantics=("arbitrary",)),
        cost_estimate=cost(2 * W * ROWS * 2 * ROWS, 2 * ROWS * 2 * ROWS + 6 * W * ROWS),
    )(place, *operands)


def pair_body(place, full, taken, *outs):
    core, x = place[1] % 2, place[1] // 2
    for i in range(SIDE):
        xs = (x + i) % SIDE
        mine = full[pl.ds(pl.multiple_of(xs * BS + core * PART, PART), PART), :]
        outs[i][...] = (mine.astype(F32) + taken[xs].astype(F32)).astype(BF)


def pair_sum(place, full, taken):
    return pl.pallas_call(
        pair_body,
        name="pair_sum",
        grid_spec=pltpu.PrefetchScalarGridSpec(
            num_scalar_prefetch=1,
            grid=(1,),
            in_specs=[whole((W, ROWS)), whole((SIDE, PART, ROWS))],
            out_specs=[whole((PART, ROWS))] * SIDE,
        ),
        out_shape=[jax.ShapeDtypeStruct((PART, ROWS), BF)] * SIDE,
        compiler_params=params(),
        cost_estimate=cost(W * ROWS, 3 * W * ROWS),
    )(place, full, taken)


def cut(outcome, pieces, first):
    rows = outcome.shape[0] // SIDE
    for p in range(16):
        up, across = p // SIDE, p % SIDE
        pieces[p] = outcome[up * rows : (up + 1) * rows, across * BS : (across + 1) * BS].astype(BF)


def slots_body(with_a, place, rows_a, counts_a, rows_b, counts_b, *refs):
    if with_a:
        s0, s1, s2, s3, fa, fb, column, pieces, natural, carried = refs
    else:
        s0, s1, s2, s3, fb, column, pieces, natural = refs
    owner = place[0]
    total = (s0[...].astype(F32) + s1[...].astype(F32)) + (
        s2[...].astype(F32) + s3[...].astype(F32)
    )
    natural[...] = (-total).astype(BF)

    def place_slots(rows, counts, target):
        for k in range(NB):
            block = rows[owner, k]
            piece = natural[:, pl.ds(pl.multiple_of(block * BS, BS), BS)]
            target[:, k * BS : (k + 1) * BS] = jnp.where(
                k < counts[owner], piece, jnp.zeros_like(piece)
            )

    if with_a:
        place_slots(rows_a, counts_a, column)
        place_slots(rows_b, counts_b, carried)
        first = jnp.dot(column[...], fa[...], preferred_element_type=F32)
        second = jnp.dot(carried[...], fb[...], preferred_element_type=F32)
        cut(jnp.concatenate([first, second], axis=0), pieces, 0)
    else:
        place_slots(rows_b, counts_b, column)
        cut(jnp.dot(column[...], fb[...], preferred_element_type=F32), pieces, 0)


def slots(place, lists, slabs, factors):
    with_a = len(factors) == 2
    rows = PART * len(factors) // SIDE
    return pl.pallas_call(
        functools.partial(slots_body, with_a),
        name="slots",
        grid_spec=pltpu.PrefetchScalarGridSpec(
            num_scalar_prefetch=5,
            grid=(1,),
            in_specs=[whole((PART, ROWS))] * SIDE + [whole((ROWS, W))] * len(factors),
            out_specs=[whole((PART, ROWS)), whole((16, rows, BS))],
            scratch_shapes=[pltpu.VMEM((PART, ROWS), BF)] * len(factors),
        ),
        out_shape=[
            jax.ShapeDtypeStruct((PART, ROWS), BF),
            jax.ShapeDtypeStruct((16, rows, BS), BF),
        ],
        compiler_params=params(),
        cost_estimate=cost(
            2 * PART * ROWS * W * len(factors), 2 * ROWS * W * len(factors) + 10 * PART * ROWS
        ),
    )(place, *lists, *slabs, *factors)


def column_body(place, *refs):
    slabs, out, scratch = refs[:8], refs[8], refs[9]
    core, x = place[1] % 2, place[1] // 2
    for i in range(8):
        xs = (x - i % SIDE + SIDE) % SIDE
        which = core if i < SIDE else 1 - core
        scratch[pl.ds(pl.multiple_of(xs * BS + which * PART, PART), PART), :] = slabs[i][...]
    out[...] = scratch[...].T


def whole_column(place, slabs):
    lanes = 4 * BS
    return pl.pallas_call(
        column_body,
        name="whole_column",
        grid_spec=pltpu.PrefetchScalarGridSpec(
            num_scalar_prefetch=1,
            grid=(ROWS // lanes,),
            in_specs=[pl.BlockSpec((PART, lanes), lambda i, *_: (0, i))] * 8,
            out_specs=pl.BlockSpec((lanes, W), lambda i, *_: (i, 0)),
            scratch_shapes=[pltpu.VMEM((W, lanes), BF)],
        ),
        out_shape=jax.ShapeDtypeStruct((ROWS, W), BF),
        compiler_params=params(dimension_semantics=("arbitrary",)),
        cost_estimate=cost(0, 4 * ROWS * W),
    )(place, *slabs)


def send(value, **by):
    return lax.ppermute(value, BOTH, shifted(**by))


def gather_factor(low, high):
    low = lax.ppermute(low, BOTH, spread_pairs(True))
    high = lax.ppermute(high, BOTH, spread_pairs(False))
    lows = [low, send(low, dz=1), send(low, dz=2), send(low, dz=-1)]
    highs = [high, send(high, dy=1), send(high, dy=2), send(high, dy=-1)]
    return lows + highs


def scatter_sum(place, full, give):
    taken = send(give, dc=1)
    own, one, two, three = pair_sum(place, full, taken)
    return [own, send(one, dx=1), send(two, dx=2), send(three, dx=-1)]


def gather_column(place, column):
    mine = [column, send(column, dx=1), send(column, dx=2), send(column, dx=-1)]
    return whole_column(place, mine + [send(slab, dc=1) for slab in mine])


def row_sum(pieces):
    count, rows, lanes = pieces.shape
    parts = lax.all_to_all(pieces, "row", 0, 0)
    summed = jnp.sum(parts.astype(F32), axis=0).astype(BF)
    spread = jnp.broadcast_to(summed[None], pieces.shape)
    got = lax.all_to_all(spread, "row", 0, 0)
    got = got.reshape(SIDE, SIDE, rows, lanes).transpose(0, 2, 1, 3)
    return got.reshape(SIDE * rows, W).astype(F32)


def on_device(
    trailing, rows_a, counts_a, factor_a, rows_b, counts_b, factor_b, factor_top, base_a, base_b
):
    place = jnp.stack([lax.axis_index("row"), lax.axis_index("col")]).astype(jnp.int32)
    lists = (rows_a, counts_a, rows_b, counts_b)
    a_lo, a_hi, b_lo, b_hi, top_t = prep(place, lists, factor_a, factor_b, factor_top)
    bufs_a = gather_factor(a_lo, a_hi)
    bufs_b = gather_factor(b_lo, b_hi)
    full_a, give_a = product(place, bufs_a, trailing)
    slabs_a = scatter_sum(place, full_a, give_a)
    full_b, give_b = product(place, bufs_b, trailing, (top_t, full_a))
    slabs_b = scatter_sum(place, full_b, give_b)

    part_a, pieces_a = slots(place, lists, slabs_a, (factor_a, factor_b))
    column_a = gather_column(place, part_a)
    sums_a = row_sum(pieces_a)
    diag_a = base_a - sums_a[:PART]
    top_b = (
        -(
            sums_a[PART:]
            + jnp.dot(diag_a, factor_top.astype(F32), precision=lax.Precision.HIGHEST)
        )
    ).astype(BF)
    blocks = top_b.reshape(PART, 8, PART).transpose(1, 0, 2)
    top_cols = lax.all_to_all(blocks, "col", 0, 0).reshape(W, PART)

    part_b, pieces_b = slots(place, lists, slabs_b, (factor_b,))
    column_b = gather_column(place, part_b)
    cross = lax.dot_general(
        top_cols, factor_top, (((0,), (0,)), ((), ())), preferred_element_type=F32
    )
    diag_b = base_b - row_sum(pieces_b) - cross
    return (column_a, diag_a, column_b, top_b, diag_b)


def solution(mesh):
    in_specs = (
        P("row", "col"),
        P(),
        P(),
        P("row", None),
        P(),
        P(),
        P("row", None),
        P(),
        P("col", None),
        P("col", None),
    )
    out_specs = (P("row", None), P("col", None), P("row", None), P("col", None), P("col", None))
    return jax.shard_map(
        on_device, mesh=mesh, in_specs=in_specs, out_specs=out_specs, check_vma=False
    )
```

time: 410 us -> 274 us (0.67)
  waiting for transfers between devices: 248 us -> 110 us
  starting transfers between devices: 0.12 us -> 96.2 us
  Pallas kernels: 0 us -> 53.6 us
  other arithmetic: 41.6 us -> 0.7 us
  matrix products: 41 us -> 1.26 us
  local copies, waits for them, and re-layouts: 48.5 us -> 9.51 us
  blocking collectives: 15.4 us -> 0 us
  between operations: 13.9 us -> 1.3 us
    psum x3 -> x0, waiting for transfers between devices: 248 us -> none  [the longest x1 83.9 us: row_sums(): return lax.psum(pieces_in, 'row')]
    ppermute x0 -> x38, waiting for transfers between devices: none -> 95.2 us  [the longest x2 48.1 us: gather_factor(): high = lax.ppermute(high, BOTH, spread_pairs(False))]
    ppermute x0 -> x38, starting transfers between devices: none -> 64.9 us  [the longest x34 52.5 us: send(): return lax.ppermute(value, BOTH, shifted(**by))]
    pallas_call x0 -> x9, Pallas kernels: none -> 53.6 us  [the longest x2 25.3 us: product(): pl.pallas_call(functools.partial(product_body, correction is not None), n...]
    dot_general x11 -> x2, matrix products: 41 us -> 1.26 us  [the longest x1 0.86 us: on_device(): lax.dot_general(top_cols, factor_top, (((0,), (0,)), ((), ())), preferred...]
    all_to_all x0 -> x5, starting transfers between devices: none -> 31.3 us  [the longest x2 15 us: row_sum(): parts = lax.all_to_all(pieces, 'row', 0, 0)]
    reshape x6 -> x2, local copies, waits for them, and re-layouts: 26.6 us -> 0.26 us  [the longest x1 0.14 us: on_device(): top_cols = lax.all_to_all(blocks, 'col', 0, 0).reshape(W, PART)]
    gather x2 -> x0, local copies, waits for them, and re-layouts: 19.9 us -> none  [partial_product(): jnp.take(slab_blocks, own_rows, axis=0)]
  transfers between devices with their start and end apart: 3 -> 43, of which waited for: 3 -> 9; matrix products, arithmetic and copies ran while one was open for 11% -> 1% of each run, Pallas kernels for 0% -> 16%
where the time goes in v1:
time: 274 us; the launch traced here: 272 us
  waiting for transfers between devices  110 us (40%)
  starting transfers between devices  96.2 us (35%)
  Pallas kernels  53.6 us (20%)
  local copies, waits for them, and re-layouts  9.51 us (3%)
    ppermute x34, starting transfers between devices, send(): return lax.ppermute(value, BOTH, shifted(**by))  52.5 us
    ppermute x2, waiting for transfers between devices, gather_factor(): high = lax.ppermute(high, BOTH, spread_pairs(False))  48.1 us
    ppermute x2, waiting for transfers between devices, gather_factor(): low = lax.ppermute(low, BOTH, spread_pairs(True))  35.7 us
    pallas_call x2, Pallas kernels, product(): pl.pallas_call(functools.partial(product_body, correction is not None), n...  25.3 us
    all_to_all x2, starting transfers between devices, row_sum(): parts = lax.all_to_all(pieces, 'row', 0, 0)  15 us
    ppermute x34, waiting for transfers between devices, send(): return lax.ppermute(value, BOTH, shifted(**by))  11.4 us
    all_to_all x2, starting transfers between devices, row_sum(): got = lax.all_to_all(spread, 'row', 0, 0)  10.3 us
    ppermute x2, starting transfers between devices, gather_factor(): low = lax.ppermute(low, BOTH, spread_pairs(True))  9.1 us
  transfers between devices with their start and end apart: 43, of which 9 were waited for; matrix products, arithmetic and copies ran while one was open for 1% of the time, Pallas kernels for 16%

profile of v1, /device:TPU:1, one launch (start us, length us, event | category | flops | bytes accessed | tf_op | source)
XLA Modules:
  0.0 272.1 jit_solution(14599074279885740859)
XLA Ops:
  0.6 0.6 pad_add_fusion.place
  1.2 4.3 %prep.1 = (bf16[6,256,128]{2,1,0:T(8,128)(2,1)}, bf16[6,256,128]{2,1,0:T(8,128)(2,1)}, bf16[6,256,128]{2,1,0:T(8,128)(2,1)}, bf16[6,256,128]{2,1,0:T(8,128)(2,1)}, bf16[512,512]{1,0:T(8,128)(2,1)}) custom-call(s32[2]{0:T(128)} %pad_add_fusion.place, s32[16,12]{1,0:T(8,128)} %rows_a.5, s32[16]{0:T(128)} %counts_a.5, s32[16,12]{1,0:T(8,128)} %rows_b.5, ...), custom_call_target="tpu_custom_call" | custom-call | bytes 3145728 | tf_op jit(solution)/shard_map/prep/pallas_call | solution.py:98
  5.5 5.7 %collective-permute-start = (bf16[6,256,128]{2,1,0:T(8,128)(2,1)}, bf16[6,256,128]{2,1,0:T(8,128)(2,1)S(1)}, u32[]{:S(2)}, u32[]{:S(2)}) collective-permute-start(bf16[6,256,128]{2,1,0:T(8,128)(2,1)} %get-tuple-element.26), channel_id=1, source_target_pairs={{0,16},{1,48},{2,8},{3,40},{4,0},{5,32},{6,24},{7,56},{8,25},{9,57... | collective-permute-start | bytes 1179656 | tf_op jit(solution)/shard_map/ppermute | solution.py:318
  11.2 2.1 collective-permute-start.4
  13.3 3.4 %collective-permute-start.19 = (bf16[6,256,128]{2,1,0:T(8,128)(2,1)}, bf16[6,256,128]{2,1,0:T(8,128)(2,1)S(1)}, u32[]{:S(2)}, u32[]{:S(2)}) collective-permute-start(bf16[6,256,128]{2,1,0:T(8,128)(2,1)} %get-tuple-element.36), channel_id=1, source_target_pairs={{0,16},{1,48},{2,8},{3,40},{4,0},{5,32},{6,24},{7,56},{8,25},{9,57... | collective-permute-start | bytes 1179656 | tf_op jit(solution)/shard_map/ppermute | solution.py:318
  16.7 1.3 collective-permute-start.23
  18.0 35.7 %collective-permute-done.refs_0_ = bf16[6,256,128]{2,1,0:T(8,128)(2,1)S(1)} collective-permute-done((bf16[6,256,128]{2,1,0:T(8,128)(2,1)}, bf16[6,256,128]{2,1,0:T(8,128)(2,1)S(1)}, u32[]{:S(2)}, u32[]{:S(2)}) %collective-permute-start) | collective-permute-done | bytes 393248 | tf_op jit(solution)/shard_map/ppermute | solution.py:318
  53.7 1.8 collective-permute-start.1
  55.5 17.2 %collective-permute-start.2 = (bf16[6,256,128]{2,1,0:T(8,128)(2,1)S(1)}, bf16[6,256,128]{2,1,0:T(8,128)(2,1)S(1)}, u32[]{:S(2)}, u32[]{:S(2)}) collective-permute-start(bf16[6,256,128]{2,1,0:T(8,128)(2,1)S(1)} %collective-permute-done.refs_0_), channel_id=1, source_target_pairs={{0,64},{1,65},{2,66},{3,67},{4,68},{5,69},{6,70},{7,71},{8,72},{9,... | collective-permute-start | bytes 1179656 | tf_op jit(solution)/shard_map/ppermute | solution.py:314
  72.7 31.7 %collective-permute-done.4.refs_4_ = bf16[6,256,128]{2,1,0:T(8,128)(2,1)S(1)} collective-permute-done((bf16[6,256,128]{2,1,0:T(8,128)(2,1)}, bf16[6,256,128]{2,1,0:T(8,128)(2,1)S(1)}, u32[]{:S(2)}, u32[]{:S(2)}) %collective-permute-start.4) | collective-permute-done | bytes 393248 | tf_op jit(solution)/shard_map/ppermute | solution.py:319
  104.5 16.4 %collective-permute-done.23.refs_4_ = bf16[6,256,128]{2,1,0:T(8,128)(2,1)S(1)} collective-permute-done((bf16[6,256,128]{2,1,0:T(8,128)(2,1)}, bf16[6,256,128]{2,1,0:T(8,128)(2,1)S(1)}, u32[]{:S(2)}, u32[]{:S(2)}) %collective-permute-start.23) | collective-permute-done | bytes 393248 | tf_op jit(solution)/shard_map/ppermute | solution.py:319
  120.9 2.1 collective-permute-start.7
  123.0 0.3 collective-permute-start.21
  123.4 2.4 collective-permute-start.22
  125.8 3.3 %collective-permute-done.6.refs_6_ = bf16[6,256,128]{2,1,0:T(8,128)(2,1)S(1)} collective-permute-done((bf16[6,256,128]{2,1,0:T(8,128)(2,1)S(1)}, bf16[6,256,128]{2,1,0:T(8,128)(2,1)S(1)}, u32[]{:S(2)}, u32[]{:S(2)}) %collective-permute-start.6) | collective-permute-done | bytes 393248 | tf_op jit(solution)/shard_map/ppermute | solution.py:314
  129.0 8.0 %collective-permute-done.7.refs_7_ = bf16[6,256,128]{2,1,0:T(8,128)(2,1)S(1)} collective-permute-done((bf16[6,256,128]{2,1,0:T(8,128)(2,1)S(1)}, bf16[6,256,128]{2,1,0:T(8,128)(2,1)S(1)}, u32[]{:S(2)}, u32[]{:S(2)}) %collective-permute-start.7) | collective-permute-done | bytes 393248 | tf_op jit(solution)/shard_map/ppermute | solution.py:314
  137.1 3.6 %collective-permute-start.26 = (bf16[6,256,128]{2,1,0:T(8,128)(2,1)S(1)}, bf16[6,256,128]{2,1,0:T(8,128)(2,1)S(1)}, u32[]{:S(2)}, u32[]{:S(2)}) collective-permute-start(bf16[6,256,128]{2,1,0:T(8,128)(2,1)S(1)} %collective-permute-done.23.refs_4_), channel_id=1, source_target_pairs={{0,24},{1,25},{2,26},{3,27},{4,28},{5,29},{6,30},{7,31},{8,0},{9,1... | collective-permute-start | bytes 1179656 | tf_op jit(solution)/shard_map/ppermute | solution.py:314
  140.8 12.3 %product.2 = (bf16[512,1536]{1,0:T(8,128)(2,1)}, bf16[4,64,1536]{2,1,0:T(8,128)(2,1)}) custom-call(s32[2]{0:T(128)} %pad_add_fusion.place, bf16[6,256,128]{2,1,0:T(8,128)(2,1)} %copy-done.30, bf16[6,256,128]{2,1,0:T(8,128)(2,1)} %copy-done.32, bf16[6,256,128]{2,1,0:T(8,128)(2,1)} %copy-done.33, bf16[6,256,128]{2,1,0:T(8,128)(2,1)} %copy-done.35, ...), custom_call_target="tpu_custom_call" | custom-call | flops 4831838208 | bytes 14155776 | tf_op jit(solution)/shard_map/product/pallas_call | solution.py:175
  153.3 0.6 copy-done.36
  154.1 0.2 copy-done.40
  154.3 0.2 copy-done.43
  154.5 13.0 %product.3 = (bf16[512,1536]{1,0:T(8,128)(2,1)}, bf16[4,64,1536]{2,1,0:T(8,128)(2,1)}) custom-call(s32[2]{0:T(128)} %pad_add_fusion.place, bf16[6,256,128]{2,1,0:T(8,128)(2,1)} %copy-done.28, bf16[6,256,128]{2,1,0:T(8,128)(2,1)} %copy-done.34, bf16[6,256,128]{2,1,0:T(8,128)(2,1)} %copy-done.36, bf16[6,256,128]{2,1,0:T(8,128)(2,1)} %copy-done.38, ...), custom_call_target="tpu_custom_call" | custom-call | flops 4831838208 | bytes 14155776 | tf_op jit(solution)/shard_map/product/pallas_call | solution.py:175
  167.5 0.6 collective-permute-start.27
  168.0 0.9 copy-done.1
  168.9 3.3 %pair_sum.2 = (bf16[64,1536]{1,0:T(8,128)(2,1)}, bf16[64,1536]{1,0:T(8,128)(2,1)}, bf16[64,1536]{1,0:T(8,128)(2,1)}, bf16[64,1536]{1,0:T(8,128)(2,1)}) custom-call(s32[2]{0:T(128)} %pad_add_fusion.place, bf16[512,1536]{1,0:T(8,128)(2,1)} %get-tuple-element.28.full.refs_10_, bf16[4,64,1536]{2,1,0:T(8,128)(2,1)} %copy-done.1), custom_call_target="tpu_custom_call" | custom-call | flops 786432 | bytes 2359296 | tf_op jit(solution)/shard_map/pair_sum/pallas_call | solution.py:209
  172.2 5.8 %collective-permute-start.11 = (bf16[64,1536]{1,0:T(8,128)(2,1)}, bf16[64,1536]{1,0:T(8,128)(2,1)S(1)}, u32[]{:S(2)}, u32[]{:S(2)}) collective-permute-start(bf16[64,1536]{1,0:T(8,128)(2,1)} %get-tuple-element.33), channel_id=1, source_target_pairs={{0,6},{1,7},{2,0},{3,1},{4,2},{5,3},{6,4},{7,5},{8,14},{9,15},{10,... | collective-permute-start | bytes 589832 | tf_op jit(solution)/shard_map/ppermute | solution.py:314
  178.0 0.9 copy-done.2
  178.9 3.3 %pair_sum.3 = (bf16[64,1536]{1,0:T(8,128)(2,1)}, bf16[64,1536]{1,0:T(8,128)(2,1)}, bf16[64,1536]{1,0:T(8,128)(2,1)}, bf16[64,1536]{1,0:T(8,128)(2,1)}) custom-call(s32[2]{0:T(128)} %pad_add_fusion.place, bf16[512,1536]{1,0:T(8,128)(2,1)} %get-tuple-element.39.full, bf16[4,64,1536]{2,1,0:T(8,128)(2,1)} %copy-done.2), custom_call_target="tpu_custom_call" | custom-call | flops 786432 | bytes 2359296 | tf_op jit(solution)/shard_map/pair_sum/pallas_call | solution.py:209
  182.2 3.9 %collective-permute-start.29 = (bf16[64,1536]{1,0:T(8,128)(2,1)}, bf16[64,1536]{1,0:T(8,128)(2,1)S(1)}, u32[]{:S(2)}, u32[]{:S(2)}) collective-permute-start(bf16[64,1536]{1,0:T(8,128)(2,1)} %get-tuple-element.43), channel_id=1, source_target_pairs={{0,4},{1,5},{2,6},{3,7},{4,0},{5,1},{6,2},{7,3},{8,12},{9,13},{10,... | collective-permute-start | bytes 589832 | tf_op jit(solution)/shard_map/ppermute | solution.py:314
  186.1 0.6 copy-done.5
  186.8 4.7 %slots.2 = (bf16[64,1536]{1,0:T(8,128)(2,1)}, bf16[16,32,128]{2,1,0:T(8,128)(2,1)}) custom-call(s32[2]{0:T(128)} %pad_add_fusion.place, s32[16,12]{1,0:T(8,128)} %rows_a.5, s32[16]{0:T(128)} %counts_a.5, s32[16,12]{1,0:T(8,128)} %rows_b.5, s32[16]{0:T(128)} %counts_b.5, bf16[64,1536]{1,0:T(8,128)(2,1)} %get-tuple-element.30.refs_0_, ...), custom_call_target="tpu_custom_call" | custom-call | flops 201326592 | bytes 4128768 | tf_op jit(solution)/shard_map/slots/pallas_call | solution.py:264
  191.5 10.3 %all-to-all-start = ((bf16[16,32,128]{2,1,0:T(8,128)(2,1)}), bf16[16,32,128]{2,1,0:T(8,128)(2,1)S(1)}, u32[]{:S(2)}, u32[]{:S(2)}) async-start(bf16[16,32,128]{2,1,0:T(8,128)(2,1)} %get-tuple-element.35), calls=%async_computation | async-start | bytes 262144 | tf_op jit(solution)/shard_map/all_to_all | solution.py:338
  201.9 0.6 copy-done.8
  202.7 3.9 %slots.3 = (bf16[64,1536]{1,0:T(8,128)(2,1)}, bf16[16,16,128]{2,1,0:T(8,128)(2,1)}) custom-call(s32[2]{0:T(128)} %pad_add_fusion.place, s32[16,12]{1,0:T(8,128)} %rows_a.5, s32[16]{0:T(128)} %counts_a.5, s32[16,12]{1,0:T(8,128)} %rows_b.5, s32[16]{0:T(128)} %counts_b.5, bf16[64,1536]{1,0:T(8,128)(2,1)} %get-tuple-element.41.refs_0_, ...), custom_call_target="tpu_custom_call" | custom-call | flops 100663296 | bytes 2555904 | tf_op jit(solution)/shard_map/slots/pallas_call | solution.py:264
  206.6 2.1 all-to-all-done
  208.7 4.7 %all-to-all-start.2 = ((bf16[16,16,128]{2,1,0:T(8,128)(2,1)}), bf16[16,16,128]{2,1,0:T(8,128)(2,1)S(1)}, u32[]{:S(2)}, u32[]{:S(2)}) async-start(bf16[16,16,128]{2,1,0:T(8,128)(2,1)} %get-tuple-element.46), calls=%async_computation.2 | async-start | bytes 131072 | tf_op jit(solution)/shard_map/all_to_all | solution.py:338
  213.4 6.5 %all-to-all-done.2 = bf16[16,16,128]{2,1,0:T(8,128)(2,1)S(1)} async-done(((bf16[16,16,128]{2,1,0:T(8,128)(2,1)}), bf16[16,16,128]{2,1,0:T(8,128)(2,1)S(1)}, u32[]{:S(2)}, u32[]{:S(2)}) %all-to-all-start.2) | async-done | bytes 65568 | tf_op jit(solution)/shard_map/all_to_all | solution.py:338
  219.9 0.7 broadcast_in_dim.4
  220.6 3.5 %all-to-all-start.1 = ((bf16[16,32,128]{2,1,0:T(8,128)(2,1)}), bf16[16,32,128]{2,1,0:T(8,128)(2,1)S(1)}, u32[]{:S(2)}, u32[]{:S(2)}) async-start(bf16[16,32,128]{2,1,0:T(8,128)(2,1)} %broadcast_in_dim.4), calls=%async_computation.1 | async-start | bytes 262144 | tf_op jit(solution)/shard_map/all_to_all | solution.py:341
  224.1 1.5 collective-permute-start.31
  225.6 1.5 collective-permute-start.32
  227.1 1.8 collective-permute-start.33
  228.9 4.0 %collective-permute-start.34 = (bf16[64,1536]{1,0:T(8,128)(2,1)}, bf16[64,1536]{1,0:T(8,128)(2,1)S(1)}, u32[]{:S(2)}, u32[]{:S(2)}) collective-permute-start(bf16[64,1536]{1,0:T(8,128)(2,1)} %get-tuple-element.45.refs_0_), channel_id=1, source_target_pairs={{0,1},{1,0},{2,3},{3,2},{4,5},{5,4},{6,7},{7,6},{8,9},{9,8},{10,11... | collective-permute-start | bytes 589832 | tf_op jit(solution)/shard_map/ppermute | solution.py:314
  232.9 0.6 broadcast_in_dim.5
  233.6 6.8 %all-to-all-start.3 = ((bf16[16,16,128]{2,1,0:T(8,128)(2,1)}), bf16[16,16,128]{2,1,0:T(8,128)(2,1)S(1)}, u32[]{:S(2)}, u32[]{:S(2)}) async-start(bf16[16,16,128]{2,1,0:T(8,128)(2,1)} %broadcast_in_dim.5), calls=%async_computation.3 | async-start | bytes 131072 | tf_op jit(solution)/shard_map/all_to_all | solution.py:341
  240.7 0.4 fusion.1
  241.2 0.8 reshape.36
  242.0 1.6 collective-permute-start.13
  243.7 1.1 collective-permute-start.14
  244.8 1.1 collective-permute-start.35
  246.0 0.9 all-to-all-done.3
  246.9 5.9 %all-to-all-start.4 = ((bf16[8,2,2048]{2,1,0:T(2,128)(2,1)}), bf16[8,2,2048]{2,1,0:T(2,128)(2,1)S(1)}, u32[]{:S(2)}, u32[]{:S(2)}) async-start(bf16[8,2,2048]{2,1,0:T(2,128)(2,1)} %reshape.36), calls=%async_computation.4 | async-start | bytes 131072 | tf_op jit(solution)/shard_map/all_to_all | solution.py:370
  252.9 4.8 %all-to-all-done.4 = bf16[8,2,2048]{2,1,0:T(2,128)(2,1)S(1)} async-done(((bf16[8,2,2048]{2,1,0:T(2,128)(2,1)}), bf16[8,2,2048]{2,1,0:T(2,128)(2,1)S(1)}, u32[]{:S(2)}, u32[]{:S(2)}) %all-to-all-start.4) | async-done | bytes 65568 | tf_op jit(solution)/shard_map/all_to_all | solution.py:370
  257.7 0.1 reshape.37
  257.9 0.1 reshape.32
  258.1 0.9 collective-permute-start.15
  259.1 0.4 collective-permute-start.16
  259.6 0.4 collective-permute-start.18
  260.0 0.9 convolution_subtract_fusion
  260.9 0.7 copy-done.25
  261.6 4.5 %whole_column.3 = bf16[1536,512]{1,0:T(8,128)(2,1)} custom-call(s32[2]{0:T(128)} %pad_add_fusion.place, bf16[64,1536]{1,0:T(8,128)(2,1)} %get-tuple-element.45.refs_0_, bf16[64,1536]{1,0:T(8,128)(2,1)} %copy-done.13, bf16[64,1536]{1,0:T(8,128)(2,1)} %copy-done.14, bf16[64,1536]{1,0:T(8,128)(2,1)} %copy-done.15, bf16[64,1536]{1,0:T(8,128)(2,1)} %copy-done.16, ...), custom_call_target="tpu_custom_call" | custom-call | bytes 3145728 | tf_op jit(solution)/shard_map/whole_column/pallas_call | solution.py:297
  266.2 0.6 copy-done.21
  267.0 0.7 copy-done.24
  267.6 4.5 %whole_column.2 = bf16[1536,512]{1,0:T(8,128)(2,1)} custom-call(s32[2]{0:T(128)} %pad_add_fusion.place, bf16[64,1536]{1,0:T(8,128)(2,1)} %get-tuple-element.34.refs_0_, bf16[64,1536]{1,0:T(8,128)(2,1)} %copy-done.12, bf16[64,1536]{1,0:T(8,128)(2,1)} %copy-done.17, bf16[64,1536]{1,0:T(8,128)(2,1)} %copy-done.18, bf16[64,1536]{1,0:T(8,128)(2,1)} %copy-done.21, ...), custom_call_target="tpu_custom_call" | custom-call | bytes 3145728 | tf_op jit(solution)/shard_map/whole_column/pallas_call | solution.py:297
  (138 shorter events, 1.9 us)
Async XLA Ops:
  5.5 48.2 %collective-permute-start = (bf16[6,256,128]{2,1,0:T(8,128)(2,1)}, bf16[6,256,128]{2,1,0:T(8,128)(2,1)S(1)}, u32[]{:S(2)}, u32[]{:S(2)}) collective-permute-start(bf16[6,256,128]{2,1,0:T(8,128)(2,1)} %get-tuple-element.26), channel_id=1, source_target_pairs={{0,16},{1,48},{2,8},{3,40},{4,0},{5,32},{6,24},{7,56},{8,25},{9,57... | collective-permute-start | bytes 1179656 | tf_op jit(solution)/shard_map/ppermute | solution.py:318
  11.2 93.2 %collective-permute-start.4 = (bf16[6,256,128]{2,1,0:T(8,128)(2,1)}, bf16[6,256,128]{2,1,0:T(8,128)(2,1)S(1)}, u32[]{:S(2)}, u32[]{:S(2)}) collective-permute-start(bf16[6,256,128]{2,1,0:T(8,128)(2,1)} %get-tuple-element.27), channel_id=1, source_target_pairs={{0,64},{1,72},{2,32},{3,40},{4,0},{5,8},{6,96},{7,104},{8,73},{9,8... | collective-permute-start | bytes 1179656 | tf_op jit(solution)/shard_map/ppermute | solution.py:319
  13.3 91.2 %collective-permute-start.19 = (bf16[6,256,128]{2,1,0:T(8,128)(2,1)}, bf16[6,256,128]{2,1,0:T(8,128)(2,1)S(1)}, u32[]{:S(2)}, u32[]{:S(2)}) collective-permute-start(bf16[6,256,128]{2,1,0:T(8,128)(2,1)} %get-tuple-element.36), channel_id=1, source_target_pairs={{0,16},{1,48},{2,8},{3,40},{4,0},{5,32},{6,24},{7,56},{8,25},{9,57... | collective-permute-start | bytes 1179656 | tf_op jit(solution)/shard_map/ppermute | solution.py:318
  16.7 104.2 %collective-permute-start.23 = (bf16[6,256,128]{2,1,0:T(8,128)(2,1)}, bf16[6,256,128]{2,1,0:T(8,128)(2,1)S(1)}, u32[]{:S(2)}, u32[]{:S(2)}) collective-permute-start(bf16[6,256,128]{2,1,0:T(8,128)(2,1)} %get-tuple-element.37), channel_id=1, source_target_pairs={{0,64},{1,72},{2,32},{3,40},{4,0},{5,8},{6,96},{7,104},{8,73},{9,8... | collective-permute-start | bytes 1179656 | tf_op jit(solution)/shard_map/ppermute | solution.py:319
  53.7 87.0 %copy-start.30 = (bf16[6,256,128]{2,1,0:T(8,128)(2,1)}, bf16[6,256,128]{2,1,0:T(8,128)(2,1)S(1)}, u32[]{:S(2)}) copy-start(bf16[6,256,128]{2,1,0:T(8,128)(2,1)S(1)} %collective-permute-done.refs_0_) | copy-start | bytes 1179652
  53.7 67.2 %collective-permute-start.1 = (bf16[6,256,128]{2,1,0:T(8,128)(2,1)S(1)}, bf16[6,256,128]{2,1,0:T(8,128)(2,1)S(1)}, u32[]{:S(2)}, u32[]{:S(2)}) collective-permute-start(bf16[6,256,128]{2,1,0:T(8,128)(2,1)S(1)} %collective-permute-done.refs_0_), channel_id=1, source_target_pairs={{0,32},{1,33},{2,34},{3,35},{4,36},{5,37},{6,38},{7,39},{8,40},{9,... | collective-permute-start | bytes 1179656 | tf_op jit(solution)/shard_map/ppermute | solution.py:314
  55.5 67.5 %collective-permute-start.2 = (bf16[6,256,128]{2,1,0:T(8,128)(2,1)S(1)}, bf16[6,256,128]{2,1,0:T(8,128)(2,1)S(1)}, u32[]{:S(2)}, u32[]{:S(2)}) collective-permute-start(bf16[6,256,128]{2,1,0:T(8,128)(2,1)S(1)} %collective-permute-done.refs_0_), channel_id=1, source_target_pairs={{0,64},{1,65},{2,66},{3,67},{4,68},{5,69},{6,70},{7,71},{8,72},{9,... | collective-permute-start | bytes 1179656 | tf_op jit(solution)/shard_map/ppermute | solution.py:314
  104.4 36.3 %copy-start.31 = (bf16[6,256,128]{2,1,0:T(8,128)(2,1)}, bf16[6,256,128]{2,1,0:T(8,128)(2,1)S(1)}, u32[]{:S(2)}) copy-start(bf16[6,256,128]{2,1,0:T(8,128)(2,1)S(1)} %collective-permute-done.4.refs_4_) | copy-start | bytes 1179652
  104.4 18.6 %collective-permute-start.3 = (bf16[6,256,128]{2,1,0:T(8,128)(2,1)S(1)}, bf16[6,256,128]{2,1,0:T(8,128)(2,1)S(1)}, u32[]{:S(2)}, u32[]{:S(2)}) collective-permute-start(bf16[6,256,128]{2,1,0:T(8,128)(2,1)S(1)} %collective-permute-done.refs_0_), channel_id=1, source_target_pairs={{0,96},{1,97},{2,98},{3,99},{4,100},{5,101},{6,102},{7,103},{8,104... | collective-permute-start | bytes 1179656 | tf_op jit(solution)/shard_map/ppermute | solution.py:314
  104.5 48.7 %copy-start.28 = (bf16[6,256,128]{2,1,0:T(8,128)(2,1)}, bf16[6,256,128]{2,1,0:T(8,128)(2,1)S(1)}, u32[]{:S(2)}) copy-start(bf16[6,256,128]{2,1,0:T(8,128)(2,1)S(1)} %collective-permute-done.19.refs_0_) | copy-start | bytes 1179652
  104.5 18.9 %collective-permute-start.5 = (bf16[6,256,128]{2,1,0:T(8,128)(2,1)S(1)}, bf16[6,256,128]{2,1,0:T(8,128)(2,1)S(1)}, u32[]{:S(2)}, u32[]{:S(2)}) collective-permute-start(bf16[6,256,128]{2,1,0:T(8,128)(2,1)S(1)} %collective-permute-done.4.refs_4_), channel_id=1, source_target_pairs={{0,8},{1,9},{2,10},{3,11},{4,12},{5,13},{6,14},{7,15},{8,16},{9,17... | collective-permute-start | bytes 1179656 | tf_op jit(solution)/shard_map/ppermute | solution.py:314
  120.9 32.2 %copy-start.29 = (bf16[6,256,128]{2,1,0:T(8,128)(2,1)}, bf16[6,256,128]{2,1,0:T(8,128)(2,1)S(1)}, u32[]{:S(2)}) copy-start(bf16[6,256,128]{2,1,0:T(8,128)(2,1)S(1)} %collective-permute-done.23.refs_4_) | copy-start | bytes 1179652
  120.9 8.1 %collective-permute-start.6 = (bf16[6,256,128]{2,1,0:T(8,128)(2,1)S(1)}, bf16[6,256,128]{2,1,0:T(8,128)(2,1)S(1)}, u32[]{:S(2)}, u32[]{:S(2)}) collective-permute-start(bf16[6,256,128]{2,1,0:T(8,128)(2,1)S(1)} %collective-permute-done.4.refs_4_), channel_id=1, source_target_pairs={{0,16},{1,17},{2,18},{3,19},{4,20},{5,21},{6,22},{7,23},{8,24},{9,... | collective-permute-start | bytes 1179656 | tf_op jit(solution)/shard_map/ppermute | solution.py:314
  120.9 19.8 %copy-start.32 = (bf16[6,256,128]{2,1,0:T(8,128)(2,1)}, bf16[6,256,128]{2,1,0:T(8,128)(2,1)S(1)}, u32[]{:S(2)}) copy-start(bf16[6,256,128]{2,1,0:T(8,128)(2,1)S(1)} %collective-permute-done.1.refs_1_) | copy-start | bytes 1179652
  120.9 16.2 %collective-permute-start.7 = (bf16[6,256,128]{2,1,0:T(8,128)(2,1)S(1)}, bf16[6,256,128]{2,1,0:T(8,128)(2,1)S(1)}, u32[]{:S(2)}, u32[]{:S(2)}) collective-permute-start(bf16[6,256,128]{2,1,0:T(8,128)(2,1)S(1)} %collective-permute-done.4.refs_4_), channel_id=1, source_target_pairs={{0,24},{1,25},{2,26},{3,27},{4,28},{5,29},{6,30},{7,31},{8,0},{9,1... | collective-permute-start | bytes 1179656 | tf_op jit(solution)/shard_map/ppermute | solution.py:314
  123.0 17.7 %copy-start.33 = (bf16[6,256,128]{2,1,0:T(8,128)(2,1)}, bf16[6,256,128]{2,1,0:T(8,128)(2,1)S(1)}, u32[]{:S(2)}) copy-start(bf16[6,256,128]{2,1,0:T(8,128)(2,1)S(1)} %collective-permute-done.2.refs_2_) | copy-start | bytes 1179652
  123.0 14.1 %collective-permute-start.20 = (bf16[6,256,128]{2,1,0:T(8,128)(2,1)S(1)}, bf16[6,256,128]{2,1,0:T(8,128)(2,1)S(1)}, u32[]{:S(2)}, u32[]{:S(2)}) collective-permute-start(bf16[6,256,128]{2,1,0:T(8,128)(2,1)S(1)} %collective-permute-done.19.refs_0_), channel_id=1, source_target_pairs={{0,32},{1,33},{2,34},{3,35},{4,36},{5,37},{6,38},{7,39},{8,40},{9,... | collective-permute-start | bytes 1179656 | tf_op jit(solution)/shard_map/ppermute | solution.py:314
  123.0 17.7 %copy-start.35 = (bf16[6,256,128]{2,1,0:T(8,128)(2,1)}, bf16[6,256,128]{2,1,0:T(8,128)(2,1)S(1)}, u32[]{:S(2)}) copy-start(bf16[6,256,128]{2,1,0:T(8,128)(2,1)S(1)} %collective-permute-done.3.refs_3_) | copy-start | bytes 1179652
  123.0 30.1 %collective-permute-start.21 = (bf16[6,256,128]{2,1,0:T(8,128)(2,1)S(1)}, bf16[6,256,128]{2,1,0:T(8,128)(2,1)S(1)}, u32[]{:S(2)}, u32[]{:S(2)}) collective-permute-start(bf16[6,256,128]{2,1,0:T(8,128)(2,1)S(1)} %collective-permute-done.19.refs_0_), channel_id=1, source_target_pairs={{0,64},{1,65},{2,66},{3,67},{4,68},{5,69},{6,70},{7,71},{8,72},{9,... | collective-permute-start | bytes 1179656 | tf_op jit(solution)/shard_map/ppermute | solution.py:314
  123.4 17.4 %copy-start.37 = (bf16[6,256,128]{2,1,0:T(8,128)(2,1)}, bf16[6,256,128]{2,1,0:T(8,128)(2,1)S(1)}, u32[]{:S(2)}) copy-start(bf16[6,256,128]{2,1,0:T(8,128)(2,1)S(1)} %collective-permute-done.5.refs_5_) | copy-start | bytes 1179652
  123.4 29.9 %collective-permute-start.22 = (bf16[6,256,128]{2,1,0:T(8,128)(2,1)S(1)}, bf16[6,256,128]{2,1,0:T(8,128)(2,1)S(1)}, u32[]{:S(2)}, u32[]{:S(2)}) collective-permute-start(bf16[6,256,128]{2,1,0:T(8,128)(2,1)S(1)} %collective-permute-done.19.refs_0_), channel_id=1, source_target_pairs={{0,96},{1,97},{2,98},{3,99},{4,100},{5,101},{6,102},{7,103},{8,104... | collective-permute-start | bytes 1179656 | tf_op jit(solution)/shard_map/ppermute | solution.py:314
  129.0 11.7 %copy-start.39 = (bf16[6,256,128]{2,1,0:T(8,128)(2,1)}, bf16[6,256,128]{2,1,0:T(8,128)(2,1)S(1)}, u32[]{:S(2)}) copy-start(bf16[6,256,128]{2,1,0:T(8,128)(2,1)S(1)} %collective-permute-done.6.refs_6_) | copy-start | bytes 1179652
  129.0 24.2 %collective-permute-start.24 = (bf16[6,256,128]{2,1,0:T(8,128)(2,1)S(1)}, bf16[6,256,128]{2,1,0:T(8,128)(2,1)S(1)}, u32[]{:S(2)}, u32[]{:S(2)}) collective-permute-start(bf16[6,256,128]{2,1,0:T(8,128)(2,1)S(1)} %collective-permute-done.23.refs_4_), channel_id=1, source_target_pairs={{0,8},{1,9},{2,10},{3,11},{4,12},{5,13},{6,14},{7,15},{8,16},{9,17... | collective-permute-start | bytes 1179656 | tf_op jit(solution)/shard_map/ppermute | solution.py:314
  137.1 16.2 %collective-permute-start.25 = (bf16[6,256,128]{2,1,0:T(8,128)(2,1)S(1)}, bf16[6,256,128]{2,1,0:T(8,128)(2,1)S(1)}, u32[]{:S(2)}, u32[]{:S(2)}) collective-permute-start(bf16[6,256,128]{2,1,0:T(8,128)(2,1)S(1)} %collective-permute-done.23.refs_4_), channel_id=1, source_target_pairs={{0,16},{1,17},{2,18},{3,19},{4,20},{5,21},{6,22},{7,23},{8,24},{9,... | collective-permute-start | bytes 1179656 | tf_op jit(solution)/shard_map/ppermute | solution.py:314
  137.1 16.0 %copy-start.34 = (bf16[6,256,128]{2,1,0:T(8,128)(2,1)}, bf16[6,256,128]{2,1,0:T(8,128)(2,1)S(1)}, u32[]{:S(2)}) copy-start(bf16[6,256,128]{2,1,0:T(8,128)(2,1)S(1)} %collective-permute-done.20.refs_1_) | copy-start | bytes 1179652
  137.1 16.2 %collective-permute-start.26 = (bf16[6,256,128]{2,1,0:T(8,128)(2,1)S(1)}, bf16[6,256,128]{2,1,0:T(8,128)(2,1)S(1)}, u32[]{:S(2)}, u32[]{:S(2)}) collective-permute-start(bf16[6,256,128]{2,1,0:T(8,128)(2,1)S(1)} %collective-permute-done.23.refs_4_), channel_id=1, source_target_pairs={{0,24},{1,25},{2,26},{3,27},{4,28},{5,29},{6,30},{7,31},{8,0},{9,1... | collective-permute-start | bytes 1179656 | tf_op jit(solution)/shard_map/ppermute | solution.py:314
  153.2 14.9 %collective-permute-start.8 = (bf16[4,64,1536]{2,1,0:T(8,128)(2,1)}, bf16[4,64,1536]{2,1,0:T(8,128)(2,1)S(1)}, u32[]{:S(2)}, u32[]{:S(2)}) collective-permute-start(bf16[4,64,1536]{2,1,0:T(8,128)(2,1)} %get-tuple-element.29), channel_id=1, source_target_pairs={{0,1},{1,0},{2,3},{3,2},{4,5},{5,4},{6,7},{7,6},{8,9},{9,8},{10,11... | collective-permute-start | bytes 2359304 | tf_op jit(solution)/shard_map/ppermute | solution.py:314
  167.5 10.6 %collective-permute-start.27 = (bf16[4,64,1536]{2,1,0:T(8,128)(2,1)}, bf16[4,64,1536]{2,1,0:T(8,128)(2,1)S(1)}, u32[]{:S(2)}, u32[]{:S(2)}) collective-permute-start(bf16[4,64,1536]{2,1,0:T(8,128)(2,1)} %get-tuple-element.40), channel_id=1, source_target_pairs={{0,1},{1,0},{2,3},{3,2},{4,5},{5,4},{6,7},{7,6},{8,9},{9,8},{10,11... | collective-permute-start | bytes 2359304 | tf_op jit(solution)/shard_map/ppermute | solution.py:314
  172.2 13.9 %collective-permute-start.10 = (bf16[64,1536]{1,0:T(8,128)(2,1)}, bf16[64,1536]{1,0:T(8,128)(2,1)S(1)}, u32[]{:S(2)}, u32[]{:S(2)}) collective-permute-start(bf16[64,1536]{1,0:T(8,128)(2,1)} %get-tuple-element.32), channel_id=1, source_target_pairs={{0,4},{1,5},{2,6},{3,7},{4,0},{5,1},{6,2},{7,3},{8,12},{9,13},{10,... | collective-permute-start | bytes 589832 | tf_op jit(solution)/shard_map/ppermute | solution.py:314
  172.2 13.9 %collective-permute-start.11 = (bf16[64,1536]{1,0:T(8,128)(2,1)}, bf16[64,1536]{1,0:T(8,128)(2,1)S(1)}, u32[]{:S(2)}, u32[]{:S(2)}) collective-permute-start(bf16[64,1536]{1,0:T(8,128)(2,1)} %get-tuple-element.33), channel_id=1, source_target_pairs={{0,6},{1,7},{2,0},{3,1},{4,2},{5,3},{6,4},{7,5},{8,14},{9,15},{10,... | collective-permute-start | bytes 589832 | tf_op jit(solution)/shard_map/ppermute | solution.py:314
  178.0 8.0 %collective-permute-start.9 = (bf16[64,1536]{1,0:T(8,128)(2,1)}, bf16[64,1536]{1,0:T(8,128)(2,1)S(1)}, u32[]{:S(2)}, u32[]{:S(2)}) collective-permute-start(bf16[64,1536]{1,0:T(8,128)(2,1)} %get-tuple-element.31), channel_id=1, source_target_pairs={{0,2},{1,3},{2,4},{3,5},{4,6},{5,7},{6,0},{7,1},{8,10},{9,11},{10,... | collective-permute-start | bytes 589832 | tf_op jit(solution)/shard_map/ppermute | solution.py:314
  182.2 19.7 %collective-permute-start.28 = (bf16[64,1536]{1,0:T(8,128)(2,1)}, bf16[64,1536]{1,0:T(8,128)(2,1)S(1)}, u32[]{:S(2)}, u32[]{:S(2)}) collective-permute-start(bf16[64,1536]{1,0:T(8,128)(2,1)} %get-tuple-element.42), channel_id=1, source_target_pairs={{0,2},{1,3},{2,4},{3,5},{4,6},{5,7},{6,0},{7,1},{8,10},{9,11},{10,... | collective-permute-start | bytes 589832 | tf_op jit(solution)/shard_map/ppermute | solution.py:314
  182.2 19.7 %collective-permute-start.29 = (bf16[64,1536]{1,0:T(8,128)(2,1)}, bf16[64,1536]{1,0:T(8,128)(2,1)S(1)}, u32[]{:S(2)}, u32[]{:S(2)}) collective-permute-start(bf16[64,1536]{1,0:T(8,128)(2,1)} %get-tuple-element.43), channel_id=1, source_target_pairs={{0,4},{1,5},{2,6},{3,7},{4,0},{5,1},{6,2},{7,3},{8,12},{9,13},{10,... | collective-permute-start | bytes 589832 | tf_op jit(solution)/shard_map/ppermute | solution.py:314
  186.0 15.9 %collective-permute-start.30 = (bf16[64,1536]{1,0:T(8,128)(2,1)}, bf16[64,1536]{1,0:T(8,128)(2,1)S(1)}, u32[]{:S(2)}, u32[]{:S(2)}) collective-permute-start(bf16[64,1536]{1,0:T(8,128)(2,1)} %get-tuple-element.44), channel_id=1, source_target_pairs={{0,6},{1,7},{2,0},{3,1},{4,2},{5,3},{6,4},{7,5},{8,14},{9,15},{10,... | collective-permute-start | bytes 589832 | tf_op jit(solution)/shard_map/ppermute | solution.py:314
  191.5 17.2 %all-to-all-start = ((bf16[16,32,128]{2,1,0:T(8,128)(2,1)}), bf16[16,32,128]{2,1,0:T(8,128)(2,1)S(1)}, u32[]{:S(2)}, u32[]{:S(2)}) async-start(bf16[16,32,128]{2,1,0:T(8,128)(2,1)} %get-tuple-element.35), calls=%async_computation | async-start | bytes 262144 | tf_op jit(solution)/shard_map/all_to_all | solution.py:338
  201.8 31.1 %copy-start.11 = (bf16[64,1536]{1,0:T(8,128)(2,1)S(1)}, bf16[64,1536]{1,0:T(8,128)(2,1)}, u32[]{:S(2)}) copy-start(bf16[64,1536]{1,0:T(8,128)(2,1)} %get-tuple-element.34.refs_0_) | copy-start | bytes 589828
  206.5 34.1 %copy-start.26 = (f32[64,512]{1,0:T(8,128)S(1)}, f32[64,512]{1,0:T(8,128)}, u32[]{:S(2)}) copy-start(f32[64,512]{1,0:T(8,128)} %param.18) | copy-start | bytes 393220
  206.6 34.1 %copy-start = (bf16[512,512]{1,0:T(8,128)(2,1)S(1)}, bf16[512,512]{1,0:T(8,128)(2,1)}, u32[]{:S(2)}) copy-start(bf16[512,512]{1,0:T(8,128)(2,1)} %top.1) | copy-start | bytes 1572868
  208.7 11.2 %all-to-all-start.2 = ((bf16[16,16,128]{2,1,0:T(8,128)(2,1)}), bf16[16,16,128]{2,1,0:T(8,128)(2,1)S(1)}, u32[]{:S(2)}, u32[]{:S(2)}) async-start(bf16[16,16,128]{2,1,0:T(8,128)(2,1)} %get-tuple-element.46), calls=%async_computation.2 | async-start | bytes 131072 | tf_op jit(solution)/shard_map/all_to_all | solution.py:338
  220.6 12.4 %all-to-all-start.1 = ((bf16[16,32,128]{2,1,0:T(8,128)(2,1)}), bf16[16,32,128]{2,1,0:T(8,128)(2,1)S(1)}, u32[]{:S(2)}, u32[]{:S(2)}) async-start(bf16[16,32,128]{2,1,0:T(8,128)(2,1)} %broadcast_in_dim.4), calls=%async_computation.1 | async-start | bytes 262144 | tf_op jit(solution)/shard_map/all_to_all | solution.py:341
  224.1 17.9 %collective-permute-start.31 = (bf16[64,1536]{1,0:T(8,128)(2,1)}, bf16[64,1536]{1,0:T(8,128)(2,1)S(1)}, u32[]{:S(2)}, u32[]{:S(2)}) collective-permute-start(bf16[64,1536]{1,0:T(8,128)(2,1)} %get-tuple-element.45.refs_0_), channel_id=1, source_target_pairs={{0,2},{1,3},{2,4},{3,5},{4,6},{5,7},{6,0},{7,1},{8,10},{9,11},{10,... | collective-permute-start | bytes 589832 | tf_op jit(solution)/shard_map/ppermute | solution.py:314
  225.6 18.1 %collective-permute-start.32 = (bf16[64,1536]{1,0:T(8,128)(2,1)}, bf16[64,1536]{1,0:T(8,128)(2,1)S(1)}, u32[]{:S(2)}, u32[]{:S(2)}) collective-permute-start(bf16[64,1536]{1,0:T(8,128)(2,1)} %get-tuple-element.45.refs_0_), channel_id=1, source_target_pairs={{0,4},{1,5},{2,6},{3,7},{4,0},{5,1},{6,2},{7,3},{8,12},{9,13},{10,... | collective-permute-start | bytes 589832 | tf_op jit(solution)/shard_map/ppermute | solution.py:314
  227.1 17.7 %collective-permute-start.33 = (bf16[64,1536]{1,0:T(8,128)(2,1)}, bf16[64,1536]{1,0:T(8,128)(2,1)S(1)}, u32[]{:S(2)}, u32[]{:S(2)}) collective-permute-start(bf16[64,1536]{1,0:T(8,128)(2,1)} %get-tuple-element.45.refs_0_), channel_id=1, source_target_pairs={{0,6},{1,7},{2,0},{3,1},{4,2},{5,3},{6,4},{7,5},{8,14},{9,15},{10,... | collective-permute-start | bytes 589832 | tf_op jit(solution)/shard_map/ppermute | solution.py:314
  228.9 17.0 %collective-permute-start.34 = (bf16[64,1536]{1,0:T(8,128)(2,1)}, bf16[64,1536]{1,0:T(8,128)(2,1)S(1)}, u32[]{:S(2)}, u32[]{:S(2)}) collective-permute-start(bf16[64,1536]{1,0:T(8,128)(2,1)} %get-tuple-element.45.refs_0_), channel_id=1, source_target_pairs={{0,1},{1,0},{2,3},{3,2},{4,5},{5,4},{6,7},{7,6},{8,9},{9,8},{10,11... | collective-permute-start | bytes 589832 | tf_op jit(solution)/shard_map/ppermute | solution.py:314
  232.9 25.2 %collective-permute-start.12 = (bf16[64,1536]{1,0:T(8,128)(2,1)S(1)}, bf16[64,1536]{1,0:T(8,128)(2,1)S(1)}, u32[]{:S(2)}, u32[]{:S(2)}) collective-permute-start(bf16[64,1536]{1,0:T(8,128)(2,1)S(1)} %copy-done.11), channel_id=1, source_target_pairs={{0,2},{1,3},{2,4},{3,5},{4,6},{5,7},{6,0},{7,1},{8,10},{9,11},{10,... | collective-permute-start | bytes 589832 | tf_op jit(solution)/shard_map/ppermute | solution.py:314
  233.6 13.3 %all-to-all-start.3 = ((bf16[16,16,128]{2,1,0:T(8,128)(2,1)}), bf16[16,16,128]{2,1,0:T(8,128)(2,1)S(1)}, u32[]{:S(2)}, u32[]{:S(2)}) async-start(bf16[16,16,128]{2,1,0:T(8,128)(2,1)} %broadcast_in_dim.5), calls=%async_computation.3 | async-start | bytes 131072 | tf_op jit(solution)/shard_map/all_to_all | solution.py:341
  240.5 19.5 %copy-start.27 = (f32[64,512]{1,0:T(8,128)S(1)}, f32[64,512]{1,0:T(8,128)}, u32[]{:S(2)}) copy-start(f32[64,512]{1,0:T(8,128)} %param.19) | copy-start | bytes 393220
  240.7 20.2 %copy-start.3 = (f32[64,512]{1,0:T(8,128)}, f32[64,512]{1,0:T(8,128)S(1)}, u32[]{:S(2)}) copy-start(f32[64,512]{1,0:T(8,128)S(1)} %bitcast_subtract_fusion.1) | copy-start | bytes 393220
  241.1 25.0 %copy-start.4 = (bf16[64,512]{1,0:T(8,128)(2,1)}, bf16[64,512]{1,0:T(8,128)(2,1)S(1)}, u32[]{:S(2)}) copy-start(bf16[64,512]{1,0:T(8,128)(2,1)S(1)} %fusion.1) | copy-start | bytes 196612
  242.0 18.8 %copy-start.13 = (bf16[64,1536]{1,0:T(8,128)(2,1)}, bf16[64,1536]{1,0:T(8,128)(2,1)S(1)}, u32[]{:S(2)}) copy-start(bf16[64,1536]{1,0:T(8,128)(2,1)S(1)} %collective-permute-done.31.refs_1_) | copy-start | bytes 589828
  242.0 16.9 %collective-permute-start.13 = (bf16[64,1536]{1,0:T(8,128)(2,1)S(1)}, bf16[64,1536]{1,0:T(8,128)(2,1)S(1)}, u32[]{:S(2)}, u32[]{:S(2)}) collective-permute-start(bf16[64,1536]{1,0:T(8,128)(2,1)S(1)} %copy-done.11), channel_id=1, source_target_pairs={{0,4},{1,5},{2,6},{3,7},{4,0},{5,1},{6,2},{7,3},{8,12},{9,13},{10,... | collective-permute-start | bytes 589832 | tf_op jit(solution)/shard_map/ppermute | solution.py:314
  243.7 17.2 %copy-start.14 = (bf16[64,1536]{1,0:T(8,128)(2,1)}, bf16[64,1536]{1,0:T(8,128)(2,1)S(1)}, u32[]{:S(2)}) copy-start(bf16[64,1536]{1,0:T(8,128)(2,1)S(1)} %collective-permute-done.32.refs_2_) | copy-start | bytes 589828
  243.7 15.4 %collective-permute-start.14 = (bf16[64,1536]{1,0:T(8,128)(2,1)S(1)}, bf16[64,1536]{1,0:T(8,128)(2,1)S(1)}, u32[]{:S(2)}, u32[]{:S(2)}) collective-permute-start(bf16[64,1536]{1,0:T(8,128)(2,1)S(1)} %copy-done.11), channel_id=1, source_target_pairs={{0,6},{1,7},{2,0},{3,1},{4,2},{5,3},{6,4},{7,5},{8,14},{9,15},{10,... | collective-permute-start | bytes 589832 | tf_op jit(solution)/shard_map/ppermute | solution.py:314
  244.8 16.1 %copy-start.15 = (bf16[64,1536]{1,0:T(8,128)(2,1)}, bf16[64,1536]{1,0:T(8,128)(2,1)S(1)}, u32[]{:S(2)}) copy-start(bf16[64,1536]{1,0:T(8,128)(2,1)S(1)} %collective-permute-done.33.refs_3_) | copy-start | bytes 589828
  244.8 14.7 %collective-permute-start.35 = (bf16[64,1536]{1,0:T(8,128)(2,1)S(1)}, bf16[64,1536]{1,0:T(8,128)(2,1)S(1)}, u32[]{:S(2)}, u32[]{:S(2)}) collective-permute-start(bf16[64,1536]{1,0:T(8,128)(2,1)S(1)} %collective-permute-done.31.refs_1_), channel_id=1, source_target_pairs={{0,1},{1,0},{2,3},{3,2},{4,5},{5,4},{6,7},{7,6},{8,9},{9,8},{10,11... | collective-permute-start | bytes 589832 | tf_op jit(solution)/shard_map/ppermute | solution.py:314
  245.9 15.0 %copy-start.16 = (bf16[64,1536]{1,0:T(8,128)(2,1)}, bf16[64,1536]{1,0:T(8,128)(2,1)S(1)}, u32[]{:S(2)}) copy-start(bf16[64,1536]{1,0:T(8,128)(2,1)S(1)} %collective-permute-done.34.refs_4_) | copy-start | bytes 589828
  245.9 13.7 %collective-permute-start.36 = (bf16[64,1536]{1,0:T(8,128)(2,1)S(1)}, bf16[64,1536]{1,0:T(8,128)(2,1)S(1)}, u32[]{:S(2)}, u32[]{:S(2)}) collective-permute-start(bf16[64,1536]{1,0:T(8,128)(2,1)S(1)} %collective-permute-done.32.refs_2_), channel_id=1, source_target_pairs={{0,1},{1,0},{2,3},{3,2},{4,5},{5,4},{6,7},{7,6},{8,9},{9,8},{10,11... | collective-permute-start | bytes 589832 | tf_op jit(solution)/shard_map/ppermute | solution.py:314
  246.9 10.8 %all-to-all-start.4 = ((bf16[8,2,2048]{2,1,0:T(2,128)(2,1)}), bf16[8,2,2048]{2,1,0:T(2,128)(2,1)S(1)}, u32[]{:S(2)}, u32[]{:S(2)}) async-start(bf16[8,2,2048]{2,1,0:T(2,128)(2,1)} %reshape.36), calls=%async_computation.4 | async-start | bytes 131072 | tf_op jit(solution)/shard_map/all_to_all | solution.py:370
  258.1 8.0 %copy-start.12 = (bf16[64,1536]{1,0:T(8,128)(2,1)}, bf16[64,1536]{1,0:T(8,128)(2,1)S(1)}, u32[]{:S(2)}) copy-start(bf16[64,1536]{1,0:T(8,128)(2,1)S(1)} %collective-permute-done.12.refs_1_) | copy-start | bytes 589828
  258.1 8.0 %collective-permute-start.15 = (bf16[64,1536]{1,0:T(8,128)(2,1)S(1)}, bf16[64,1536]{1,0:T(8,128)(2,1)S(1)}, u32[]{:S(2)}, u32[]{:S(2)}) collective-permute-start(bf16[64,1536]{1,0:T(8,128)(2,1)S(1)} %copy-done.11), channel_id=1, source_target_pairs={{0,1},{1,0},{2,3},{3,2},{4,5},{5,4},{6,7},{7,6},{8,9},{9,8},{10,11... | collective-permute-start | bytes 589832 | tf_op jit(solution)/shard_map/ppermute | solution.py:314
  259.0 1.9 collective-permute-start.37
  259.1 7.1 %collective-permute-start.16 = (bf16[64,1536]{1,0:T(8,128)(2,1)S(1)}, bf16[64,1536]{1,0:T(8,128)(2,1)S(1)}, u32[]{:S(2)}, u32[]{:S(2)}) collective-permute-start(bf16[64,1536]{1,0:T(8,128)(2,1)S(1)} %collective-permute-done.12.refs_1_), channel_id=1, source_target_pairs={{0,1},{1,0},{2,3},{3,2},{4,5},{5,4},{6,7},{7,6},{8,9},{9,8},{10,11... | collective-permute-start | bytes 589832 | tf_op jit(solution)/shard_map/ppermute | solution.py:314
  259.5 6.7 %collective-permute-start.17 = (bf16[64,1536]{1,0:T(8,128)(2,1)S(1)}, bf16[64,1536]{1,0:T(8,128)(2,1)S(1)}, u32[]{:S(2)}, u32[]{:S(2)}) collective-permute-start(bf16[64,1536]{1,0:T(8,128)(2,1)S(1)} %collective-permute-done.13.refs_2_), channel_id=1, source_target_pairs={{0,1},{1,0},{2,3},{3,2},{4,5},{5,4},{6,7},{7,6},{8,9},{9,8},{10,11... | collective-permute-start | bytes 589832 | tf_op jit(solution)/shard_map/ppermute | solution.py:314
  259.6 6.6 %collective-permute-start.18 = (bf16[64,1536]{1,0:T(8,128)(2,1)S(1)}, bf16[64,1536]{1,0:T(8,128)(2,1)S(1)}, u32[]{:S(2)}, u32[]{:S(2)}) collective-permute-start(bf16[64,1536]{1,0:T(8,128)(2,1)S(1)} %collective-permute-done.14.refs_3_), channel_id=1, source_target_pairs={{0,1},{1,0},{2,3},{3,2},{4,5},{5,4},{6,7},{7,6},{8,9},{9,8},{10,11... | collective-permute-start | bytes 589832 | tf_op jit(solution)/shard_map/ppermute | solution.py:314
  (23 other events, 35.0 us)

commit v2 on v0

v2 whole, which is shorter than its diff:
```python
import functools

import jax
import jax.numpy as jnp
from jax import lax
from jax.experimental import pallas as pl
from jax.experimental.pallas import tpu as pltpu
from jax.sharding import PartitionSpec as P

BS = 128
W = 512
NB = 12
ROWS = NB * BS
SIDE = 4
PART = 64
COLS = 8
PAIR = 2 * PART
BOTH = ("row", "col")
MIB = 1024 * 1024
BF = jnp.bfloat16
F32 = jnp.float32


def device(z, y, x, core):
    return ((z % SIDE) * SIDE + y % SIDE) * 8 + (x % SIDE) * 2 + core % 2


def all_places():
    return [
        (z, y, x, core)
        for z in range(SIDE)
        for y in range(SIDE)
        for x in range(SIDE)
        for core in range(2)
    ]


def shifted(dz=0, dy=0, dx=0, dc=0):
    return [
        (device(z, y, x, c), device(z + dz, y + dy, x + dx, c + dc))
        for z, y, x, c in all_places()
    ]


def spread_pairs():
    pairs = []
    for z, y, x, core in all_places():
        plane = (z * SIDE + y) % 8
        far = (2 - (x - plane // 2)) % SIDE
        to = device(z + core, y + far, plane // 2, plane % 2)
        pairs.append((device(z, y, x, core), to))
    return pairs


def params(mib=24, **more):
    return pltpu.CompilerParams(vmem_limit_bytes=mib * MIB, **more)


def cost(flops, moved):
    return pl.CostEstimate(flops=flops, bytes_accessed=moved, transcendentals=0)


def whole(shape):
    return pl.BlockSpec(shape, lambda *_: (0,) * len(shape))


def find_slot(rows, counts, owner, block):
    slot = jnp.int32(0)
    live = jnp.int32(0)
    for k in range(NB):
        hit = (rows[owner, k] == block) & (k < counts[owner])
        slot = jnp.where(hit, k, slot)
        live = jnp.where(hit, 1, live)
    return slot, live


def prep_body(place, rows_a, counts_a, rows_b, counts_b, fa, fb, top, out, top_t):
    owner = place[0]
    upper = place[1] % 2
    for first, rows, counts, factor in (
        (0, rows_a, counts_a, fa),
        (PART, rows_b, counts_b, fb),
    ):
        for block in range(NB):
            slot, live = find_slot(rows, counts, owner, block)
            piece = factor[pl.ds(pl.multiple_of(slot * BS, BS), BS), :].T
            piece = jnp.where(upper > 0, piece[PART:], piece[:PART])
            piece = jnp.where(live > 0, piece, jnp.zeros_like(piece))
            out[block, first : first + PART, :] = piece
    top_t[...] = top[...].T


def prep(place, lists, factor_a, factor_b, factor_top):
    slice_spec = pl.BlockSpec((ROWS, BS), lambda i, place, *_: (0, place[1] // 2))
    return pl.pallas_call(
        prep_body,
        name="prep",
        grid_spec=pltpu.PrefetchScalarGridSpec(
            num_scalar_prefetch=5,
            grid=(1,),
            in_specs=[slice_spec, slice_spec, whole((W, W))],
            out_specs=[whole((NB, PAIR, BS)), whole((W, W))],
        ),
        out_shape=[
            jax.ShapeDtypeStruct((NB, PAIR, BS), BF),
            jax.ShapeDtypeStruct((W, W), BF),
        ],
        compiler_params=params(),
        cost_estimate=cost(0, 4 * ROWS * BS),
    )(place, *lists, factor_a, factor_b, factor_top)


def product_body(place, gathered, tile, top_t, keep, give, spread, sums, ready, sems):
    plane = place[1]
    core = plane % 2

    @pl.when(pl.program_id(0) == 0)
    def _():
        copies = []
        for h in range(2):
            for c in range(COLS):
                far = (2 - (c // 2 - plane // 2) + SIDE) % SIDE
                z = (plane // SIDE + 2 * h + c % 2) % SIDE
                y = (plane % SIDE + far) % SIDE
                copies.append(
                    pltpu.make_async_copy(
                        gathered.at[z * SIDE + y],
                        spread.at[:, h, pl.ds(c * PAIR, PAIR), :],
                        sems.at[h * COLS + c],
                    )
                )
        for copy in copies:
            copy.start()
        for copy in copies:
            copy.wait()

    for c in range(0, COLS, 2):
        at = slice(c * PAIR, (c + 2) * PAIR)
        left = jnp.concatenate(
            [spread[n, h, at, :] for n in range(NB) for h in range(2)], axis=1
        )
        value = lax.dot_general(
            left, tile[...], (((1,), (1,)), ((), ())), preferred_element_type=F32
        )
        sums[c : c + 2] = value.reshape(2, PAIR, value.shape[1])
    first = sums[:, :PART, :].astype(BF)
    fix = jnp.dot(top_t[...], first.reshape(W, first.shape[2]), preferred_element_type=F32)
    ready[:, :PART, :] = first
    ready[:, PART:, :] = (sums[:, PART:, :] - fix.reshape(COLS, PART, fix.shape[1])).astype(BF)
    for x in range(SIDE):
        keep[x] = ready[2 * x + core]
        give[x] = ready[2 * x + 1 - core]


def product(place, gathered, trailing, top_t):
    width = 2 * BS
    deep = trailing.shape[1]
    out = jax.ShapeDtypeStruct((SIDE, PAIR, ROWS), BF)
    spec = pl.BlockSpec((SIDE, PAIR, width), lambda i, *_: (0, 0, i))
    return pl.pallas_call(
        product_body,
        name="product",
        grid_spec=pltpu.PrefetchScalarGridSpec(
            num_scalar_prefetch=1,
            grid=(ROWS // width,),
            in_specs=[
                pl.BlockSpec(memory_space=pl.ANY),
                pl.BlockSpec((width, deep), lambda i, *_: (i, 0)),
                whole((W, W)),
            ],
            out_specs=[spec, spec],
            scratch_shapes=[
                pltpu.VMEM((NB, 2, 2 * W, BS), BF),
                pltpu.VMEM((COLS, PAIR, width), F32),
                pltpu.VMEM((COLS, PAIR, width), BF),
                pltpu.SemaphoreType.DMA((2 * COLS,)),
            ],
        ),
        out_shape=[out, out],
        compiler_params=params(56, dimension_semantics=("arbitrary",)),
        cost_estimate=cost(4 * W * ROWS * deep, 2 * ROWS * deep + 4 * W * deep + 4 * W * ROWS),
    )(place, gathered, trailing, top_t)


def pair_body(place, mine, taken, *outs):
    x = place[1] // 2
    for i in range(SIDE):
        at = (x + i) % SIDE
        outs[i][...] = (mine[at].astype(F32) + taken[at].astype(F32)).astype(BF)


def pair_sum(place, mine, taken):
    lanes = 4 * BS
    spec = pl.BlockSpec((SIDE, PAIR, lanes), lambda i, *_: (0, 0, i))
    return pl.pallas_call(
        pair_body,
        name="pair_sum",
        grid_spec=pltpu.PrefetchScalarGridSpec(
            num_scalar_prefetch=1,
            grid=(ROWS // lanes,),
            in_specs=[spec, spec],
            out_specs=[pl.BlockSpec((PAIR, lanes), lambda i, *_: (0, i))] * SIDE,
        ),
        out_shape=[jax.ShapeDtypeStruct((PAIR, ROWS), BF)] * SIDE,
        compiler_params=params(dimension_semantics=("arbitrary",)),
        cost_estimate=cost(W * ROWS, 6 * W * ROWS),
    )(place, mine, taken)


def slots_body(
    place, rows_a, counts_a, rows_b, counts_b, s0, s1, s2, s3, fa, fb, columns, pieces, natural, left
):
    owner = place[0]
    total = (s0[...].astype(F32) + s1[...].astype(F32)) + (
        s2[...].astype(F32) + s3[...].astype(F32)
    )
    natural[...] = (-total).astype(BF)
    for k in range(NB):
        at = slice(k * BS, (k + 1) * BS)
        block = natural[:PART, pl.ds(pl.multiple_of(rows_a[owner, k] * BS, BS), BS)]
        columns[:PART, at] = jnp.where(k < counts_a[owner], block, jnp.zeros_like(block))
        block = natural[:, pl.ds(pl.multiple_of(rows_b[owner, k] * BS, BS), BS)]
        block = jnp.where(k < counts_b[owner], block, jnp.zeros_like(block))
        left[:, at] = block
        columns[PART:, at] = block[PART:]
    one = jnp.dot(columns[:PART, :], fa[...], preferred_element_type=F32)
    two = jnp.dot(left[...], fb[...], preferred_element_type=F32)
    outcome = jnp.concatenate([one, two], axis=0).astype(BF)
    rows = outcome.shape[0] // SIDE
    for p in range(SIDE * SIDE):
        up, across = p // SIDE, p % SIDE
        pieces[p] = outcome[up * rows : (up + 1) * rows, across * BS : (across + 1) * BS]


def slots(place, lists, slabs, factors):
    rows = 3 * PART // SIDE
    return pl.pallas_call(
        slots_body,
        name="slots",
        grid_spec=pltpu.PrefetchScalarGridSpec(
            num_scalar_prefetch=5,
            grid=(1,),
            in_specs=[whole((PAIR, ROWS))] * SIDE + [whole((ROWS, W))] * 2,
            out_specs=[whole((PAIR, ROWS)), whole((SIDE * SIDE, rows, BS))],
            scratch_shapes=[pltpu.VMEM((PAIR, ROWS), BF)] * 2,
        ),
        out_shape=[
            jax.ShapeDtypeStruct((PAIR, ROWS), BF),
            jax.ShapeDtypeStruct((SIDE * SIDE, rows, BS), BF),
        ],
        compiler_params=params(),
        cost_estimate=cost(6 * PART * ROWS * W, 4 * ROWS * W + 10 * PAIR * ROWS),
    )(place, *lists, *slabs, *factors)


def column_body(slabs, column_a, column_b):
    for first, out in ((0, column_a), (PART, column_b)):
        out[...] = slabs[:, first : first + PART, :].reshape(W, slabs.shape[2]).T


def whole_columns(slabs):
    lanes = 2 * BS
    out = jax.ShapeDtypeStruct((ROWS, W), BF)
    return pl.pallas_call(
        column_body,
        name="whole_columns",
        grid=(ROWS // lanes,),
        in_specs=[pl.BlockSpec((COLS, PAIR, lanes), lambda i: (0, 0, i))],
        out_specs=[pl.BlockSpec((lanes, W), lambda i: (i, 0))] * 2,
        out_shape=[out, out],
        compiler_params=params(dimension_semantics=("arbitrary",)),
        cost_estimate=cost(0, 8 * ROWS * W),
    )(slabs)


def fold_body(parts, out):
    total = jnp.sum(parts[...].astype(F32), axis=0).astype(BF)
    out[...] = jnp.broadcast_to(total[None], out.shape)


def row_sum(pieces):
    parts = lax.all_to_all(pieces, "row", 0, 0)
    spread = pl.pallas_call(
        fold_body,
        name="fold",
        out_shape=jax.ShapeDtypeStruct(pieces.shape, BF),
        compiler_params=params(8),
        cost_estimate=cost(pieces.size, 4 * pieces.size),
    )(parts)
    return lax.all_to_all(spread, "row", 0, 0)


def sums_of(got, first, last):
    rows = got.shape[1]
    up = range(first // rows, (last + rows - 1) // rows)
    wide = [
        jnp.concatenate([got[u * SIDE + v] for v in range(SIDE)], axis=1).astype(F32) for u in up
    ]
    start = first - up[0] * rows
    return jnp.concatenate(wide, axis=0)[start : start + last - first]


def top_body(got, base, top, diag_a, top_b, sent):
    value = base[...] - sums_of(got, 0, PART)
    diag_a[...] = value
    total = sums_of(got, PART, 2 * PART)
    for _ in range(3):
        part = value.astype(BF)
        value = value - part.astype(F32)
        total = total + jnp.dot(part, top[...], preferred_element_type=F32)
    total = (-total).astype(BF)
    top_b[...] = total
    for c in range(COLS):
        sent[c] = jnp.concatenate([total[:, c * PART : (c + 1) * PART]] * 2, axis=1)


def top_part(got, base_a, factor_top):
    return pl.pallas_call(
        top_body,
        name="top_part",
        out_shape=[
            jax.ShapeDtypeStruct((PART, W), F32),
            jax.ShapeDtypeStruct((PART, W), BF),
            jax.ShapeDtypeStruct((COLS, PART, 2 * PART), BF),
        ],
        compiler_params=params(8),
        cost_estimate=cost(6 * PART * W * W, 2 * W * W),
    )(got, base_a, factor_top)


def last_body(got, base, taken, top, diag_b):
    across = taken[...].reshape(W, 2 * PART)
    cross = lax.dot_general(
        across, top[...], (((0,), (0,)), ((), ())), preferred_element_type=F32
    )
    diag_b[...] = base[...] - sums_of(got, 2 * PART, 3 * PART) - cross[:PART]


def last_part(got, base_b, taken, factor_top):
    return pl.pallas_call(
        last_body,
        name="last_part",
        out_shape=jax.ShapeDtypeStruct((PART, W), F32),
        compiler_params=params(8),
        cost_estimate=cost(4 * PART * W * W, 2 * W * W),
    )(got, base_b, taken, factor_top)


def send(value, **by):
    return lax.ppermute(value, BOTH, shifted(**by))


def on_device(
    trailing, rows_a, counts_a, factor_a, rows_b, counts_b, factor_b, factor_top, base_a, base_b
):
    place = jnp.stack([lax.axis_index("row"), lax.axis_index("col")]).astype(jnp.int32)
    lists = (rows_a, counts_a, rows_b, counts_b)
    chunk, top_t = prep(place, lists, factor_a, factor_b, factor_top)
    chunk = lax.ppermute(chunk, BOTH, spread_pairs())
    gathered = lax.all_gather(chunk, "row", axis=0)
    keep, give = product(place, gathered, trailing, top_t)
    own, one, two, three = pair_sum(place, keep, send(give, dc=1))
    slabs = [own, send(one, dx=1), send(two, dx=2), send(three, dx=-1)]
    columns, pieces = slots(place, lists, slabs, (factor_a, factor_b))
    column_a, column_b = whole_columns(lax.all_gather(columns, "col", axis=0))
    got = row_sum(pieces)
    diag_a, top_b, sent = top_part(got, base_a, factor_top)
    taken = lax.all_to_all(sent, "col", 0, 0)
    diag_b = last_part(got, base_b, taken, factor_top)
    return (column_a, diag_a, column_b, top_b, diag_b)


def solution(mesh):
    in_specs = (
        P("row", "col"),
        P(),
        P(),
        P("row", None),
        P(),
        P(),
        P("row", None),
        P(),
        P("col", None),
        P("col", None),
    )
    out_specs = (P("row", None), P("col", None), P("row", None), P("col", None), P("col", None))
    return jax.shard_map(
        on_device, mesh=mesh, in_specs=in_specs, out_specs=out_specs, check_vma=False
    )
```

time: 410 us -> 203 us (0.50)
  waiting for transfers between devices: 248 us -> 99.8 us
  other arithmetic: 41.6 us -> 0.08 us
  matrix products: 41 us -> 0 us
  local copies, waits for them, and re-layouts: 48.5 us -> 11.4 us
  Pallas kernels: 0 us -> 30.1 us
  blocking collectives: 15.4 us -> 35.1 us
  starting transfers between devices: 0.12 us -> 11.3 us
    psum x3 -> x0, waiting for transfers between devices: 248 us -> none  [the longest x1 83.9 us: row_sums(): return lax.psum(pieces_in, 'row')]
    all_gather x0 -> x2, waiting for transfers between devices: none -> 63.4 us  [the longest x1 63.4 us: on_device(): gathered = lax.all_gather(chunk, 'row', axis=0)]
    dot_general x11 -> x0, matrix products: 41 us -> none  [the longest x2 17.6 us: partial_product(): jnp.dot(row_slab, spread.reshape(col_blocks * BS, W), preferred_element_t...]
    ppermute x0 -> x5, waiting for transfers between devices: none -> 36.4 us  [the longest x4 19.4 us: send(): return lax.ppermute(value, BOTH, shifted(**by))]
    all_to_all x0 -> x3, blocking collectives: none -> 35.1 us  [the longest x1 12.8 us: on_device(): taken = lax.all_to_all(sent, 'col', 0, 0)]
    pallas_call x0 -> x8, Pallas kernels: none -> 30.1 us  [the longest x1 19.3 us: product(): pl.pallas_call(product_body, name='product', grid_spec=pltpu.PrefetchScal...]
    reshape x6 -> x0, local copies, waits for them, and re-layouts: 26.6 us -> none  [the longest x2 10.5 us: partial_product(): spread.reshape(col_blocks * BS, W)]
    gather x2 -> x0, local copies, waits for them, and re-layouts: 19.9 us -> none  [partial_product(): jnp.take(slab_blocks, own_rows, axis=0)]
  transfers between devices with their start and end apart: 3 -> 7, of which waited for: 3 -> 5; matrix products, arithmetic and copies ran while one was open for 11% -> 0% of each run, Pallas kernels for 0% -> 1%
where the time goes in v2:
time: 203 us; the launch traced here: 202 us
  waiting for transfers between devices  99.8 us (49%)
  blocking collectives  35.1 us (17%)
  Pallas kernels  30.1 us (15%)
  between operations  14.1 us (7%)
  local copies, waits for them, and re-layouts  11.4 us (6%)
  starting transfers between devices  11.3 us (6%)
    all_gather x1, waiting for transfers between devices, on_device(): gathered = lax.all_gather(chunk, 'row', axis=0)  63.4 us
    ppermute x4, waiting for transfers between devices, send(): return lax.ppermute(value, BOTH, shifted(**by))  19.4 us
    pallas_call x1, Pallas kernels, product(): pl.pallas_call(product_body, name='product', grid_spec=pltpu.PrefetchScal...  19.3 us
    ppermute x1, waiting for transfers between devices, on_device(): chunk = lax.ppermute(chunk, BOTH, spread_pairs())  17 us
    all_to_all x1, blocking collectives, on_device(): taken = lax.all_to_all(sent, 'col', 0, 0)  12.8 us
    all_to_all x1, blocking collectives, row_sum(): parts = lax.all_to_all(pieces, 'row', 0, 0)  12.2 us
    unnamed x44, local copies, waits for them, and re-layouts  11.4 us
    all_to_all x1, blocking collectives, row_sum(): return lax.all_to_all(spread, 'row', 0, 0)  10.1 us
  transfers between devices with their start and end apart: 7, of which 5 were waited for; matrix products, arithmetic and copies ran while one was open for 0% of the time, Pallas kernels for 1%

profile of v2, /device:TPU:1, one launch (start us, length us, event | category | flops | bytes accessed | tf_op | source)
XLA Modules:
  0.0 202.0 jit_solution(16580331825301794068)
XLA Ops:
  7.2 0.0 all-gather.5.cloned.1.call-start
  7.2 0.1 pad_add_fusion.place
  7.3 0.0 copy-start
  7.3 1.4 copy-done
  8.7 0.0 copy-start.2
  8.7 1.4 copy-done.2
  10.1 1.0 copy-done.4
  11.1 0.0 copy-start.10
  11.2 0.7 copy-done.10
  11.8 0.0 copy-start.12
  11.8 0.7 copy-done.12
  12.5 0.0 copy-start.16
  12.5 0.7 copy-done.16
  13.2 0.0 copy-start.18
  13.2 0.7 copy-done.18
  13.9 0.0 copy-start.14
  13.9 2.0 prep.1
  15.8 0.0 copy-done.14
  15.8 0.0 copy-start.20
  15.8 0.8 copy-done.20
  16.7 5.7 %collective-permute-start = (bf16[12,128,128]{2,1,0:T(8,128)(2,1)S(1)}, bf16[12,128,128]{2,1,0:T(8,128)(2,1)S(1)}, u32[]{:S(2)}, u32[]{:S(2)}) collective-permute-start(bf16[12,128,128]{2,1,0:T(8,128)(2,1)S(1)} %get-tuple-element.20), channel_id=1, source_target_pairs={{0,16},{1,48},{2,8},{3,40},{4,0},{5,32},{6,24},{7,56},{8,25},{9,57... | collective-permute-start | bytes 1179656 | tf_op jit(solution)/shard_map/ppermute | solution.py:359
  22.3 17.0 %collective-permute-done = bf16[12,128,128]{2,1,0:T(8,128)(2,1)S(1)} collective-permute-done((bf16[12,128,128]{2,1,0:T(8,128)(2,1)S(1)}, bf16[12,128,128]{2,1,0:T(8,128)(2,1)S(1)}, u32[]{:S(2)}, u32[]{:S(2)}) %collective-permute-start) | collective-permute-done | bytes 393248 | tf_op jit(solution)/shard_map/ppermute | solution.py:359
  39.3 0.0 copy-start.21
  39.3 0.7 copy-done.21
  40.1 0.0 all-gather.5.cloned.1.call-update
  40.1 0.0 all-gather.7.cloned.1.call-start
  40.1 63.4 %all-gather.5.cloned.1.call-done = bf16[192,128,128]{2,1,0:T(8,128)(2,1)} async-done(((bf16[12,128,128]{2,1,0:T(8,128)(2,1)}), bf16[192,128,128]{2,1,0:T(8,128)(2,1)}) %all-gather.5.cloned.1.call-update) | async-done | bytes 6291472 | tf_op jit(solution)/shard_map/all_gather | solution.py:360
  103.5 0.0 copy-start.15
  103.5 0.0 copy-start.13
  103.5 0.0 copy-start.17
  103.6 0.0 copy-start.19
  103.6 19.3 %product.1 = (bf16[4,128,1536]{2,1,0:T(8,128)(2,1)}, bf16[4,128,1536]{2,1,0:T(8,128)(2,1)}) custom-call(s32[2]{0:T(128)} %copy-done.14, bf16[16,12,128,128]{3,2,1,0:T(8,128)(2,1)} %bitcast.5, bf16[1536,3072]{1,0:T(8,128)(2,1)} %tile.1, bf16[512,512]{1,0:T(8,128)(2,1)} %copy-done.20), custom_call_target="tpu_custom_call" | custom-call | flops 9663676416 | bytes 18874368 | tf_op jit(solution)/shard_map/product/pallas_call | solution.py:160
  122.8 0.8 collective-permute-start.1
  123.6 3.2 %collective-permute-done.1.taken = bf16[4,128,1536]{2,1,0:T(8,128)(2,1)S(1)} collective-permute-done((bf16[4,128,1536]{2,1,0:T(8,128)(2,1)}, bf16[4,128,1536]{2,1,0:T(8,128)(2,1)S(1)}, u32[]{:S(2)}, u32[]{:S(2)}) %collective-permute-start.1) | collective-permute-done | bytes 1572896 | tf_op jit(solution)/shard_map/ppermute | solution.py:350
  126.8 0.0 copy-done.15
  126.8 0.0 copy-start.7
  126.8 1.4 copy-done.7
  128.2 0.0 copy-start.1
  128.2 0.0 copy-start.3
  128.2 1.3 pair_sum.1
  129.6 1.3 collective-permute-start.2
  130.8 2.4 %collective-permute-start.3 = (bf16[128,1536]{1,0:T(8,128)(2,1)S(1)}, bf16[128,1536]{1,0:T(8,128)(2,1)S(1)}, u32[]{:S(2)}, u32[]{:S(2)}) collective-permute-start(bf16[128,1536]{1,0:T(8,128)(2,1)S(1)} %get-tuple-element.26), channel_id=1, source_target_pairs={{0,4},{1,5},{2,6},{3,7},{4,0},{5,1},{6,2},{7,3},{8,12},{9,13},{10,... | collective-permute-start | bytes 1179656 | tf_op jit(solution)/shard_map/ppermute | solution.py:350
  133.2 1.2 collective-permute-start.4
  134.4 6.8 %collective-permute-done.2.s1 = bf16[128,1536]{1,0:T(8,128)(2,1)S(1)} collective-permute-done((bf16[128,1536]{1,0:T(8,128)(2,1)S(1)}, bf16[128,1536]{1,0:T(8,128)(2,1)S(1)}, u32[]{:S(2)}, u32[]{:S(2)}) %collective-permute-start.2) | collective-permute-done | bytes 393248 | tf_op jit(solution)/shard_map/ppermute | solution.py:350
  141.2 9.3 %collective-permute-done.3.s2 = bf16[128,1536]{1,0:T(8,128)(2,1)S(1)} collective-permute-done((bf16[128,1536]{1,0:T(8,128)(2,1)S(1)}, bf16[128,1536]{1,0:T(8,128)(2,1)S(1)}, u32[]{:S(2)}, u32[]{:S(2)}) %collective-permute-start.3) | collective-permute-done | bytes 393248 | tf_op jit(solution)/shard_map/ppermute | solution.py:350
  150.5 0.0 collective-permute-done.4.s3
  150.5 0.0 copy-done.13
  150.5 0.0 copy-done.17
  150.5 0.0 copy-done.19
  150.6 0.0 copy-done.1
  150.6 0.0 copy-done.3
  150.6 0.0 copy-done.11
  150.6 2.5 %slots.1 = (bf16[128,1536]{1,0:T(8,128)(2,1)}, bf16[16,48,128]{2,1,0:T(8,128)(2,1)S(1)}) custom-call(s32[2]{0:T(128)S(1)} %copy-done.15, s32[16,12]{1,0:T(8,128)S(1)} %copy-done.11, s32[16]{0:T(128)S(1)} %copy-done.17, s32[16,12]{1,0:T(8,128)S(1)} %copy-done.13, s32[16]{0:T(128)S(1)} %copy-done.19, bf16[128,1536]{1,0:T(8,128)(2,1)S(1)} %get-tuple-element.24.s0, ...), custom_call_target="tpu_custom_call" | custom-call | flops 301989888 | bytes 5111808 | tf_op jit(solution)/shard_map/slots/pallas_call | solution.py:237
  153.0 0.0 all-gather.7.cloned.1.call-update
  153.1 12.2 %all_to_all.15.parts = bf16[16,48,128]{2,1,0:T(8,128)(2,1)S(1)} all-to-all(bf16[16,48,128]{2,1,0:T(8,128)(2,1)S(1)} %get-tuple-element.30), channel_id=1, replica_groups=mesh['row'=16,'col'=8] {'row'}, dimensions={0} | all-to-all | bytes 393216 | tf_op jit(solution)/shard_map/all_to_all | solution.py:282
  165.3 10.1 %all_to_all.16.got = bf16[16,48,128]{2,1,0:T(8,128)(2,1)S(1)} all-to-all(bf16[16,48,128]{2,1,0:T(8,128)(2,1)S(1)} %fold.1), channel_id=1, replica_groups=mesh['row'=16,'col'=8] {'row'}, dimensions={0} | all-to-all | bytes 393216 | tf_op jit(solution)/shard_map/all_to_all | solution.py:290
  175.4 0.0 copy-done.5
  175.4 0.0 copy-done.9
  175.4 1.1 top_part.1
  176.5 12.8 %all_to_all.17.taken = bf16[8,64,128]{2,1,0:T(8,128)(2,1)S(1)} all-to-all(bf16[8,64,128]{2,1,0:T(8,128)(2,1)S(1)} %get-tuple-element.34), channel_id=1, replica_groups=mesh['row'=16,'col'=8] {'col'}, dimensions={0} | all-to-all | bytes 262144 | tf_op jit(solution)/shard_map/all_to_all | solution.py:368
  189.3 0.0 copy-done.8
  189.3 0.9 last_part.1
  190.2 1.9 copy-done.6
  192.0 3.1 %whole_columns.1 = (bf16[1536,512]{1,0:T(8,128)(2,1)}, bf16[1536,512]{1,0:T(8,128)(2,1)}) custom-call(bf16[8,128,1536]{2,1,0:T(8,128)(2,1)S(1)} %bitcast.4), custom_call_target="tpu_custom_call" | custom-call | bytes 6291456 | tf_op jit(solution)/shard_map/whole_columns/pallas_call | solution.py:264
  (8 shorter events, 0.0 us)
Async XLA Ops:
  7.2 96.4 %all-gather.5.cloned.1.call-start = ((), (), s32[]{:S(2)}) async-start(), calls=%async_computation.3 | async-start | bytes 6684672 | tf_op jit(solution)/shard_map/all_gather | solution.py:360
  7.3 1.4 copy-start
  8.7 1.4 copy-start.2
  10.1 1.0 copy-start.4
  11.1 0.7 copy-start.10
  11.8 0.7 copy-start.12
  12.5 0.7 copy-start.16
  13.2 0.7 copy-start.18
  13.9 2.0 copy-start.14
  15.8 0.8 copy-start.20
  16.7 22.7 %collective-permute-start = (bf16[12,128,128]{2,1,0:T(8,128)(2,1)S(1)}, bf16[12,128,128]{2,1,0:T(8,128)(2,1)S(1)}, u32[]{:S(2)}, u32[]{:S(2)}) collective-permute-start(bf16[12,128,128]{2,1,0:T(8,128)(2,1)S(1)} %get-tuple-element.20), channel_id=1, source_target_pairs={{0,16},{1,48},{2,8},{3,40},{4,0},{5,32},{6,24},{7,56},{8,25},{9,57... | collective-permute-start | bytes 1179656 | tf_op jit(solution)/shard_map/ppermute | solution.py:359
  39.3 0.7 copy-start.21
  40.1 150.1 %all-gather.7.cloned.1.call-start = ((), (), s32[]{:S(2)}) async-start(), calls=%async_computation.4 | async-start | bytes 3538944 | tf_op jit(solution)/shard_map/all_gather | solution.py:365
  103.5 23.3 %copy-start.15 = (s32[2]{0:T(128)S(1)}, s32[2]{0:T(128)}, u32[]{:S(2)}) copy-start(s32[2]{0:T(128)} %copy-done.14) | copy-start | bytes 28
  103.5 47.0 %copy-start.13 = (s32[16,12]{1,0:T(8,128)S(1)}, s32[16,12]{1,0:T(8,128)}, u32[]{:S(2)}) copy-start(s32[16,12]{1,0:T(8,128)} %rows_b.3) | copy-start | bytes 2308
  103.5 47.0 %copy-start.17 = (s32[16]{0:T(128)S(1)}, s32[16]{0:T(128)}, u32[]{:S(2)}) copy-start(s32[16]{0:T(128)} %counts_a.3) | copy-start | bytes 196
  103.6 47.0 %copy-start.19 = (s32[16]{0:T(128)S(1)}, s32[16]{0:T(128)}, u32[]{:S(2)}) copy-start(s32[16]{0:T(128)} %counts_b.3) | copy-start | bytes 196
  122.8 4.0 %collective-permute-start.1 = (bf16[4,128,1536]{2,1,0:T(8,128)(2,1)}, bf16[4,128,1536]{2,1,0:T(8,128)(2,1)S(1)}, u32[]{:S(2)}, u32[]{:S(2)}) collective-permute-start(bf16[4,128,1536]{2,1,0:T(8,128)(2,1)} %get-tuple-element.23), channel_id=1, source_target_pairs={{0,1},{1,0},{2,3},{3,2},{4,5},{5,4},{6,7},{7,6},{8,9},{9,8},{10,11... | collective-permute-start | bytes 4718600 | tf_op jit(solution)/shard_map/ppermute | solution.py:350
  126.8 1.4 copy-start.7
  128.2 22.3 %copy-start.1 = (bf16[1536,512]{1,0:T(8,128)(2,1)S(1)}, bf16[1536,512]{1,0:T(8,128)(2,1)}, u32[]{:S(2)}) copy-start(bf16[1536,512]{1,0:T(8,128)(2,1)} %fa.3) | copy-start | bytes 4718596
  128.2 22.3 %copy-start.3 = (bf16[1536,512]{1,0:T(8,128)(2,1)S(1)}, bf16[1536,512]{1,0:T(8,128)(2,1)}, u32[]{:S(2)}) copy-start(bf16[1536,512]{1,0:T(8,128)(2,1)} %fb.3) | copy-start | bytes 4718596
  128.2 22.3 %copy-start.11 = (s32[16,12]{1,0:T(8,128)S(1)}, s32[16,12]{1,0:T(8,128)}, u32[]{:S(2)}) copy-start(s32[16,12]{1,0:T(8,128)} %rows_a.3) | copy-start | bytes 2308
  129.6 11.6 %collective-permute-start.2 = (bf16[128,1536]{1,0:T(8,128)(2,1)S(1)}, bf16[128,1536]{1,0:T(8,128)(2,1)S(1)}, u32[]{:S(2)}, u32[]{:S(2)}) collective-permute-start(bf16[128,1536]{1,0:T(8,128)(2,1)S(1)} %get-tuple-element.25), channel_id=1, source_target_pairs={{0,2},{1,3},{2,4},{3,5},{4,6},{5,7},{6,0},{7,1},{8,10},{9,11},{10,... | collective-permute-start | bytes 1179656 | tf_op jit(solution)/shard_map/ppermute | solution.py:350
  130.8 19.7 %collective-permute-start.3 = (bf16[128,1536]{1,0:T(8,128)(2,1)S(1)}, bf16[128,1536]{1,0:T(8,128)(2,1)S(1)}, u32[]{:S(2)}, u32[]{:S(2)}) collective-permute-start(bf16[128,1536]{1,0:T(8,128)(2,1)S(1)} %get-tuple-element.26), channel_id=1, source_target_pairs={{0,4},{1,5},{2,6},{3,7},{4,0},{5,1},{6,2},{7,3},{8,12},{9,13},{10,... | collective-permute-start | bytes 1179656 | tf_op jit(solution)/shard_map/ppermute | solution.py:350
  133.2 17.3 %collective-permute-start.4 = (bf16[128,1536]{1,0:T(8,128)(2,1)S(1)}, bf16[128,1536]{1,0:T(8,128)(2,1)S(1)}, u32[]{:S(2)}, u32[]{:S(2)}) collective-permute-start(bf16[128,1536]{1,0:T(8,128)(2,1)S(1)} %get-tuple-element.27), channel_id=1, source_target_pairs={{0,6},{1,7},{2,0},{3,1},{4,2},{5,3},{6,4},{7,5},{8,14},{9,15},{10,... | collective-permute-start | bytes 1179656 | tf_op jit(solution)/shard_map/ppermute | solution.py:350
  153.0 22.4 %copy-start.5 = (bf16[512,512]{1,0:T(8,128)(2,1)S(1)}, bf16[512,512]{1,0:T(8,128)(2,1)}, u32[]{:S(2)}) copy-start(bf16[512,512]{1,0:T(8,128)(2,1)} %top.5) | copy-start | bytes 1572868
  153.0 22.4 %copy-start.9 = (f32[64,512]{1,0:T(8,128)S(1)}, f32[64,512]{1,0:T(8,128)}, u32[]{:S(2)}) copy-start(f32[64,512]{1,0:T(8,128)} %base.2) | copy-start | bytes 393220
  153.0 36.2 %copy-start.8 = (f32[64,512]{1,0:T(8,128)S(1)}, f32[64,512]{1,0:T(8,128)}, u32[]{:S(2)}) copy-start(f32[64,512]{1,0:T(8,128)} %base.3) | copy-start | bytes 393220
  190.2 1.9 copy-start.6
Sparse Core Ops, SparseCore 0:
  40.2 63.2 all-gather.4
  153.2 27.9 all-gather.6

commit v3 on v2

v3 whole, which is shorter than its diff:
```python
import functools

import jax
import jax.numpy as jnp
from jax import lax
from jax.experimental import pallas as pl
from jax.experimental.pallas import tpu as pltpu
from jax.sharding import PartitionSpec as P

BS = 128
W = 512
NB = 12
ROWS = NB * BS
SIDE = 4
PART = 64
COLS = 8
STEPS = (0, 1, -1, 2)
PAIR = 2 * PART
BOTH = ("row", "col")
MIB = 1024 * 1024
BF = jnp.bfloat16
F32 = jnp.float32


def device(z, y, x, core):
    return ((z % SIDE) * SIDE + y % SIDE) * 8 + (x % SIDE) * 2 + core % 2


def all_places():
    return [
        (z, y, x, core)
        for z in range(SIDE)
        for y in range(SIDE)
        for x in range(SIDE)
        for core in range(2)
    ]


def shifted(dz=0, dy=0, dx=0, dc=0):
    return [
        (device(z, y, x, c), device(z + dz, y + dy, x + dx, c + dc))
        for z, y, x, c in all_places()
    ]


def spread_pairs():
    pairs = []
    for z, y, x, core in all_places():
        plane = (z * SIDE + y) % 8
        to = device(z + core, y + x, plane // 2, plane % 2)
        pairs.append((device(z, y, x, core), to))
    return pairs


def params(mib=24, **more):
    return pltpu.CompilerParams(vmem_limit_bytes=mib * MIB, **more)


def cost(flops, moved):
    return pl.CostEstimate(flops=flops, bytes_accessed=moved, transcendentals=0)


def whole(shape):
    return pl.BlockSpec(shape, lambda *_: (0,) * len(shape))


def find_slot(rows, counts, owner, block):
    slot = jnp.int32(0)
    live = jnp.int32(0)
    for k in range(NB):
        hit = (rows[owner, k] == block) & (k < counts[owner])
        slot = jnp.where(hit, k, slot)
        live = jnp.where(hit, 1, live)
    return slot, live


def prep_body(place, rows_a, counts_a, rows_b, counts_b, fa, part_a, part_b, top, out_a, out_b, fix):
    owner = place[0]
    upper = place[1] % 2
    fix[...] = lax.dot_general(
        top[...], fa[...], (((0,), (1,)), ((), ())), preferred_element_type=F32
    )

    def half(value):
        return jnp.where(upper > 0, value[PART:], value[:PART])

    for block in range(NB):
        slot_a, live_a = find_slot(rows_a, counts_a, owner, block)
        slot_b, live_b = find_slot(rows_b, counts_b, owner, block)
        at_a = pl.ds(pl.multiple_of(slot_a * BS, BS), BS)
        at_b = pl.ds(pl.multiple_of(slot_b * BS, BS), BS)
        piece = half(part_a[at_a, :].T)
        out_a[block] = jnp.where(live_a > 0, piece, jnp.zeros_like(piece))
        moved = half(fix[:, at_a])
        piece = half(part_b[at_b, :].T).astype(F32)
        piece = jnp.where(live_b > 0, piece, jnp.zeros_like(piece))
        out_b[block] = (piece - jnp.where(live_a > 0, moved, jnp.zeros_like(moved))).astype(BF)


def prep(place, lists, factor_a, factor_b, factor_top):
    slice_spec = pl.BlockSpec((ROWS, BS), lambda i, place, *_: (0, place[1] // 2))
    out = jax.ShapeDtypeStruct((NB, PART, BS), BF)
    return pl.pallas_call(
        prep_body,
        name="prep",
        grid_spec=pltpu.PrefetchScalarGridSpec(
            num_scalar_prefetch=5,
            grid=(1,),
            in_specs=[
                whole((ROWS, W)),
                slice_spec,
                slice_spec,
                pl.BlockSpec((W, BS), lambda i, place, *_: (0, place[1] // 2)),
            ],
            out_specs=[whole((NB, PART, BS))] * 2,
            scratch_shapes=[pltpu.VMEM((BS, ROWS), F32)],
        ),
        out_shape=[out, out],
        compiler_params=params(56),
        cost_estimate=cost(2 * BS * ROWS * W, 2 * ROWS * (W + 4 * BS)),
    )(place, *lists, factor_a, factor_a, factor_b, factor_top)


def where(place):
    z, y, plane = place[0] // SIDE, place[0] % SIDE, place[1]
    u = (z - plane // SIDE + SIDE) % SIDE
    v = (y - plane % SIDE + SIDE) % SIDE
    return u, v


def turn(value, by):
    return (value + by + SIDE) % SIDE


def load_a(copies, buf, picks, u, spread, sems):
    for i, member in picks:
        copies.append((buf.at[member], spread.at[:, u // 2, i * PART : (i + 1) * PART, :]))


def load_b(copies, buf, picks, u, first, spread, sems):
    for i, member in picks:
        ui = turn(u, -STEPS[i])
        at = pl.ds(pl.multiple_of(first + (ui % 2) * PART, PART), PART)
        copies.append((buf.at[member], spread.at[:, ui // 2, at, :]))


def run_copies(copies, sems):
    started = [pltpu.make_async_copy(a, b, sems.at[i]) for i, (a, b) in enumerate(copies)]
    for copy in started:
        copy.start()
    for copy in started:
        copy.wait()


def multiply(spread, tile, first, last):
    left = jnp.concatenate(
        [spread[n, h, first:last, :] for n in range(NB) for h in range(2)], axis=1
    )
    return lax.dot_general(
        left, tile[...], (((1,), (1,)), ((), ())), preferred_element_type=F32
    ).astype(BF)


ALL = tuple((i, i) for i in range(SIDE))
FIRST = ((0, 0), (1, 1))
LAST = ((2, 0), (3, 1))


def early_body(place, a_down, a_up, b_own, b_down, b_up, tile, out, spread, sems):
    u, v = where(place)

    @pl.when(pl.program_id(0) == 0)
    def _():
        copies = []
        load_a(copies, a_down, ALL, turn(u, -1), spread, sems)
        load_a(copies, a_up, ALL, turn(u, 1), spread, sems)
        for t, buf in enumerate((b_own, b_down, b_up)):
            load_b(copies, buf, ALL, u, W // 2 + 2 * t * PART, spread, sems)
        run_copies(copies, sems)

    value = multiply(spread, tile, 0, W // 2)
    for i, step in enumerate(STEPS):
        out[2 * turn(v, -step) + (u + 1) % 2, :PART, :] = value[i * PART : (i + 1) * PART]
    for first, many in ((0, 2), (2, 1)):
        value = multiply(
            spread, tile, W // 2 + 2 * first * PART, W // 2 + 2 * (first + many) * PART
        )
        for j in range(2 * many):
            to = 2 * turn(v, -STEPS[first + j // 2]) + j % 2
            out[to, PART:, :] = value[j * PART : (j + 1) * PART]


def early_product(place, bufs, trailing):
    width = 2 * BS
    deep = trailing.shape[1]
    rows = W // 2 + 6 * PART
    return pl.pallas_call(
        early_body,
        name="early_product",
        grid_spec=pltpu.PrefetchScalarGridSpec(
            num_scalar_prefetch=1,
            grid=(ROWS // width,),
            in_specs=[pl.BlockSpec(memory_space=pl.ANY)] * 5
            + [pl.BlockSpec((width, deep), lambda i, *_: (i, 0))],
            out_specs=pl.BlockSpec((COLS, PAIR, width), lambda i, *_: (0, 0, i)),
            scratch_shapes=[
                pltpu.VMEM((NB, 2, rows, BS), BF),
                pltpu.SemaphoreType.DMA((20,)),
            ],
        ),
        out_shape=jax.ShapeDtypeStruct((COLS, PAIR, ROWS), BF),
        compiler_params=params(52, dimension_semantics=("arbitrary",)),
        cost_estimate=cost(2 * rows * ROWS * deep, 2 * ROWS * deep + 2 * rows * deep + 4 * W * ROWS),
    )(place, *bufs, trailing)


def late_body(
    place, a_own, a_far, a_far_more, b_far, b_far_more, tile, before, keep, give, spread, ready, sems
):
    u, v = where(place)
    core = place[1] % 2

    @pl.when(pl.program_id(0) == 0)
    def _():
        copies = []
        load_a(copies, a_own, ALL, u, spread, sems)
        load_a(copies, a_far, FIRST, turn(u, 2), spread, sems)
        load_a(copies, a_far_more, LAST, turn(u, 2), spread, sems)
        load_b(copies, b_far, FIRST, u, W // 2, spread, sems)
        load_b(copies, b_far_more, LAST, u, W // 2, spread, sems)
        run_copies(copies, sems)

    ready[...] = before[...]
    value = multiply(spread, tile, 0, W // 2)
    for i, step in enumerate(STEPS):
        ready[2 * turn(v, -step) + u % 2, :PART, :] = value[i * PART : (i + 1) * PART]
    value = multiply(spread, tile, W // 2, W // 2 + 2 * PART)
    for j in range(2):
        ready[2 * turn(v, 2) + j, PART:, :] = value[j * PART : (j + 1) * PART]
    for x in range(SIDE):
        keep[x] = ready[2 * x + core]
        give[x] = ready[2 * x + 1 - core]


def late_product(place, bufs, trailing, before):
    width = 2 * BS
    deep = trailing.shape[1]
    rows = W // 2 + 2 * PART
    out = jax.ShapeDtypeStruct((SIDE, PAIR, ROWS), BF)
    spec = pl.BlockSpec((SIDE, PAIR, width), lambda i, *_: (0, 0, i))
    return pl.pallas_call(
        late_body,
        name="late_product",
        grid_spec=pltpu.PrefetchScalarGridSpec(
            num_scalar_prefetch=1,
            grid=(ROWS // width,),
            in_specs=[pl.BlockSpec(memory_space=pl.ANY)] * 5
            + [
                pl.BlockSpec((width, deep), lambda i, *_: (i, 0)),
                pl.BlockSpec((COLS, PAIR, width), lambda i, *_: (0, 0, i)),
            ],
            out_specs=[spec, spec],
            scratch_shapes=[
                pltpu.VMEM((NB, 2, rows, BS), BF),
                pltpu.VMEM((COLS, PAIR, width), BF),
                pltpu.SemaphoreType.DMA((12,)),
            ],
        ),
        out_shape=[out, out],
        compiler_params=params(52, dimension_semantics=("arbitrary",)),
        cost_estimate=cost(2 * rows * ROWS * deep, 2 * ROWS * deep + 2 * rows * deep + 8 * W * ROWS),
    )(place, *bufs, trailing, before)


def pair_body(place, mine, taken, *outs):
    x = place[1] // 2
    for i in range(SIDE):
        at = (x + i) % SIDE
        outs[i][...] = (mine[at].astype(F32) + taken[at].astype(F32)).astype(BF)


def pair_sum(place, mine, taken):
    lanes = 4 * BS
    spec = pl.BlockSpec((SIDE, PAIR, lanes), lambda i, *_: (0, 0, i))
    return pl.pallas_call(
        pair_body,
        name="pair_sum",
        grid_spec=pltpu.PrefetchScalarGridSpec(
            num_scalar_prefetch=1,
            grid=(ROWS // lanes,),
            in_specs=[spec, spec],
            out_specs=[pl.BlockSpec((PAIR, lanes), lambda i, *_: (0, i))] * SIDE,
        ),
        out_shape=[jax.ShapeDtypeStruct((PAIR, ROWS), BF)] * SIDE,
        compiler_params=params(dimension_semantics=("arbitrary",)),
        cost_estimate=cost(W * ROWS, 6 * W * ROWS),
    )(place, mine, taken)


def slots_body(
    place, rows_a, counts_a, rows_b, counts_b, s0, s1, s2, s3, fa, fb, columns, pieces, natural, left
):
    owner = place[0]
    total = (s0[...].astype(F32) + s1[...].astype(F32)) + (
        s2[...].astype(F32) + s3[...].astype(F32)
    )
    natural[...] = (-total).astype(BF)
    for k in range(NB):
        at = slice(k * BS, (k + 1) * BS)
        block = natural[:PART, pl.ds(pl.multiple_of(rows_a[owner, k] * BS, BS), BS)]
        columns[:PART, at] = jnp.where(k < counts_a[owner], block, jnp.zeros_like(block))
        block = natural[:, pl.ds(pl.multiple_of(rows_b[owner, k] * BS, BS), BS)]
        block = jnp.where(k < counts_b[owner], block, jnp.zeros_like(block))
        left[:, at] = block
        columns[PART:, at] = block[PART:]
    one = jnp.dot(columns[:PART, :], fa[...], preferred_element_type=F32)
    two = jnp.dot(left[...], fb[...], preferred_element_type=F32)
    pieces[:PART, :] = one.astype(BF)
    pieces[PART:, :] = two.astype(BF)


def slots(place, lists, slabs, factors):
    return pl.pallas_call(
        slots_body,
        name="slots",
        grid_spec=pltpu.PrefetchScalarGridSpec(
            num_scalar_prefetch=5,
            grid=(1,),
            in_specs=[whole((PAIR, ROWS))] * SIDE + [whole((ROWS, W))] * 2,
            out_specs=[whole((PAIR, ROWS)), whole((3 * PART, W))],
            scratch_shapes=[pltpu.VMEM((PAIR, ROWS), BF)] * 2,
        ),
        out_shape=[
            jax.ShapeDtypeStruct((PAIR, ROWS), BF),
            jax.ShapeDtypeStruct((3 * PART, W), BF),
        ],
        compiler_params=params(),
        cost_estimate=cost(6 * PART * ROWS * W, 4 * ROWS * W + 10 * PAIR * ROWS),
    )(place, *lists, *slabs, *factors)


def column_body(place, *refs):
    slabs, column_a, column_b, wide = refs[:8], refs[8], refs[9], refs[10]
    core, x = place[1] % 2, place[1] // 2
    for i in range(8):
        at = 2 * turn(x, -STEPS[i % SIDE]) + (core if i < SIDE else 1 - core)
        wide[at] = slabs[i][...]
    for first, out in ((0, column_a), (PART, column_b)):
        out[...] = wide[:, first : first + PART, :].reshape(W, wide.shape[2]).T


def whole_columns(place, slabs):
    lanes = 2 * BS
    out = jax.ShapeDtypeStruct((ROWS, W), BF)
    return pl.pallas_call(
        column_body,
        name="whole_columns",
        grid_spec=pltpu.PrefetchScalarGridSpec(
            num_scalar_prefetch=1,
            grid=(ROWS // lanes,),
            in_specs=[pl.BlockSpec((PAIR, lanes), lambda i, *_: (0, i))] * 8,
            out_specs=[pl.BlockSpec((lanes, W), lambda i, *_: (i, 0))] * 2,
            scratch_shapes=[pltpu.VMEM((COLS, PAIR, lanes), BF)],
        ),
        out_shape=[out, out],
        compiler_params=params(dimension_semantics=("arbitrary",)),
        cost_estimate=cost(0, 8 * ROWS * W),
    )(place, *slabs)


def total_of(refs, rows):
    parts = [ref[rows, :].astype(F32) for ref in refs]
    return (parts[0] + parts[1]) + (parts[2] + parts[3])


def fold_body(one, two, three, four, out):
    out[...] = total_of((one, two, three, four), slice(None)).astype(BF)


def fold(parts):
    return pl.pallas_call(
        fold_body,
        name="fold",
        out_shape=jax.ShapeDtypeStruct(parts[0].shape, BF),
        compiler_params=params(8),
        cost_estimate=cost(4 * parts[0].size, 10 * parts[0].size),
    )(*parts)


def top_body(one, two, three, four, base, top, diag_a, top_b, sent):
    got = (one, two, three, four)
    value = base[...] - total_of(got, slice(0, PART))
    diag_a[...] = value
    total = total_of(got, slice(PART, 2 * PART))
    for _ in range(3):
        part = value.astype(BF)
        value = value - part.astype(F32)
        total = total + jnp.dot(part, top[...], preferred_element_type=F32)
    total = (-total).astype(BF)
    top_b[...] = total
    for c in range(COLS):
        sent[c] = jnp.concatenate([total[:, c * PART : (c + 1) * PART]] * 2, axis=1)


def top_part(got, base_a, factor_top):
    return pl.pallas_call(
        top_body,
        name="top_part",
        out_shape=[
            jax.ShapeDtypeStruct((PART, W), F32),
            jax.ShapeDtypeStruct((PART, W), BF),
            jax.ShapeDtypeStruct((COLS, PART, 2 * PART), BF),
        ],
        compiler_params=params(8),
        cost_estimate=cost(6 * PART * W * W, 2 * W * W),
    )(*got, base_a, factor_top)


def last_body(one, two, three, four, base, taken, top, diag_b):
    across = taken[...].reshape(W, 2 * PART)
    cross = lax.dot_general(
        across, top[...], (((0,), (0,)), ((), ())), preferred_element_type=F32
    )
    total = total_of((one, two, three, four), slice(2 * PART, 3 * PART))
    diag_b[...] = base[...] - total - cross[:PART]


def last_part(got, base_b, taken, factor_top):
    return pl.pallas_call(
        last_body,
        name="last_part",
        out_shape=jax.ShapeDtypeStruct((PART, W), F32),
        compiler_params=params(8),
        cost_estimate=cost(4 * PART * W * W, 2 * W * W),
    )(*got, base_b, taken, factor_top)


def send(value, **by):
    return lax.ppermute(value, BOTH, shifted(**by))


def around(value, axis):
    return [value] + [send(value, **{axis: step}) for step in STEPS[1:]]


def on_device(
    trailing, rows_a, counts_a, factor_a, rows_b, counts_b, factor_b, factor_top, base_a, base_b
):
    place = jnp.stack([lax.axis_index("row"), lax.axis_index("col")]).astype(jnp.int32)
    lists = (rows_a, counts_a, rows_b, counts_b)
    part_a, part_b = prep(place, lists, factor_a, factor_b, factor_top)
    part_a = lax.ppermute(part_a, BOTH, spread_pairs())
    part_b = lax.ppermute(part_b, BOTH, spread_pairs())
    a_own = jnp.stack(around(part_a, "dy"))
    b_own = jnp.stack(around(part_b, "dz"))
    a_down, a_up = send(a_own, dz=1), send(a_own, dz=-1)
    b_down, b_up = send(b_own, dy=1), send(b_own, dy=-1)
    a_far, a_far_more = send(a_down[:2], dz=1), send(a_up[2:], dz=-1)
    b_far, b_far_more = send(b_down[:2], dy=1), send(b_up[2:], dy=-1)
    before = early_product(place, (a_down, a_up, b_own, b_down, b_up), trailing)
    keep, give = late_product(
        place, (a_own, a_far, a_far_more, b_far, b_far_more), trailing, before
    )

    own, one, two, three = pair_sum(place, keep, send(give, dc=1))
    slabs = [own, send(one, dx=1), send(two, dx=2), send(three, dx=-1)]
    columns, pieces = slots(place, lists, slabs, (factor_a, factor_b))
    got = around(fold(around(pieces, "dy")), "dz")
    mine = around(columns, "dx")
    column_a, column_b = whole_columns(place, mine + [send(slab, dc=1) for slab in mine])
    diag_a, top_b, sent = top_part(got, base_a, factor_top)
    taken = lax.all_to_all(sent, "col", 0, 0)
    diag_b = last_part(got, base_b, taken, factor_top)
    return (column_a, diag_a, column_b, top_b, diag_b)


def solution(mesh):
    in_specs = (
        P("row", "col"),
        P(),
        P(),
        P("row", None),
        P(),
        P(),
        P("row", None),
        P(),
        P("col", None),
        P("col", None),
    )
    out_specs = (P("row", None), P("col", None), P("row", None), P("col", None), P("col", None))
    return jax.shard_map(
        on_device, mesh=mesh, in_specs=in_specs, out_specs=out_specs, check_vma=False
    )
```

time: 203 us -> 177 us (0.87)
  starting transfers between devices: 11.3 us -> 55.6 us
  waiting for transfers between devices: 99.8 us -> 68.7 us
  blocking collectives: 35.1 us -> 8.97 us
  between operations: 14.1 us -> 0.98 us
  local copies, waits for them, and re-layouts: 11.4 us -> 1.59 us
  Pallas kernels: 30.1 us -> 39.9 us
    all_gather x2 -> x0, waiting for transfers between devices: 63.4 us -> none  [the longest x1 63.4 us: on_device(): gathered = lax.all_gather(chunk, 'row', axis=0)]
    ppermute x4 -> x31, starting transfers between devices: 5.59 us -> 45.8 us  [send(): return lax.ppermute(value, BOTH, shifted(**by))]
    ppermute x4 -> x31, waiting for transfers between devices: 19.4 us -> 55.3 us  [send(): return lax.ppermute(value, BOTH, shifted(**by))]
    all_to_all x2 -> x0, blocking collectives: 22.3 us -> none  [the longest x1 12.2 us: row_sum(): parts = lax.all_to_all(pieces, 'row', 0, 0)]
    unnamed x44 -> x30, local copies, waits for them, and re-layouts: 11.4 us -> 1.48 us
    pallas_call x3 -> x4, Pallas kernels: 22.4 us -> 30.2 us  [the longest x1 13.9 us: early_product(): pl.pallas_call(early_body, name='early_product', grid_spec=pltpu.Prefetch...]
    ppermute x1 -> x2, starting transfers between devices: 5.66 us -> 9.86 us  [the longest x1 4.94 us: on_device(): part_a = lax.ppermute(part_a, BOTH, spread_pairs())]
    all_to_all x1, blocking collectives: 12.8 us -> 8.97 us  [on_device(): taken = lax.all_to_all(sent, 'col', 0, 0)]
  transfers between devices with their start and end apart: 7 -> 33, of which waited for: 5 -> 13; matrix products, arithmetic and copies ran while one was open for 0% -> 0% of each run, Pallas kernels for 1% -> 9%
where the time goes in v3:
time: 177 us
  waiting for transfers between devices  68.7 us (39%)
  starting transfers between devices  55.6 us (31%)
  Pallas kernels  39.9 us (23%)
  blocking collectives  8.97 us (5%)
    ppermute x31, waiting for transfers between devices, send(): return lax.ppermute(value, BOTH, shifted(**by))  55.3 us
    ppermute x31, starting transfers between devices, send(): return lax.ppermute(value, BOTH, shifted(**by))  45.8 us
    pallas_call x1, Pallas kernels, early_product(): pl.pallas_call(early_body, name='early_product', grid_spec=pltpu.Prefetch...  13.9 us
    ppermute x1, waiting for transfers between devices, on_device(): part_b = lax.ppermute(part_b, BOTH, spread_pairs())  13.4 us
    pallas_call x1, Pallas kernels, late_product(): pl.pallas_call(late_body, name='late_product', grid_spec=pltpu.PrefetchSc...  12.3 us
    all_to_all x1, blocking collectives, on_device(): taken = lax.all_to_all(sent, 'col', 0, 0)  8.97 us
    ppermute x1, starting transfers between devices, on_device(): part_a = lax.ppermute(part_a, BOTH, spread_pairs())  4.94 us
    ppermute x1, starting transfers between devices, on_device(): part_b = lax.ppermute(part_b, BOTH, spread_pairs())  4.92 us
  transfers between devices with their start and end apart: 33, of which 13 were waited for; matrix products, arithmetic and copies ran while one was open for 0% of the time, Pallas kernels for 9%

profile of v3, /device:TPU:1, one launch (start us, length us, event | category | flops | bytes accessed | tf_op | source)
XLA Modules:
  0.0 176.5 jit_solution(13702378069328315260)
XLA Ops:
  0.6 0.6 pad_add_fusion.place
  1.2 4.5 %prep.1 = (bf16[12,64,128]{2,1,0:T(8,128)(2,1)}, bf16[12,64,128]{2,1,0:T(8,128)(2,1)}) custom-call(s32[2]{0:T(128)} %pad_add_fusion.place, s32[16,12]{1,0:T(8,128)} %rows_a.3, s32[16]{0:T(128)} %counts_a.3, s32[16,12]{1,0:T(8,128)} %rows_b.3, s32[16]{0:T(128)} %counts_b.3, bf16[1536,512]{1,0:T(8,128)(2,1)} %fa.3, bf16[1536,512]{1,0:T(8,128)(2,1)} %fa.3, ...), custom_call_target="tpu_custom_call" | custom-call | flops 201326592 | bytes 3145728 | tf_op jit(solution)/shard_map/prep/pallas_call | solution.py:103
  5.7 4.9 %collective-permute-start.8 = (bf16[12,64,128]{2,1,0:T(8,128)(2,1)}, bf16[12,64,128]{2,1,0:T(8,128)(2,1)S(1)}, u32[]{:S(2)}, u32[]{:S(2)}) collective-permute-start(bf16[12,64,128]{2,1,0:T(8,128)(2,1)} %get-tuple-element.21), channel_id=1, source_target_pairs={{0,0},{1,32},{2,8},{3,40},{4,16},{5,48},{6,24},{7,56},{8,9},{9,41}... | collective-permute-start | bytes 589832 | tf_op jit(solution)/shard_map/ppermute | solution.py:453
  10.7 4.9 %collective-permute-start = (bf16[12,64,128]{2,1,0:T(8,128)(2,1)}, bf16[12,64,128]{2,1,0:T(8,128)(2,1)S(1)}, u32[]{:S(2)}, u32[]{:S(2)}) collective-permute-start(bf16[12,64,128]{2,1,0:T(8,128)(2,1)} %get-tuple-element.20), channel_id=1, source_target_pairs={{0,0},{1,32},{2,8},{3,40},{4,16},{5,48},{6,24},{7,56},{8,9},{9,41}... | collective-permute-start | bytes 589832 | tf_op jit(solution)/shard_map/ppermute | solution.py:452
  15.6 13.4 %collective-permute-done.8 = bf16[12,64,128]{2,1,0:T(8,128)(2,1)S(1)} collective-permute-done((bf16[12,64,128]{2,1,0:T(8,128)(2,1)}, bf16[12,64,128]{2,1,0:T(8,128)(2,1)S(1)}, u32[]{:S(2)}, u32[]{:S(2)}) %collective-permute-start.8) | collective-permute-done | bytes 196640 | tf_op jit(solution)/shard_map/ppermute | solution.py:453
  29.0 2.2 %collective-permute-start.9 = (bf16[12,64,128]{2,1,0:T(8,128)(2,1)S(1)}, bf16[12,64,128]{2,1,0:T(8,128)(2,1)S(1)}, u32[]{:S(2)}, u32[]{:S(2)}) collective-permute-start(bf16[12,64,128]{2,1,0:T(8,128)(2,1)S(1)} %collective-permute-done.8), channel_id=1, source_target_pairs={{0,32},{1,33},{2,34},{3,35},{4,36},{5,37},{6,38},{7,39},{8,40},{9,... | collective-permute-start | bytes 589832 | tf_op jit(solution)/shard_map/ppermute | solution.py:439
  31.2 2.2 %collective-permute-start.10 = (bf16[12,64,128]{2,1,0:T(8,128)(2,1)S(1)}, bf16[12,64,128]{2,1,0:T(8,128)(2,1)S(1)}, u32[]{:S(2)}, u32[]{:S(2)}) collective-permute-start(bf16[12,64,128]{2,1,0:T(8,128)(2,1)S(1)} %collective-permute-done.8), channel_id=1, source_target_pairs={{0,96},{1,97},{2,98},{3,99},{4,100},{5,101},{6,102},{7,103},{8,104... | collective-permute-start | bytes 589832 | tf_op jit(solution)/shard_map/ppermute | solution.py:439
  33.4 1.2 collective-permute-start.11
  34.6 2.7 %collective-permute-start.2 = (bf16[12,64,128]{2,1,0:T(8,128)(2,1)S(1)}, bf16[12,64,128]{2,1,0:T(8,128)(2,1)S(1)}, u32[]{:S(2)}, u32[]{:S(2)}) collective-permute-start(bf16[12,64,128]{2,1,0:T(8,128)(2,1)S(1)} %collective-permute-done), channel_id=1, source_target_pairs={{0,24},{1,25},{2,26},{3,27},{4,28},{5,29},{6,30},{7,31},{8,0},{9,1... | collective-permute-start | bytes 589832 | tf_op jit(solution)/shard_map/ppermute | solution.py:439
  37.3 0.8 collective-permute-done.10
  38.1 2.5 %collective-permute-done.11 = bf16[12,64,128]{2,1,0:T(8,128)(2,1)S(1)} collective-permute-done((bf16[12,64,128]{2,1,0:T(8,128)(2,1)S(1)}, bf16[12,64,128]{2,1,0:T(8,128)(2,1)S(1)}, u32[]{:S(2)}, u32[]{:S(2)}) %collective-permute-start.11) | collective-permute-done | bytes 196640 | tf_op jit(solution)/shard_map/ppermute | solution.py:439
  40.6 0.1 pad_maximum_fusion.1.b_own
  40.7 0.0 copy-start.12
  40.8 0.1 collective-permute-start.12
  40.8 2.7 %collective-permute-start.14 = (bf16[4,12,64,128]{3,2,1,0:T(8,128)(2,1)S(1)}, bf16[4,12,64,128]{3,2,1,0:T(8,128)(2,1)S(1)}, u32[]{:S(2)}, u32[]{:S(2)}) collective-permute-start(bf16[4,12,64,128]{3,2,1,0:T(8,128)(2,1)S(1)} %pad_maximum_fusion.1.b_own), channel_id=1, source_target_pairs={{0,24},{1,25},{2,26},{3,27},{4,28},{5,29},{6,30},{7,31},{8,0},{9,1... | collective-permute-start | bytes 2359304 | tf_op jit(solution)/shard_map/ppermute | solution.py:439
  43.5 2.4 %collective-permute-done.1 = bf16[12,64,128]{2,1,0:T(8,128)(2,1)S(1)} collective-permute-done((bf16[12,64,128]{2,1,0:T(8,128)(2,1)S(1)}, bf16[12,64,128]{2,1,0:T(8,128)(2,1)S(1)}, u32[]{:S(2)}, u32[]{:S(2)}) %collective-permute-start.1) | collective-permute-done | bytes 196640 | tf_op jit(solution)/shard_map/ppermute | solution.py:439
  45.9 0.1 pad_maximum_fusion.a_own
  46.1 0.0 copy-start.8
  46.1 0.7 collective-permute-start.4
  46.7 3.3 %collective-permute-start.6 = (bf16[4,12,64,128]{3,2,1,0:T(8,128)(2,1)S(1)}, bf16[4,12,64,128]{3,2,1,0:T(8,128)(2,1)S(1)}, u32[]{:S(2)}, u32[]{:S(2)}) collective-permute-start(bf16[4,12,64,128]{3,2,1,0:T(8,128)(2,1)S(1)} %pad_maximum_fusion.a_own), channel_id=1, source_target_pairs={{0,96},{1,97},{2,98},{3,99},{4,100},{5,101},{6,102},{7,103},{8,104... | collective-permute-start | bytes 2359304 | tf_op jit(solution)/shard_map/ppermute | solution.py:439
  50.0 13.5 %collective-permute-done.12.b_down = bf16[4,12,64,128]{3,2,1,0:T(8,128)(2,1)S(1)} collective-permute-done((bf16[4,12,64,128]{3,2,1,0:T(8,128)(2,1)S(1)}, bf16[4,12,64,128]{3,2,1,0:T(8,128)(2,1)S(1)}, u32[]{:S(2)}, u32[]{:S(2)}) %collective-permute-start.12) | collective-permute-done | bytes 786464 | tf_op jit(solution)/shard_map/ppermute | solution.py:439
  63.6 0.1 collective-permute-start.13
  63.7 2.7 %collective-permute-start.15 = (bf16[2,12,64,128]{3,2,1,0:T(8,128)(2,1)S(1)}, bf16[2,12,64,128]{3,2,1,0:T(8,128)(2,1)S(1)}, u32[]{:S(2)}, u32[]{:S(2)}) collective-permute-start(bf16[2,12,64,128]{3,2,1,0:T(8,128)(2,1)S(1)} %slice.19), channel_id=1, source_target_pairs={{0,24},{1,25},{2,26},{3,27},{4,28},{5,29},{6,30},{7,31},{8,0},{9,1... | collective-permute-start | bytes 1179656 | tf_op jit(solution)/shard_map/ppermute | solution.py:439
  66.4 0.4 collective-permute-done.4.a_down
  66.8 0.8 collective-permute-start.5
  67.7 2.0 %collective-permute-start.7 = (bf16[2,12,64,128]{3,2,1,0:T(8,128)(2,1)S(1)}, bf16[2,12,64,128]{3,2,1,0:T(8,128)(2,1)S(1)}, u32[]{:S(2)}, u32[]{:S(2)}) collective-permute-start(bf16[2,12,64,128]{3,2,1,0:T(8,128)(2,1)S(1)} %slice.17), channel_id=1, source_target_pairs={{0,96},{1,97},{2,98},{3,99},{4,100},{5,101},{6,102},{7,103},{8,104... | collective-permute-start | bytes 1179656 | tf_op jit(solution)/shard_map/ppermute | solution.py:439
  69.7 13.9 %early_product.1.before = bf16[8,128,1536]{2,1,0:T(8,128)(2,1)} custom-call(s32[2]{0:T(128)S(1)} %copy-done.8, bf16[4,12,64,128]{3,2,1,0:T(8,128)(2,1)S(1)} %collective-permute-done.4.a_down, bf16[4,12,64,128]{3,2,1,0:T(8,128)(2,1)S(1)} %collective-permute-done.6.a_up, bf16[4,12,64,128]{3,2,1,0:T(8,128)(2,1)} %copy-done.12, ...), custom_call_target="tpu_custom_call" | custom-call | flops 6039797760 | bytes 16515072 | tf_op jit(solution)/shard_map/early_product/pallas_call | solution.py:197
  83.6 0.0 copy-start.7
  83.6 0.0 copy-start.9
  83.6 0.0 copy-start.10
  83.6 12.3 %late_product.1 = (bf16[4,128,1536]{2,1,0:T(8,128)(2,1)}, bf16[4,128,1536]{2,1,0:T(8,128)(2,1)}) custom-call(s32[2]{0:T(128)S(1)} %copy-done.8, bf16[4,12,64,128]{3,2,1,0:T(8,128)(2,1)} %copy-done.11, bf16[2,12,64,128]{3,2,1,0:T(8,128)(2,1)S(1)} %collective-permute-done.5.a_far, bf16[2,12,64,128]{3,2,1,0:T(8,128)(2,1)S(1)} %collective-permute-done.7.a_far_more, ...), custom_call_target="tpu_custom_call" | custom-call | flops 3623878656 | bytes 18087936 | tf_op jit(solution)/shard_map/late_product/pallas_call | solution.py:251
  95.9 2.3 %collective-permute-start.16 = (bf16[4,128,1536]{2,1,0:T(8,128)(2,1)}, bf16[4,128,1536]{2,1,0:T(8,128)(2,1)S(1)}, u32[]{:S(2)}, u32[]{:S(2)}) collective-permute-start(bf16[4,128,1536]{2,1,0:T(8,128)(2,1)} %get-tuple-element.23), channel_id=1, source_target_pairs={{0,1},{1,0},{2,3},{3,2},{4,5},{5,4},{6,7},{7,6},{8,9},{9,8},{10,11... | collective-permute-start | bytes 4718600 | tf_op jit(solution)/shard_map/ppermute | solution.py:439
  98.2 3.2 %collective-permute-done.16.taken = bf16[4,128,1536]{2,1,0:T(8,128)(2,1)S(1)} collective-permute-done((bf16[4,128,1536]{2,1,0:T(8,128)(2,1)}, bf16[4,128,1536]{2,1,0:T(8,128)(2,1)S(1)}, u32[]{:S(2)}, u32[]{:S(2)}) %collective-permute-start.16) | collective-permute-done | bytes 1572896 | tf_op jit(solution)/shard_map/ppermute | solution.py:439
  101.4 1.4 copy-done.3
  102.8 1.3 pair_sum.1
  104.2 0.1 collective-permute-start.17
  104.3 4.2 %collective-permute-start.18 = (bf16[128,1536]{1,0:T(8,128)(2,1)S(1)}, bf16[128,1536]{1,0:T(8,128)(2,1)S(1)}, u32[]{:S(2)}, u32[]{:S(2)}) collective-permute-start(bf16[128,1536]{1,0:T(8,128)(2,1)S(1)} %get-tuple-element.26), channel_id=1, source_target_pairs={{0,4},{1,5},{2,6},{3,7},{4,0},{5,1},{6,2},{7,3},{8,12},{9,13},{10,... | collective-permute-start | bytes 1179656 | tf_op jit(solution)/shard_map/ppermute | solution.py:439
  108.4 8.0 %collective-permute-done.17.s1 = bf16[128,1536]{1,0:T(8,128)(2,1)S(1)} collective-permute-done((bf16[128,1536]{1,0:T(8,128)(2,1)S(1)}, bf16[128,1536]{1,0:T(8,128)(2,1)S(1)}, u32[]{:S(2)}, u32[]{:S(2)}) %collective-permute-start.17) | collective-permute-done | bytes 393248 | tf_op jit(solution)/shard_map/ppermute | solution.py:439
  116.4 9.3 %collective-permute-done.18.s2 = bf16[128,1536]{1,0:T(8,128)(2,1)S(1)} collective-permute-done((bf16[128,1536]{1,0:T(8,128)(2,1)S(1)}, bf16[128,1536]{1,0:T(8,128)(2,1)S(1)}, u32[]{:S(2)}, u32[]{:S(2)}) %collective-permute-start.18) | collective-permute-done | bytes 393248 | tf_op jit(solution)/shard_map/ppermute | solution.py:439
  125.8 0.0 copy-start.2
  125.8 1.9 %slots.1 = (bf16[128,1536]{1,0:T(8,128)(2,1)S(1)}, bf16[192,512]{1,0:T(8,128)(2,1)S(1)}) custom-call(s32[2]{0:T(128)S(1)} %copy-done.8, s32[16,12]{1,0:T(8,128)S(1)} %copy-done.6, s32[16]{0:T(128)S(1)} %copy-done.9, s32[16,12]{1,0:T(8,128)S(1)} %copy-done.7, s32[16]{0:T(128)S(1)} %copy-done.10, bf16[128,1536]{1,0:T(8,128)(2,1)S(1)} %get-tuple-element.24.s0, ...), custom_call_target="tpu_custom_call" | custom-call | flops 301989888 | bytes 5111808 | tf_op jit(solution)/shard_map/slots/pallas_call | solution.py:323
  127.7 0.0 copy-start.5
  127.7 0.1 collective-permute-start.27
  127.8 2.7 %collective-permute-start.28 = (bf16[192,512]{1,0:T(8,128)(2,1)S(1)}, bf16[192,512]{1,0:T(8,128)(2,1)S(1)}, u32[]{:S(2)}, u32[]{:S(2)}) collective-permute-start(bf16[192,512]{1,0:T(8,128)(2,1)S(1)} %get-tuple-element.30.one), channel_id=1, source_target_pairs={{0,24},{1,25},{2,26},{3,27},{4,28},{5,29},{6,30},{7,31},{8,0},{9,1... | collective-permute-start | bytes 589832 | tf_op jit(solution)/shard_map/ppermute | solution.py:439
  130.5 0.0 collective-permute-start.29
  130.5 1.3 collective-permute-start.20
  131.8 2.1 %collective-permute-start.21 = (bf16[128,1536]{1,0:T(8,128)(2,1)S(1)}, bf16[128,1536]{1,0:T(8,128)(2,1)S(1)}, u32[]{:S(2)}, u32[]{:S(2)}) collective-permute-start(bf16[128,1536]{1,0:T(8,128)(2,1)S(1)} %get-tuple-element.28.refs_0_), channel_id=1, source_target_pairs={{0,6},{1,7},{2,0},{3,1},{4,2},{5,3},{6,4},{7,5},{8,14},{9,15},{10,... | collective-permute-start | bytes 1179656 | tf_op jit(solution)/shard_map/ppermute | solution.py:439
  133.9 0.3 collective-permute-done.27.two
  134.2 0.9 collective-permute-start.22
  135.1 3.8 %collective-permute-done.29.four = bf16[192,512]{1,0:T(8,128)(2,1)S(1)} collective-permute-done((bf16[192,512]{1,0:T(8,128)(2,1)S(1)}, bf16[192,512]{1,0:T(8,128)(2,1)S(1)}, u32[]{:S(2)}, u32[]{:S(2)}) %collective-permute-start.29) | collective-permute-done | bytes 196640 | tf_op jit(solution)/shard_map/ppermute | solution.py:439
  138.9 0.1 fold.1.one
  139.0 0.1 collective-permute-start.30
  139.1 2.7 %collective-permute-start.31 = (bf16[192,512]{1,0:T(8,128)(2,1)S(1)}, bf16[192,512]{1,0:T(8,128)(2,1)S(1)}, u32[]{:S(2)}, u32[]{:S(2)}) collective-permute-start(bf16[192,512]{1,0:T(8,128)(2,1)S(1)} %fold.1.one), channel_id=1, source_target_pairs={{0,96},{1,97},{2,98},{3,99},{4,100},{5,101},{6,102},{7,103},{8,104... | collective-permute-start | bytes 589832 | tf_op jit(solution)/shard_map/ppermute | solution.py:439
  141.7 3.1 %collective-permute-done.30.two = bf16[192,512]{1,0:T(8,128)(2,1)S(1)} collective-permute-done((bf16[192,512]{1,0:T(8,128)(2,1)S(1)}, bf16[192,512]{1,0:T(8,128)(2,1)S(1)}, u32[]{:S(2)}, u32[]{:S(2)}) %collective-permute-start.30) | collective-permute-done | bytes 196640 | tf_op jit(solution)/shard_map/ppermute | solution.py:439
  144.8 2.8 %collective-permute-start.23 = (bf16[128,1536]{1,0:T(8,128)(2,1)S(1)}, bf16[128,1536]{1,0:T(8,128)(2,1)S(1)}, u32[]{:S(2)}, u32[]{:S(2)}) collective-permute-start(bf16[128,1536]{1,0:T(8,128)(2,1)S(1)} %get-tuple-element.28.refs_0_), channel_id=1, source_target_pairs={{0,1},{1,0},{2,3},{3,2},{4,5},{5,4},{6,7},{7,6},{8,9},{9,8},{10,11... | collective-permute-start | bytes 1179656 | tf_op jit(solution)/shard_map/ppermute | solution.py:439
  147.6 0.0 collective-permute-start.24
  147.6 4.0 %collective-permute-start.25 = (bf16[128,1536]{1,0:T(8,128)(2,1)S(1)}, bf16[128,1536]{1,0:T(8,128)(2,1)S(1)}, u32[]{:S(2)}, u32[]{:S(2)}) collective-permute-start(bf16[128,1536]{1,0:T(8,128)(2,1)S(1)} %collective-permute-done.21.refs_2_), channel_id=1, source_target_pairs={{0,1},{1,0},{2,3},{3,2},{4,5},{5,4},{6,7},{7,6},{8,9},{9,8},{10,11... | collective-permute-start | bytes 1179656 | tf_op jit(solution)/shard_map/ppermute | solution.py:439
  151.7 1.9 %collective-permute-start.26 = (bf16[128,1536]{1,0:T(8,128)(2,1)S(1)}, bf16[128,1536]{1,0:T(8,128)(2,1)S(1)}, u32[]{:S(2)}, u32[]{:S(2)}) collective-permute-start(bf16[128,1536]{1,0:T(8,128)(2,1)S(1)} %collective-permute-done.22.refs_3_), channel_id=1, source_target_pairs={{0,1},{1,0},{2,3},{3,2},{4,5},{5,4},{6,7},{7,6},{8,9},{9,8},{10,11... | collective-permute-start | bytes 1179656 | tf_op jit(solution)/shard_map/ppermute | solution.py:439
  153.5 0.2 collective-permute-start.32
  153.8 7.8 %collective-permute-done.32.four = bf16[192,512]{1,0:T(8,128)(2,1)S(1)} collective-permute-done((bf16[192,512]{1,0:T(8,128)(2,1)S(1)}, bf16[192,512]{1,0:T(8,128)(2,1)S(1)}, u32[]{:S(2)}, u32[]{:S(2)}) %collective-permute-start.32) | collective-permute-done | bytes 196640 | tf_op jit(solution)/shard_map/ppermute | solution.py:439
  161.6 1.0 top_part.1
  162.6 9.0 %all_to_all.5.taken = bf16[8,64,128]{2,1,0:T(8,128)(2,1)S(1)} all-to-all(bf16[8,64,128]{2,1,0:T(8,128)(2,1)S(1)} %get-tuple-element.34), channel_id=1, replica_groups=mesh['row'=16,'col'=8] {'col'}, dimensions={0} | all-to-all | bytes 262144 | tf_op jit(solution)/shard_map/all_to_all | solution.py:472
  171.6 0.9 last_part.1
  172.5 4.0 %whole_columns.1 = (bf16[1536,512]{1,0:T(8,128)(2,1)}, bf16[1536,512]{1,0:T(8,128)(2,1)}) custom-call(s32[2]{0:T(128)S(1)} %copy-done.8, bf16[128,1536]{1,0:T(8,128)(2,1)S(1)} %get-tuple-element.28.refs_0_, bf16[128,1536]{1,0:T(8,128)(2,1)S(1)} %collective-permute-done.20.refs_1_, bf16[128,1536]{1,0:T(8,128)(2,1)S(1)} %collective-permute-done.21.refs_2_, ...), custom_call_target="tpu_custom_call" | custom-call | bytes 6291456 | tf_op jit(solution)/shard_map/whole_columns/pallas_call | solution.py:355
  (49 shorter events, 0.2 us)
Async XLA Ops:
  5.7 23.3 %collective-permute-start.8 = (bf16[12,64,128]{2,1,0:T(8,128)(2,1)}, bf16[12,64,128]{2,1,0:T(8,128)(2,1)S(1)}, u32[]{:S(2)}, u32[]{:S(2)}) collective-permute-start(bf16[12,64,128]{2,1,0:T(8,128)(2,1)} %get-tuple-element.21), channel_id=1, source_target_pairs={{0,0},{1,32},{2,8},{3,40},{4,16},{5,48},{6,24},{7,56},{8,9},{9,41}... | collective-permute-start | bytes 589832 | tf_op jit(solution)/shard_map/ppermute | solution.py:453
  10.7 23.9 %collective-permute-start = (bf16[12,64,128]{2,1,0:T(8,128)(2,1)}, bf16[12,64,128]{2,1,0:T(8,128)(2,1)S(1)}, u32[]{:S(2)}, u32[]{:S(2)}) collective-permute-start(bf16[12,64,128]{2,1,0:T(8,128)(2,1)} %get-tuple-element.20), channel_id=1, source_target_pairs={{0,0},{1,32},{2,8},{3,40},{4,16},{5,48},{6,24},{7,56},{8,9},{9,41}... | collective-permute-start | bytes 589832 | tf_op jit(solution)/shard_map/ppermute | solution.py:452
  29.0 8.3 %collective-permute-start.9 = (bf16[12,64,128]{2,1,0:T(8,128)(2,1)S(1)}, bf16[12,64,128]{2,1,0:T(8,128)(2,1)S(1)}, u32[]{:S(2)}, u32[]{:S(2)}) collective-permute-start(bf16[12,64,128]{2,1,0:T(8,128)(2,1)S(1)} %collective-permute-done.8), channel_id=1, source_target_pairs={{0,32},{1,33},{2,34},{3,35},{4,36},{5,37},{6,38},{7,39},{8,40},{9,... | collective-permute-start | bytes 589832 | tf_op jit(solution)/shard_map/ppermute | solution.py:439
  31.2 6.9 %collective-permute-start.10 = (bf16[12,64,128]{2,1,0:T(8,128)(2,1)S(1)}, bf16[12,64,128]{2,1,0:T(8,128)(2,1)S(1)}, u32[]{:S(2)}, u32[]{:S(2)}) collective-permute-start(bf16[12,64,128]{2,1,0:T(8,128)(2,1)S(1)} %collective-permute-done.8), channel_id=1, source_target_pairs={{0,96},{1,97},{2,98},{3,99},{4,100},{5,101},{6,102},{7,103},{8,104... | collective-permute-start | bytes 589832 | tf_op jit(solution)/shard_map/ppermute | solution.py:439
  33.4 7.2 %collective-permute-start.11 = (bf16[12,64,128]{2,1,0:T(8,128)(2,1)S(1)}, bf16[12,64,128]{2,1,0:T(8,128)(2,1)S(1)}, u32[]{:S(2)}, u32[]{:S(2)}) collective-permute-start(bf16[12,64,128]{2,1,0:T(8,128)(2,1)S(1)} %collective-permute-done.8), channel_id=1, source_target_pairs={{0,64},{1,65},{2,66},{3,67},{4,68},{5,69},{6,70},{7,71},{8,72},{9,... | collective-permute-start | bytes 589832 | tf_op jit(solution)/shard_map/ppermute | solution.py:439
  34.6 11.4 %collective-permute-start.1 = (bf16[12,64,128]{2,1,0:T(8,128)(2,1)S(1)}, bf16[12,64,128]{2,1,0:T(8,128)(2,1)S(1)}, u32[]{:S(2)}, u32[]{:S(2)}) collective-permute-start(bf16[12,64,128]{2,1,0:T(8,128)(2,1)S(1)} %collective-permute-done), channel_id=1, source_target_pairs={{0,8},{1,9},{2,10},{3,11},{4,12},{5,13},{6,14},{7,15},{8,16},{9,17... | collective-permute-start | bytes 589832 | tf_op jit(solution)/shard_map/ppermute | solution.py:439
  34.6 11.4 %collective-permute-start.2 = (bf16[12,64,128]{2,1,0:T(8,128)(2,1)S(1)}, bf16[12,64,128]{2,1,0:T(8,128)(2,1)S(1)}, u32[]{:S(2)}, u32[]{:S(2)}) collective-permute-start(bf16[12,64,128]{2,1,0:T(8,128)(2,1)S(1)} %collective-permute-done), channel_id=1, source_target_pairs={{0,24},{1,25},{2,26},{3,27},{4,28},{5,29},{6,30},{7,31},{8,0},{9,1... | collective-permute-start | bytes 589832 | tf_op jit(solution)/shard_map/ppermute | solution.py:439
  37.3 8.7 %collective-permute-start.3 = (bf16[12,64,128]{2,1,0:T(8,128)(2,1)S(1)}, bf16[12,64,128]{2,1,0:T(8,128)(2,1)S(1)}, u32[]{:S(2)}, u32[]{:S(2)}) collective-permute-start(bf16[12,64,128]{2,1,0:T(8,128)(2,1)S(1)} %collective-permute-done), channel_id=1, source_target_pairs={{0,16},{1,17},{2,18},{3,19},{4,20},{5,21},{6,22},{7,23},{8,24},{9,... | collective-permute-start | bytes 589832 | tf_op jit(solution)/shard_map/ppermute | solution.py:439
  40.7 23.0 %copy-start.12 = (bf16[4,12,64,128]{3,2,1,0:T(8,128)(2,1)}, bf16[4,12,64,128]{3,2,1,0:T(8,128)(2,1)S(1)}, u32[]{:S(2)}) copy-start(bf16[4,12,64,128]{3,2,1,0:T(8,128)(2,1)S(1)} %pad_maximum_fusion.1.b_own) | copy-start | bytes 2359300
  40.8 22.8 %collective-permute-start.12 = (bf16[4,12,64,128]{3,2,1,0:T(8,128)(2,1)S(1)}, bf16[4,12,64,128]{3,2,1,0:T(8,128)(2,1)S(1)}, u32[]{:S(2)}, u32[]{:S(2)}) collective-permute-start(bf16[4,12,64,128]{3,2,1,0:T(8,128)(2,1)S(1)} %pad_maximum_fusion.1.b_own), channel_id=1, source_target_pairs={{0,8},{1,9},{2,10},{3,11},{4,12},{5,13},{6,14},{7,15},{8,16},{9,17... | collective-permute-start | bytes 2359304 | tf_op jit(solution)/shard_map/ppermute | solution.py:439
  40.8 22.8 %collective-permute-start.14 = (bf16[4,12,64,128]{3,2,1,0:T(8,128)(2,1)S(1)}, bf16[4,12,64,128]{3,2,1,0:T(8,128)(2,1)S(1)}, u32[]{:S(2)}, u32[]{:S(2)}) collective-permute-start(bf16[4,12,64,128]{3,2,1,0:T(8,128)(2,1)S(1)} %pad_maximum_fusion.1.b_own), channel_id=1, source_target_pairs={{0,24},{1,25},{2,26},{3,27},{4,28},{5,29},{6,30},{7,31},{8,0},{9,1... | collective-permute-start | bytes 2359304 | tf_op jit(solution)/shard_map/ppermute | solution.py:439
  46.1 21.6 %copy-start.11 = (bf16[4,12,64,128]{3,2,1,0:T(8,128)(2,1)}, bf16[4,12,64,128]{3,2,1,0:T(8,128)(2,1)S(1)}, u32[]{:S(2)}) copy-start(bf16[4,12,64,128]{3,2,1,0:T(8,128)(2,1)S(1)} %pad_maximum_fusion.a_own) | copy-start | bytes 2359300
  46.1 23.6 %copy-start.8 = (s32[2]{0:T(128)S(1)}, s32[2]{0:T(128)}, u32[]{:S(2)}) copy-start(s32[2]{0:T(128)} %pad_add_fusion.place) | copy-start | bytes 28
  46.1 20.7 %collective-permute-start.4 = (bf16[4,12,64,128]{3,2,1,0:T(8,128)(2,1)S(1)}, bf16[4,12,64,128]{3,2,1,0:T(8,128)(2,1)S(1)}, u32[]{:S(2)}, u32[]{:S(2)}) collective-permute-start(bf16[4,12,64,128]{3,2,1,0:T(8,128)(2,1)S(1)} %pad_maximum_fusion.a_own), channel_id=1, source_target_pairs={{0,32},{1,33},{2,34},{3,35},{4,36},{5,37},{6,38},{7,39},{8,40},{9,... | collective-permute-start | bytes 2359304 | tf_op jit(solution)/shard_map/ppermute | solution.py:439
  46.7 20.9 %collective-permute-start.6 = (bf16[4,12,64,128]{3,2,1,0:T(8,128)(2,1)S(1)}, bf16[4,12,64,128]{3,2,1,0:T(8,128)(2,1)S(1)}, u32[]{:S(2)}, u32[]{:S(2)}) collective-permute-start(bf16[4,12,64,128]{3,2,1,0:T(8,128)(2,1)S(1)} %pad_maximum_fusion.a_own), channel_id=1, source_target_pairs={{0,96},{1,97},{2,98},{3,99},{4,100},{5,101},{6,102},{7,103},{8,104... | collective-permute-start | bytes 2359304 | tf_op jit(solution)/shard_map/ppermute | solution.py:439
  63.5 4.2 %copy-start.13 = (bf16[4,12,64,128]{3,2,1,0:T(8,128)(2,1)}, bf16[4,12,64,128]{3,2,1,0:T(8,128)(2,1)S(1)}, u32[]{:S(2)}) copy-start(bf16[4,12,64,128]{3,2,1,0:T(8,128)(2,1)S(1)} %collective-permute-done.12.b_down) | copy-start | bytes 2359300
  63.6 20.0 %collective-permute-start.13 = (bf16[2,12,64,128]{3,2,1,0:T(8,128)(2,1)S(1)}, bf16[2,12,64,128]{3,2,1,0:T(8,128)(2,1)S(1)}, u32[]{:S(2)}, u32[]{:S(2)}) collective-permute-start(bf16[2,12,64,128]{3,2,1,0:T(8,128)(2,1)S(1)} %slice.18), channel_id=1, source_target_pairs={{0,8},{1,9},{2,10},{3,11},{4,12},{5,13},{6,14},{7,15},{8,16},{9,17... | collective-permute-start | bytes 1179656 | tf_op jit(solution)/shard_map/ppermute | solution.py:439
  63.6 6.1 %copy-start.14 = (bf16[4,12,64,128]{3,2,1,0:T(8,128)(2,1)}, bf16[4,12,64,128]{3,2,1,0:T(8,128)(2,1)S(1)}, u32[]{:S(2)}) copy-start(bf16[4,12,64,128]{3,2,1,0:T(8,128)(2,1)S(1)} %collective-permute-done.14.b_up) | copy-start | bytes 2359300
  63.7 19.9 %collective-permute-start.15 = (bf16[2,12,64,128]{3,2,1,0:T(8,128)(2,1)S(1)}, bf16[2,12,64,128]{3,2,1,0:T(8,128)(2,1)S(1)}, u32[]{:S(2)}, u32[]{:S(2)}) collective-permute-start(bf16[2,12,64,128]{3,2,1,0:T(8,128)(2,1)S(1)} %slice.19), channel_id=1, source_target_pairs={{0,24},{1,25},{2,26},{3,27},{4,28},{5,29},{6,30},{7,31},{8,0},{9,1... | collective-permute-start | bytes 1179656 | tf_op jit(solution)/shard_map/ppermute | solution.py:439
  66.8 16.8 %collective-permute-start.5 = (bf16[2,12,64,128]{3,2,1,0:T(8,128)(2,1)S(1)}, bf16[2,12,64,128]{3,2,1,0:T(8,128)(2,1)S(1)}, u32[]{:S(2)}, u32[]{:S(2)}) collective-permute-start(bf16[2,12,64,128]{3,2,1,0:T(8,128)(2,1)S(1)} %slice.16), channel_id=1, source_target_pairs={{0,32},{1,33},{2,34},{3,35},{4,36},{5,37},{6,38},{7,39},{8,40},{9,... | collective-permute-start | bytes 1179656 | tf_op jit(solution)/shard_map/ppermute | solution.py:439
  67.7 15.9 %collective-permute-start.7 = (bf16[2,12,64,128]{3,2,1,0:T(8,128)(2,1)S(1)}, bf16[2,12,64,128]{3,2,1,0:T(8,128)(2,1)S(1)}, u32[]{:S(2)}, u32[]{:S(2)}) collective-permute-start(bf16[2,12,64,128]{3,2,1,0:T(8,128)(2,1)S(1)} %slice.17), channel_id=1, source_target_pairs={{0,96},{1,97},{2,98},{3,99},{4,100},{5,101},{6,102},{7,103},{8,104... | collective-permute-start | bytes 1179656 | tf_op jit(solution)/shard_map/ppermute | solution.py:439
  83.6 42.1 %copy-start.7 = (s32[16,12]{1,0:T(8,128)S(1)}, s32[16,12]{1,0:T(8,128)}, u32[]{:S(2)}) copy-start(s32[16,12]{1,0:T(8,128)} %rows_b.3) | copy-start | bytes 2308
  83.6 42.1 %copy-start.9 = (s32[16]{0:T(128)S(1)}, s32[16]{0:T(128)}, u32[]{:S(2)}) copy-start(s32[16]{0:T(128)} %counts_a.3) | copy-start | bytes 196
  83.6 42.1 %copy-start.10 = (s32[16]{0:T(128)S(1)}, s32[16]{0:T(128)}, u32[]{:S(2)}) copy-start(s32[16]{0:T(128)} %counts_b.3) | copy-start | bytes 196
  95.9 5.5 %collective-permute-start.16 = (bf16[4,128,1536]{2,1,0:T(8,128)(2,1)}, bf16[4,128,1536]{2,1,0:T(8,128)(2,1)S(1)}, u32[]{:S(2)}, u32[]{:S(2)}) collective-permute-start(bf16[4,128,1536]{2,1,0:T(8,128)(2,1)} %get-tuple-element.23), channel_id=1, source_target_pairs={{0,1},{1,0},{2,3},{3,2},{4,5},{5,4},{6,7},{7,6},{8,9},{9,8},{10,11... | collective-permute-start | bytes 4718600 | tf_op jit(solution)/shard_map/ppermute | solution.py:439
  101.4 1.4 copy-start.3
  102.8 22.9 %copy-start = (bf16[1536,512]{1,0:T(8,128)(2,1)S(1)}, bf16[1536,512]{1,0:T(8,128)(2,1)}, u32[]{:S(2)}) copy-start(bf16[1536,512]{1,0:T(8,128)(2,1)} %fa.3) | copy-start | bytes 4718596
  102.8 22.9 %copy-start.1 = (bf16[1536,512]{1,0:T(8,128)(2,1)S(1)}, bf16[1536,512]{1,0:T(8,128)(2,1)}, u32[]{:S(2)}) copy-start(bf16[1536,512]{1,0:T(8,128)(2,1)} %fb.1) | copy-start | bytes 4718596
  102.8 22.9 %copy-start.6 = (s32[16,12]{1,0:T(8,128)S(1)}, s32[16,12]{1,0:T(8,128)}, u32[]{:S(2)}) copy-start(s32[16,12]{1,0:T(8,128)} %rows_a.3) | copy-start | bytes 2308
  104.2 12.3 %collective-permute-start.17 = (bf16[128,1536]{1,0:T(8,128)(2,1)S(1)}, bf16[128,1536]{1,0:T(8,128)(2,1)S(1)}, u32[]{:S(2)}, u32[]{:S(2)}) collective-permute-start(bf16[128,1536]{1,0:T(8,128)(2,1)S(1)} %get-tuple-element.25), channel_id=1, source_target_pairs={{0,2},{1,3},{2,4},{3,5},{4,6},{5,7},{6,0},{7,1},{8,10},{9,11},{10,... | collective-permute-start | bytes 1179656 | tf_op jit(solution)/shard_map/ppermute | solution.py:439
  104.3 21.5 %collective-permute-start.18 = (bf16[128,1536]{1,0:T(8,128)(2,1)S(1)}, bf16[128,1536]{1,0:T(8,128)(2,1)S(1)}, u32[]{:S(2)}, u32[]{:S(2)}) collective-permute-start(bf16[128,1536]{1,0:T(8,128)(2,1)S(1)} %get-tuple-element.26), channel_id=1, source_target_pairs={{0,4},{1,5},{2,6},{3,7},{4,0},{5,1},{6,2},{7,3},{8,12},{9,13},{10,... | collective-permute-start | bytes 1179656 | tf_op jit(solution)/shard_map/ppermute | solution.py:439
  108.4 17.3 %collective-permute-start.19 = (bf16[128,1536]{1,0:T(8,128)(2,1)S(1)}, bf16[128,1536]{1,0:T(8,128)(2,1)S(1)}, u32[]{:S(2)}, u32[]{:S(2)}) collective-permute-start(bf16[128,1536]{1,0:T(8,128)(2,1)S(1)} %get-tuple-element.27), channel_id=1, source_target_pairs={{0,6},{1,7},{2,0},{3,1},{4,2},{5,3},{6,4},{7,5},{8,14},{9,15},{10,... | collective-permute-start | bytes 1179656 | tf_op jit(solution)/shard_map/ppermute | solution.py:439
  125.8 35.8 %copy-start.2 = (bf16[512,512]{1,0:T(8,128)(2,1)S(1)}, bf16[512,512]{1,0:T(8,128)(2,1)}, u32[]{:S(2)}) copy-start(bf16[512,512]{1,0:T(8,128)(2,1)} %top.5) | copy-start | bytes 1572868
  125.8 35.8 %copy-start.4 = (f32[64,512]{1,0:T(8,128)S(1)}, f32[64,512]{1,0:T(8,128)}, u32[]{:S(2)}) copy-start(f32[64,512]{1,0:T(8,128)} %base.2) | copy-start | bytes 393220
  127.7 43.9 %copy-start.5 = (f32[64,512]{1,0:T(8,128)S(1)}, f32[64,512]{1,0:T(8,128)}, u32[]{:S(2)}) copy-start(f32[64,512]{1,0:T(8,128)} %base.3) | copy-start | bytes 393220
  127.7 6.5 %collective-permute-start.27 = (bf16[192,512]{1,0:T(8,128)(2,1)S(1)}, bf16[192,512]{1,0:T(8,128)(2,1)S(1)}, u32[]{:S(2)}, u32[]{:S(2)}) collective-permute-start(bf16[192,512]{1,0:T(8,128)(2,1)S(1)} %get-tuple-element.30.one), channel_id=1, source_target_pairs={{0,8},{1,9},{2,10},{3,11},{4,12},{5,13},{6,14},{7,15},{8,16},{9,17... | collective-permute-start | bytes 589832 | tf_op jit(solution)/shard_map/ppermute | solution.py:439
  127.8 7.3 %collective-permute-start.28 = (bf16[192,512]{1,0:T(8,128)(2,1)S(1)}, bf16[192,512]{1,0:T(8,128)(2,1)S(1)}, u32[]{:S(2)}, u32[]{:S(2)}) collective-permute-start(bf16[192,512]{1,0:T(8,128)(2,1)S(1)} %get-tuple-element.30.one), channel_id=1, source_target_pairs={{0,24},{1,25},{2,26},{3,27},{4,28},{5,29},{6,30},{7,31},{8,0},{9,1... | collective-permute-start | bytes 589832 | tf_op jit(solution)/shard_map/ppermute | solution.py:439
  130.5 8.4 %collective-permute-start.29 = (bf16[192,512]{1,0:T(8,128)(2,1)S(1)}, bf16[192,512]{1,0:T(8,128)(2,1)S(1)}, u32[]{:S(2)}, u32[]{:S(2)}) collective-permute-start(bf16[192,512]{1,0:T(8,128)(2,1)S(1)} %get-tuple-element.30.one), channel_id=1, source_target_pairs={{0,16},{1,17},{2,18},{3,19},{4,20},{5,21},{6,22},{7,23},{8,24},{9,... | collective-permute-start | bytes 589832 | tf_op jit(solution)/shard_map/ppermute | solution.py:439
  130.5 17.1 %collective-permute-start.20 = (bf16[128,1536]{1,0:T(8,128)(2,1)S(1)}, bf16[128,1536]{1,0:T(8,128)(2,1)S(1)}, u32[]{:S(2)}, u32[]{:S(2)}) collective-permute-start(bf16[128,1536]{1,0:T(8,128)(2,1)S(1)} %get-tuple-element.28.refs_0_), channel_id=1, source_target_pairs={{0,2},{1,3},{2,4},{3,5},{4,6},{5,7},{6,0},{7,1},{8,10},{9,11},{10,... | collective-permute-start | bytes 1179656 | tf_op jit(solution)/shard_map/ppermute | solution.py:439
  131.8 15.8 %collective-permute-start.21 = (bf16[128,1536]{1,0:T(8,128)(2,1)S(1)}, bf16[128,1536]{1,0:T(8,128)(2,1)S(1)}, u32[]{:S(2)}, u32[]{:S(2)}) collective-permute-start(bf16[128,1536]{1,0:T(8,128)(2,1)S(1)} %get-tuple-element.28.refs_0_), channel_id=1, source_target_pairs={{0,6},{1,7},{2,0},{3,1},{4,2},{5,3},{6,4},{7,5},{8,14},{9,15},{10,... | collective-permute-start | bytes 1179656 | tf_op jit(solution)/shard_map/ppermute | solution.py:439
  134.2 17.5 %collective-permute-start.22 = (bf16[128,1536]{1,0:T(8,128)(2,1)S(1)}, bf16[128,1536]{1,0:T(8,128)(2,1)S(1)}, u32[]{:S(2)}, u32[]{:S(2)}) collective-permute-start(bf16[128,1536]{1,0:T(8,128)(2,1)S(1)} %get-tuple-element.28.refs_0_), channel_id=1, source_target_pairs={{0,4},{1,5},{2,6},{3,7},{4,0},{5,1},{6,2},{7,3},{8,12},{9,13},{10,... | collective-permute-start | bytes 1179656 | tf_op jit(solution)/shard_map/ppermute | solution.py:439
  139.0 5.8 %collective-permute-start.30 = (bf16[192,512]{1,0:T(8,128)(2,1)S(1)}, bf16[192,512]{1,0:T(8,128)(2,1)S(1)}, u32[]{:S(2)}, u32[]{:S(2)}) collective-permute-start(bf16[192,512]{1,0:T(8,128)(2,1)S(1)} %fold.1.one), channel_id=1, source_target_pairs={{0,32},{1,33},{2,34},{3,35},{4,36},{5,37},{6,38},{7,39},{8,40},{9,... | collective-permute-start | bytes 589832 | tf_op jit(solution)/shard_map/ppermute | solution.py:439
  139.1 14.5 %collective-permute-start.31 = (bf16[192,512]{1,0:T(8,128)(2,1)S(1)}, bf16[192,512]{1,0:T(8,128)(2,1)S(1)}, u32[]{:S(2)}, u32[]{:S(2)}) collective-permute-start(bf16[192,512]{1,0:T(8,128)(2,1)S(1)} %fold.1.one), channel_id=1, source_target_pairs={{0,96},{1,97},{2,98},{3,99},{4,100},{5,101},{6,102},{7,103},{8,104... | collective-permute-start | bytes 589832 | tf_op jit(solution)/shard_map/ppermute | solution.py:439
  144.8 27.7 %collective-permute-start.23 = (bf16[128,1536]{1,0:T(8,128)(2,1)S(1)}, bf16[128,1536]{1,0:T(8,128)(2,1)S(1)}, u32[]{:S(2)}, u32[]{:S(2)}) collective-permute-start(bf16[128,1536]{1,0:T(8,128)(2,1)S(1)} %get-tuple-element.28.refs_0_), channel_id=1, source_target_pairs={{0,1},{1,0},{2,3},{3,2},{4,5},{5,4},{6,7},{7,6},{8,9},{9,8},{10,11... | collective-permute-start | bytes 1179656 | tf_op jit(solution)/shard_map/ppermute | solution.py:439
  147.6 24.9 %collective-permute-start.24 = (bf16[128,1536]{1,0:T(8,128)(2,1)S(1)}, bf16[128,1536]{1,0:T(8,128)(2,1)S(1)}, u32[]{:S(2)}, u32[]{:S(2)}) collective-permute-start(bf16[128,1536]{1,0:T(8,128)(2,1)S(1)} %collective-permute-done.20.refs_1_), channel_id=1, source_target_pairs={{0,1},{1,0},{2,3},{3,2},{4,5},{5,4},{6,7},{7,6},{8,9},{9,8},{10,11... | collective-permute-start | bytes 1179656 | tf_op jit(solution)/shard_map/ppermute | solution.py:439
  147.6 24.9 %collective-permute-start.25 = (bf16[128,1536]{1,0:T(8,128)(2,1)S(1)}, bf16[128,1536]{1,0:T(8,128)(2,1)S(1)}, u32[]{:S(2)}, u32[]{:S(2)}) collective-permute-start(bf16[128,1536]{1,0:T(8,128)(2,1)S(1)} %collective-permute-done.21.refs_2_), channel_id=1, source_target_pairs={{0,1},{1,0},{2,3},{3,2},{4,5},{5,4},{6,7},{7,6},{8,9},{9,8},{10,11... | collective-permute-start | bytes 1179656 | tf_op jit(solution)/shard_map/ppermute | solution.py:439
  151.7 20.9 %collective-permute-start.26 = (bf16[128,1536]{1,0:T(8,128)(2,1)S(1)}, bf16[128,1536]{1,0:T(8,128)(2,1)S(1)}, u32[]{:S(2)}, u32[]{:S(2)}) collective-permute-start(bf16[128,1536]{1,0:T(8,128)(2,1)S(1)} %collective-permute-done.22.refs_3_), channel_id=1, source_target_pairs={{0,1},{1,0},{2,3},{3,2},{4,5},{5,4},{6,7},{7,6},{8,9},{9,8},{10,11... | collective-permute-start | bytes 1179656 | tf_op jit(solution)/shard_map/ppermute | solution.py:439
  153.5 8.0 %collective-permute-start.32 = (bf16[192,512]{1,0:T(8,128)(2,1)S(1)}, bf16[192,512]{1,0:T(8,128)(2,1)S(1)}, u32[]{:S(2)}, u32[]{:S(2)}) collective-permute-start(bf16[192,512]{1,0:T(8,128)(2,1)S(1)} %fold.1.one), channel_id=1, source_target_pairs={{0,64},{1,65},{2,66},{3,67},{4,68},{5,69},{6,70},{7,71},{8,72},{9,... | collective-permute-start | bytes 589832 | tf_op jit(solution)/shard_map/ppermute | solution.py:439

commit v4 on v3

--- a/solution.py
+++ b/solution.py
@@ -15,6 +15,7 @@
 PART = 64
 COLS = 8
 STEPS = (0, 1, -1, 2)
+STRIP = 2 * BS
 PAIR = 2 * PART
 BOTH = ("row", "col")
 MIB = 1024 * 1024
@@ -152,13 +153,34 @@
         copy.wait()
 
 
-def multiply(spread, tile, first, last):
-    left = jnp.concatenate(
-        [spread[n, h, first:last, :] for n in range(NB) for h in range(2)], axis=1
-    )
+def multiply(spread, tile):
+    left = jnp.concatenate([spread[n, h] for n in range(NB) for h in range(2)], axis=1)
     return lax.dot_general(
-        left, tile[...], (((1,), (1,)), ((), ())), preferred_element_type=F32
+        left, tile, (((1,), (1,)), ((), ())), preferred_element_type=F32
     ).astype(BF)
+
+
+def hold_body(source, _, target, sem):
+    copy = pltpu.make_async_copy(source, target, sem)
+    copy.start()
+    copy.wait()
+
+
+def hold(trailing, after):
+    return pl.pallas_call(
+        hold_body,
+        name="hold",
+        in_specs=[pl.BlockSpec(memory_space=pltpu.HBM), pl.BlockSpec(memory_space=pl.ANY)],
+        out_specs=pl.BlockSpec(memory_space=pltpu.VMEM),
+        out_shape=pltpu.VMEM(trailing.shape, BF),
+        scratch_shapes=[pltpu.SemaphoreType.DMA],
+        compiler_params=params(8),
+        cost_estimate=cost(0, 2 * trailing.size),
+    )(trailing, after)
+
+
+def rows_of(tile, step):
+    return tile[pl.ds(pl.multiple_of(step * STRIP, STRIP), STRIP), :]
 
 
 ALL = tuple((i, i) for i in range(SIDE))
@@ -178,20 +200,15 @@
             load_b(copies, buf, ALL, u, W // 2 + 2 * t * PART, spread, sems)
         run_copies(copies, sems)
 
-    value = multiply(spread, tile, 0, W // 2)
+    value = multiply(spread, rows_of(tile, pl.program_id(0)))
     for i, step in enumerate(STEPS):
         out[2 * turn(v, -step) + (u + 1) % 2, :PART, :] = value[i * PART : (i + 1) * PART]
-    for first, many in ((0, 2), (2, 1)):
-        value = multiply(
-            spread, tile, W // 2 + 2 * first * PART, W // 2 + 2 * (first + many) * PART
-        )
-        for j in range(2 * many):
-            to = 2 * turn(v, -STEPS[first + j // 2]) + j % 2
-            out[to, PART:, :] = value[j * PART : (j + 1) * PART]
+    for j in range(6):
+        to = 2 * turn(v, -STEPS[j // 2]) + j % 2
+        out[to, PART:, :] = value[W // 2 + j * PART : W // 2 + (j + 1) * PART]
 
 
 def early_product(place, bufs, trailing):
-    width = 2 * BS
     deep = trailing.shape[1]
     rows = W // 2 + 6 * PART
     return pl.pallas_call(
@@ -199,23 +216,23 @@
         name="early_product",
         grid_spec=pltpu.PrefetchScalarGridSpec(
             num_scalar_prefetch=1,
-            grid=(ROWS // width,),
+            grid=(ROWS // STRIP,),
             in_specs=[pl.BlockSpec(memory_space=pl.ANY)] * 5
-            + [pl.BlockSpec((width, deep), lambda i, *_: (i, 0))],
-            out_specs=pl.BlockSpec((COLS, PAIR, width), lambda i, *_: (0, 0, i)),
+            + [pl.BlockSpec(memory_space=pltpu.VMEM)],
+            out_specs=pl.BlockSpec((COLS, PAIR, STRIP), lambda i, *_: (0, 0, i)),
             scratch_shapes=[
                 pltpu.VMEM((NB, 2, rows, BS), BF),
                 pltpu.SemaphoreType.DMA((20,)),
             ],
         ),
         out_shape=jax.ShapeDtypeStruct((COLS, PAIR, ROWS), BF),
-        compiler_params=params(52, dimension_semantics=("arbitrary",)),
-        cost_estimate=cost(2 * rows * ROWS * deep, 2 * ROWS * deep + 2 * rows * deep + 4 * W * ROWS),
+        compiler_params=params(20, dimension_semantics=("arbitrary",)),
+        cost_estimate=cost(2 * rows * ROWS * deep, 2 * rows * deep + 4 * W * ROWS),
     )(place, *bufs, trailing)
 
 
 def late_body(
-    place, a_own, a_far, a_far_more, b_far, b_far_more, tile, before, keep, give, spread, ready, sems
+    half, place, a_own, a_far, a_far_more, b_far, b_far_more, tile, before, keep, give, spread, ready, sems
 ):
     u, v = where(place)
     core = place[1] % 2
@@ -231,44 +248,45 @@
         run_copies(copies, sems)
 
     ready[...] = before[...]
-    value = multiply(spread, tile, 0, W // 2)
+    value = multiply(spread, rows_of(tile, half * HALF_STEPS + pl.program_id(0)))
     for i, step in enumerate(STEPS):
         ready[2 * turn(v, -step) + u % 2, :PART, :] = value[i * PART : (i + 1) * PART]
-    value = multiply(spread, tile, W // 2, W // 2 + 2 * PART)
     for j in range(2):
-        ready[2 * turn(v, 2) + j, PART:, :] = value[j * PART : (j + 1) * PART]
+        ready[2 * turn(v, 2) + j, PART:, :] = value[W // 2 + j * PART : W // 2 + (j + 1) * PART]
     for x in range(SIDE):
         keep[x] = ready[2 * x + core]
         give[x] = ready[2 * x + 1 - core]
 
 
-def late_product(place, bufs, trailing, before):
-    width = 2 * BS
+HALF_STEPS = ROWS // STRIP // 2
+
+
+def late_product(half, place, bufs, trailing, before):
     deep = trailing.shape[1]
     rows = W // 2 + 2 * PART
-    out = jax.ShapeDtypeStruct((SIDE, PAIR, ROWS), BF)
-    spec = pl.BlockSpec((SIDE, PAIR, width), lambda i, *_: (0, 0, i))
-    return pl.pallas_call(
-        late_body,
+    out = jax.ShapeDtypeStruct((SIDE, PAIR, ROWS // 2), BF)
+    spec = pl.BlockSpec((SIDE, PAIR, STRIP), lambda i, *_: (0, 0, i))
+    return pl.pallas_call(
+        functools.partial(late_body, half),
         name="late_product",
         grid_spec=pltpu.PrefetchScalarGridSpec(
             num_scalar_prefetch=1,
-            grid=(ROWS // width,),
+            grid=(HALF_STEPS,),
             in_specs=[pl.BlockSpec(memory_space=pl.ANY)] * 5
             + [
-                pl.BlockSpec((width, deep), lambda i, *_: (i, 0)),
-                pl.BlockSpec((COLS, PAIR, width), lambda i, *_: (0, 0, i)),
+                pl.BlockSpec(memory_space=pltpu.VMEM),
+                pl.BlockSpec((COLS, PAIR, STRIP), lambda i, *_: (0, 0, half * HALF_STEPS + i)),
             ],
             out_specs=[spec, spec],
             scratch_shapes=[
                 pltpu.VMEM((NB, 2, rows, BS), BF),
-                pltpu.VMEM((COLS, PAIR, width), BF),
+                pltpu.VMEM((COLS, PAIR, STRIP), BF),
                 pltpu.SemaphoreType.DMA((12,)),
             ],
         ),
         out_shape=[out, out],
-        compiler_params=params(52, dimension_semantics=("arbitrary",)),
-        cost_estimate=cost(2 * rows * ROWS * deep, 2 * ROWS * deep + 2 * rows * deep + 8 * W * ROWS),
+        compiler_params=params(20, dimension_semantics=("arbitrary",)),
+        cost_estimate=cost(rows * ROWS * deep, 2 * rows * deep + 4 * W * ROWS),
     )(place, *bufs, trailing, before)
 
 
@@ -280,31 +298,33 @@
 
 
 def pair_sum(place, mine, taken):
-    lanes = 4 * BS
+    lanes = 3 * BS
+    width = mine.shape[2]
     spec = pl.BlockSpec((SIDE, PAIR, lanes), lambda i, *_: (0, 0, i))
     return pl.pallas_call(
         pair_body,
         name="pair_sum",
         grid_spec=pltpu.PrefetchScalarGridSpec(
             num_scalar_prefetch=1,
-            grid=(ROWS // lanes,),
+            grid=(width // lanes,),
             in_specs=[spec, spec],
             out_specs=[pl.BlockSpec((PAIR, lanes), lambda i, *_: (0, i))] * SIDE,
         ),
-        out_shape=[jax.ShapeDtypeStruct((PAIR, ROWS), BF)] * SIDE,
+        out_shape=[jax.ShapeDtypeStruct((PAIR, width), BF)] * SIDE,
         compiler_params=params(dimension_semantics=("arbitrary",)),
-        cost_estimate=cost(W * ROWS, 6 * W * ROWS),
+        cost_estimate=cost(W * width, 6 * W * width),
     )(place, mine, taken)
 
 
 def slots_body(
-    place, rows_a, counts_a, rows_b, counts_b, s0, s1, s2, s3, fa, fb, columns, pieces, natural, left
+    place, rows_a, counts_a, rows_b, counts_b, *refs
 ):
+    slabs, (fa, fb, columns, pieces, natural, left) = refs[:8], refs[8:]
     owner = place[0]
-    total = (s0[...].astype(F32) + s1[...].astype(F32)) + (
-        s2[...].astype(F32) + s3[...].astype(F32)
-    )
-    natural[...] = (-total).astype(BF)
+    width = ROWS // 2
+    for half in range(2):
+        total = total_of(slabs[half * SIDE : (half + 1) * SIDE], slice(None))
+        natural[:, half * width : (half + 1) * width] = (-total).astype(BF)
     for k in range(NB):
         at = slice(k * BS, (k + 1) * BS)
         block = natural[:PART, pl.ds(pl.multiple_of(rows_a[owner, k] * BS, BS), BS)]
@@ -326,7 +346,7 @@
         grid_spec=pltpu.PrefetchScalarGridSpec(
             num_scalar_prefetch=5,
             grid=(1,),
-            in_specs=[whole((PAIR, ROWS))] * SIDE + [whole((ROWS, W))] * 2,
+            in_specs=[whole((PAIR, ROWS // 2))] * 8 + [whole((ROWS, W))] * 2,
             out_specs=[whole((PAIR, ROWS)), whole((3 * PART, W))],
             scratch_shapes=[pltpu.VMEM((PAIR, ROWS), BF)] * 2,
         ),
@@ -457,16 +477,21 @@
     b_down, b_up = send(b_own, dy=1), send(b_own, dy=-1)
     a_far, a_far_more = send(a_down[:2], dz=1), send(a_up[2:], dz=-1)
     b_far, b_far_more = send(b_down[:2], dy=1), send(b_up[2:], dy=-1)
+    trailing = hold(trailing, a_own)
     before = early_product(place, (a_down, a_up, b_own, b_down, b_up), trailing)
-    keep, give = late_product(
-        place, (a_own, a_far, a_far_more, b_far, b_far_more), trailing, before
-    )
-
-    own, one, two, three = pair_sum(place, keep, send(give, dc=1))
-    slabs = [own, send(one, dx=1), send(two, dx=2), send(three, dx=-1)]
+    slabs = []
+    for half in range(2):
+        keep, give = late_product(
+            half, place, (a_own, a_far, a_far_more, b_far, b_far_more), trailing, before
+        )
+        own, one, two, three = pair_sum(place, keep, send(give, dc=1))
+        slabs += [own, send(one, dx=1), send(two, dx=2), send(three, dx=-1)]
     columns, pieces = slots(place, lists, slabs, (factor_a, factor_b))
-    got = around(fold(around(pieces, "dy")), "dz")
-    mine = around(columns, "dx")
+    near, other = send(columns, dx=1), send(columns, dx=-1)
+    folded = fold(around(pieces, "dy"))
+    got = around(folded, "dz")
+    own, near, other, got[1] = lax.optimization_barrier((columns, near, other, got[1]))
+    mine = [own, near, other, send(own, dx=2)]
     column_a, column_b = whole_columns(place, mine + [send(slab, dc=1) for slab in mine])
     diag_a, top_b, sent = top_part(got, base_a, factor_top)
     taken = lax.all_to_all(sent, "col", 0, 0)

time: 177 us -> 171 us (0.966)
  Pallas kernels: 39.9 us -> 32.4 us
  waiting for transfers between devices: 68.7 us -> 65.7 us
  local copies, waits for them, and re-layouts: 1.59 us -> 3.85 us
    ppermute x1, waiting for transfers between devices: 0.01 us -> 13.5 us  [on_device(): part_a = lax.ppermute(part_a, BOTH, spread_pairs())]
    ppermute x1, waiting for transfers between devices: 13.4 us -> 1.53 us  [on_device(): part_b = lax.ppermute(part_b, BOTH, spread_pairs())]
    pallas_call x1, Pallas kernels: 13.9 us -> 9.15 us  [early_product(): pl.pallas_call(early_body, name='early_product', grid_spec=pltpu.Prefetch...]
    ppermute x31 -> x35, waiting for transfers between devices: 55.3 us -> 50.6 us  [send(): return lax.ppermute(value, BOTH, shifted(**by))]
    pallas_call x1 -> x3, Pallas kernels: 12.3 us -> 8.69 us  [the longest x2 8.05 us: late_product(): pl.pallas_call(functools.partial(late_body, half), name='late_product', g...]
    unnamed x30 -> x22, local copies, waits for them, and re-layouts: 1.48 us -> 3.74 us
    ppermute x31 -> x35, starting transfers between devices: 45.8 us -> 46.4 us  [send(): return lax.ppermute(value, BOTH, shifted(**by))]
  transfers between devices with their start and end apart: 33 -> 37, of which waited for: 13 -> 14; matrix products, arithmetic and copies ran while one was open for 0% -> 0% of each run, Pallas kernels for 9% -> 11%
where the time goes in v4:
time: 171 us
  waiting for transfers between devices  65.7 us (38%)
  starting transfers between devices  56.3 us (33%)
  Pallas kernels  32.4 us (19%)
  blocking collectives  10.7 us (6%)
  local copies, waits for them, and re-layouts  3.85 us (2%)
    ppermute x35, waiting for transfers between devices, send(): return lax.ppermute(value, BOTH, shifted(**by))  50.6 us
    ppermute x35, starting transfers between devices, send(): return lax.ppermute(value, BOTH, shifted(**by))  46.4 us
    ppermute x1, waiting for transfers between devices, on_device(): part_a = lax.ppermute(part_a, BOTH, spread_pairs())  13.5 us
    all_to_all x1, blocking collectives, on_device(): taken = lax.all_to_all(sent, 'col', 0, 0)  10.7 us
    pallas_call x1, Pallas kernels, early_product(): pl.pallas_call(early_body, name='early_product', grid_spec=pltpu.Prefetch...  9.15 us
    pallas_call x2, Pallas kernels, late_product(): pl.pallas_call(functools.partial(late_body, half), name='late_product', g...  8.05 us
    ppermute x1, starting transfers between devices, on_device(): part_b = lax.ppermute(part_b, BOTH, spread_pairs())  4.94 us
    ppermute x1, starting transfers between devices, on_device(): part_a = lax.ppermute(part_a, BOTH, spread_pairs())  4.92 us
  transfers between devices with their start and end apart: 37, of which 14 were waited for; matrix products, arithmetic and copies ran while one was open for 0% of the time, Pallas kernels for 11%

profile of v4, /device:TPU:1, one launch (start us, length us, event | category | flops | bytes accessed | tf_op | source)
XLA Modules:
  0.0 170.7 jit_solution(3021171861649002877)
XLA Ops:
  0.6 0.6 pad_add_fusion.place
  1.2 4.5 %prep.1 = (bf16[12,64,128]{2,1,0:T(8,128)(2,1)}, bf16[12,64,128]{2,1,0:T(8,128)(2,1)}) custom-call(s32[2]{0:T(128)} %pad_add_fusion.place, s32[16,12]{1,0:T(8,128)} %rows_a.3, s32[16]{0:T(128)} %counts_a.3, s32[16,12]{1,0:T(8,128)} %rows_b.3, s32[16]{0:T(128)} %counts_b.3, bf16[1536,512]{1,0:T(8,128)(2,1)} %refs_8_.1, bf16[1536,512]{1,0:T(8,128)(2,1)} %refs_8_.1, ...), custom_call_target="tpu_custom_call" | custom-call | flops 201326592 | bytes 3145728 | tf_op jit(solution)/shard_map/prep/pallas_call | solution.py:104
  5.7 4.9 %collective-permute-start = (bf16[12,64,128]{2,1,0:T(8,128)(2,1)}, bf16[12,64,128]{2,1,0:T(8,128)(2,1)S(1)}, u32[]{:S(2)}, u32[]{:S(2)}) collective-permute-start(bf16[12,64,128]{2,1,0:T(8,128)(2,1)} %get-tuple-element.30), channel_id=1, source_target_pairs={{0,0},{1,32},{2,8},{3,40},{4,16},{5,48},{6,24},{7,56},{8,9},{9,41}... | collective-permute-start | bytes 589832 | tf_op jit(solution)/shard_map/ppermute | solution.py:472
  10.7 4.9 %collective-permute-start.8 = (bf16[12,64,128]{2,1,0:T(8,128)(2,1)}, bf16[12,64,128]{2,1,0:T(8,128)(2,1)S(1)}, u32[]{:S(2)}, u32[]{:S(2)}) collective-permute-start(bf16[12,64,128]{2,1,0:T(8,128)(2,1)} %get-tuple-element.31), channel_id=1, source_target_pairs={{0,0},{1,32},{2,8},{3,40},{4,16},{5,48},{6,24},{7,56},{8,9},{9,41}... | collective-permute-start | bytes 589832 | tf_op jit(solution)/shard_map/ppermute | solution.py:473
  15.6 13.5 %collective-permute-done = bf16[12,64,128]{2,1,0:T(8,128)(2,1)S(1)} collective-permute-done((bf16[12,64,128]{2,1,0:T(8,128)(2,1)}, bf16[12,64,128]{2,1,0:T(8,128)(2,1)S(1)}, u32[]{:S(2)}, u32[]{:S(2)}) %collective-permute-start) | collective-permute-done | bytes 196640 | tf_op jit(solution)/shard_map/ppermute | solution.py:472
  29.1 2.7 %collective-permute-start.2 = (bf16[12,64,128]{2,1,0:T(8,128)(2,1)S(1)}, bf16[12,64,128]{2,1,0:T(8,128)(2,1)S(1)}, u32[]{:S(2)}, u32[]{:S(2)}) collective-permute-start(bf16[12,64,128]{2,1,0:T(8,128)(2,1)S(1)} %collective-permute-done), channel_id=1, source_target_pairs={{0,24},{1,25},{2,26},{3,27},{4,28},{5,29},{6,30},{7,31},{8,0},{9,1... | collective-permute-start | bytes 589832 | tf_op jit(solution)/shard_map/ppermute | solution.py:459
  31.8 1.5 collective-permute-done.8
  33.4 1.7 collective-permute-start.9
  35.1 2.4 %collective-permute-start.10 = (bf16[12,64,128]{2,1,0:T(8,128)(2,1)S(1)}, bf16[12,64,128]{2,1,0:T(8,128)(2,1)S(1)}, u32[]{:S(2)}, u32[]{:S(2)}) collective-permute-start(bf16[12,64,128]{2,1,0:T(8,128)(2,1)S(1)} %collective-permute-done.8), channel_id=1, source_target_pairs={{0,96},{1,97},{2,98},{3,99},{4,100},{5,101},{6,102},{7,103},{8,104... | collective-permute-start | bytes 589832 | tf_op jit(solution)/shard_map/ppermute | solution.py:459
  37.5 3.3 %collective-permute-done.1 = bf16[12,64,128]{2,1,0:T(8,128)(2,1)S(1)} collective-permute-done((bf16[12,64,128]{2,1,0:T(8,128)(2,1)S(1)}, bf16[12,64,128]{2,1,0:T(8,128)(2,1)S(1)}, u32[]{:S(2)}, u32[]{:S(2)}) %collective-permute-start.1) | collective-permute-done | bytes 196640 | tf_op jit(solution)/shard_map/ppermute | solution.py:459
  40.8 3.5 %collective-permute-start.11 = (bf16[12,64,128]{2,1,0:T(8,128)(2,1)S(1)}, bf16[12,64,128]{2,1,0:T(8,128)(2,1)S(1)}, u32[]{:S(2)}, u32[]{:S(2)}) collective-permute-start(bf16[12,64,128]{2,1,0:T(8,128)(2,1)S(1)} %collective-permute-done.8), channel_id=1, source_target_pairs={{0,64},{1,65},{2,66},{3,67},{4,68},{5,69},{6,70},{7,71},{8,72},{9,... | collective-permute-start | bytes 589832 | tf_op jit(solution)/shard_map/ppermute | solution.py:459
  44.3 0.1 pad_maximum_fusion._.a_own
  44.4 1.8 %collective-permute-start.4 = (bf16[4,12,64,128]{3,2,1,0:T(8,128)(2,1)S(1)}, bf16[4,12,64,128]{3,2,1,0:T(8,128)(2,1)S(1)}, u32[]{:S(2)}, u32[]{:S(2)}) collective-permute-start(bf16[4,12,64,128]{3,2,1,0:T(8,128)(2,1)S(1)} %pad_maximum_fusion._.a_own), channel_id=1, source_target_pairs={{0,32},{1,33},{2,34},{3,35},{4,36},{5,37},{6,38},{7,39},{8,40},{9,... | collective-permute-start | bytes 2359304 | tf_op jit(solution)/shard_map/ppermute | solution.py:459
  46.2 1.0 collective-permute-start.6
  47.2 0.9 collective-permute-done.11
  48.1 0.1 pad_maximum_fusion.1.b_own
  48.3 0.1 collective-permute-start.12
  48.3 2.7 %collective-permute-start.14 = (bf16[4,12,64,128]{3,2,1,0:T(8,128)(2,1)S(1)}, bf16[4,12,64,128]{3,2,1,0:T(8,128)(2,1)S(1)}, u32[]{:S(2)}, u32[]{:S(2)}) collective-permute-start(bf16[4,12,64,128]{3,2,1,0:T(8,128)(2,1)S(1)} %pad_maximum_fusion.1.b_own), channel_id=1, source_target_pairs={{0,24},{1,25},{2,26},{3,27},{4,28},{5,29},{6,30},{7,31},{8,0},{9,1... | collective-permute-start | bytes 2359304 | tf_op jit(solution)/shard_map/ppermute | solution.py:459
  51.0 3.7 %copy-done.1 = bf16[1536,3072]{1,0:T(8,128)(2,1)S(1)} copy-done((bf16[1536,3072]{1,0:T(8,128)(2,1)S(1)}, bf16[1536,3072]{1,0:T(8,128)(2,1)}, u32[]{:S(2)}) %copy-start.1) | copy-done | bytes 9437208
  54.7 0.6 hold.1.tile
  55.3 9.9 %collective-permute-done.4.a_down = bf16[4,12,64,128]{3,2,1,0:T(8,128)(2,1)S(1)} collective-permute-done((bf16[4,12,64,128]{3,2,1,0:T(8,128)(2,1)S(1)}, bf16[4,12,64,128]{3,2,1,0:T(8,128)(2,1)S(1)}, u32[]{:S(2)}, u32[]{:S(2)}) %collective-permute-start.4) | collective-permute-done | bytes 786464 | tf_op jit(solution)/shard_map/ppermute | solution.py:459
  65.2 0.3 collective-permute-start.5
  65.5 2.5 %collective-permute-done.6.a_up = bf16[4,12,64,128]{3,2,1,0:T(8,128)(2,1)S(1)} collective-permute-done((bf16[4,12,64,128]{3,2,1,0:T(8,128)(2,1)S(1)}, bf16[4,12,64,128]{3,2,1,0:T(8,128)(2,1)S(1)}, u32[]{:S(2)}, u32[]{:S(2)}) %collective-permute-start.6) | collective-permute-done | bytes 786464 | tf_op jit(solution)/shard_map/ppermute | solution.py:459
  68.0 2.8 %collective-permute-start.7 = (bf16[2,12,64,128]{3,2,1,0:T(8,128)(2,1)S(1)}, bf16[2,12,64,128]{3,2,1,0:T(8,128)(2,1)S(1)}, u32[]{:S(2)}, u32[]{:S(2)}) collective-permute-start(bf16[2,12,64,128]{3,2,1,0:T(8,128)(2,1)S(1)} %slice.17), channel_id=1, source_target_pairs={{0,96},{1,97},{2,98},{3,99},{4,100},{5,101},{6,102},{7,103},{8,104... | collective-permute-start | bytes 1179656 | tf_op jit(solution)/shard_map/ppermute | solution.py:459
  70.9 0.1 collective-permute-start.13
  71.0 2.7 %collective-permute-start.15 = (bf16[2,12,64,128]{3,2,1,0:T(8,128)(2,1)S(1)}, bf16[2,12,64,128]{3,2,1,0:T(8,128)(2,1)S(1)}, u32[]{:S(2)}, u32[]{:S(2)}) collective-permute-start(bf16[2,12,64,128]{3,2,1,0:T(8,128)(2,1)S(1)} %slice.19), channel_id=1, source_target_pairs={{0,24},{1,25},{2,26},{3,27},{4,28},{5,29},{6,30},{7,31},{8,0},{9,1... | collective-permute-start | bytes 1179656 | tf_op jit(solution)/shard_map/ppermute | solution.py:459
  73.7 9.1 %early_product.1.before = bf16[8,128,1536]{2,1,0:T(8,128)(2,1)S(1)} custom-call(s32[2]{0:T(128)S(1)} %copy-done.8, bf16[4,12,64,128]{3,2,1,0:T(8,128)(2,1)S(1)} %collective-permute-done.4.a_down, bf16[4,12,64,128]{3,2,1,0:T(8,128)(2,1)S(1)} %collective-permute-done.6.a_up, bf16[4,12,64,128]{3,2,1,0:T(8,128)(2,1)S(1)} %pad_maximum_fusion.1.b_own, ...), custom_call_target="tpu_custom_call" | custom-call | flops 6039797760 | bytes 7077888 | tf_op jit(solution)/shard_map/early_product/pallas_call | solution.py:214
  82.9 4.0 %late_product.3 = (bf16[4,128,768]{2,1,0:T(8,128)(2,1)S(1)}, bf16[4,128,768]{2,1,0:T(8,128)(2,1)S(1)}) custom-call(s32[2]{0:T(128)S(1)} %copy-done.8, bf16[4,12,64,128]{3,2,1,0:T(8,128)(2,1)S(1)} %pad_maximum_fusion._.a_own, bf16[2,12,64,128]{3,2,1,0:T(8,128)(2,1)S(1)} %collective-permute-done.5.a_far, ...), custom_call_target="tpu_custom_call" | custom-call | flops 1811939328 | bytes 5505024 | tf_op jit(solution)/shard_map/late_product/pallas_call | solution.py:269
  86.9 1.3 collective-permute-start.20
  88.2 4.0 %late_product.2 = (bf16[4,128,768]{2,1,0:T(8,128)(2,1)S(1)}, bf16[4,128,768]{2,1,0:T(8,128)(2,1)S(1)}) custom-call(s32[2]{0:T(128)S(1)} %copy-done.8, bf16[4,12,64,128]{3,2,1,0:T(8,128)(2,1)S(1)} %pad_maximum_fusion._.a_own, bf16[2,12,64,128]{3,2,1,0:T(8,128)(2,1)S(1)} %collective-permute-done.5.a_far, ...), custom_call_target="tpu_custom_call" | custom-call | flops 1811939328 | bytes 5505024 | tf_op jit(solution)/shard_map/late_product/pallas_call | solution.py:269
  92.3 0.1 collective-permute-start.16
  92.4 1.1 pair_sum.3
  93.5 0.1 collective-permute-start.21
  93.6 0.1 collective-permute-start.22
  93.7 2.6 %collective-permute-start.23 = (bf16[128,768]{1,0:T(8,128)(2,1)S(1)}, bf16[128,768]{1,0:T(8,128)(2,1)S(1)}, u32[]{:S(2)}, u32[]{:S(2)}) collective-permute-start(bf16[128,768]{1,0:T(8,128)(2,1)S(1)} %get-tuple-element.43), channel_id=1, source_target_pairs={{0,6},{1,7},{2,0},{3,1},{4,2},{5,3},{6,4},{7,5},{8,14},{9,15},{10,... | collective-permute-start | bytes 589832 | tf_op jit(solution)/shard_map/ppermute | solution.py:459
  96.3 1.1 pair_sum.2
  97.3 0.8 collective-permute-start.17
  98.2 1.9 %collective-permute-start.18 = (bf16[128,768]{1,0:T(8,128)(2,1)S(1)}, bf16[128,768]{1,0:T(8,128)(2,1)S(1)}, u32[]{:S(2)}, u32[]{:S(2)}) collective-permute-start(bf16[128,768]{1,0:T(8,128)(2,1)S(1)} %get-tuple-element.36), channel_id=1, source_target_pairs={{0,4},{1,5},{2,6},{3,7},{4,0},{5,1},{6,2},{7,3},{8,12},{9,13},{10,... | collective-permute-start | bytes 589832 | tf_op jit(solution)/shard_map/ppermute | solution.py:459
  100.0 5.4 %collective-permute-done.21.refs_5_ = bf16[128,768]{1,0:T(8,128)(2,1)S(1)} collective-permute-done((bf16[128,768]{1,0:T(8,128)(2,1)S(1)}, bf16[128,768]{1,0:T(8,128)(2,1)S(1)}, u32[]{:S(2)}, u32[]{:S(2)}) %collective-permute-start.21) | collective-permute-done | bytes 196640 | tf_op jit(solution)/shard_map/ppermute | solution.py:459
  105.5 8.4 %collective-permute-done.17.refs_1_ = bf16[128,768]{1,0:T(8,128)(2,1)S(1)} collective-permute-done((bf16[128,768]{1,0:T(8,128)(2,1)S(1)}, bf16[128,768]{1,0:T(8,128)(2,1)S(1)}, u32[]{:S(2)}, u32[]{:S(2)}) %collective-permute-start.17) | collective-permute-done | bytes 196640 | tf_op jit(solution)/shard_map/ppermute | solution.py:459
  114.0 1.9 %slots.1 = (bf16[128,1536]{1,0:T(8,128)(2,1)S(1)}, bf16[192,512]{1,0:T(8,128)(2,1)S(1)}) custom-call(s32[2]{0:T(128)S(1)} %copy-done.8, s32[16,12]{1,0:T(8,128)S(1)} %copy-done.6, s32[16]{0:T(128)S(1)} %copy-done.9, s32[16,12]{1,0:T(8,128)S(1)} %copy-done.7, s32[16]{0:T(128)S(1)} %copy-done.10, bf16[128,768]{1,0:T(8,128)(2,1)S(1)} %get-tuple-element.34.refs_0_, ...), custom_call_target="tpu_custom_call" | custom-call | flops 301989888 | bytes 5111808 | tf_op jit(solution)/shard_map/slots/pallas_call | solution.py:343
  115.9 0.1 collective-permute-start.26
  116.0 2.7 %collective-permute-start.27 = (bf16[192,512]{1,0:T(8,128)(2,1)S(1)}, bf16[192,512]{1,0:T(8,128)(2,1)S(1)}, u32[]{:S(2)}, u32[]{:S(2)}) collective-permute-start(bf16[192,512]{1,0:T(8,128)(2,1)S(1)} %get-tuple-element.45.one), channel_id=1, source_target_pairs={{0,24},{1,25},{2,26},{3,27},{4,28},{5,29},{6,30},{7,31},{8,0},{9,1... | collective-permute-start | bytes 589832 | tf_op jit(solution)/shard_map/ppermute | solution.py:459
  118.6 0.8 collective-permute-start.28
  119.4 0.9 collective-permute-start.24
  120.4 1.7 %collective-permute-start.25 = (bf16[128,1536]{1,0:T(8,128)(2,1)S(1)}, bf16[128,1536]{1,0:T(8,128)(2,1)S(1)}, u32[]{:S(2)}, u32[]{:S(2)}) collective-permute-start(bf16[128,1536]{1,0:T(8,128)(2,1)S(1)} %get-tuple-element.46.refs_0_), channel_id=1, source_target_pairs={{0,6},{1,7},{2,0},{3,1},{4,2},{5,3},{6,4},{7,5},{8,14},{9,15},{10,... | collective-permute-start | bytes 1179656 | tf_op jit(solution)/shard_map/ppermute | solution.py:459
  122.1 4.9 %collective-permute-done.28.four = bf16[192,512]{1,0:T(8,128)(2,1)S(1)} collective-permute-done((bf16[192,512]{1,0:T(8,128)(2,1)S(1)}, bf16[192,512]{1,0:T(8,128)(2,1)S(1)}, u32[]{:S(2)}, u32[]{:S(2)}) %collective-permute-start.28) | collective-permute-done | bytes 196640 | tf_op jit(solution)/shard_map/ppermute | solution.py:459
  127.1 0.1 fold.1.one
  127.2 0.1 collective-permute-start.29
  127.2 1.9 %collective-permute-done.24.refs_1_ = bf16[128,1536]{1,0:T(8,128)(2,1)S(1)} collective-permute-done((bf16[128,1536]{1,0:T(8,128)(2,1)S(1)}, bf16[128,1536]{1,0:T(8,128)(2,1)S(1)}, u32[]{:S(2)}, u32[]{:S(2)}) %collective-permute-start.24) | collective-permute-done | bytes 393248 | tf_op jit(solution)/shard_map/ppermute | solution.py:459
  129.2 0.5 collective-permute-done.25.refs_2_
  129.7 3.3 %collective-permute-done.29.two = bf16[192,512]{1,0:T(8,128)(2,1)S(1)} collective-permute-done((bf16[192,512]{1,0:T(8,128)(2,1)S(1)}, bf16[192,512]{1,0:T(8,128)(2,1)S(1)}, u32[]{:S(2)}, u32[]{:S(2)}) %collective-permute-start.29) | collective-permute-done | bytes 196640 | tf_op jit(solution)/shard_map/ppermute | solution.py:459
  133.0 1.0 collective-permute-start.30
  134.0 1.1 collective-permute-start.35
  135.1 4.2 %collective-permute-start.31 = (bf16[128,1536]{1,0:T(8,128)(2,1)S(1)}, bf16[128,1536]{1,0:T(8,128)(2,1)S(1)}, u32[]{:S(2)}, u32[]{:S(2)}) collective-permute-start(bf16[128,1536]{1,0:T(8,128)(2,1)S(1)} %get-tuple-element.46.refs_0_), channel_id=1, source_target_pairs={{0,1},{1,0},{2,3},{3,2},{4,5},{5,4},{6,7},{7,6},{8,9},{9,8},{10,11... | collective-permute-start | bytes 1179656 | tf_op jit(solution)/shard_map/ppermute | solution.py:459
  139.3 0.5 collective-permute-start.33
  139.8 1.7 collective-permute-done.30.refs_3_
  141.5 4.5 %collective-permute-start.34 = (bf16[128,1536]{1,0:T(8,128)(2,1)S(1)}, bf16[128,1536]{1,0:T(8,128)(2,1)S(1)}, u32[]{:S(2)}, u32[]{:S(2)}) collective-permute-start(bf16[128,1536]{1,0:T(8,128)(2,1)S(1)} %collective-permute-done.30.refs_3_), channel_id=1, source_target_pairs={{0,1},{1,0},{2,3},{3,2},{4,5},{5,4},{6,7},{7,6},{8,9},{9,8},{10,11... | collective-permute-start | bytes 1179656 | tf_op jit(solution)/shard_map/ppermute | solution.py:459
  146.0 0.2 collective-permute-start.36
  146.2 7.9 %collective-permute-done.36.four = bf16[192,512]{1,0:T(8,128)(2,1)S(1)} collective-permute-done((bf16[192,512]{1,0:T(8,128)(2,1)S(1)}, bf16[192,512]{1,0:T(8,128)(2,1)S(1)}, u32[]{:S(2)}, u32[]{:S(2)}) %collective-permute-start.36) | collective-permute-done | bytes 196640 | tf_op jit(solution)/shard_map/ppermute | solution.py:459
  154.0 1.0 top_part.1
  155.1 10.7 %all_to_all.5.taken = bf16[8,64,128]{2,1,0:T(8,128)(2,1)S(1)} all-to-all(bf16[8,64,128]{2,1,0:T(8,128)(2,1)S(1)} %get-tuple-element.54), channel_id=1, replica_groups=mesh['row'=16,'col'=8] {'col'}, dimensions={0} | all-to-all | bytes 262144 | tf_op jit(solution)/shard_map/all_to_all | solution.py:497
  165.8 0.9 last_part.1
  166.7 4.0 %whole_columns.1 = (bf16[1536,512]{1,0:T(8,128)(2,1)}, bf16[1536,512]{1,0:T(8,128)(2,1)}) custom-call(s32[2]{0:T(128)S(1)} %copy-done.8, bf16[128,1536]{1,0:T(8,128)(2,1)S(1)} %get-tuple-element.46.refs_0_, bf16[128,1536]{1,0:T(8,128)(2,1)S(1)} %collective-permute-done.24.refs_1_, bf16[128,1536]{1,0:T(8,128)(2,1)S(1)} %collective-permute-done.25.refs_2_, ...), custom_call_target="tpu_custom_call" | custom-call | bytes 6291456 | tf_op jit(solution)/shard_map/whole_columns/pallas_call | solution.py:375
  (52 shorter events, 0.2 us)
Async XLA Ops:
  5.7 23.4 %collective-permute-start = (bf16[12,64,128]{2,1,0:T(8,128)(2,1)}, bf16[12,64,128]{2,1,0:T(8,128)(2,1)S(1)}, u32[]{:S(2)}, u32[]{:S(2)}) collective-permute-start(bf16[12,64,128]{2,1,0:T(8,128)(2,1)} %get-tuple-element.30), channel_id=1, source_target_pairs={{0,0},{1,32},{2,8},{3,40},{4,16},{5,48},{6,24},{7,56},{8,9},{9,41}... | collective-permute-start | bytes 589832 | tf_op jit(solution)/shard_map/ppermute | solution.py:472
  10.7 22.7 %collective-permute-start.8 = (bf16[12,64,128]{2,1,0:T(8,128)(2,1)}, bf16[12,64,128]{2,1,0:T(8,128)(2,1)S(1)}, u32[]{:S(2)}, u32[]{:S(2)}) collective-permute-start(bf16[12,64,128]{2,1,0:T(8,128)(2,1)} %get-tuple-element.31), channel_id=1, source_target_pairs={{0,0},{1,32},{2,8},{3,40},{4,16},{5,48},{6,24},{7,56},{8,9},{9,41}... | collective-permute-start | bytes 589832 | tf_op jit(solution)/shard_map/ppermute | solution.py:473
  29.1 11.6 %collective-permute-start.1 = (bf16[12,64,128]{2,1,0:T(8,128)(2,1)S(1)}, bf16[12,64,128]{2,1,0:T(8,128)(2,1)S(1)}, u32[]{:S(2)}, u32[]{:S(2)}) collective-permute-start(bf16[12,64,128]{2,1,0:T(8,128)(2,1)S(1)} %collective-permute-done), channel_id=1, source_target_pairs={{0,8},{1,9},{2,10},{3,11},{4,12},{5,13},{6,14},{7,15},{8,16},{9,17... | collective-permute-start | bytes 589832 | tf_op jit(solution)/shard_map/ppermute | solution.py:459
  29.1 15.2 %collective-permute-start.2 = (bf16[12,64,128]{2,1,0:T(8,128)(2,1)S(1)}, bf16[12,64,128]{2,1,0:T(8,128)(2,1)S(1)}, u32[]{:S(2)}, u32[]{:S(2)}) collective-permute-start(bf16[12,64,128]{2,1,0:T(8,128)(2,1)S(1)} %collective-permute-done), channel_id=1, source_target_pairs={{0,24},{1,25},{2,26},{3,27},{4,28},{5,29},{6,30},{7,31},{8,0},{9,1... | collective-permute-start | bytes 589832 | tf_op jit(solution)/shard_map/ppermute | solution.py:459
  31.8 12.5 %collective-permute-start.3 = (bf16[12,64,128]{2,1,0:T(8,128)(2,1)S(1)}, bf16[12,64,128]{2,1,0:T(8,128)(2,1)S(1)}, u32[]{:S(2)}, u32[]{:S(2)}) collective-permute-start(bf16[12,64,128]{2,1,0:T(8,128)(2,1)S(1)} %collective-permute-done), channel_id=1, source_target_pairs={{0,16},{1,17},{2,18},{3,19},{4,20},{5,21},{6,22},{7,23},{8,24},{9,... | collective-permute-start | bytes 589832 | tf_op jit(solution)/shard_map/ppermute | solution.py:459
  33.4 13.8 %collective-permute-start.9 = (bf16[12,64,128]{2,1,0:T(8,128)(2,1)S(1)}, bf16[12,64,128]{2,1,0:T(8,128)(2,1)S(1)}, u32[]{:S(2)}, u32[]{:S(2)}) collective-permute-start(bf16[12,64,128]{2,1,0:T(8,128)(2,1)S(1)} %collective-permute-done.8), channel_id=1, source_target_pairs={{0,32},{1,33},{2,34},{3,35},{4,36},{5,37},{6,38},{7,39},{8,40},{9,... | collective-permute-start | bytes 589832 | tf_op jit(solution)/shard_map/ppermute | solution.py:459
  35.1 12.1 %collective-permute-start.10 = (bf16[12,64,128]{2,1,0:T(8,128)(2,1)S(1)}, bf16[12,64,128]{2,1,0:T(8,128)(2,1)S(1)}, u32[]{:S(2)}, u32[]{:S(2)}) collective-permute-start(bf16[12,64,128]{2,1,0:T(8,128)(2,1)S(1)} %collective-permute-done.8), channel_id=1, source_target_pairs={{0,96},{1,97},{2,98},{3,99},{4,100},{5,101},{6,102},{7,103},{8,104... | collective-permute-start | bytes 589832 | tf_op jit(solution)/shard_map/ppermute | solution.py:459
  40.8 7.4 %collective-permute-start.11 = (bf16[12,64,128]{2,1,0:T(8,128)(2,1)S(1)}, bf16[12,64,128]{2,1,0:T(8,128)(2,1)S(1)}, u32[]{:S(2)}, u32[]{:S(2)}) collective-permute-start(bf16[12,64,128]{2,1,0:T(8,128)(2,1)S(1)} %collective-permute-done.8), channel_id=1, source_target_pairs={{0,64},{1,65},{2,66},{3,67},{4,68},{5,69},{6,70},{7,71},{8,72},{9,... | collective-permute-start | bytes 589832 | tf_op jit(solution)/shard_map/ppermute | solution.py:459
  44.4 20.8 %collective-permute-start.4 = (bf16[4,12,64,128]{3,2,1,0:T(8,128)(2,1)S(1)}, bf16[4,12,64,128]{3,2,1,0:T(8,128)(2,1)S(1)}, u32[]{:S(2)}, u32[]{:S(2)}) collective-permute-start(bf16[4,12,64,128]{3,2,1,0:T(8,128)(2,1)S(1)} %pad_maximum_fusion._.a_own), channel_id=1, source_target_pairs={{0,32},{1,33},{2,34},{3,35},{4,36},{5,37},{6,38},{7,39},{8,40},{9,... | collective-permute-start | bytes 2359304 | tf_op jit(solution)/shard_map/ppermute | solution.py:459
  46.2 21.8 %collective-permute-start.6 = (bf16[4,12,64,128]{3,2,1,0:T(8,128)(2,1)S(1)}, bf16[4,12,64,128]{3,2,1,0:T(8,128)(2,1)S(1)}, u32[]{:S(2)}, u32[]{:S(2)}) collective-permute-start(bf16[4,12,64,128]{3,2,1,0:T(8,128)(2,1)S(1)} %pad_maximum_fusion._.a_own), channel_id=1, source_target_pairs={{0,96},{1,97},{2,98},{3,99},{4,100},{5,101},{6,102},{7,103},{8,104... | collective-permute-start | bytes 2359304 | tf_op jit(solution)/shard_map/ppermute | solution.py:459
  48.3 22.6 %collective-permute-start.12 = (bf16[4,12,64,128]{3,2,1,0:T(8,128)(2,1)S(1)}, bf16[4,12,64,128]{3,2,1,0:T(8,128)(2,1)S(1)}, u32[]{:S(2)}, u32[]{:S(2)}) collective-permute-start(bf16[4,12,64,128]{3,2,1,0:T(8,128)(2,1)S(1)} %pad_maximum_fusion.1.b_own), channel_id=1, source_target_pairs={{0,8},{1,9},{2,10},{3,11},{4,12},{5,13},{6,14},{7,15},{8,16},{9,17... | collective-permute-start | bytes 2359304 | tf_op jit(solution)/shard_map/ppermute | solution.py:459
  48.3 22.6 %collective-permute-start.14 = (bf16[4,12,64,128]{3,2,1,0:T(8,128)(2,1)S(1)}, bf16[4,12,64,128]{3,2,1,0:T(8,128)(2,1)S(1)}, u32[]{:S(2)}, u32[]{:S(2)}) collective-permute-start(bf16[4,12,64,128]{3,2,1,0:T(8,128)(2,1)S(1)} %pad_maximum_fusion.1.b_own), channel_id=1, source_target_pairs={{0,24},{1,25},{2,26},{3,27},{4,28},{5,29},{6,30},{7,31},{8,0},{9,1... | collective-permute-start | bytes 2359304 | tf_op jit(solution)/shard_map/ppermute | solution.py:459
  51.0 3.7 %copy-start.1 = (bf16[1536,3072]{1,0:T(8,128)(2,1)S(1)}, bf16[1536,3072]{1,0:T(8,128)(2,1)}, u32[]{:S(2)}) copy-start(bf16[1536,3072]{1,0:T(8,128)(2,1)} %source.1) | copy-start | bytes 28311556
  55.3 18.4 %copy-start.8 = (s32[2]{0:T(128)S(1)}, s32[2]{0:T(128)}, u32[]{:S(2)}) copy-start(s32[2]{0:T(128)} %pad_add_fusion.place) | copy-start | bytes 28
  65.2 17.6 %collective-permute-start.5 = (bf16[2,12,64,128]{3,2,1,0:T(8,128)(2,1)S(1)}, bf16[2,12,64,128]{3,2,1,0:T(8,128)(2,1)S(1)}, u32[]{:S(2)}, u32[]{:S(2)}) collective-permute-start(bf16[2,12,64,128]{3,2,1,0:T(8,128)(2,1)S(1)} %slice.16), channel_id=1, source_target_pairs={{0,32},{1,33},{2,34},{3,35},{4,36},{5,37},{6,38},{7,39},{8,40},{9,... | collective-permute-start | bytes 1179656 | tf_op jit(solution)/shard_map/ppermute | solution.py:459
  68.0 14.9 %collective-permute-start.7 = (bf16[2,12,64,128]{3,2,1,0:T(8,128)(2,1)S(1)}, bf16[2,12,64,128]{3,2,1,0:T(8,128)(2,1)S(1)}, u32[]{:S(2)}, u32[]{:S(2)}) collective-permute-start(bf16[2,12,64,128]{3,2,1,0:T(8,128)(2,1)S(1)} %slice.17), channel_id=1, source_target_pairs={{0,96},{1,97},{2,98},{3,99},{4,100},{5,101},{6,102},{7,103},{8,104... | collective-permute-start | bytes 1179656 | tf_op jit(solution)/shard_map/ppermute | solution.py:459
  70.9 12.0 %collective-permute-start.13 = (bf16[2,12,64,128]{3,2,1,0:T(8,128)(2,1)S(1)}, bf16[2,12,64,128]{3,2,1,0:T(8,128)(2,1)S(1)}, u32[]{:S(2)}, u32[]{:S(2)}) collective-permute-start(bf16[2,12,64,128]{3,2,1,0:T(8,128)(2,1)S(1)} %slice.18), channel_id=1, source_target_pairs={{0,8},{1,9},{2,10},{3,11},{4,12},{5,13},{6,14},{7,15},{8,16},{9,17... | collective-permute-start | bytes 1179656 | tf_op jit(solution)/shard_map/ppermute | solution.py:459
  71.0 11.9 %collective-permute-start.15 = (bf16[2,12,64,128]{3,2,1,0:T(8,128)(2,1)S(1)}, bf16[2,12,64,128]{3,2,1,0:T(8,128)(2,1)S(1)}, u32[]{:S(2)}, u32[]{:S(2)}) collective-permute-start(bf16[2,12,64,128]{3,2,1,0:T(8,128)(2,1)S(1)} %slice.19), channel_id=1, source_target_pairs={{0,24},{1,25},{2,26},{3,27},{4,28},{5,29},{6,30},{7,31},{8,0},{9,1... | collective-permute-start | bytes 1179656 | tf_op jit(solution)/shard_map/ppermute | solution.py:459
  86.9 5.4 %collective-permute-start.20 = (bf16[4,128,768]{2,1,0:T(8,128)(2,1)S(1)}, bf16[4,128,768]{2,1,0:T(8,128)(2,1)S(1)}, u32[]{:S(2)}, u32[]{:S(2)}) collective-permute-start(bf16[4,128,768]{2,1,0:T(8,128)(2,1)S(1)} %get-tuple-element.39), channel_id=1, source_target_pairs={{0,1},{1,0},{2,3},{3,2},{4,5},{5,4},{6,7},{7,6},{8,9},{9,8},{10,11... | collective-permute-start | bytes 2359304 | tf_op jit(solution)/shard_map/ppermute | solution.py:459
  92.3 4.0 %collective-permute-start.16 = (bf16[4,128,768]{2,1,0:T(8,128)(2,1)S(1)}, bf16[4,128,768]{2,1,0:T(8,128)(2,1)S(1)}, u32[]{:S(2)}, u32[]{:S(2)}) collective-permute-start(bf16[4,128,768]{2,1,0:T(8,128)(2,1)S(1)} %get-tuple-element.33), channel_id=1, source_target_pairs={{0,1},{1,0},{2,3},{3,2},{4,5},{5,4},{6,7},{7,6},{8,9},{9,8},{10,11... | collective-permute-start | bytes 2359304 | tf_op jit(solution)/shard_map/ppermute | solution.py:459
  92.4 21.5 %copy-start = (bf16[1536,512]{1,0:T(8,128)(2,1)S(1)}, bf16[1536,512]{1,0:T(8,128)(2,1)}, u32[]{:S(2)}) copy-start(bf16[1536,512]{1,0:T(8,128)(2,1)} %refs_8_.1) | copy-start | bytes 4718596
  92.4 21.5 %copy-start.2 = (bf16[1536,512]{1,0:T(8,128)(2,1)S(1)}, bf16[1536,512]{1,0:T(8,128)(2,1)}, u32[]{:S(2)}) copy-start(bf16[1536,512]{1,0:T(8,128)(2,1)} %refs_9_.1) | copy-start | bytes 4718596
  92.4 21.5 %copy-start.6 = (s32[16,12]{1,0:T(8,128)S(1)}, s32[16,12]{1,0:T(8,128)}, u32[]{:S(2)}) copy-start(s32[16,12]{1,0:T(8,128)} %rows_a.3) | copy-start | bytes 2308
  92.4 21.5 %copy-start.7 = (s32[16,12]{1,0:T(8,128)S(1)}, s32[16,12]{1,0:T(8,128)}, u32[]{:S(2)}) copy-start(s32[16,12]{1,0:T(8,128)} %rows_b.3) | copy-start | bytes 2308
  92.4 21.5 %copy-start.9 = (s32[16]{0:T(128)S(1)}, s32[16]{0:T(128)}, u32[]{:S(2)}) copy-start(s32[16]{0:T(128)} %counts_a.3) | copy-start | bytes 196
  92.4 21.5 %copy-start.10 = (s32[16]{0:T(128)S(1)}, s32[16]{0:T(128)}, u32[]{:S(2)}) copy-start(s32[16]{0:T(128)} %counts_b.3) | copy-start | bytes 196
  93.5 11.9 %collective-permute-start.21 = (bf16[128,768]{1,0:T(8,128)(2,1)S(1)}, bf16[128,768]{1,0:T(8,128)(2,1)S(1)}, u32[]{:S(2)}, u32[]{:S(2)}) collective-permute-start(bf16[128,768]{1,0:T(8,128)(2,1)S(1)} %get-tuple-element.41), channel_id=1, source_target_pairs={{0,2},{1,3},{2,4},{3,5},{4,6},{5,7},{6,0},{7,1},{8,10},{9,11},{10,... | collective-permute-start | bytes 589832 | tf_op jit(solution)/shard_map/ppermute | solution.py:459
  93.6 11.9 %collective-permute-start.22 = (bf16[128,768]{1,0:T(8,128)(2,1)S(1)}, bf16[128,768]{1,0:T(8,128)(2,1)S(1)}, u32[]{:S(2)}, u32[]{:S(2)}) collective-permute-start(bf16[128,768]{1,0:T(8,128)(2,1)S(1)} %get-tuple-element.42), channel_id=1, source_target_pairs={{0,4},{1,5},{2,6},{3,7},{4,0},{5,1},{6,2},{7,3},{8,12},{9,13},{10,... | collective-permute-start | bytes 589832 | tf_op jit(solution)/shard_map/ppermute | solution.py:459
  93.7 11.8 %collective-permute-start.23 = (bf16[128,768]{1,0:T(8,128)(2,1)S(1)}, bf16[128,768]{1,0:T(8,128)(2,1)S(1)}, u32[]{:S(2)}, u32[]{:S(2)}) collective-permute-start(bf16[128,768]{1,0:T(8,128)(2,1)S(1)} %get-tuple-element.43), channel_id=1, source_target_pairs={{0,6},{1,7},{2,0},{3,1},{4,2},{5,3},{6,4},{7,5},{8,14},{9,15},{10,... | collective-permute-start | bytes 589832 | tf_op jit(solution)/shard_map/ppermute | solution.py:459
  97.3 16.5 %collective-permute-start.17 = (bf16[128,768]{1,0:T(8,128)(2,1)S(1)}, bf16[128,768]{1,0:T(8,128)(2,1)S(1)}, u32[]{:S(2)}, u32[]{:S(2)}) collective-permute-start(bf16[128,768]{1,0:T(8,128)(2,1)S(1)} %get-tuple-element.35), channel_id=1, source_target_pairs={{0,2},{1,3},{2,4},{3,5},{4,6},{5,7},{6,0},{7,1},{8,10},{9,11},{10,... | collective-permute-start | bytes 589832 | tf_op jit(solution)/shard_map/ppermute | solution.py:459
  98.2 15.7 %collective-permute-start.18 = (bf16[128,768]{1,0:T(8,128)(2,1)S(1)}, bf16[128,768]{1,0:T(8,128)(2,1)S(1)}, u32[]{:S(2)}, u32[]{:S(2)}) collective-permute-start(bf16[128,768]{1,0:T(8,128)(2,1)S(1)} %get-tuple-element.36), channel_id=1, source_target_pairs={{0,4},{1,5},{2,6},{3,7},{4,0},{5,1},{6,2},{7,3},{8,12},{9,13},{10,... | collective-permute-start | bytes 589832 | tf_op jit(solution)/shard_map/ppermute | solution.py:459
  105.4 8.4 %collective-permute-start.19 = (bf16[128,768]{1,0:T(8,128)(2,1)S(1)}, bf16[128,768]{1,0:T(8,128)(2,1)S(1)}, u32[]{:S(2)}, u32[]{:S(2)}) collective-permute-start(bf16[128,768]{1,0:T(8,128)(2,1)S(1)} %get-tuple-element.37), channel_id=1, source_target_pairs={{0,6},{1,7},{2,0},{3,1},{4,2},{5,3},{6,4},{7,5},{8,14},{9,15},{10,... | collective-permute-start | bytes 589832 | tf_op jit(solution)/shard_map/ppermute | solution.py:459
  113.9 40.1 %copy-start.3 = (bf16[512,512]{1,0:T(8,128)(2,1)S(1)}, bf16[512,512]{1,0:T(8,128)(2,1)}, u32[]{:S(2)}) copy-start(bf16[512,512]{1,0:T(8,128)(2,1)} %top.5) | copy-start | bytes 1572868
  114.0 40.1 %copy-start.4 = (f32[64,512]{1,0:T(8,128)S(1)}, f32[64,512]{1,0:T(8,128)}, u32[]{:S(2)}) copy-start(f32[64,512]{1,0:T(8,128)} %base.2) | copy-start | bytes 393220
  115.9 49.9 %copy-start.5 = (f32[64,512]{1,0:T(8,128)S(1)}, f32[64,512]{1,0:T(8,128)}, u32[]{:S(2)}) copy-start(f32[64,512]{1,0:T(8,128)} %base.3) | copy-start | bytes 393220
  115.9 6.2 %collective-permute-start.26 = (bf16[192,512]{1,0:T(8,128)(2,1)S(1)}, bf16[192,512]{1,0:T(8,128)(2,1)S(1)}, u32[]{:S(2)}, u32[]{:S(2)}) collective-permute-start(bf16[192,512]{1,0:T(8,128)(2,1)S(1)} %get-tuple-element.45.one), channel_id=1, source_target_pairs={{0,8},{1,9},{2,10},{3,11},{4,12},{5,13},{6,14},{7,15},{8,16},{9,17... | collective-permute-start | bytes 589832 | tf_op jit(solution)/shard_map/ppermute | solution.py:459
  116.0 6.2 %collective-permute-start.27 = (bf16[192,512]{1,0:T(8,128)(2,1)S(1)}, bf16[192,512]{1,0:T(8,128)(2,1)S(1)}, u32[]{:S(2)}, u32[]{:S(2)}) collective-permute-start(bf16[192,512]{1,0:T(8,128)(2,1)S(1)} %get-tuple-element.45.one), channel_id=1, source_target_pairs={{0,24},{1,25},{2,26},{3,27},{4,28},{5,29},{6,30},{7,31},{8,0},{9,1... | collective-permute-start | bytes 589832 | tf_op jit(solution)/shard_map/ppermute | solution.py:459
  118.6 8.4 %collective-permute-start.28 = (bf16[192,512]{1,0:T(8,128)(2,1)S(1)}, bf16[192,512]{1,0:T(8,128)(2,1)S(1)}, u32[]{:S(2)}, u32[]{:S(2)}) collective-permute-start(bf16[192,512]{1,0:T(8,128)(2,1)S(1)} %get-tuple-element.45.one), channel_id=1, source_target_pairs={{0,16},{1,17},{2,18},{3,19},{4,20},{5,21},{6,22},{7,23},{8,24},{9,... | collective-permute-start | bytes 589832 | tf_op jit(solution)/shard_map/ppermute | solution.py:459
  119.4 9.7 %collective-permute-start.24 = (bf16[128,1536]{1,0:T(8,128)(2,1)S(1)}, bf16[128,1536]{1,0:T(8,128)(2,1)S(1)}, u32[]{:S(2)}, u32[]{:S(2)}) collective-permute-start(bf16[128,1536]{1,0:T(8,128)(2,1)S(1)} %get-tuple-element.46.refs_0_), channel_id=1, source_target_pairs={{0,2},{1,3},{2,4},{3,5},{4,6},{5,7},{6,0},{7,1},{8,10},{9,11},{10,... | collective-permute-start | bytes 1179656 | tf_op jit(solution)/shard_map/ppermute | solution.py:459
  120.4 9.3 %collective-permute-start.25 = (bf16[128,1536]{1,0:T(8,128)(2,1)S(1)}, bf16[128,1536]{1,0:T(8,128)(2,1)S(1)}, u32[]{:S(2)}, u32[]{:S(2)}) collective-permute-start(bf16[128,1536]{1,0:T(8,128)(2,1)S(1)} %get-tuple-element.46.refs_0_), channel_id=1, source_target_pairs={{0,6},{1,7},{2,0},{3,1},{4,2},{5,3},{6,4},{7,5},{8,14},{9,15},{10,... | collective-permute-start | bytes 1179656 | tf_op jit(solution)/shard_map/ppermute | solution.py:459
  127.2 5.8 %collective-permute-start.29 = (bf16[192,512]{1,0:T(8,128)(2,1)S(1)}, bf16[192,512]{1,0:T(8,128)(2,1)S(1)}, u32[]{:S(2)}, u32[]{:S(2)}) collective-permute-start(bf16[192,512]{1,0:T(8,128)(2,1)S(1)} %fold.1.one), channel_id=1, source_target_pairs={{0,32},{1,33},{2,34},{3,35},{4,36},{5,37},{6,38},{7,39},{8,40},{9,... | collective-permute-start | bytes 589832 | tf_op jit(solution)/shard_map/ppermute | solution.py:459
  133.0 8.5 %collective-permute-start.30 = (bf16[128,1536]{1,0:T(8,128)(2,1)S(1)}, bf16[128,1536]{1,0:T(8,128)(2,1)S(1)}, u32[]{:S(2)}, u32[]{:S(2)}) collective-permute-start(bf16[128,1536]{1,0:T(8,128)(2,1)S(1)} %get-tuple-element.46.refs_0_), channel_id=1, source_target_pairs={{0,4},{1,5},{2,6},{3,7},{4,0},{5,1},{6,2},{7,3},{8,12},{9,13},{10,... | collective-permute-start | bytes 1179656 | tf_op jit(solution)/shard_map/ppermute | solution.py:459
  134.0 12.0 %collective-permute-start.35 = (bf16[192,512]{1,0:T(8,128)(2,1)S(1)}, bf16[192,512]{1,0:T(8,128)(2,1)S(1)}, u32[]{:S(2)}, u32[]{:S(2)}) collective-permute-start(bf16[192,512]{1,0:T(8,128)(2,1)S(1)} %fold.1.one), channel_id=1, source_target_pairs={{0,96},{1,97},{2,98},{3,99},{4,100},{5,101},{6,102},{7,103},{8,104... | collective-permute-start | bytes 589832 | tf_op jit(solution)/shard_map/ppermute | solution.py:459
  135.1 31.6 %collective-permute-start.31 = (bf16[128,1536]{1,0:T(8,128)(2,1)S(1)}, bf16[128,1536]{1,0:T(8,128)(2,1)S(1)}, u32[]{:S(2)}, u32[]{:S(2)}) collective-permute-start(bf16[128,1536]{1,0:T(8,128)(2,1)S(1)} %get-tuple-element.46.refs_0_), channel_id=1, source_target_pairs={{0,1},{1,0},{2,3},{3,2},{4,5},{5,4},{6,7},{7,6},{8,9},{9,8},{10,11... | collective-permute-start | bytes 1179656 | tf_op jit(solution)/shard_map/ppermute | solution.py:459
  139.3 27.4 %collective-permute-start.32 = (bf16[128,1536]{1,0:T(8,128)(2,1)S(1)}, bf16[128,1536]{1,0:T(8,128)(2,1)S(1)}, u32[]{:S(2)}, u32[]{:S(2)}) collective-permute-start(bf16[128,1536]{1,0:T(8,128)(2,1)S(1)} %collective-permute-done.24.refs_1_), channel_id=1, source_target_pairs={{0,1},{1,0},{2,3},{3,2},{4,5},{5,4},{6,7},{7,6},{8,9},{9,8},{10,11... | collective-permute-start | bytes 1179656 | tf_op jit(solution)/shard_map/ppermute | solution.py:459
  139.3 27.4 %collective-permute-start.33 = (bf16[128,1536]{1,0:T(8,128)(2,1)S(1)}, bf16[128,1536]{1,0:T(8,128)(2,1)S(1)}, u32[]{:S(2)}, u32[]{:S(2)}) collective-permute-start(bf16[128,1536]{1,0:T(8,128)(2,1)S(1)} %collective-permute-done.25.refs_2_), channel_id=1, source_target_pairs={{0,1},{1,0},{2,3},{3,2},{4,5},{5,4},{6,7},{7,6},{8,9},{9,8},{10,11... | collective-permute-start | bytes 1179656 | tf_op jit(solution)/shard_map/ppermute | solution.py:459
  141.5 25.2 %collective-permute-start.34 = (bf16[128,1536]{1,0:T(8,128)(2,1)S(1)}, bf16[128,1536]{1,0:T(8,128)(2,1)S(1)}, u32[]{:S(2)}, u32[]{:S(2)}) collective-permute-start(bf16[128,1536]{1,0:T(8,128)(2,1)S(1)} %collective-permute-done.30.refs_3_), channel_id=1, source_target_pairs={{0,1},{1,0},{2,3},{3,2},{4,5},{5,4},{6,7},{7,6},{8,9},{9,8},{10,11... | collective-permute-start | bytes 1179656 | tf_op jit(solution)/shard_map/ppermute | solution.py:459
  146.0 8.0 %collective-permute-start.36 = (bf16[192,512]{1,0:T(8,128)(2,1)S(1)}, bf16[192,512]{1,0:T(8,128)(2,1)S(1)}, u32[]{:S(2)}, u32[]{:S(2)}) collective-permute-start(bf16[192,512]{1,0:T(8,128)(2,1)S(1)} %fold.1.one), channel_id=1, source_target_pairs={{0,64},{1,65},{2,66},{3,67},{4,68},{5,69},{6,70},{7,71},{8,72},{9,... | collective-permute-start | bytes 589832 | tf_op jit(solution)/shard_map/ppermute | solution.py:459

commit v5 on v4

--- a/solution.py
+++ b/solution.py
@@ -133,16 +133,16 @@
     return (value + by + SIDE) % SIDE
 
 
-def load_a(copies, buf, picks, u, spread, sems):
-    for i, member in picks:
-        copies.append((buf.at[member], spread.at[:, u // 2, i * PART : (i + 1) * PART, :]))
-
-
-def load_b(copies, buf, picks, u, first, spread, sems):
-    for i, member in picks:
+def load_a(copies, buf, u, spread):
+    for i in range(SIDE):
+        copies.append((buf.at[i], spread.at[:, u // 2, i * PART : (i + 1) * PART, :]))
+
+
+def load_b(copies, buf, u, first, spread):
+    for i in range(SIDE):
         ui = turn(u, -STEPS[i])
         at = pl.ds(pl.multiple_of(first + (ui % 2) * PART, PART), PART)
-        copies.append((buf.at[member], spread.at[:, ui // 2, at, :]))
+        copies.append((buf.at[i], spread.at[:, ui // 2, at, :]))
 
 
 def run_copies(copies, sems):
@@ -183,21 +183,16 @@
     return tile[pl.ds(pl.multiple_of(step * STRIP, STRIP), STRIP), :]
 
 
-ALL = tuple((i, i) for i in range(SIDE))
-FIRST = ((0, 0), (1, 1))
-LAST = ((2, 0), (3, 1))
-
-
 def early_body(place, a_down, a_up, b_own, b_down, b_up, tile, out, spread, sems):
     u, v = where(place)
 
     @pl.when(pl.program_id(0) == 0)
     def _():
         copies = []
-        load_a(copies, a_down, ALL, turn(u, -1), spread, sems)
-        load_a(copies, a_up, ALL, turn(u, 1), spread, sems)
+        load_a(copies, a_down, turn(u, -1), spread)
+        load_a(copies, a_up, turn(u, 1), spread)
         for t, buf in enumerate((b_own, b_down, b_up)):
-            load_b(copies, buf, ALL, u, W // 2 + 2 * t * PART, spread, sems)
+            load_b(copies, buf, u, W // 2 + 2 * t * PART, spread)
         run_copies(copies, sems)
 
     value = multiply(spread, rows_of(tile, pl.program_id(0)))
@@ -232,7 +227,7 @@
 
 
 def late_body(
-    half, place, a_own, a_far, a_far_more, b_far, b_far_more, tile, before, keep, give, spread, ready, sems
+    half, place, a_own, a_far, b_far, tile, before, keep, give, spread, ready, sems
 ):
     u, v = where(place)
     core = place[1] % 2
@@ -240,11 +235,9 @@
     @pl.when(pl.program_id(0) == 0)
     def _():
         copies = []
-        load_a(copies, a_own, ALL, u, spread, sems)
-        load_a(copies, a_far, FIRST, turn(u, 2), spread, sems)
-        load_a(copies, a_far_more, LAST, turn(u, 2), spread, sems)
-        load_b(copies, b_far, FIRST, u, W // 2, spread, sems)
-        load_b(copies, b_far_more, LAST, u, W // 2, spread, sems)
+        load_a(copies, a_own, u, spread)
+        load_a(copies, a_far, turn(u, 2), spread)
+        load_b(copies, b_far, u, W // 2, spread)
         run_copies(copies, sems)
 
     ready[...] = before[...]
@@ -272,7 +265,7 @@
         grid_spec=pltpu.PrefetchScalarGridSpec(
             num_scalar_prefetch=1,
             grid=(HALF_STEPS,),
-            in_specs=[pl.BlockSpec(memory_space=pl.ANY)] * 5
+            in_specs=[pl.BlockSpec(memory_space=pl.ANY)] * 3
             + [
                 pl.BlockSpec(memory_space=pltpu.VMEM),
                 pl.BlockSpec((COLS, PAIR, STRIP), lambda i, *_: (0, 0, half * HALF_STEPS + i)),
@@ -475,14 +468,14 @@
     b_own = jnp.stack(around(part_b, "dz"))
     a_down, a_up = send(a_own, dz=1), send(a_own, dz=-1)
     b_down, b_up = send(b_own, dy=1), send(b_own, dy=-1)
-    a_far, a_far_more = send(a_down[:2], dz=1), send(a_up[2:], dz=-1)
-    b_far, b_far_more = send(b_down[:2], dy=1), send(b_up[2:], dy=-1)
     trailing = hold(trailing, a_own)
+    a_next, b_next, _ = lax.optimization_barrier((a_down, b_down, trailing))
+    a_far, b_far = send(a_next, dz=1), send(b_next, dy=1)
     before = early_product(place, (a_down, a_up, b_own, b_down, b_up), trailing)
     slabs = []
     for half in range(2):
         keep, give = late_product(
-            half, place, (a_own, a_far, a_far_more, b_far, b_far_more), trailing, before
+            half, place, (a_own, a_far, b_far), trailing, before
         )
         own, one, two, three = pair_sum(place, keep, send(give, dc=1))
         slabs += [own, send(one, dx=1), send(two, dx=2), send(three, dx=-1)]
@@ -490,11 +483,14 @@
     near, other = send(columns, dx=1), send(columns, dx=-1)
     folded = fold(around(pieces, "dy"))
     got = around(folded, "dz")
-    own, near, other, got[1] = lax.optimization_barrier((columns, near, other, got[1]))
-    mine = [own, near, other, send(own, dx=2)]
-    column_a, column_b = whole_columns(place, mine + [send(slab, dc=1) for slab in mine])
+    far = send(lax.optimization_barrier((columns, folded))[0], dx=2)
+    _, (own, near, other) = lax.optimization_barrier((got, (columns, near, other)))
+    mates = [send(slab, dc=1) for slab in (own, near, other)]
     diag_a, top_b, sent = top_part(got, base_a, factor_top)
+    far, _ = lax.optimization_barrier((far, sent))
     taken = lax.all_to_all(sent, "col", 0, 0)
+    column_a, column_b = whole_columns(place, [own, near, other, far, *mates, send(far, dc=1)])
+    base_b, _ = lax.optimization_barrier((base_b, column_a))
     diag_b = last_part(got, base_b, taken, factor_top)
     return (column_a, diag_a, column_b, top_b, diag_b)
 

time: 171 us -> 168 us (0.982)
  blocking collectives: 10.7 us -> 0 us
  starting transfers between devices: 56.3 us -> 66 us
  waiting for transfers between devices: 65.7 us -> 61.2 us
  Pallas kernels: 32.4 us -> 34.2 us
    all_to_all x1 -> x0, blocking collectives: 10.7 us -> none  [on_device(): taken = lax.all_to_all(sent, 'col', 0, 0)]
    ppermute x35 -> x33, starting transfers between devices: 46.4 us -> 51.3 us  [send(): return lax.ppermute(value, BOTH, shifted(**by))]
    all_to_all x0 -> x1, starting transfers between devices: none -> 4.86 us  [on_device(): taken = lax.all_to_all(sent, 'col', 0, 0)]
    ppermute x35 -> x33, waiting for transfers between devices: 50.6 us -> 46.1 us  [send(): return lax.ppermute(value, BOTH, shifted(**by))]
  transfers between devices with their start and end apart: 37 -> 36, of which waited for: 14 -> 15; matrix products, arithmetic and copies ran while one was open for 0% -> 0% of each run, Pallas kernels for 11% -> 14%
where the time goes in v5:
time: 168 us; the launch traced here: 167 us
  starting transfers between devices  66 us (39%)
  waiting for transfers between devices  61.2 us (36%)
  Pallas kernels  34.2 us (20%)
  local copies, waits for them, and re-layouts  3.74 us (2%)
    ppermute x33, starting transfers between devices, send(): return lax.ppermute(value, BOTH, shifted(**by))  51.3 us
    ppermute x33, waiting for transfers between devices, send(): return lax.ppermute(value, BOTH, shifted(**by))  46.1 us
    ppermute x1, waiting for transfers between devices, on_device(): part_a = lax.ppermute(part_a, BOTH, spread_pairs())  13.5 us
    pallas_call x1, Pallas kernels, early_product(): pl.pallas_call(early_body, name='early_product', grid_spec=pltpu.Prefetch...  9.17 us
    pallas_call x2, Pallas kernels, late_product(): pl.pallas_call(functools.partial(late_body, half), name='late_product', g...  8.04 us
    pallas_call x1, Pallas kernels, whole_columns(): pl.pallas_call(column_body, name='whole_columns', grid_spec=pltpu.Prefetc...  5.69 us
    ppermute x1, starting transfers between devices, on_device(): part_b = lax.ppermute(part_b, BOTH, spread_pairs())  4.94 us
    ppermute x1, starting transfers between devices, on_device(): part_a = lax.ppermute(part_a, BOTH, spread_pairs())  4.92 us
  transfers between devices with their start and end apart: 36, of which 15 were waited for; matrix products, arithmetic and copies ran while one was open for 0% of the time, Pallas kernels for 14%

profile of v5, /device:TPU:1, one launch (start us, length us, event | category | flops | bytes accessed | tf_op | source)
XLA Modules:
  0.0 166.9 jit_solution(12873623681244182037)
XLA Ops:
  0.6 0.6 pad_add_fusion.place
  1.2 4.5 %prep.1 = (bf16[12,64,128]{2,1,0:T(8,128)(2,1)}, bf16[12,64,128]{2,1,0:T(8,128)(2,1)}) custom-call(s32[2]{0:T(128)} %pad_add_fusion.place, s32[16,12]{1,0:T(8,128)} %rows_a.3, s32[16]{0:T(128)} %counts_a.3, s32[16,12]{1,0:T(8,128)} %rows_b.3, s32[16]{0:T(128)} %counts_b.3, bf16[1536,512]{1,0:T(8,128)(2,1)} %refs_8_.1, bf16[1536,512]{1,0:T(8,128)(2,1)} %refs_8_.1, ...), custom_call_target="tpu_custom_call" | custom-call | flops 201326592 | bytes 3145728 | tf_op jit(solution)/shard_map/prep/pallas_call | solution.py:104
  5.7 4.9 %collective-permute-start = (bf16[12,64,128]{2,1,0:T(8,128)(2,1)}, bf16[12,64,128]{2,1,0:T(8,128)(2,1)S(1)}, u32[]{:S(2)}, u32[]{:S(2)}) collective-permute-start(bf16[12,64,128]{2,1,0:T(8,128)(2,1)} %get-tuple-element.34), channel_id=1, source_target_pairs={{0,0},{1,32},{2,8},{3,40},{4,16},{5,48},{6,24},{7,56},{8,9},{9,41}... | collective-permute-start | bytes 589832 | tf_op jit(solution)/shard_map/ppermute | solution.py:465
  10.7 4.9 %collective-permute-start.5 = (bf16[12,64,128]{2,1,0:T(8,128)(2,1)}, bf16[12,64,128]{2,1,0:T(8,128)(2,1)S(1)}, u32[]{:S(2)}, u32[]{:S(2)}) collective-permute-start(bf16[12,64,128]{2,1,0:T(8,128)(2,1)} %get-tuple-element.35), channel_id=1, source_target_pairs={{0,0},{1,32},{2,8},{3,40},{4,16},{5,48},{6,24},{7,56},{8,9},{9,41}... | collective-permute-start | bytes 589832 | tf_op jit(solution)/shard_map/ppermute | solution.py:466
  15.6 13.5 %collective-permute-done = bf16[12,64,128]{2,1,0:T(8,128)(2,1)S(1)} collective-permute-done((bf16[12,64,128]{2,1,0:T(8,128)(2,1)}, bf16[12,64,128]{2,1,0:T(8,128)(2,1)S(1)}, u32[]{:S(2)}, u32[]{:S(2)}) %collective-permute-start) | collective-permute-done | bytes 196640 | tf_op jit(solution)/shard_map/ppermute | solution.py:465
  29.1 2.7 %collective-permute-start.2 = (bf16[12,64,128]{2,1,0:T(8,128)(2,1)S(1)}, bf16[12,64,128]{2,1,0:T(8,128)(2,1)S(1)}, u32[]{:S(2)}, u32[]{:S(2)}) collective-permute-start(bf16[12,64,128]{2,1,0:T(8,128)(2,1)S(1)} %collective-permute-done), channel_id=1, source_target_pairs={{0,24},{1,25},{2,26},{3,27},{4,28},{5,29},{6,30},{7,31},{8,0},{9,1... | collective-permute-start | bytes 589832 | tf_op jit(solution)/shard_map/ppermute | solution.py:452
  31.8 1.5 collective-permute-done.5
  33.4 1.7 %collective-permute-start.6 = (bf16[12,64,128]{2,1,0:T(8,128)(2,1)S(1)}, bf16[12,64,128]{2,1,0:T(8,128)(2,1)S(1)}, u32[]{:S(2)}, u32[]{:S(2)}) collective-permute-start(bf16[12,64,128]{2,1,0:T(8,128)(2,1)S(1)} %collective-permute-done.5), channel_id=1, source_target_pairs={{0,32},{1,33},{2,34},{3,35},{4,36},{5,37},{6,38},{7,39},{8,40},{9,... | collective-permute-start | bytes 589832 | tf_op jit(solution)/shard_map/ppermute | solution.py:452
  35.0 2.4 %collective-permute-start.7 = (bf16[12,64,128]{2,1,0:T(8,128)(2,1)S(1)}, bf16[12,64,128]{2,1,0:T(8,128)(2,1)S(1)}, u32[]{:S(2)}, u32[]{:S(2)}) collective-permute-start(bf16[12,64,128]{2,1,0:T(8,128)(2,1)S(1)} %collective-permute-done.5), channel_id=1, source_target_pairs={{0,96},{1,97},{2,98},{3,99},{4,100},{5,101},{6,102},{7,103},{8,104... | collective-permute-start | bytes 589832 | tf_op jit(solution)/shard_map/ppermute | solution.py:452
  37.5 3.3 %collective-permute-done.1 = bf16[12,64,128]{2,1,0:T(8,128)(2,1)S(1)} collective-permute-done((bf16[12,64,128]{2,1,0:T(8,128)(2,1)S(1)}, bf16[12,64,128]{2,1,0:T(8,128)(2,1)S(1)}, u32[]{:S(2)}, u32[]{:S(2)}) %collective-permute-start.1) | collective-permute-done | bytes 196640 | tf_op jit(solution)/shard_map/ppermute | solution.py:452
  40.8 3.5 %collective-permute-start.8 = (bf16[12,64,128]{2,1,0:T(8,128)(2,1)S(1)}, bf16[12,64,128]{2,1,0:T(8,128)(2,1)S(1)}, u32[]{:S(2)}, u32[]{:S(2)}) collective-permute-start(bf16[12,64,128]{2,1,0:T(8,128)(2,1)S(1)} %collective-permute-done.5), channel_id=1, source_target_pairs={{0,64},{1,65},{2,66},{3,67},{4,68},{5,69},{6,70},{7,71},{8,72},{9,... | collective-permute-start | bytes 589832 | tf_op jit(solution)/shard_map/ppermute | solution.py:452
  44.3 0.1 pad_maximum_fusion._.a_own
  44.4 1.8 %collective-permute-start.4 = (bf16[4,12,64,128]{3,2,1,0:T(8,128)(2,1)S(1)}, bf16[4,12,64,128]{3,2,1,0:T(8,128)(2,1)S(1)}, u32[]{:S(2)}, u32[]{:S(2)}) collective-permute-start(bf16[4,12,64,128]{3,2,1,0:T(8,128)(2,1)S(1)} %pad_maximum_fusion._.a_own), channel_id=1, source_target_pairs={{0,32},{1,33},{2,34},{3,35},{4,36},{5,37},{6,38},{7,39},{8,40},{9,... | collective-permute-start | bytes 2359304 | tf_op jit(solution)/shard_map/ppermute | solution.py:452
  46.2 1.9 %collective-permute-done.8 = bf16[12,64,128]{2,1,0:T(8,128)(2,1)S(1)} collective-permute-done((bf16[12,64,128]{2,1,0:T(8,128)(2,1)S(1)}, bf16[12,64,128]{2,1,0:T(8,128)(2,1)S(1)}, u32[]{:S(2)}, u32[]{:S(2)}) %collective-permute-start.8) | collective-permute-done | bytes 196640 | tf_op jit(solution)/shard_map/ppermute | solution.py:452
  48.1 0.1 pad_maximum_fusion.1.b_own
  48.3 0.1 collective-permute-start.9
  48.3 5.4 %collective-permute-start.12 = (bf16[4,12,64,128]{3,2,1,0:T(8,128)(2,1)S(1)}, bf16[4,12,64,128]{3,2,1,0:T(8,128)(2,1)S(1)}, u32[]{:S(2)}, u32[]{:S(2)}) collective-permute-start(bf16[4,12,64,128]{3,2,1,0:T(8,128)(2,1)S(1)} %pad_maximum_fusion._.a_own), channel_id=1, source_target_pairs={{0,96},{1,97},{2,98},{3,99},{4,100},{5,101},{6,102},{7,103},{8,104... | collective-permute-start | bytes 2359304 | tf_op jit(solution)/shard_map/ppermute | solution.py:452
  53.7 2.6 %collective-permute-start.13 = (bf16[4,12,64,128]{3,2,1,0:T(8,128)(2,1)S(1)}, bf16[4,12,64,128]{3,2,1,0:T(8,128)(2,1)S(1)}, u32[]{:S(2)}, u32[]{:S(2)}) collective-permute-start(bf16[4,12,64,128]{3,2,1,0:T(8,128)(2,1)S(1)} %pad_maximum_fusion.1.b_own), channel_id=1, source_target_pairs={{0,24},{1,25},{2,26},{3,27},{4,28},{5,29},{6,30},{7,31},{8,0},{9,1... | collective-permute-start | bytes 2359304 | tf_op jit(solution)/shard_map/ppermute | solution.py:452
  56.3 3.7 %copy-done.1 = bf16[1536,3072]{1,0:T(8,128)(2,1)S(1)} copy-done((bf16[1536,3072]{1,0:T(8,128)(2,1)S(1)}, bf16[1536,3072]{1,0:T(8,128)(2,1)}, u32[]{:S(2)}) %copy-start.1) | copy-done | bytes 9437208
  60.0 0.6 hold.1.tile
  60.6 4.5 %collective-permute-done.4.a_down = bf16[4,12,64,128]{3,2,1,0:T(8,128)(2,1)S(1)} collective-permute-done((bf16[4,12,64,128]{3,2,1,0:T(8,128)(2,1)S(1)}, bf16[4,12,64,128]{3,2,1,0:T(8,128)(2,1)S(1)}, u32[]{:S(2)}, u32[]{:S(2)}) %collective-permute-start.4) | collective-permute-done | bytes 786464 | tf_op jit(solution)/shard_map/ppermute | solution.py:452
  65.2 3.1 %collective-permute-done.9.b_down = bf16[4,12,64,128]{3,2,1,0:T(8,128)(2,1)S(1)} collective-permute-done((bf16[4,12,64,128]{3,2,1,0:T(8,128)(2,1)S(1)}, bf16[4,12,64,128]{3,2,1,0:T(8,128)(2,1)S(1)}, u32[]{:S(2)}, u32[]{:S(2)}) %collective-permute-start.9) | collective-permute-done | bytes 786464 | tf_op jit(solution)/shard_map/ppermute | solution.py:452
  68.3 2.3 %collective-permute-start.10 = (bf16[4,12,64,128]{3,2,1,0:T(8,128)(2,1)S(1)}, bf16[4,12,64,128]{3,2,1,0:T(8,128)(2,1)S(1)}, u32[]{:S(2)}, u32[]{:S(2)}) collective-permute-start(bf16[4,12,64,128]{3,2,1,0:T(8,128)(2,1)S(1)} %collective-permute-done.4.a_down), channel_id=1, source_target_pairs={{0,32},{1,33},{2,34},{3,35},{4,36},{5,37},{6,38},{7,39},{8,40},{9,... | collective-permute-start | bytes 2359304 | tf_op jit(solution)/shard_map/ppermute | solution.py:452
  70.6 1.2 collective-permute-done.13.b_up
  71.8 9.2 %early_product.1.before = bf16[8,128,1536]{2,1,0:T(8,128)(2,1)S(1)} custom-call(s32[2]{0:T(128)S(1)} %copy-done.8, bf16[4,12,64,128]{3,2,1,0:T(8,128)(2,1)S(1)} %collective-permute-done.4.a_down, bf16[4,12,64,128]{3,2,1,0:T(8,128)(2,1)S(1)} %collective-permute-done.12.a_up, bf16[4,12,64,128]{3,2,1,0:T(8,128)(2,1)S(1)} %pad_maximum_fusion.1.b_own, ...), custom_call_target="tpu_custom_call" | custom-call | flops 6039797760 | bytes 7077888 | tf_op jit(solution)/shard_map/early_product/pallas_call | solution.py:209
  81.0 8.3 %collective-permute-done.10.a_far = bf16[4,12,64,128]{3,2,1,0:T(8,128)(2,1)S(1)} collective-permute-done((bf16[4,12,64,128]{3,2,1,0:T(8,128)(2,1)S(1)}, bf16[4,12,64,128]{3,2,1,0:T(8,128)(2,1)S(1)}, u32[]{:S(2)}, u32[]{:S(2)}) %collective-permute-start.10) | collective-permute-done | bytes 786464 | tf_op jit(solution)/shard_map/ppermute | solution.py:452
  89.3 4.0 %late_product.3 = (bf16[4,128,768]{2,1,0:T(8,128)(2,1)S(1)}, bf16[4,128,768]{2,1,0:T(8,128)(2,1)S(1)}) custom-call(s32[2]{0:T(128)S(1)} %copy-done.8, bf16[4,12,64,128]{3,2,1,0:T(8,128)(2,1)S(1)} %pad_maximum_fusion._.a_own, bf16[4,12,64,128]{3,2,1,0:T(8,128)(2,1)S(1)} %collective-permute-done.10.a_far, ...), custom_call_target="tpu_custom_call" | custom-call | flops 1811939328 | bytes 5505024 | tf_op jit(solution)/shard_map/late_product/pallas_call | solution.py:262
  93.3 2.6 %collective-permute-start.18 = (bf16[4,128,768]{2,1,0:T(8,128)(2,1)S(1)}, bf16[4,128,768]{2,1,0:T(8,128)(2,1)S(1)}, u32[]{:S(2)}, u32[]{:S(2)}) collective-permute-start(bf16[4,128,768]{2,1,0:T(8,128)(2,1)S(1)} %get-tuple-element.45), channel_id=1, source_target_pairs={{0,1},{1,0},{2,3},{3,2},{4,5},{5,4},{6,7},{7,6},{8,9},{9,8},{10,11... | collective-permute-start | bytes 2359304 | tf_op jit(solution)/shard_map/ppermute | solution.py:452
  95.9 4.0 %late_product.2 = (bf16[4,128,768]{2,1,0:T(8,128)(2,1)S(1)}, bf16[4,128,768]{2,1,0:T(8,128)(2,1)S(1)}) custom-call(s32[2]{0:T(128)S(1)} %copy-done.8, bf16[4,12,64,128]{3,2,1,0:T(8,128)(2,1)S(1)} %pad_maximum_fusion._.a_own, bf16[4,12,64,128]{3,2,1,0:T(8,128)(2,1)S(1)} %collective-permute-done.10.a_far, ...), custom_call_target="tpu_custom_call" | custom-call | flops 1811939328 | bytes 5505024 | tf_op jit(solution)/shard_map/late_product/pallas_call | solution.py:262
  99.9 0.1 collective-permute-start.14
  100.1 0.0 copy-start.6
  100.1 0.0 copy-start.7
  100.1 1.1 pair_sum.3
  101.2 0.1 collective-permute-start.19
  101.3 0.1 collective-permute-start.20
  101.4 2.6 %collective-permute-start.21 = (bf16[128,768]{1,0:T(8,128)(2,1)S(1)}, bf16[128,768]{1,0:T(8,128)(2,1)S(1)}, u32[]{:S(2)}, u32[]{:S(2)}) collective-permute-start(bf16[128,768]{1,0:T(8,128)(2,1)S(1)} %get-tuple-element.49), channel_id=1, source_target_pairs={{0,6},{1,7},{2,0},{3,1},{4,2},{5,3},{6,4},{7,5},{8,14},{9,15},{10,... | collective-permute-start | bytes 589832 | tf_op jit(solution)/shard_map/ppermute | solution.py:452
  103.9 1.1 pair_sum.2
  105.0 0.6 collective-permute-start.15
  105.6 1.9 %collective-permute-start.16 = (bf16[128,768]{1,0:T(8,128)(2,1)S(1)}, bf16[128,768]{1,0:T(8,128)(2,1)S(1)}, u32[]{:S(2)}, u32[]{:S(2)}) collective-permute-start(bf16[128,768]{1,0:T(8,128)(2,1)S(1)} %get-tuple-element.42), channel_id=1, source_target_pairs={{0,4},{1,5},{2,6},{3,7},{4,0},{5,1},{6,2},{7,3},{8,12},{9,13},{10,... | collective-permute-start | bytes 589832 | tf_op jit(solution)/shard_map/ppermute | solution.py:452
  107.5 5.6 %collective-permute-done.19.refs_5_ = bf16[128,768]{1,0:T(8,128)(2,1)S(1)} collective-permute-done((bf16[128,768]{1,0:T(8,128)(2,1)S(1)}, bf16[128,768]{1,0:T(8,128)(2,1)S(1)}, u32[]{:S(2)}, u32[]{:S(2)}) %collective-permute-start.19) | collective-permute-done | bytes 196640 | tf_op jit(solution)/shard_map/ppermute | solution.py:452
  113.1 8.4 %collective-permute-done.15.refs_1_ = bf16[128,768]{1,0:T(8,128)(2,1)S(1)} collective-permute-done((bf16[128,768]{1,0:T(8,128)(2,1)S(1)}, bf16[128,768]{1,0:T(8,128)(2,1)S(1)}, u32[]{:S(2)}, u32[]{:S(2)}) %collective-permute-start.15) | collective-permute-done | bytes 196640 | tf_op jit(solution)/shard_map/ppermute | solution.py:452
  121.6 0.0 copy-start.4
  121.6 1.9 %slots.1 = (bf16[128,1536]{1,0:T(8,128)(2,1)S(1)}, bf16[192,512]{1,0:T(8,128)(2,1)S(1)}) custom-call(s32[2]{0:T(128)S(1)} %copy-done.8, s32[16,12]{1,0:T(8,128)S(1)} %copy-done.6, s32[16]{0:T(128)S(1)} %copy-done.9, s32[16,12]{1,0:T(8,128)S(1)} %copy-done.7, s32[16]{0:T(128)S(1)} %copy-done.10, bf16[128,768]{1,0:T(8,128)(2,1)S(1)} %get-tuple-element.40.refs_0_, ...), custom_call_target="tpu_custom_call" | custom-call | flops 301989888 | bytes 5111808 | tf_op jit(solution)/shard_map/slots/pallas_call | solution.py:336
  123.5 0.1 collective-permute-start.22
  123.6 2.7 %collective-permute-start.23 = (bf16[192,512]{1,0:T(8,128)(2,1)S(1)}, bf16[192,512]{1,0:T(8,128)(2,1)S(1)}, u32[]{:S(2)}, u32[]{:S(2)}) collective-permute-start(bf16[192,512]{1,0:T(8,128)(2,1)S(1)} %get-tuple-element.50.one), channel_id=1, source_target_pairs={{0,24},{1,25},{2,26},{3,27},{4,28},{5,29},{6,30},{7,31},{8,0},{9,1... | collective-permute-start | bytes 589832 | tf_op jit(solution)/shard_map/ppermute | solution.py:452
  126.3 3.4 %collective-permute-done.22.two = bf16[192,512]{1,0:T(8,128)(2,1)S(1)} collective-permute-done((bf16[192,512]{1,0:T(8,128)(2,1)S(1)}, bf16[192,512]{1,0:T(8,128)(2,1)S(1)}, u32[]{:S(2)}, u32[]{:S(2)}) %collective-permute-start.22) | collective-permute-done | bytes 196640 | tf_op jit(solution)/shard_map/ppermute | solution.py:452
  129.7 1.1 collective-permute-done.23.three
  130.8 1.6 collective-permute-done.24.four
  132.4 0.1 fold.1.one
  132.5 0.1 collective-permute-start.25
  132.6 3.6 %collective-permute-start.28 = (bf16[128,1536]{1,0:T(8,128)(2,1)S(1)}, bf16[128,1536]{1,0:T(8,128)(2,1)S(1)}, u32[]{:S(2)}, u32[]{:S(2)}) collective-permute-start(bf16[128,1536]{1,0:T(8,128)(2,1)S(1)} %get-tuple-element.55.refs_0_), channel_id=1, source_target_pairs={{0,2},{1,3},{2,4},{3,5},{4,6},{5,7},{6,0},{7,1},{8,10},{9,11},{10,... | collective-permute-start | bytes 1179656 | tf_op jit(solution)/shard_map/ppermute | solution.py:452
  136.2 1.9 %collective-permute-start.30 = (bf16[128,1536]{1,0:T(8,128)(2,1)S(1)}, bf16[128,1536]{1,0:T(8,128)(2,1)S(1)}, u32[]{:S(2)}, u32[]{:S(2)}) collective-permute-start(bf16[128,1536]{1,0:T(8,128)(2,1)S(1)} %get-tuple-element.55.refs_0_), channel_id=1, source_target_pairs={{0,4},{1,5},{2,6},{3,7},{4,0},{5,1},{6,2},{7,3},{8,12},{9,13},{10,... | collective-permute-start | bytes 1179656 | tf_op jit(solution)/shard_map/ppermute | solution.py:452
  138.1 2.5 %collective-permute-start.26 = (bf16[192,512]{1,0:T(8,128)(2,1)S(1)}, bf16[192,512]{1,0:T(8,128)(2,1)S(1)}, u32[]{:S(2)}, u32[]{:S(2)}) collective-permute-start(bf16[192,512]{1,0:T(8,128)(2,1)S(1)} %fold.1.one), channel_id=1, source_target_pairs={{0,96},{1,97},{2,98},{3,99},{4,100},{5,101},{6,102},{7,103},{8,104... | collective-permute-start | bytes 589832 | tf_op jit(solution)/shard_map/ppermute | solution.py:452
  140.6 2.5 %collective-permute-start.27 = (bf16[192,512]{1,0:T(8,128)(2,1)S(1)}, bf16[192,512]{1,0:T(8,128)(2,1)S(1)}, u32[]{:S(2)}, u32[]{:S(2)}) collective-permute-start(bf16[192,512]{1,0:T(8,128)(2,1)S(1)} %fold.1.one), channel_id=1, source_target_pairs={{0,64},{1,65},{2,66},{3,67},{4,68},{5,69},{6,70},{7,71},{8,72},{9,... | collective-permute-start | bytes 589832 | tf_op jit(solution)/shard_map/ppermute | solution.py:452
  143.1 1.6 collective-permute-done.26.three
  144.6 2.0 %collective-permute-done.27.four = bf16[192,512]{1,0:T(8,128)(2,1)S(1)} collective-permute-done((bf16[192,512]{1,0:T(8,128)(2,1)S(1)}, bf16[192,512]{1,0:T(8,128)(2,1)S(1)}, u32[]{:S(2)}, u32[]{:S(2)}) %collective-permute-start.27) | collective-permute-done | bytes 196640 | tf_op jit(solution)/shard_map/ppermute | solution.py:452
  146.6 4.7 %collective-permute-start.31 = (bf16[128,1536]{1,0:T(8,128)(2,1)S(1)}, bf16[128,1536]{1,0:T(8,128)(2,1)S(1)}, u32[]{:S(2)}, u32[]{:S(2)}) collective-permute-start(bf16[128,1536]{1,0:T(8,128)(2,1)S(1)} %get-tuple-element.55.refs_0_), channel_id=1, source_target_pairs={{0,1},{1,0},{2,3},{3,2},{4,5},{5,4},{6,7},{7,6},{8,9},{9,8},{10,11... | collective-permute-start | bytes 1179656 | tf_op jit(solution)/shard_map/ppermute | solution.py:452
  151.3 0.1 collective-permute-start.32
  151.4 0.4 collective-permute-start.33
  151.8 1.1 top_part.1
  153.0 2.4 %collective-permute-start.34 = (bf16[128,1536]{1,0:T(8,128)(2,1)S(1)}, bf16[128,1536]{1,0:T(8,128)(2,1)}, u32[]{:S(2)}, u32[]{:S(2)}) collective-permute-start(bf16[128,1536]{1,0:T(8,128)(2,1)S(1)} %collective-permute-done.30.refs_3_), channel_id=1, source_target_pairs={{0,1},{1,0},{2,3},{3,2},{4,5},{5,4},{6,7},{7,6},{8,9},{9,8},{10,11... | collective-permute-start | bytes 1179656 | tf_op jit(solution)/shard_map/ppermute | solution.py:452
  155.4 4.9 %all-to-all-start = ((bf16[8,64,128]{2,1,0:T(8,128)(2,1)}), bf16[8,64,128]{2,1,0:T(8,128)(2,1)S(1)}, u32[]{:S(2)}, u32[]{:S(2)}) async-start(bf16[8,64,128]{2,1,0:T(8,128)(2,1)} %get-tuple-element.56), calls=%async_computation | async-start | bytes 262144 | tf_op jit(solution)/shard_map/all_to_all | solution.py:491
  160.3 5.7 %whole_columns.1 = (bf16[1536,512]{1,0:T(8,128)(2,1)}, bf16[1536,512]{1,0:T(8,128)(2,1)}) custom-call(s32[2]{0:T(128)S(1)} %copy-done.8, bf16[128,1536]{1,0:T(8,128)(2,1)S(1)} %get-tuple-element.55.refs_0_, bf16[128,1536]{1,0:T(8,128)(2,1)S(1)} %collective-permute-done.28.refs_1_, bf16[128,1536]{1,0:T(8,128)(2,1)S(1)} %collective-permute-done.29.refs_2_, ...), custom_call_target="tpu_custom_call" | custom-call | bytes 6291456 | tf_op jit(solution)/shard_map/whole_columns/pallas_call | solution.py:368
  166.0 0.9 last_part.1
  (45 shorter events, 0.1 us)
Async XLA Ops:
  5.7 23.4 %collective-permute-start = (bf16[12,64,128]{2,1,0:T(8,128)(2,1)}, bf16[12,64,128]{2,1,0:T(8,128)(2,1)S(1)}, u32[]{:S(2)}, u32[]{:S(2)}) collective-permute-start(bf16[12,64,128]{2,1,0:T(8,128)(2,1)} %get-tuple-element.34), channel_id=1, source_target_pairs={{0,0},{1,32},{2,8},{3,40},{4,16},{5,48},{6,24},{7,56},{8,9},{9,41}... | collective-permute-start | bytes 589832 | tf_op jit(solution)/shard_map/ppermute | solution.py:465
  10.7 22.7 %collective-permute-start.5 = (bf16[12,64,128]{2,1,0:T(8,128)(2,1)}, bf16[12,64,128]{2,1,0:T(8,128)(2,1)S(1)}, u32[]{:S(2)}, u32[]{:S(2)}) collective-permute-start(bf16[12,64,128]{2,1,0:T(8,128)(2,1)} %get-tuple-element.35), channel_id=1, source_target_pairs={{0,0},{1,32},{2,8},{3,40},{4,16},{5,48},{6,24},{7,56},{8,9},{9,41}... | collective-permute-start | bytes 589832 | tf_op jit(solution)/shard_map/ppermute | solution.py:466
  29.1 11.6 %collective-permute-start.1 = (bf16[12,64,128]{2,1,0:T(8,128)(2,1)S(1)}, bf16[12,64,128]{2,1,0:T(8,128)(2,1)S(1)}, u32[]{:S(2)}, u32[]{:S(2)}) collective-permute-start(bf16[12,64,128]{2,1,0:T(8,128)(2,1)S(1)} %collective-permute-done), channel_id=1, source_target_pairs={{0,8},{1,9},{2,10},{3,11},{4,12},{5,13},{6,14},{7,15},{8,16},{9,17... | collective-permute-start | bytes 589832 | tf_op jit(solution)/shard_map/ppermute | solution.py:452
  29.1 15.2 %collective-permute-start.2 = (bf16[12,64,128]{2,1,0:T(8,128)(2,1)S(1)}, bf16[12,64,128]{2,1,0:T(8,128)(2,1)S(1)}, u32[]{:S(2)}, u32[]{:S(2)}) collective-permute-start(bf16[12,64,128]{2,1,0:T(8,128)(2,1)S(1)} %collective-permute-done), channel_id=1, source_target_pairs={{0,24},{1,25},{2,26},{3,27},{4,28},{5,29},{6,30},{7,31},{8,0},{9,1... | collective-permute-start | bytes 589832 | tf_op jit(solution)/shard_map/ppermute | solution.py:452
  31.8 12.5 %collective-permute-start.3 = (bf16[12,64,128]{2,1,0:T(8,128)(2,1)S(1)}, bf16[12,64,128]{2,1,0:T(8,128)(2,1)S(1)}, u32[]{:S(2)}, u32[]{:S(2)}) collective-permute-start(bf16[12,64,128]{2,1,0:T(8,128)(2,1)S(1)} %collective-permute-done), channel_id=1, source_target_pairs={{0,16},{1,17},{2,18},{3,19},{4,20},{5,21},{6,22},{7,23},{8,24},{9,... | collective-permute-start | bytes 589832 | tf_op jit(solution)/shard_map/ppermute | solution.py:452
  33.4 12.9 %collective-permute-start.6 = (bf16[12,64,128]{2,1,0:T(8,128)(2,1)S(1)}, bf16[12,64,128]{2,1,0:T(8,128)(2,1)S(1)}, u32[]{:S(2)}, u32[]{:S(2)}) collective-permute-start(bf16[12,64,128]{2,1,0:T(8,128)(2,1)S(1)} %collective-permute-done.5), channel_id=1, source_target_pairs={{0,32},{1,33},{2,34},{3,35},{4,36},{5,37},{6,38},{7,39},{8,40},{9,... | collective-permute-start | bytes 589832 | tf_op jit(solution)/shard_map/ppermute | solution.py:452
  35.0 11.2 %collective-permute-start.7 = (bf16[12,64,128]{2,1,0:T(8,128)(2,1)S(1)}, bf16[12,64,128]{2,1,0:T(8,128)(2,1)S(1)}, u32[]{:S(2)}, u32[]{:S(2)}) collective-permute-start(bf16[12,64,128]{2,1,0:T(8,128)(2,1)S(1)} %collective-permute-done.5), channel_id=1, source_target_pairs={{0,96},{1,97},{2,98},{3,99},{4,100},{5,101},{6,102},{7,103},{8,104... | collective-permute-start | bytes 589832 | tf_op jit(solution)/shard_map/ppermute | solution.py:452
  40.8 7.4 %collective-permute-start.8 = (bf16[12,64,128]{2,1,0:T(8,128)(2,1)S(1)}, bf16[12,64,128]{2,1,0:T(8,128)(2,1)S(1)}, u32[]{:S(2)}, u32[]{:S(2)}) collective-permute-start(bf16[12,64,128]{2,1,0:T(8,128)(2,1)S(1)} %collective-permute-done.5), channel_id=1, source_target_pairs={{0,64},{1,65},{2,66},{3,67},{4,68},{5,69},{6,70},{7,71},{8,72},{9,... | collective-permute-start | bytes 589832 | tf_op jit(solution)/shard_map/ppermute | solution.py:452
  44.4 20.8 %collective-permute-start.4 = (bf16[4,12,64,128]{3,2,1,0:T(8,128)(2,1)S(1)}, bf16[4,12,64,128]{3,2,1,0:T(8,128)(2,1)S(1)}, u32[]{:S(2)}, u32[]{:S(2)}) collective-permute-start(bf16[4,12,64,128]{3,2,1,0:T(8,128)(2,1)S(1)} %pad_maximum_fusion._.a_own), channel_id=1, source_target_pairs={{0,32},{1,33},{2,34},{3,35},{4,36},{5,37},{6,38},{7,39},{8,40},{9,... | collective-permute-start | bytes 2359304 | tf_op jit(solution)/shard_map/ppermute | solution.py:452
  48.1 23.7 %copy-start.8 = (s32[2]{0:T(128)S(1)}, s32[2]{0:T(128)}, u32[]{:S(2)}) copy-start(s32[2]{0:T(128)} %pad_add_fusion.place) | copy-start | bytes 28
  48.3 20.1 %collective-permute-start.9 = (bf16[4,12,64,128]{3,2,1,0:T(8,128)(2,1)S(1)}, bf16[4,12,64,128]{3,2,1,0:T(8,128)(2,1)S(1)}, u32[]{:S(2)}, u32[]{:S(2)}) collective-permute-start(bf16[4,12,64,128]{3,2,1,0:T(8,128)(2,1)S(1)} %pad_maximum_fusion.1.b_own), channel_id=1, source_target_pairs={{0,8},{1,9},{2,10},{3,11},{4,12},{5,13},{6,14},{7,15},{8,16},{9,17... | collective-permute-start | bytes 2359304 | tf_op jit(solution)/shard_map/ppermute | solution.py:452
  48.3 22.3 %collective-permute-start.12 = (bf16[4,12,64,128]{3,2,1,0:T(8,128)(2,1)S(1)}, bf16[4,12,64,128]{3,2,1,0:T(8,128)(2,1)S(1)}, u32[]{:S(2)}, u32[]{:S(2)}) collective-permute-start(bf16[4,12,64,128]{3,2,1,0:T(8,128)(2,1)S(1)} %pad_maximum_fusion._.a_own), channel_id=1, source_target_pairs={{0,96},{1,97},{2,98},{3,99},{4,100},{5,101},{6,102},{7,103},{8,104... | collective-permute-start | bytes 2359304 | tf_op jit(solution)/shard_map/ppermute | solution.py:452
  53.7 18.1 %collective-permute-start.13 = (bf16[4,12,64,128]{3,2,1,0:T(8,128)(2,1)S(1)}, bf16[4,12,64,128]{3,2,1,0:T(8,128)(2,1)S(1)}, u32[]{:S(2)}, u32[]{:S(2)}) collective-permute-start(bf16[4,12,64,128]{3,2,1,0:T(8,128)(2,1)S(1)} %pad_maximum_fusion.1.b_own), channel_id=1, source_target_pairs={{0,24},{1,25},{2,26},{3,27},{4,28},{5,29},{6,30},{7,31},{8,0},{9,1... | collective-permute-start | bytes 2359304 | tf_op jit(solution)/shard_map/ppermute | solution.py:452
  56.3 3.7 %copy-start.1 = (bf16[1536,3072]{1,0:T(8,128)(2,1)S(1)}, bf16[1536,3072]{1,0:T(8,128)(2,1)}, u32[]{:S(2)}) copy-start(bf16[1536,3072]{1,0:T(8,128)(2,1)} %source.1) | copy-start | bytes 28311556
  68.3 21.0 %collective-permute-start.10 = (bf16[4,12,64,128]{3,2,1,0:T(8,128)(2,1)S(1)}, bf16[4,12,64,128]{3,2,1,0:T(8,128)(2,1)S(1)}, u32[]{:S(2)}, u32[]{:S(2)}) collective-permute-start(bf16[4,12,64,128]{3,2,1,0:T(8,128)(2,1)S(1)} %collective-permute-done.4.a_down), channel_id=1, source_target_pairs={{0,32},{1,33},{2,34},{3,35},{4,36},{5,37},{6,38},{7,39},{8,40},{9,... | collective-permute-start | bytes 2359304 | tf_op jit(solution)/shard_map/ppermute | solution.py:452
  70.6 18.7 %collective-permute-start.11 = (bf16[4,12,64,128]{3,2,1,0:T(8,128)(2,1)S(1)}, bf16[4,12,64,128]{3,2,1,0:T(8,128)(2,1)S(1)}, u32[]{:S(2)}, u32[]{:S(2)}) collective-permute-start(bf16[4,12,64,128]{3,2,1,0:T(8,128)(2,1)S(1)} %collective-permute-done.9.b_down), channel_id=1, source_target_pairs={{0,8},{1,9},{2,10},{3,11},{4,12},{5,13},{6,14},{7,15},{8,16},{9,17... | collective-permute-start | bytes 2359304 | tf_op jit(solution)/shard_map/ppermute | solution.py:452
  93.3 6.7 %collective-permute-start.18 = (bf16[4,128,768]{2,1,0:T(8,128)(2,1)S(1)}, bf16[4,128,768]{2,1,0:T(8,128)(2,1)S(1)}, u32[]{:S(2)}, u32[]{:S(2)}) collective-permute-start(bf16[4,128,768]{2,1,0:T(8,128)(2,1)S(1)} %get-tuple-element.45), channel_id=1, source_target_pairs={{0,1},{1,0},{2,3},{3,2},{4,5},{5,4},{6,7},{7,6},{8,9},{9,8},{10,11... | collective-permute-start | bytes 2359304 | tf_op jit(solution)/shard_map/ppermute | solution.py:452
  99.9 4.0 %collective-permute-start.14 = (bf16[4,128,768]{2,1,0:T(8,128)(2,1)S(1)}, bf16[4,128,768]{2,1,0:T(8,128)(2,1)S(1)}, u32[]{:S(2)}, u32[]{:S(2)}) collective-permute-start(bf16[4,128,768]{2,1,0:T(8,128)(2,1)S(1)} %get-tuple-element.39), channel_id=1, source_target_pairs={{0,1},{1,0},{2,3},{3,2},{4,5},{5,4},{6,7},{7,6},{8,9},{9,8},{10,11... | collective-permute-start | bytes 2359304 | tf_op jit(solution)/shard_map/ppermute | solution.py:452
  100.0 21.5 %copy-start = (bf16[1536,512]{1,0:T(8,128)(2,1)S(1)}, bf16[1536,512]{1,0:T(8,128)(2,1)}, u32[]{:S(2)}) copy-start(bf16[1536,512]{1,0:T(8,128)(2,1)} %refs_8_.1) | copy-start | bytes 4718596
  100.0 21.5 %copy-start.2 = (bf16[1536,512]{1,0:T(8,128)(2,1)S(1)}, bf16[1536,512]{1,0:T(8,128)(2,1)}, u32[]{:S(2)}) copy-start(bf16[1536,512]{1,0:T(8,128)(2,1)} %refs_9_.1) | copy-start | bytes 4718596
  100.1 21.5 %copy-start.6 = (s32[16,12]{1,0:T(8,128)S(1)}, s32[16,12]{1,0:T(8,128)}, u32[]{:S(2)}) copy-start(s32[16,12]{1,0:T(8,128)} %rows_a.3) | copy-start | bytes 2308
  100.1 21.5 %copy-start.7 = (s32[16,12]{1,0:T(8,128)S(1)}, s32[16,12]{1,0:T(8,128)}, u32[]{:S(2)}) copy-start(s32[16,12]{1,0:T(8,128)} %rows_b.3) | copy-start | bytes 2308
  100.1 21.5 %copy-start.9 = (s32[16]{0:T(128)S(1)}, s32[16]{0:T(128)}, u32[]{:S(2)}) copy-start(s32[16]{0:T(128)} %counts_a.3) | copy-start | bytes 196
  100.1 21.5 %copy-start.10 = (s32[16]{0:T(128)S(1)}, s32[16]{0:T(128)}, u32[]{:S(2)}) copy-start(s32[16]{0:T(128)} %counts_b.3) | copy-start | bytes 196
  101.2 11.9 %collective-permute-start.19 = (bf16[128,768]{1,0:T(8,128)(2,1)S(1)}, bf16[128,768]{1,0:T(8,128)(2,1)S(1)}, u32[]{:S(2)}, u32[]{:S(2)}) collective-permute-start(bf16[128,768]{1,0:T(8,128)(2,1)S(1)} %get-tuple-element.47), channel_id=1, source_target_pairs={{0,2},{1,3},{2,4},{3,5},{4,6},{5,7},{6,0},{7,1},{8,10},{9,11},{10,... | collective-permute-start | bytes 589832 | tf_op jit(solution)/shard_map/ppermute | solution.py:452
  101.3 11.9 %collective-permute-start.20 = (bf16[128,768]{1,0:T(8,128)(2,1)S(1)}, bf16[128,768]{1,0:T(8,128)(2,1)S(1)}, u32[]{:S(2)}, u32[]{:S(2)}) collective-permute-start(bf16[128,768]{1,0:T(8,128)(2,1)S(1)} %get-tuple-element.48), channel_id=1, source_target_pairs={{0,4},{1,5},{2,6},{3,7},{4,0},{5,1},{6,2},{7,3},{8,12},{9,13},{10,... | collective-permute-start | bytes 589832 | tf_op jit(solution)/shard_map/ppermute | solution.py:452
  101.4 11.8 %collective-permute-start.21 = (bf16[128,768]{1,0:T(8,128)(2,1)S(1)}, bf16[128,768]{1,0:T(8,128)(2,1)S(1)}, u32[]{:S(2)}, u32[]{:S(2)}) collective-permute-start(bf16[128,768]{1,0:T(8,128)(2,1)S(1)} %get-tuple-element.49), channel_id=1, source_target_pairs={{0,6},{1,7},{2,0},{3,1},{4,2},{5,3},{6,4},{7,5},{8,14},{9,15},{10,... | collective-permute-start | bytes 589832 | tf_op jit(solution)/shard_map/ppermute | solution.py:452
  105.0 16.5 %collective-permute-start.15 = (bf16[128,768]{1,0:T(8,128)(2,1)S(1)}, bf16[128,768]{1,0:T(8,128)(2,1)S(1)}, u32[]{:S(2)}, u32[]{:S(2)}) collective-permute-start(bf16[128,768]{1,0:T(8,128)(2,1)S(1)} %get-tuple-element.41), channel_id=1, source_target_pairs={{0,2},{1,3},{2,4},{3,5},{4,6},{5,7},{6,0},{7,1},{8,10},{9,11},{10,... | collective-permute-start | bytes 589832 | tf_op jit(solution)/shard_map/ppermute | solution.py:452
  105.6 15.9 %collective-permute-start.16 = (bf16[128,768]{1,0:T(8,128)(2,1)S(1)}, bf16[128,768]{1,0:T(8,128)(2,1)S(1)}, u32[]{:S(2)}, u32[]{:S(2)}) collective-permute-start(bf16[128,768]{1,0:T(8,128)(2,1)S(1)} %get-tuple-element.42), channel_id=1, source_target_pairs={{0,4},{1,5},{2,6},{3,7},{4,0},{5,1},{6,2},{7,3},{8,12},{9,13},{10,... | collective-permute-start | bytes 589832 | tf_op jit(solution)/shard_map/ppermute | solution.py:452
  113.1 8.4 %collective-permute-start.17 = (bf16[128,768]{1,0:T(8,128)(2,1)S(1)}, bf16[128,768]{1,0:T(8,128)(2,1)S(1)}, u32[]{:S(2)}, u32[]{:S(2)}) collective-permute-start(bf16[128,768]{1,0:T(8,128)(2,1)S(1)} %get-tuple-element.43), channel_id=1, source_target_pairs={{0,6},{1,7},{2,0},{3,1},{4,2},{5,3},{6,4},{7,5},{8,14},{9,15},{10,... | collective-permute-start | bytes 589832 | tf_op jit(solution)/shard_map/ppermute | solution.py:452
  121.6 30.2 %copy-start.3 = (bf16[512,512]{1,0:T(8,128)(2,1)S(1)}, bf16[512,512]{1,0:T(8,128)(2,1)}, u32[]{:S(2)}) copy-start(bf16[512,512]{1,0:T(8,128)(2,1)} %top.5) | copy-start | bytes 1572868
  121.6 30.2 %copy-start.4 = (f32[64,512]{1,0:T(8,128)S(1)}, f32[64,512]{1,0:T(8,128)}, u32[]{:S(2)}) copy-start(f32[64,512]{1,0:T(8,128)} %base.1) | copy-start | bytes 393220
  123.5 6.2 %collective-permute-start.22 = (bf16[192,512]{1,0:T(8,128)(2,1)S(1)}, bf16[192,512]{1,0:T(8,128)(2,1)S(1)}, u32[]{:S(2)}, u32[]{:S(2)}) collective-permute-start(bf16[192,512]{1,0:T(8,128)(2,1)S(1)} %get-tuple-element.50.one), channel_id=1, source_target_pairs={{0,8},{1,9},{2,10},{3,11},{4,12},{5,13},{6,14},{7,15},{8,16},{9,17... | collective-permute-start | bytes 589832 | tf_op jit(solution)/shard_map/ppermute | solution.py:452
  123.6 7.2 %collective-permute-start.23 = (bf16[192,512]{1,0:T(8,128)(2,1)S(1)}, bf16[192,512]{1,0:T(8,128)(2,1)S(1)}, u32[]{:S(2)}, u32[]{:S(2)}) collective-permute-start(bf16[192,512]{1,0:T(8,128)(2,1)S(1)} %get-tuple-element.50.one), channel_id=1, source_target_pairs={{0,24},{1,25},{2,26},{3,27},{4,28},{5,29},{6,30},{7,31},{8,0},{9,1... | collective-permute-start | bytes 589832 | tf_op jit(solution)/shard_map/ppermute | solution.py:452
  126.3 6.1 %collective-permute-start.24 = (bf16[192,512]{1,0:T(8,128)(2,1)S(1)}, bf16[192,512]{1,0:T(8,128)(2,1)S(1)}, u32[]{:S(2)}, u32[]{:S(2)}) collective-permute-start(bf16[192,512]{1,0:T(8,128)(2,1)S(1)} %get-tuple-element.50.one), channel_id=1, source_target_pairs={{0,16},{1,17},{2,18},{3,19},{4,20},{5,21},{6,22},{7,23},{8,24},{9,... | collective-permute-start | bytes 589832 | tf_op jit(solution)/shard_map/ppermute | solution.py:452
  132.5 8.1 %collective-permute-start.25 = (bf16[192,512]{1,0:T(8,128)(2,1)S(1)}, bf16[192,512]{1,0:T(8,128)(2,1)S(1)}, u32[]{:S(2)}, u32[]{:S(2)}) collective-permute-start(bf16[192,512]{1,0:T(8,128)(2,1)S(1)} %fold.1.one), channel_id=1, source_target_pairs={{0,32},{1,33},{2,34},{3,35},{4,36},{5,37},{6,38},{7,39},{8,40},{9,... | collective-permute-start | bytes 589832 | tf_op jit(solution)/shard_map/ppermute | solution.py:452
  132.6 14.0 %collective-permute-start.28 = (bf16[128,1536]{1,0:T(8,128)(2,1)S(1)}, bf16[128,1536]{1,0:T(8,128)(2,1)S(1)}, u32[]{:S(2)}, u32[]{:S(2)}) collective-permute-start(bf16[128,1536]{1,0:T(8,128)(2,1)S(1)} %get-tuple-element.55.refs_0_), channel_id=1, source_target_pairs={{0,2},{1,3},{2,4},{3,5},{4,6},{5,7},{6,0},{7,1},{8,10},{9,11},{10,... | collective-permute-start | bytes 1179656 | tf_op jit(solution)/shard_map/ppermute | solution.py:452
  136.2 10.4 %collective-permute-start.29 = (bf16[128,1536]{1,0:T(8,128)(2,1)S(1)}, bf16[128,1536]{1,0:T(8,128)(2,1)S(1)}, u32[]{:S(2)}, u32[]{:S(2)}) collective-permute-start(bf16[128,1536]{1,0:T(8,128)(2,1)S(1)} %get-tuple-element.55.refs_0_), channel_id=1, source_target_pairs={{0,6},{1,7},{2,0},{3,1},{4,2},{5,3},{6,4},{7,5},{8,14},{9,15},{10,... | collective-permute-start | bytes 1179656 | tf_op jit(solution)/shard_map/ppermute | solution.py:452
  136.2 16.8 %collective-permute-start.30 = (bf16[128,1536]{1,0:T(8,128)(2,1)S(1)}, bf16[128,1536]{1,0:T(8,128)(2,1)S(1)}, u32[]{:S(2)}, u32[]{:S(2)}) collective-permute-start(bf16[128,1536]{1,0:T(8,128)(2,1)S(1)} %get-tuple-element.55.refs_0_), channel_id=1, source_target_pairs={{0,4},{1,5},{2,6},{3,7},{4,0},{5,1},{6,2},{7,3},{8,12},{9,13},{10,... | collective-permute-start | bytes 1179656 | tf_op jit(solution)/shard_map/ppermute | solution.py:452
  138.1 6.5 %collective-permute-start.26 = (bf16[192,512]{1,0:T(8,128)(2,1)S(1)}, bf16[192,512]{1,0:T(8,128)(2,1)S(1)}, u32[]{:S(2)}, u32[]{:S(2)}) collective-permute-start(bf16[192,512]{1,0:T(8,128)(2,1)S(1)} %fold.1.one), channel_id=1, source_target_pairs={{0,96},{1,97},{2,98},{3,99},{4,100},{5,101},{6,102},{7,103},{8,104... | collective-permute-start | bytes 589832 | tf_op jit(solution)/shard_map/ppermute | solution.py:452
  140.6 6.0 %collective-permute-start.27 = (bf16[192,512]{1,0:T(8,128)(2,1)S(1)}, bf16[192,512]{1,0:T(8,128)(2,1)S(1)}, u32[]{:S(2)}, u32[]{:S(2)}) collective-permute-start(bf16[192,512]{1,0:T(8,128)(2,1)S(1)} %fold.1.one), channel_id=1, source_target_pairs={{0,64},{1,65},{2,66},{3,67},{4,68},{5,69},{6,70},{7,71},{8,72},{9,... | collective-permute-start | bytes 589832 | tf_op jit(solution)/shard_map/ppermute | solution.py:452
  146.6 13.6 %collective-permute-start.31 = (bf16[128,1536]{1,0:T(8,128)(2,1)S(1)}, bf16[128,1536]{1,0:T(8,128)(2,1)S(1)}, u32[]{:S(2)}, u32[]{:S(2)}) collective-permute-start(bf16[128,1536]{1,0:T(8,128)(2,1)S(1)} %get-tuple-element.55.refs_0_), channel_id=1, source_target_pairs={{0,1},{1,0},{2,3},{3,2},{4,5},{5,4},{6,7},{7,6},{8,9},{9,8},{10,11... | collective-permute-start | bytes 1179656 | tf_op jit(solution)/shard_map/ppermute | solution.py:452
  151.3 8.9 %collective-permute-start.32 = (bf16[128,1536]{1,0:T(8,128)(2,1)S(1)}, bf16[128,1536]{1,0:T(8,128)(2,1)}, u32[]{:S(2)}, u32[]{:S(2)}) collective-permute-start(bf16[128,1536]{1,0:T(8,128)(2,1)S(1)} %collective-permute-done.28.refs_1_), channel_id=1, source_target_pairs={{0,1},{1,0},{2,3},{3,2},{4,5},{5,4},{6,7},{7,6},{8,9},{9,8},{10,11... | collective-permute-start | bytes 1179656 | tf_op jit(solution)/shard_map/ppermute | solution.py:452
  151.4 8.8 %collective-permute-start.33 = (bf16[128,1536]{1,0:T(8,128)(2,1)S(1)}, bf16[128,1536]{1,0:T(8,128)(2,1)}, u32[]{:S(2)}, u32[]{:S(2)}) collective-permute-start(bf16[128,1536]{1,0:T(8,128)(2,1)S(1)} %collective-permute-done.29.refs_2_), channel_id=1, source_target_pairs={{0,1},{1,0},{2,3},{3,2},{4,5},{5,4},{6,7},{7,6},{8,9},{9,8},{10,11... | collective-permute-start | bytes 1179656 | tf_op jit(solution)/shard_map/ppermute | solution.py:452
  153.0 7.3 %collective-permute-start.34 = (bf16[128,1536]{1,0:T(8,128)(2,1)S(1)}, bf16[128,1536]{1,0:T(8,128)(2,1)}, u32[]{:S(2)}, u32[]{:S(2)}) collective-permute-start(bf16[128,1536]{1,0:T(8,128)(2,1)S(1)} %collective-permute-done.30.refs_3_), channel_id=1, source_target_pairs={{0,1},{1,0},{2,3},{3,2},{4,5},{5,4},{6,7},{7,6},{8,9},{9,8},{10,11... | collective-permute-start | bytes 1179656 | tf_op jit(solution)/shard_map/ppermute | solution.py:452
  155.4 10.6 %all-to-all-start = ((bf16[8,64,128]{2,1,0:T(8,128)(2,1)}), bf16[8,64,128]{2,1,0:T(8,128)(2,1)S(1)}, u32[]{:S(2)}, u32[]{:S(2)}) async-start(bf16[8,64,128]{2,1,0:T(8,128)(2,1)} %get-tuple-element.56), calls=%async_computation | async-start | bytes 262144 | tf_op jit(solution)/shard_map/all_to_all | solution.py:491
  160.2 5.7 %copy-start.5 = (f32[64,512]{1,0:T(8,128)S(1)}, f32[64,512]{1,0:T(8,128)}, u32[]{:S(2)}) copy-start(f32[64,512]{1,0:T(8,128)} %base.2) | copy-start | bytes 393220

commit v6 on v5

--- a/solution.py
+++ b/solution.py
@@ -75,51 +75,70 @@
     return slot, live
 
 
-def prep_body(place, rows_a, counts_a, rows_b, counts_b, fa, part_a, part_b, top, out_a, out_b, fix):
+def half_of(value, upper):
+    return jnp.where(upper > 0, value[PART:], value[:PART])
+
+
+def prep_a_body(place, rows_a, counts_a, part_a, out_a):
+    for block in range(NB):
+        slot, live = find_slot(rows_a, counts_a, place[0], block)
+        at = pl.ds(pl.multiple_of(slot * BS, BS), BS)
+        piece = half_of(part_a[at, :].T, place[1] % 2)
+        out_a[block] = jnp.where(live > 0, piece, jnp.zeros_like(piece))
+
+
+def width_slice(rows):
+    return pl.BlockSpec((rows, BS), lambda i, place, *_: (0, place[1] // 2))
+
+
+def prep_a(place, lists, factor_a):
+    return pl.pallas_call(
+        prep_a_body,
+        name="prep_a",
+        grid_spec=pltpu.PrefetchScalarGridSpec(
+            num_scalar_prefetch=3,
+            grid=(1,),
+            in_specs=[width_slice(ROWS)],
+            out_specs=whole((NB, PART, BS)),
+        ),
+        out_shape=jax.ShapeDtypeStruct((NB, PART, BS), BF),
+        compiler_params=params(56),
+        cost_estimate=cost(0, 4 * ROWS * BS),
+    )(place, *lists[:2], factor_a)
+
+
+def prep_b_body(place, rows_a, counts_a, rows_b, counts_b, fa, part_b, top, out_b, fix):
     owner = place[0]
     upper = place[1] % 2
     fix[...] = lax.dot_general(
         top[...], fa[...], (((0,), (1,)), ((), ())), preferred_element_type=F32
     )
-
-    def half(value):
-        return jnp.where(upper > 0, value[PART:], value[:PART])
-
     for block in range(NB):
         slot_a, live_a = find_slot(rows_a, counts_a, owner, block)
         slot_b, live_b = find_slot(rows_b, counts_b, owner, block)
         at_a = pl.ds(pl.multiple_of(slot_a * BS, BS), BS)
         at_b = pl.ds(pl.multiple_of(slot_b * BS, BS), BS)
-        piece = half(part_a[at_a, :].T)
-        out_a[block] = jnp.where(live_a > 0, piece, jnp.zeros_like(piece))
-        moved = half(fix[:, at_a])
-        piece = half(part_b[at_b, :].T).astype(F32)
+        moved = half_of(fix[:, at_a], upper)
+        piece = half_of(part_b[at_b, :].T, upper).astype(F32)
         piece = jnp.where(live_b > 0, piece, jnp.zeros_like(piece))
         out_b[block] = (piece - jnp.where(live_a > 0, moved, jnp.zeros_like(moved))).astype(BF)
 
 
-def prep(place, lists, factor_a, factor_b, factor_top):
-    slice_spec = pl.BlockSpec((ROWS, BS), lambda i, place, *_: (0, place[1] // 2))
-    out = jax.ShapeDtypeStruct((NB, PART, BS), BF)
-    return pl.pallas_call(
-        prep_body,
-        name="prep",
+def prep_b(place, lists, factor_a, factor_b, factor_top):
+    return pl.pallas_call(
+        prep_b_body,
+        name="prep_b",
         grid_spec=pltpu.PrefetchScalarGridSpec(
             num_scalar_prefetch=5,
             grid=(1,),
-            in_specs=[
-                whole((ROWS, W)),
-                slice_spec,
-                slice_spec,
-                pl.BlockSpec((W, BS), lambda i, place, *_: (0, place[1] // 2)),
-            ],
-            out_specs=[whole((NB, PART, BS))] * 2,
+            in_specs=[whole((ROWS, W)), width_slice(ROWS), width_slice(W)],
+            out_specs=whole((NB, PART, BS)),
             scratch_shapes=[pltpu.VMEM((BS, ROWS), F32)],
         ),
-        out_shape=[out, out],
+        out_shape=jax.ShapeDtypeStruct((NB, PART, BS), BF),
         compiler_params=params(56),
         cost_estimate=cost(2 * BS * ROWS * W, 2 * ROWS * (W + 4 * BS)),
-    )(place, *lists, factor_a, factor_a, factor_b, factor_top)
+    )(place, *lists, factor_a, factor_b, factor_top)
 
 
 def where(place):
@@ -133,16 +152,16 @@
     return (value + by + SIDE) % SIDE
 
 
-def load_a(copies, buf, u, spread):
-    for i in range(SIDE):
-        copies.append((buf.at[i], spread.at[:, u // 2, i * PART : (i + 1) * PART, :]))
-
-
-def load_b(copies, buf, u, first, spread):
-    for i in range(SIDE):
+def load_a(copies, buf, u, spread, start=0, many=SIDE):
+    for i in range(start, start + many):
+        copies.append((buf.at[i - start], spread.at[:, u // 2, i * PART : (i + 1) * PART, :]))
+
+
+def load_b(copies, buf, u, first, spread, start=0, many=SIDE):
+    for i in range(start, start + many):
         ui = turn(u, -STEPS[i])
         at = pl.ds(pl.multiple_of(first + (ui % 2) * PART, PART), PART)
-        copies.append((buf.at[i], spread.at[:, ui // 2, at, :]))
+        copies.append((buf.at[i - start], spread.at[:, ui // 2, at, :]))
 
 
 def run_copies(copies, sems):
@@ -227,7 +246,7 @@
 
 
 def late_body(
-    half, place, a_own, a_far, b_far, tile, before, keep, give, spread, ready, sems
+    half, place, a_own, a_far, a_far_more, b_far, b_far_more, tile, before, keep, give, spread, ready, sems
 ):
     u, v = where(place)
     core = place[1] % 2
@@ -236,8 +255,10 @@
     def _():
         copies = []
         load_a(copies, a_own, u, spread)
-        load_a(copies, a_far, turn(u, 2), spread)
-        load_b(copies, b_far, u, W // 2, spread)
+        load_a(copies, a_far, turn(u, 2), spread, 0, 2)
+        load_a(copies, a_far_more, turn(u, 2), spread, 2, 2)
+        load_b(copies, b_far, u, W // 2, spread, 0, 2)
+        load_b(copies, b_far_more, u, W // 2, spread, 2, 2)
         run_copies(copies, sems)
 
     ready[...] = before[...]
@@ -265,7 +286,7 @@
         grid_spec=pltpu.PrefetchScalarGridSpec(
             num_scalar_prefetch=1,
             grid=(HALF_STEPS,),
-            in_specs=[pl.BlockSpec(memory_space=pl.ANY)] * 3
+            in_specs=[pl.BlockSpec(memory_space=pl.ANY)] * 5
             + [
                 pl.BlockSpec(memory_space=pltpu.VMEM),
                 pl.BlockSpec((COLS, PAIR, STRIP), lambda i, *_: (0, 0, half * HALF_STEPS + i)),
@@ -283,40 +304,51 @@
     )(place, *bufs, trailing, before)
 
 
-def pair_body(place, mine, taken, *outs):
+def pair_body(joined, place, mine, taken, *refs):
+    before, outs = refs[: joined], refs[joined:]
     x = place[1] // 2
     for i in range(SIDE):
         at = (x + i) % SIDE
-        outs[i][...] = (mine[at].astype(F32) + taken[at].astype(F32)).astype(BF)
-
-
-def pair_sum(place, mine, taken):
+        total = (mine[at].astype(F32) + taken[at].astype(F32)).astype(BF)
+        if joined and i == 2:
+            outs[i][0] = before[0][...]
+            outs[i][1] = total
+        else:
+            outs[i][...] = total
+
+
+def pair_sum(place, mine, taken, *before):
     lanes = 3 * BS
     width = mine.shape[2]
     spec = pl.BlockSpec((SIDE, PAIR, lanes), lambda i, *_: (0, 0, i))
-    return pl.pallas_call(
-        pair_body,
+    one = pl.BlockSpec((PAIR, lanes), lambda i, *_: (0, i))
+    two = pl.BlockSpec((2, PAIR, lanes), lambda i, *_: (0, 0, i))
+    shape = jax.ShapeDtypeStruct((PAIR, width), BF)
+    double = jax.ShapeDtypeStruct((2, PAIR, width), BF)
+    joined = len(before)
+    return pl.pallas_call(
+        functools.partial(pair_body, joined),
         name="pair_sum",
         grid_spec=pltpu.PrefetchScalarGridSpec(
             num_scalar_prefetch=1,
             grid=(width // lanes,),
-            in_specs=[spec, spec],
-            out_specs=[pl.BlockSpec((PAIR, lanes), lambda i, *_: (0, i))] * SIDE,
-        ),
-        out_shape=[jax.ShapeDtypeStruct((PAIR, width), BF)] * SIDE,
+            in_specs=[spec, spec] + [one] * joined,
+            out_specs=[one, one, two if joined else one, one],
+        ),
+        out_shape=[shape, shape, double if joined else shape, shape],
         compiler_params=params(dimension_semantics=("arbitrary",)),
         cost_estimate=cost(W * width, 6 * W * width),
-    )(place, mine, taken)
+    )(place, mine, taken, *before)
 
 
 def slots_body(
     place, rows_a, counts_a, rows_b, counts_b, *refs
 ):
-    slabs, (fa, fb, columns, pieces, natural, left) = refs[:8], refs[8:]
+    slabs, far, (fa, fb, columns, pieces, natural, left) = refs[:6], refs[6], refs[7:]
     owner = place[0]
     width = ROWS // 2
     for half in range(2):
-        total = total_of(slabs[half * SIDE : (half + 1) * SIDE], slice(None))
+        total = total_of((*slabs[half * 3 : half * 3 + 3], far.at[half]), slice(None))
         natural[:, half * width : (half + 1) * width] = (-total).astype(BF)
     for k in range(NB):
         at = slice(k * BS, (k + 1) * BS)
@@ -339,7 +371,9 @@
         grid_spec=pltpu.PrefetchScalarGridSpec(
             num_scalar_prefetch=5,
             grid=(1,),
-            in_specs=[whole((PAIR, ROWS // 2))] * 8 + [whole((ROWS, W))] * 2,
+            in_specs=[whole((PAIR, ROWS // 2))] * 6
+            + [whole((2, PAIR, ROWS // 2))]
+            + [whole((ROWS, W))] * 2,
             out_specs=[whole((PAIR, ROWS)), whole((3 * PART, W))],
             scratch_shapes=[pltpu.VMEM((PAIR, ROWS), BF)] * 2,
         ),
@@ -461,8 +495,8 @@
 ):
     place = jnp.stack([lax.axis_index("row"), lax.axis_index("col")]).astype(jnp.int32)
     lists = (rows_a, counts_a, rows_b, counts_b)
-    part_a, part_b = prep(place, lists, factor_a, factor_b, factor_top)
-    part_a = lax.ppermute(part_a, BOTH, spread_pairs())
+    part_a = lax.ppermute(prep_a(place, lists, factor_a), BOTH, spread_pairs())
+    part_b = prep_b(place, lists, factor_a, factor_b, factor_top)
     part_b = lax.ppermute(part_b, BOTH, spread_pairs())
     a_own = jnp.stack(around(part_a, "dy"))
     b_own = jnp.stack(around(part_b, "dz"))
@@ -470,18 +504,21 @@
     b_down, b_up = send(b_own, dy=1), send(b_own, dy=-1)
     trailing = hold(trailing, a_own)
     a_next, b_next, _ = lax.optimization_barrier((a_down, b_down, trailing))
-    a_far, b_far = send(a_next, dz=1), send(b_next, dy=1)
+    a_far, b_far = send(a_next[:2], dz=1), send(b_next[:2], dy=1)
+    a_far_more, b_far_more = send(a_up[2:], dz=-1), send(b_up[2:], dy=-1)
     before = early_product(place, (a_down, a_up, b_own, b_down, b_up), trailing)
-    slabs = []
+    slabs, far = [], ()
     for half in range(2):
         keep, give = late_product(
-            half, place, (a_own, a_far, b_far), trailing, before
+            half, place, (a_own, a_far, a_far_more, b_far, b_far_more), trailing, before
         )
-        own, one, two, three = pair_sum(place, keep, send(give, dc=1))
-        slabs += [own, send(one, dx=1), send(two, dx=2), send(three, dx=-1)]
+        own, one, *far, three = pair_sum(place, keep, send(give, dc=1), *far)
+        slabs += [own, send(one, dx=1), send(three, dx=-1)]
+    slabs.append(send(far[0], dx=2))
     columns, pieces = slots(place, lists, slabs, (factor_a, factor_b))
     near, other = send(columns, dx=1), send(columns, dx=-1)
-    folded = fold(around(pieces, "dy"))
+    first, near, other = lax.optimization_barrier((around(pieces, "dy"), near, other))
+    folded = fold(first)
     got = around(folded, "dz")
     far = send(lax.optimization_barrier((columns, folded))[0], dx=2)
     _, (own, near, other) = lax.optimization_barrier((got, (columns, near, other)))

time: 168 us -> 159 us (0.946)
  starting transfers between devices: 66 us -> 59.1 us
  waiting for transfers between devices: 61.2 us -> 56.2 us
  Pallas kernels: 34.2 us -> 36.9 us
    ppermute x1, waiting for transfers between devices: 13.5 us -> 2.72 us  [on_device(): part_a = lax.ppermute(prep_a(place, lists, factor_a), BOTH, spread_pairs())]
    ppermute x33 -> x34, starting transfers between devices: 51.3 us -> 45.4 us  [send(): return lax.ppermute(value, BOTH, shifted(**by))]
    ppermute x1, waiting for transfers between devices: 1.53 us -> 5.6 us  [on_device(): part_b = lax.ppermute(part_b, BOTH, spread_pairs())]
    pallas_call x3 -> x4, Pallas kernels: 6.64 us -> 9.36 us  [the longest x1 4.3 us: prep_b(): pl.pallas_call(prep_b_body, name='prep_b', grid_spec=pltpu.PrefetchScalar...]
    ppermute x33 -> x34, waiting for transfers between devices: 46.1 us -> 47.9 us  [send(): return lax.ppermute(value, BOTH, shifted(**by))]
  transfers between devices with their start and end apart: 36 -> 37, of which waited for: 15 -> 16; matrix products, arithmetic and copies ran while one was open for 0% -> 0% of each run, Pallas kernels for 14% -> 16%
where the time goes in v6:
time: 159 us; the launch traced here: 158 us
  starting transfers between devices  59.1 us (37%)
  waiting for transfers between devices  56.2 us (35%)
  Pallas kernels  36.9 us (23%)
  local copies, waits for them, and re-layouts  3.85 us (2%)
    ppermute x34, waiting for transfers between devices, send(): return lax.ppermute(value, BOTH, shifted(**by))  47.9 us
    ppermute x34, starting transfers between devices, send(): return lax.ppermute(value, BOTH, shifted(**by))  45.4 us
    pallas_call x1, Pallas kernels, early_product(): pl.pallas_call(early_body, name='early_product', grid_spec=pltpu.Prefetch...  9.19 us
    pallas_call x2, Pallas kernels, late_product(): pl.pallas_call(functools.partial(late_body, half), name='late_product', g...  8.03 us
    pallas_call x1, Pallas kernels, whole_columns(): pl.pallas_call(column_body, name='whole_columns', grid_spec=pltpu.Prefetc...  5.69 us
    ppermute x1, waiting for transfers between devices, on_device(): part_b = lax.ppermute(part_b, BOTH, spread_pairs())  5.6 us
    ppermute x1, starting transfers between devices, on_device(): part_b = lax.ppermute(part_b, BOTH, spread_pairs())  4.93 us
    ppermute x1, starting transfers between devices, on_device(): part_a = lax.ppermute(prep_a(place, lists, factor_a), BOTH, spread_pairs())  4.92 us
  transfers between devices with their start and end apart: 37, of which 16 were waited for; matrix products, arithmetic and copies ran while one was open for 0% of the time, Pallas kernels for 16%

profile of v6, /device:TPU:1, one launch (start us, length us, event | category | flops | bytes accessed | tf_op | source)
XLA Modules:
  0.0 157.8 jit_solution(5656355266821523715)
XLA Ops:
  0.6 0.6 pad_add_fusion.place
  1.2 2.9 %prep_a.1 = bf16[12,64,128]{2,1,0:T(8,128)(2,1)} custom-call(s32[2]{0:T(128)} %pad_add_fusion.place, s32[16,12]{1,0:T(8,128)} %rows_a.5, s32[16]{0:T(128)} %counts_a.5, bf16[1536,512]{1,0:T(8,128)(2,1)} %refs_7_.1), custom_call_target="tpu_custom_call" | custom-call | bytes 786432 | tf_op jit(solution)/shard_map/prep_a/pallas_call | solution.py:95
  4.1 4.9 %collective-permute-start = (bf16[12,64,128]{2,1,0:T(8,128)(2,1)}, bf16[12,64,128]{2,1,0:T(8,128)(2,1)S(1)}, u32[]{:S(2)}, u32[]{:S(2)}) collective-permute-start(bf16[12,64,128]{2,1,0:T(8,128)(2,1)} %prep_a.1), channel_id=1, source_target_pairs={{0,0},{1,32},{2,8},{3,40},{4,16},{5,48},{6,24},{7,56},{8,9},{9,41}... | collective-permute-start | bytes 589832 | tf_op jit(solution)/shard_map/ppermute | solution.py:498
  9.0 4.3 %prep_b.1 = bf16[12,64,128]{2,1,0:T(8,128)(2,1)} custom-call(s32[2]{0:T(128)} %pad_add_fusion.place, s32[16,12]{1,0:T(8,128)} %rows_a.5, s32[16]{0:T(128)} %counts_a.5, s32[16,12]{1,0:T(8,128)} %rows_b.3, s32[16]{0:T(128)} %counts_b.3, bf16[1536,512]{1,0:T(8,128)(2,1)} %refs_7_.1, bf16[1536,512]{1,0:T(8,128)(2,1)} %refs_8_.1, bf16[512,512]{1,0:T(8,128)(2,1)} %top.5), custom_call_target="tpu_custom_call" | custom-call | flops 201326592 | bytes 3145728 | tf_op jit(solution)/shard_map/prep_b/pallas_call | solution.py:128
  13.3 4.9 %collective-permute-start.5 = (bf16[12,64,128]{2,1,0:T(8,128)(2,1)}, bf16[12,64,128]{2,1,0:T(8,128)(2,1)S(1)}, u32[]{:S(2)}, u32[]{:S(2)}) collective-permute-start(bf16[12,64,128]{2,1,0:T(8,128)(2,1)} %prep_b.1), channel_id=1, source_target_pairs={{0,0},{1,32},{2,8},{3,40},{4,16},{5,48},{6,24},{7,56},{8,9},{9,41}... | collective-permute-start | bytes 589832 | tf_op jit(solution)/shard_map/ppermute | solution.py:500
  18.3 2.7 %collective-permute-done = bf16[12,64,128]{2,1,0:T(8,128)(2,1)S(1)} collective-permute-done((bf16[12,64,128]{2,1,0:T(8,128)(2,1)}, bf16[12,64,128]{2,1,0:T(8,128)(2,1)S(1)}, u32[]{:S(2)}, u32[]{:S(2)}) %collective-permute-start) | collective-permute-done | bytes 196640 | tf_op jit(solution)/shard_map/ppermute | solution.py:498
  21.0 2.7 %collective-permute-start.2 = (bf16[12,64,128]{2,1,0:T(8,128)(2,1)S(1)}, bf16[12,64,128]{2,1,0:T(8,128)(2,1)S(1)}, u32[]{:S(2)}, u32[]{:S(2)}) collective-permute-start(bf16[12,64,128]{2,1,0:T(8,128)(2,1)S(1)} %collective-permute-done), channel_id=1, source_target_pairs={{0,24},{1,25},{2,26},{3,27},{4,28},{5,29},{6,30},{7,31},{8,0},{9,1... | collective-permute-start | bytes 589832 | tf_op jit(solution)/shard_map/ppermute | solution.py:486
  23.7 5.6 %collective-permute-done.5 = bf16[12,64,128]{2,1,0:T(8,128)(2,1)S(1)} collective-permute-done((bf16[12,64,128]{2,1,0:T(8,128)(2,1)}, bf16[12,64,128]{2,1,0:T(8,128)(2,1)S(1)}, u32[]{:S(2)}, u32[]{:S(2)}) %collective-permute-start.5) | collective-permute-done | bytes 196640 | tf_op jit(solution)/shard_map/ppermute | solution.py:500
  29.3 2.9 %collective-permute-start.6 = (bf16[12,64,128]{2,1,0:T(8,128)(2,1)S(1)}, bf16[12,64,128]{2,1,0:T(8,128)(2,1)S(1)}, u32[]{:S(2)}, u32[]{:S(2)}) collective-permute-start(bf16[12,64,128]{2,1,0:T(8,128)(2,1)S(1)} %collective-permute-done.5), channel_id=1, source_target_pairs={{0,32},{1,33},{2,34},{3,35},{4,36},{5,37},{6,38},{7,39},{8,40},{9,... | collective-permute-start | bytes 589832 | tf_op jit(solution)/shard_map/ppermute | solution.py:486
  32.2 2.1 %collective-permute-start.7 = (bf16[12,64,128]{2,1,0:T(8,128)(2,1)S(1)}, bf16[12,64,128]{2,1,0:T(8,128)(2,1)S(1)}, u32[]{:S(2)}, u32[]{:S(2)}) collective-permute-start(bf16[12,64,128]{2,1,0:T(8,128)(2,1)S(1)} %collective-permute-done.5), channel_id=1, source_target_pairs={{0,96},{1,97},{2,98},{3,99},{4,100},{5,101},{6,102},{7,103},{8,104... | collective-permute-start | bytes 589832 | tf_op jit(solution)/shard_map/ppermute | solution.py:486
  34.4 1.3 collective-permute-start.8
  35.6 3.9 %collective-permute-done.2 = bf16[12,64,128]{2,1,0:T(8,128)(2,1)S(1)} collective-permute-done((bf16[12,64,128]{2,1,0:T(8,128)(2,1)S(1)}, bf16[12,64,128]{2,1,0:T(8,128)(2,1)S(1)}, u32[]{:S(2)}, u32[]{:S(2)}) %collective-permute-start.2) | collective-permute-done | bytes 196640 | tf_op jit(solution)/shard_map/ppermute | solution.py:486
  39.5 0.1 pad_maximum_fusion._.a_own
  39.6 0.1 collective-permute-start.4
  39.7 4.2 %collective-permute-done.8 = bf16[12,64,128]{2,1,0:T(8,128)(2,1)S(1)} collective-permute-done((bf16[12,64,128]{2,1,0:T(8,128)(2,1)S(1)}, bf16[12,64,128]{2,1,0:T(8,128)(2,1)S(1)}, u32[]{:S(2)}, u32[]{:S(2)}) %collective-permute-start.8) | collective-permute-done | bytes 196640 | tf_op jit(solution)/shard_map/ppermute | solution.py:486
  43.9 0.1 pad_maximum_fusion.1.b_own
  44.0 1.9 %collective-permute-start.9 = (bf16[4,12,64,128]{3,2,1,0:T(8,128)(2,1)S(1)}, bf16[4,12,64,128]{3,2,1,0:T(8,128)(2,1)S(1)}, u32[]{:S(2)}, u32[]{:S(2)}) collective-permute-start(bf16[4,12,64,128]{3,2,1,0:T(8,128)(2,1)S(1)} %pad_maximum_fusion.1.b_own), channel_id=1, source_target_pairs={{0,8},{1,9},{2,10},{3,11},{4,12},{5,13},{6,14},{7,15},{8,16},{9,17... | collective-permute-start | bytes 2359304 | tf_op jit(solution)/shard_map/ppermute | solution.py:486
  46.0 1.3 collective-permute-start.14
  47.2 3.7 %copy-done.1 = bf16[1536,3072]{1,0:T(8,128)(2,1)S(1)} copy-done((bf16[1536,3072]{1,0:T(8,128)(2,1)S(1)}, bf16[1536,3072]{1,0:T(8,128)(2,1)}, u32[]{:S(2)}) %copy-start.1) | copy-done | bytes 9437208
  50.9 0.6 hold.1.tile
  51.6 10.2 %collective-permute-done.4.a_down = bf16[4,12,64,128]{3,2,1,0:T(8,128)(2,1)S(1)} collective-permute-done((bf16[4,12,64,128]{3,2,1,0:T(8,128)(2,1)S(1)}, bf16[4,12,64,128]{3,2,1,0:T(8,128)(2,1)S(1)}, u32[]{:S(2)}, u32[]{:S(2)}) %collective-permute-start.4) | collective-permute-done | bytes 786464 | tf_op jit(solution)/shard_map/ppermute | solution.py:486
  61.8 1.2 collective-permute-start.10
  63.0 1.1 collective-permute-start.13
  64.2 2.1 %collective-permute-start.12 = (bf16[2,12,64,128]{3,2,1,0:T(8,128)(2,1)S(1)}, bf16[2,12,64,128]{3,2,1,0:T(8,128)(2,1)S(1)}, u32[]{:S(2)}, u32[]{:S(2)}) collective-permute-start(bf16[2,12,64,128]{3,2,1,0:T(8,128)(2,1)S(1)} %slice.16), channel_id=1, source_target_pairs={{0,96},{1,97},{2,98},{3,99},{4,100},{5,101},{6,102},{7,103},{8,104... | collective-permute-start | bytes 1179656 | tf_op jit(solution)/shard_map/ppermute | solution.py:486
  66.3 1.7 %collective-permute-start.15 = (bf16[2,12,64,128]{3,2,1,0:T(8,128)(2,1)S(1)}, bf16[2,12,64,128]{3,2,1,0:T(8,128)(2,1)S(1)}, u32[]{:S(2)}, u32[]{:S(2)}) collective-permute-start(bf16[2,12,64,128]{3,2,1,0:T(8,128)(2,1)S(1)} %slice.17), channel_id=1, source_target_pairs={{0,24},{1,25},{2,26},{3,27},{4,28},{5,29},{6,30},{7,31},{8,0},{9,1... | collective-permute-start | bytes 1179656 | tf_op jit(solution)/shard_map/ppermute | solution.py:486
  68.0 9.2 %early_product.1.before = bf16[8,128,1536]{2,1,0:T(8,128)(2,1)S(1)} custom-call(s32[2]{0:T(128)S(1)} %copy-done.8, bf16[4,12,64,128]{3,2,1,0:T(8,128)(2,1)S(1)} %collective-permute-done.4.a_down, bf16[4,12,64,128]{3,2,1,0:T(8,128)(2,1)S(1)} %collective-permute-done.11.a_up, bf16[4,12,64,128]{3,2,1,0:T(8,128)(2,1)S(1)} %pad_maximum_fusion.1.b_own, ...), custom_call_target="tpu_custom_call" | custom-call | flops 6039797760 | bytes 7077888 | tf_op jit(solution)/shard_map/early_product/pallas_call | solution.py:228
  77.3 4.0 %late_product.2 = (bf16[4,128,768]{2,1,0:T(8,128)(2,1)S(1)}, bf16[4,128,768]{2,1,0:T(8,128)(2,1)S(1)}) custom-call(s32[2]{0:T(128)S(1)} %copy-done.8, bf16[4,12,64,128]{3,2,1,0:T(8,128)(2,1)S(1)} %pad_maximum_fusion._.a_own, bf16[2,12,64,128]{3,2,1,0:T(8,128)(2,1)S(1)} %collective-permute-done.10.a_far, ...), custom_call_target="tpu_custom_call" | custom-call | flops 1811939328 | bytes 5505024 | tf_op jit(solution)/shard_map/late_product/pallas_call | solution.py:283
  81.3 4.2 %collective-permute-start.16 = (bf16[4,128,768]{2,1,0:T(8,128)(2,1)S(1)}, bf16[4,128,768]{2,1,0:T(8,128)(2,1)S(1)}, u32[]{:S(2)}, u32[]{:S(2)}) collective-permute-start(bf16[4,128,768]{2,1,0:T(8,128)(2,1)S(1)} %get-tuple-element.41), channel_id=1, source_target_pairs={{0,1},{1,0},{2,3},{3,2},{4,5},{5,4},{6,7},{7,6},{8,9},{9,8},{10,11... | collective-permute-start | bytes 2359304 | tf_op jit(solution)/shard_map/ppermute | solution.py:486
  85.5 4.0 %late_product.3 = (bf16[4,128,768]{2,1,0:T(8,128)(2,1)S(1)}, bf16[4,128,768]{2,1,0:T(8,128)(2,1)S(1)}) custom-call(s32[2]{0:T(128)S(1)} %copy-done.8, bf16[4,12,64,128]{3,2,1,0:T(8,128)(2,1)S(1)} %pad_maximum_fusion._.a_own, bf16[2,12,64,128]{3,2,1,0:T(8,128)(2,1)S(1)} %collective-permute-done.10.a_far, ...), custom_call_target="tpu_custom_call" | custom-call | flops 1811939328 | bytes 5505024 | tf_op jit(solution)/shard_map/late_product/pallas_call | solution.py:283
  89.5 0.1 collective-permute-start.19
  89.6 0.0 copy-start
  89.7 1.1 pair_sum.2
  90.7 1.1 collective-permute-done.19.taken
  91.9 1.1 pair_sum.3
  93.0 1.8 %collective-permute-start.22 = (bf16[2,128,768]{2,1,0:T(8,128)(2,1)S(1)}, bf16[2,128,768]{2,1,0:T(8,128)(2,1)S(1)}, u32[]{:S(2)}, u32[]{:S(2)}) collective-permute-start(bf16[2,128,768]{2,1,0:T(8,128)(2,1)S(1)} %get-tuple-element.51), channel_id=1, source_target_pairs={{0,4},{1,5},{2,6},{3,7},{4,0},{5,1},{6,2},{7,3},{8,12},{9,13},{10,... | collective-permute-start | bytes 1179656 | tf_op jit(solution)/shard_map/ppermute | solution.py:486
  94.8 3.6 %collective-permute-start.20 = (bf16[128,768]{1,0:T(8,128)(2,1)S(1)}, bf16[128,768]{1,0:T(8,128)(2,1)S(1)}, u32[]{:S(2)}, u32[]{:S(2)}) collective-permute-start(bf16[128,768]{1,0:T(8,128)(2,1)S(1)} %get-tuple-element.49), channel_id=1, source_target_pairs={{0,2},{1,3},{2,4},{3,5},{4,6},{5,7},{6,0},{7,1},{8,10},{9,11},{10,... | collective-permute-start | bytes 589832 | tf_op jit(solution)/shard_map/ppermute | solution.py:486
  98.4 1.5 collective-permute-start.17
  99.9 1.2 collective-permute-start.18
  101.1 8.8 %collective-permute-done.20.refs_4_ = bf16[128,768]{1,0:T(8,128)(2,1)S(1)} collective-permute-done((bf16[128,768]{1,0:T(8,128)(2,1)S(1)}, bf16[128,768]{1,0:T(8,128)(2,1)S(1)}, u32[]{:S(2)}, u32[]{:S(2)}) %collective-permute-start.20) | collective-permute-done | bytes 196640 | tf_op jit(solution)/shard_map/ppermute | solution.py:486
  109.9 1.9 %collective-permute-done.21.refs_5_ = bf16[128,768]{1,0:T(8,128)(2,1)S(1)} collective-permute-done((bf16[128,768]{1,0:T(8,128)(2,1)S(1)}, bf16[128,768]{1,0:T(8,128)(2,1)S(1)}, u32[]{:S(2)}, u32[]{:S(2)}) %collective-permute-start.21) | collective-permute-done | bytes 196640 | tf_op jit(solution)/shard_map/ppermute | solution.py:486
  111.8 2.3 %collective-permute-done.17.refs_1_ = bf16[128,768]{1,0:T(8,128)(2,1)S(1)} collective-permute-done((bf16[128,768]{1,0:T(8,128)(2,1)S(1)}, bf16[128,768]{1,0:T(8,128)(2,1)S(1)}, u32[]{:S(2)}, u32[]{:S(2)}) %collective-permute-start.17) | collective-permute-done | bytes 196640 | tf_op jit(solution)/shard_map/ppermute | solution.py:486
  114.1 1.9 %collective-permute-done.18.refs_2_ = bf16[128,768]{1,0:T(8,128)(2,1)S(1)} collective-permute-done((bf16[128,768]{1,0:T(8,128)(2,1)S(1)}, bf16[128,768]{1,0:T(8,128)(2,1)S(1)}, u32[]{:S(2)}, u32[]{:S(2)}) %collective-permute-start.18) | collective-permute-done | bytes 196640 | tf_op jit(solution)/shard_map/ppermute | solution.py:486
  116.0 1.9 %slots.1 = (bf16[128,1536]{1,0:T(8,128)(2,1)S(1)}, bf16[192,512]{1,0:T(8,128)(2,1)S(1)}) custom-call(s32[2]{0:T(128)S(1)} %copy-done.8, s32[16,12]{1,0:T(8,128)S(1)} %copy-done.6, s32[16]{0:T(128)S(1)} %copy-done.9, s32[16,12]{1,0:T(8,128)S(1)} %copy-done.7, s32[16]{0:T(128)S(1)} %copy-done.10, bf16[128,768]{1,0:T(8,128)(2,1)S(1)} %get-tuple-element.42.refs_0_, ...), custom_call_target="tpu_custom_call" | custom-call | flops 301989888 | bytes 5111808 | tf_op jit(solution)/shard_map/slots/pallas_call | solution.py:368
  117.9 0.5 collective-permute-start.26
  118.4 2.5 %collective-permute-start.27 = (bf16[128,1536]{1,0:T(8,128)(2,1)S(1)}, bf16[128,1536]{1,0:T(8,128)(2,1)S(1)}, u32[]{:S(2)}, u32[]{:S(2)}) collective-permute-start(bf16[128,1536]{1,0:T(8,128)(2,1)S(1)} %get-tuple-element.63.refs_0_), channel_id=1, source_target_pairs={{0,6},{1,7},{2,0},{3,1},{4,2},{5,3},{6,4},{7,5},{8,14},{9,15},{10,... | collective-permute-start | bytes 1179656 | tf_op jit(solution)/shard_map/ppermute | solution.py:486
  120.9 2.7 %collective-permute-start.24 = (bf16[192,512]{1,0:T(8,128)(2,1)S(1)}, bf16[192,512]{1,0:T(8,128)(2,1)S(1)}, u32[]{:S(2)}, u32[]{:S(2)}) collective-permute-start(bf16[192,512]{1,0:T(8,128)(2,1)S(1)} %get-tuple-element.54.one), channel_id=1, source_target_pairs={{0,24},{1,25},{2,26},{3,27},{4,28},{5,29},{6,30},{7,31},{8,0},{9,1... | collective-permute-start | bytes 589832 | tf_op jit(solution)/shard_map/ppermute | solution.py:486
  123.6 3.6 %collective-permute-done.23.two = bf16[192,512]{1,0:T(8,128)(2,1)S(1)} collective-permute-done((bf16[192,512]{1,0:T(8,128)(2,1)S(1)}, bf16[192,512]{1,0:T(8,128)(2,1)S(1)}, u32[]{:S(2)}, u32[]{:S(2)}) %collective-permute-start.23) | collective-permute-done | bytes 196640 | tf_op jit(solution)/shard_map/ppermute | solution.py:486
  127.2 0.8 collective-permute-done.24.three
  128.0 1.8 %collective-permute-done.25.four = bf16[192,512]{1,0:T(8,128)(2,1)S(1)} collective-permute-done((bf16[192,512]{1,0:T(8,128)(2,1)S(1)}, bf16[192,512]{1,0:T(8,128)(2,1)S(1)}, u32[]{:S(2)}, u32[]{:S(2)}) %collective-permute-start.25) | collective-permute-done | bytes 196640 | tf_op jit(solution)/shard_map/ppermute | solution.py:486
  129.8 0.1 fold.1.one
  130.0 2.1 %collective-permute-start.31 = (bf16[128,1536]{1,0:T(8,128)(2,1)S(1)}, bf16[128,1536]{1,0:T(8,128)(2,1)S(1)}, u32[]{:S(2)}, u32[]{:S(2)}) collective-permute-start(bf16[128,1536]{1,0:T(8,128)(2,1)S(1)} %get-tuple-element.63.refs_0_), channel_id=1, source_target_pairs={{0,4},{1,5},{2,6},{3,7},{4,0},{5,1},{6,2},{7,3},{8,12},{9,13},{10,... | collective-permute-start | bytes 1179656 | tf_op jit(solution)/shard_map/ppermute | solution.py:486
  132.0 0.5 collective-permute-start.28
  132.6 2.1 %collective-permute-start.29 = (bf16[192,512]{1,0:T(8,128)(2,1)S(1)}, bf16[192,512]{1,0:T(8,128)(2,1)S(1)}, u32[]{:S(2)}, u32[]{:S(2)}) collective-permute-start(bf16[192,512]{1,0:T(8,128)(2,1)S(1)} %fold.1.one), channel_id=1, source_target_pairs={{0,96},{1,97},{2,98},{3,99},{4,100},{5,101},{6,102},{7,103},{8,104... | collective-permute-start | bytes 589832 | tf_op jit(solution)/shard_map/ppermute | solution.py:486
  134.7 0.2 collective-permute-start.30
  135.0 2.8 %collective-permute-done.28.two = bf16[192,512]{1,0:T(8,128)(2,1)S(1)} collective-permute-done((bf16[192,512]{1,0:T(8,128)(2,1)S(1)}, bf16[192,512]{1,0:T(8,128)(2,1)S(1)}, u32[]{:S(2)}, u32[]{:S(2)}) %collective-permute-start.28) | collective-permute-done | bytes 196640 | tf_op jit(solution)/shard_map/ppermute | solution.py:486
  137.8 1.8 %collective-permute-done.29.three = bf16[192,512]{1,0:T(8,128)(2,1)S(1)} collective-permute-done((bf16[192,512]{1,0:T(8,128)(2,1)S(1)}, bf16[192,512]{1,0:T(8,128)(2,1)S(1)}, u32[]{:S(2)}, u32[]{:S(2)}) %collective-permute-start.29) | collective-permute-done | bytes 196640 | tf_op jit(solution)/shard_map/ppermute | solution.py:486
  139.5 2.7 %collective-permute-done.30.four = bf16[192,512]{1,0:T(8,128)(2,1)S(1)} collective-permute-done((bf16[192,512]{1,0:T(8,128)(2,1)S(1)}, bf16[192,512]{1,0:T(8,128)(2,1)S(1)}, u32[]{:S(2)}, u32[]{:S(2)}) %collective-permute-start.30) | collective-permute-done | bytes 196640 | tf_op jit(solution)/shard_map/ppermute | solution.py:486
  142.3 3.4 %collective-permute-start.32 = (bf16[128,1536]{1,0:T(8,128)(2,1)S(1)}, bf16[128,1536]{1,0:T(8,128)(2,1)S(1)}, u32[]{:S(2)}, u32[]{:S(2)}) collective-permute-start(bf16[128,1536]{1,0:T(8,128)(2,1)S(1)} %get-tuple-element.63.refs_0_), channel_id=1, source_target_pairs={{0,1},{1,0},{2,3},{3,2},{4,5},{5,4},{6,7},{7,6},{8,9},{9,8},{10,11... | collective-permute-start | bytes 1179656 | tf_op jit(solution)/shard_map/ppermute | solution.py:486
  145.7 0.5 collective-permute-start.34
  146.2 1.1 top_part.1
  147.3 0.0 collective-permute-start.35
  147.3 3.9 %all-to-all-start = ((bf16[8,64,128]{2,1,0:T(8,128)(2,1)}), bf16[8,64,128]{2,1,0:T(8,128)(2,1)S(1)}, u32[]{:S(2)}, u32[]{:S(2)}) async-start(bf16[8,64,128]{2,1,0:T(8,128)(2,1)} %get-tuple-element.64), calls=%async_computation | async-start | bytes 262144 | tf_op jit(solution)/shard_map/all_to_all | solution.py:528
  151.3 5.7 %whole_columns.1 = (bf16[1536,512]{1,0:T(8,128)(2,1)}, bf16[1536,512]{1,0:T(8,128)(2,1)}) custom-call(s32[2]{0:T(128)S(1)} %copy-done.8, bf16[128,1536]{1,0:T(8,128)(2,1)S(1)} %get-tuple-element.63.refs_0_, bf16[128,1536]{1,0:T(8,128)(2,1)S(1)} %collective-permute-done.26.refs_1_, bf16[128,1536]{1,0:T(8,128)(2,1)S(1)} %collective-permute-done.27.refs_2_, ...), custom_call_target="tpu_custom_call" | custom-call | bytes 6291456 | tf_op jit(solution)/shard_map/whole_columns/pallas_call | solution.py:402
  156.9 0.9 last_part.1
  (52 shorter events, 0.2 us)
Async XLA Ops:
  4.1 16.9 %collective-permute-start = (bf16[12,64,128]{2,1,0:T(8,128)(2,1)}, bf16[12,64,128]{2,1,0:T(8,128)(2,1)S(1)}, u32[]{:S(2)}, u32[]{:S(2)}) collective-permute-start(bf16[12,64,128]{2,1,0:T(8,128)(2,1)} %prep_a.1), channel_id=1, source_target_pairs={{0,0},{1,32},{2,8},{3,40},{4,16},{5,48},{6,24},{7,56},{8,9},{9,41}... | collective-permute-start | bytes 589832 | tf_op jit(solution)/shard_map/ppermute | solution.py:498
  13.3 15.9 %collective-permute-start.5 = (bf16[12,64,128]{2,1,0:T(8,128)(2,1)}, bf16[12,64,128]{2,1,0:T(8,128)(2,1)S(1)}, u32[]{:S(2)}, u32[]{:S(2)}) collective-permute-start(bf16[12,64,128]{2,1,0:T(8,128)(2,1)} %prep_b.1), channel_id=1, source_target_pairs={{0,0},{1,32},{2,8},{3,40},{4,16},{5,48},{6,24},{7,56},{8,9},{9,41}... | collective-permute-start | bytes 589832 | tf_op jit(solution)/shard_map/ppermute | solution.py:500
  21.0 13.4 %collective-permute-start.1 = (bf16[12,64,128]{2,1,0:T(8,128)(2,1)S(1)}, bf16[12,64,128]{2,1,0:T(8,128)(2,1)S(1)}, u32[]{:S(2)}, u32[]{:S(2)}) collective-permute-start(bf16[12,64,128]{2,1,0:T(8,128)(2,1)S(1)} %collective-permute-done), channel_id=1, source_target_pairs={{0,8},{1,9},{2,10},{3,11},{4,12},{5,13},{6,14},{7,15},{8,16},{9,17... | collective-permute-start | bytes 589832 | tf_op jit(solution)/shard_map/ppermute | solution.py:486
  21.0 18.5 %collective-permute-start.2 = (bf16[12,64,128]{2,1,0:T(8,128)(2,1)S(1)}, bf16[12,64,128]{2,1,0:T(8,128)(2,1)S(1)}, u32[]{:S(2)}, u32[]{:S(2)}) collective-permute-start(bf16[12,64,128]{2,1,0:T(8,128)(2,1)S(1)} %collective-permute-done), channel_id=1, source_target_pairs={{0,24},{1,25},{2,26},{3,27},{4,28},{5,29},{6,30},{7,31},{8,0},{9,1... | collective-permute-start | bytes 589832 | tf_op jit(solution)/shard_map/ppermute | solution.py:486
  23.7 15.8 %collective-permute-start.3 = (bf16[12,64,128]{2,1,0:T(8,128)(2,1)S(1)}, bf16[12,64,128]{2,1,0:T(8,128)(2,1)S(1)}, u32[]{:S(2)}, u32[]{:S(2)}) collective-permute-start(bf16[12,64,128]{2,1,0:T(8,128)(2,1)S(1)} %collective-permute-done), channel_id=1, source_target_pairs={{0,16},{1,17},{2,18},{3,19},{4,20},{5,21},{6,22},{7,23},{8,24},{9,... | collective-permute-start | bytes 589832 | tf_op jit(solution)/shard_map/ppermute | solution.py:486
  29.3 10.4 %collective-permute-start.6 = (bf16[12,64,128]{2,1,0:T(8,128)(2,1)S(1)}, bf16[12,64,128]{2,1,0:T(8,128)(2,1)S(1)}, u32[]{:S(2)}, u32[]{:S(2)}) collective-permute-start(bf16[12,64,128]{2,1,0:T(8,128)(2,1)S(1)} %collective-permute-done.5), channel_id=1, source_target_pairs={{0,32},{1,33},{2,34},{3,35},{4,36},{5,37},{6,38},{7,39},{8,40},{9,... | collective-permute-start | bytes 589832 | tf_op jit(solution)/shard_map/ppermute | solution.py:486
  32.2 7.5 %collective-permute-start.7 = (bf16[12,64,128]{2,1,0:T(8,128)(2,1)S(1)}, bf16[12,64,128]{2,1,0:T(8,128)(2,1)S(1)}, u32[]{:S(2)}, u32[]{:S(2)}) collective-permute-start(bf16[12,64,128]{2,1,0:T(8,128)(2,1)S(1)} %collective-permute-done.5), channel_id=1, source_target_pairs={{0,96},{1,97},{2,98},{3,99},{4,100},{5,101},{6,102},{7,103},{8,104... | collective-permute-start | bytes 589832 | tf_op jit(solution)/shard_map/ppermute | solution.py:486
  34.4 9.6 %collective-permute-start.8 = (bf16[12,64,128]{2,1,0:T(8,128)(2,1)S(1)}, bf16[12,64,128]{2,1,0:T(8,128)(2,1)S(1)}, u32[]{:S(2)}, u32[]{:S(2)}) collective-permute-start(bf16[12,64,128]{2,1,0:T(8,128)(2,1)S(1)} %collective-permute-done.5), channel_id=1, source_target_pairs={{0,64},{1,65},{2,66},{3,67},{4,68},{5,69},{6,70},{7,71},{8,72},{9,... | collective-permute-start | bytes 589832 | tf_op jit(solution)/shard_map/ppermute | solution.py:486
  39.6 22.1 %collective-permute-start.4 = (bf16[4,12,64,128]{3,2,1,0:T(8,128)(2,1)S(1)}, bf16[4,12,64,128]{3,2,1,0:T(8,128)(2,1)S(1)}, u32[]{:S(2)}, u32[]{:S(2)}) collective-permute-start(bf16[4,12,64,128]{3,2,1,0:T(8,128)(2,1)S(1)} %pad_maximum_fusion._.a_own), channel_id=1, source_target_pairs={{0,32},{1,33},{2,34},{3,35},{4,36},{5,37},{6,38},{7,39},{8,40},{9,... | collective-permute-start | bytes 2359304 | tf_op jit(solution)/shard_map/ppermute | solution.py:486
  44.0 17.7 %collective-permute-start.9 = (bf16[4,12,64,128]{3,2,1,0:T(8,128)(2,1)S(1)}, bf16[4,12,64,128]{3,2,1,0:T(8,128)(2,1)S(1)}, u32[]{:S(2)}, u32[]{:S(2)}) collective-permute-start(bf16[4,12,64,128]{3,2,1,0:T(8,128)(2,1)S(1)} %pad_maximum_fusion.1.b_own), channel_id=1, source_target_pairs={{0,8},{1,9},{2,10},{3,11},{4,12},{5,13},{6,14},{7,15},{8,16},{9,17... | collective-permute-start | bytes 2359304 | tf_op jit(solution)/shard_map/ppermute | solution.py:486
  45.9 18.2 %collective-permute-start.11 = (bf16[4,12,64,128]{3,2,1,0:T(8,128)(2,1)S(1)}, bf16[4,12,64,128]{3,2,1,0:T(8,128)(2,1)S(1)}, u32[]{:S(2)}, u32[]{:S(2)}) collective-permute-start(bf16[4,12,64,128]{3,2,1,0:T(8,128)(2,1)S(1)} %pad_maximum_fusion._.a_own), channel_id=1, source_target_pairs={{0,96},{1,97},{2,98},{3,99},{4,100},{5,101},{6,102},{7,103},{8,104... | collective-permute-start | bytes 2359304 | tf_op jit(solution)/shard_map/ppermute | solution.py:486
  46.0 20.3 %collective-permute-start.14 = (bf16[4,12,64,128]{3,2,1,0:T(8,128)(2,1)S(1)}, bf16[4,12,64,128]{3,2,1,0:T(8,128)(2,1)S(1)}, u32[]{:S(2)}, u32[]{:S(2)}) collective-permute-start(bf16[4,12,64,128]{3,2,1,0:T(8,128)(2,1)S(1)} %pad_maximum_fusion.1.b_own), channel_id=1, source_target_pairs={{0,24},{1,25},{2,26},{3,27},{4,28},{5,29},{6,30},{7,31},{8,0},{9,1... | collective-permute-start | bytes 2359304 | tf_op jit(solution)/shard_map/ppermute | solution.py:486
  47.2 3.7 %copy-start.1 = (bf16[1536,3072]{1,0:T(8,128)(2,1)S(1)}, bf16[1536,3072]{1,0:T(8,128)(2,1)}, u32[]{:S(2)}) copy-start(bf16[1536,3072]{1,0:T(8,128)(2,1)} %source.1) | copy-start | bytes 28311556
  51.6 16.5 %copy-start.8 = (s32[2]{0:T(128)S(1)}, s32[2]{0:T(128)}, u32[]{:S(2)}) copy-start(s32[2]{0:T(128)} %pad_add_fusion.place) | copy-start | bytes 28
  61.8 15.5 %collective-permute-start.10 = (bf16[2,12,64,128]{3,2,1,0:T(8,128)(2,1)S(1)}, bf16[2,12,64,128]{3,2,1,0:T(8,128)(2,1)S(1)}, u32[]{:S(2)}, u32[]{:S(2)}) collective-permute-start(bf16[2,12,64,128]{3,2,1,0:T(8,128)(2,1)S(1)} %slice.12), channel_id=1, source_target_pairs={{0,32},{1,33},{2,34},{3,35},{4,36},{5,37},{6,38},{7,39},{8,40},{9,... | collective-permute-start | bytes 1179656 | tf_op jit(solution)/shard_map/ppermute | solution.py:486
  63.0 14.2 %collective-permute-start.13 = (bf16[2,12,64,128]{3,2,1,0:T(8,128)(2,1)S(1)}, bf16[2,12,64,128]{3,2,1,0:T(8,128)(2,1)S(1)}, u32[]{:S(2)}, u32[]{:S(2)}) collective-permute-start(bf16[2,12,64,128]{3,2,1,0:T(8,128)(2,1)S(1)} %slice.14), channel_id=1, source_target_pairs={{0,8},{1,9},{2,10},{3,11},{4,12},{5,13},{6,14},{7,15},{8,16},{9,17... | collective-permute-start | bytes 1179656 | tf_op jit(solution)/shard_map/ppermute | solution.py:486
  64.2 13.0 %collective-permute-start.12 = (bf16[2,12,64,128]{3,2,1,0:T(8,128)(2,1)S(1)}, bf16[2,12,64,128]{3,2,1,0:T(8,128)(2,1)S(1)}, u32[]{:S(2)}, u32[]{:S(2)}) collective-permute-start(bf16[2,12,64,128]{3,2,1,0:T(8,128)(2,1)S(1)} %slice.16), channel_id=1, source_target_pairs={{0,96},{1,97},{2,98},{3,99},{4,100},{5,101},{6,102},{7,103},{8,104... | collective-permute-start | bytes 1179656 | tf_op jit(solution)/shard_map/ppermute | solution.py:486
  66.3 11.0 %collective-permute-start.15 = (bf16[2,12,64,128]{3,2,1,0:T(8,128)(2,1)S(1)}, bf16[2,12,64,128]{3,2,1,0:T(8,128)(2,1)S(1)}, u32[]{:S(2)}, u32[]{:S(2)}) collective-permute-start(bf16[2,12,64,128]{3,2,1,0:T(8,128)(2,1)S(1)} %slice.17), channel_id=1, source_target_pairs={{0,24},{1,25},{2,26},{3,27},{4,28},{5,29},{6,30},{7,31},{8,0},{9,1... | collective-permute-start | bytes 1179656 | tf_op jit(solution)/shard_map/ppermute | solution.py:486
  81.3 8.3 %collective-permute-start.16 = (bf16[4,128,768]{2,1,0:T(8,128)(2,1)S(1)}, bf16[4,128,768]{2,1,0:T(8,128)(2,1)S(1)}, u32[]{:S(2)}, u32[]{:S(2)}) collective-permute-start(bf16[4,128,768]{2,1,0:T(8,128)(2,1)S(1)} %get-tuple-element.41), channel_id=1, source_target_pairs={{0,1},{1,0},{2,3},{3,2},{4,5},{5,4},{6,7},{7,6},{8,9},{9,8},{10,11... | collective-permute-start | bytes 2359304 | tf_op jit(solution)/shard_map/ppermute | solution.py:486
  89.5 2.4 %collective-permute-start.19 = (bf16[4,128,768]{2,1,0:T(8,128)(2,1)S(1)}, bf16[4,128,768]{2,1,0:T(8,128)(2,1)S(1)}, u32[]{:S(2)}, u32[]{:S(2)}) collective-permute-start(bf16[4,128,768]{2,1,0:T(8,128)(2,1)S(1)} %get-tuple-element.46), channel_id=1, source_target_pairs={{0,1},{1,0},{2,3},{3,2},{4,5},{5,4},{6,7},{7,6},{8,9},{9,8},{10,11... | collective-permute-start | bytes 2359304 | tf_op jit(solution)/shard_map/ppermute | solution.py:486
  89.6 26.4 %copy-start = (bf16[1536,512]{1,0:T(8,128)(2,1)S(1)}, bf16[1536,512]{1,0:T(8,128)(2,1)}, u32[]{:S(2)}) copy-start(bf16[1536,512]{1,0:T(8,128)(2,1)} %refs_7_.1) | copy-start | bytes 4718596
  89.6 26.4 %copy-start.2 = (bf16[1536,512]{1,0:T(8,128)(2,1)S(1)}, bf16[1536,512]{1,0:T(8,128)(2,1)}, u32[]{:S(2)}) copy-start(bf16[1536,512]{1,0:T(8,128)(2,1)} %refs_8_.1) | copy-start | bytes 4718596
  89.6 26.4 %copy-start.6 = (s32[16,12]{1,0:T(8,128)S(1)}, s32[16,12]{1,0:T(8,128)}, u32[]{:S(2)}) copy-start(s32[16,12]{1,0:T(8,128)} %rows_a.5) | copy-start | bytes 2308
  89.6 26.4 %copy-start.7 = (s32[16,12]{1,0:T(8,128)S(1)}, s32[16,12]{1,0:T(8,128)}, u32[]{:S(2)}) copy-start(s32[16,12]{1,0:T(8,128)} %rows_b.3) | copy-start | bytes 2308
  89.7 26.3 %copy-start.9 = (s32[16]{0:T(128)S(1)}, s32[16]{0:T(128)}, u32[]{:S(2)}) copy-start(s32[16]{0:T(128)} %counts_a.5) | copy-start | bytes 196
  89.7 26.3 %copy-start.10 = (s32[16]{0:T(128)S(1)}, s32[16]{0:T(128)}, u32[]{:S(2)}) copy-start(s32[16]{0:T(128)} %counts_b.3) | copy-start | bytes 196
  93.0 23.0 %collective-permute-start.22 = (bf16[2,128,768]{2,1,0:T(8,128)(2,1)S(1)}, bf16[2,128,768]{2,1,0:T(8,128)(2,1)S(1)}, u32[]{:S(2)}, u32[]{:S(2)}) collective-permute-start(bf16[2,128,768]{2,1,0:T(8,128)(2,1)S(1)} %get-tuple-element.51), channel_id=1, source_target_pairs={{0,4},{1,5},{2,6},{3,7},{4,0},{5,1},{6,2},{7,3},{8,12},{9,13},{10,... | collective-permute-start | bytes 1179656 | tf_op jit(solution)/shard_map/ppermute | solution.py:486
  94.8 15.1 %collective-permute-start.20 = (bf16[128,768]{1,0:T(8,128)(2,1)S(1)}, bf16[128,768]{1,0:T(8,128)(2,1)S(1)}, u32[]{:S(2)}, u32[]{:S(2)}) collective-permute-start(bf16[128,768]{1,0:T(8,128)(2,1)S(1)} %get-tuple-element.49), channel_id=1, source_target_pairs={{0,2},{1,3},{2,4},{3,5},{4,6},{5,7},{6,0},{7,1},{8,10},{9,11},{10,... | collective-permute-start | bytes 589832 | tf_op jit(solution)/shard_map/ppermute | solution.py:486
  98.4 13.4 %collective-permute-start.21 = (bf16[128,768]{1,0:T(8,128)(2,1)S(1)}, bf16[128,768]{1,0:T(8,128)(2,1)S(1)}, u32[]{:S(2)}, u32[]{:S(2)}) collective-permute-start(bf16[128,768]{1,0:T(8,128)(2,1)S(1)} %get-tuple-element.50), channel_id=1, source_target_pairs={{0,6},{1,7},{2,0},{3,1},{4,2},{5,3},{6,4},{7,5},{8,14},{9,15},{10,... | collective-permute-start | bytes 589832 | tf_op jit(solution)/shard_map/ppermute | solution.py:486
  98.4 15.7 %collective-permute-start.17 = (bf16[128,768]{1,0:T(8,128)(2,1)S(1)}, bf16[128,768]{1,0:T(8,128)(2,1)S(1)}, u32[]{:S(2)}, u32[]{:S(2)}) collective-permute-start(bf16[128,768]{1,0:T(8,128)(2,1)S(1)} %get-tuple-element.43), channel_id=1, source_target_pairs={{0,2},{1,3},{2,4},{3,5},{4,6},{5,7},{6,0},{7,1},{8,10},{9,11},{10,... | collective-permute-start | bytes 589832 | tf_op jit(solution)/shard_map/ppermute | solution.py:486
  99.9 16.1 %collective-permute-start.18 = (bf16[128,768]{1,0:T(8,128)(2,1)S(1)}, bf16[128,768]{1,0:T(8,128)(2,1)S(1)}, u32[]{:S(2)}, u32[]{:S(2)}) collective-permute-start(bf16[128,768]{1,0:T(8,128)(2,1)S(1)} %get-tuple-element.44), channel_id=1, source_target_pairs={{0,6},{1,7},{2,0},{3,1},{4,2},{5,3},{6,4},{7,5},{8,14},{9,15},{10,... | collective-permute-start | bytes 589832 | tf_op jit(solution)/shard_map/ppermute | solution.py:486
  116.0 30.1 %copy-start.3 = (bf16[512,512]{1,0:T(8,128)(2,1)S(1)}, bf16[512,512]{1,0:T(8,128)(2,1)}, u32[]{:S(2)}) copy-start(bf16[512,512]{1,0:T(8,128)(2,1)} %top.5) | copy-start | bytes 1572868
  116.0 30.1 %copy-start.4 = (f32[64,512]{1,0:T(8,128)S(1)}, f32[64,512]{1,0:T(8,128)}, u32[]{:S(2)}) copy-start(f32[64,512]{1,0:T(8,128)} %base.1) | copy-start | bytes 393220
  117.9 11.9 %collective-permute-start.26 = (bf16[128,1536]{1,0:T(8,128)(2,1)S(1)}, bf16[128,1536]{1,0:T(8,128)(2,1)S(1)}, u32[]{:S(2)}, u32[]{:S(2)}) collective-permute-start(bf16[128,1536]{1,0:T(8,128)(2,1)S(1)} %get-tuple-element.63.refs_0_), channel_id=1, source_target_pairs={{0,2},{1,3},{2,4},{3,5},{4,6},{5,7},{6,0},{7,1},{8,10},{9,11},{10,... | collective-permute-start | bytes 1179656 | tf_op jit(solution)/shard_map/ppermute | solution.py:486
  118.4 11.4 %collective-permute-start.27 = (bf16[128,1536]{1,0:T(8,128)(2,1)S(1)}, bf16[128,1536]{1,0:T(8,128)(2,1)S(1)}, u32[]{:S(2)}, u32[]{:S(2)}) collective-permute-start(bf16[128,1536]{1,0:T(8,128)(2,1)S(1)} %get-tuple-element.63.refs_0_), channel_id=1, source_target_pairs={{0,6},{1,7},{2,0},{3,1},{4,2},{5,3},{6,4},{7,5},{8,14},{9,15},{10,... | collective-permute-start | bytes 1179656 | tf_op jit(solution)/shard_map/ppermute | solution.py:486
  120.9 6.3 %collective-permute-start.23 = (bf16[192,512]{1,0:T(8,128)(2,1)S(1)}, bf16[192,512]{1,0:T(8,128)(2,1)S(1)}, u32[]{:S(2)}, u32[]{:S(2)}) collective-permute-start(bf16[192,512]{1,0:T(8,128)(2,1)S(1)} %get-tuple-element.54.one), channel_id=1, source_target_pairs={{0,8},{1,9},{2,10},{3,11},{4,12},{5,13},{6,14},{7,15},{8,16},{9,17... | collective-permute-start | bytes 589832 | tf_op jit(solution)/shard_map/ppermute | solution.py:486
  120.9 7.1 %collective-permute-start.24 = (bf16[192,512]{1,0:T(8,128)(2,1)S(1)}, bf16[192,512]{1,0:T(8,128)(2,1)S(1)}, u32[]{:S(2)}, u32[]{:S(2)}) collective-permute-start(bf16[192,512]{1,0:T(8,128)(2,1)S(1)} %get-tuple-element.54.one), channel_id=1, source_target_pairs={{0,24},{1,25},{2,26},{3,27},{4,28},{5,29},{6,30},{7,31},{8,0},{9,1... | collective-permute-start | bytes 589832 | tf_op jit(solution)/shard_map/ppermute | solution.py:486
  123.6 6.3 %collective-permute-start.25 = (bf16[192,512]{1,0:T(8,128)(2,1)S(1)}, bf16[192,512]{1,0:T(8,128)(2,1)S(1)}, u32[]{:S(2)}, u32[]{:S(2)}) collective-permute-start(bf16[192,512]{1,0:T(8,128)(2,1)S(1)} %get-tuple-element.54.one), channel_id=1, source_target_pairs={{0,16},{1,17},{2,18},{3,19},{4,20},{5,21},{6,22},{7,23},{8,24},{9,... | collective-permute-start | bytes 589832 | tf_op jit(solution)/shard_map/ppermute | solution.py:486
  130.0 17.4 %collective-permute-start.31 = (bf16[128,1536]{1,0:T(8,128)(2,1)S(1)}, bf16[128,1536]{1,0:T(8,128)(2,1)S(1)}, u32[]{:S(2)}, u32[]{:S(2)}) collective-permute-start(bf16[128,1536]{1,0:T(8,128)(2,1)S(1)} %get-tuple-element.63.refs_0_), channel_id=1, source_target_pairs={{0,4},{1,5},{2,6},{3,7},{4,0},{5,1},{6,2},{7,3},{8,12},{9,13},{10,... | collective-permute-start | bytes 1179656 | tf_op jit(solution)/shard_map/ppermute | solution.py:486
  132.0 5.7 %collective-permute-start.28 = (bf16[192,512]{1,0:T(8,128)(2,1)S(1)}, bf16[192,512]{1,0:T(8,128)(2,1)S(1)}, u32[]{:S(2)}, u32[]{:S(2)}) collective-permute-start(bf16[192,512]{1,0:T(8,128)(2,1)S(1)} %fold.1.one), channel_id=1, source_target_pairs={{0,32},{1,33},{2,34},{3,35},{4,36},{5,37},{6,38},{7,39},{8,40},{9,... | collective-permute-start | bytes 589832 | tf_op jit(solution)/shard_map/ppermute | solution.py:486
  132.6 6.9 %collective-permute-start.29 = (bf16[192,512]{1,0:T(8,128)(2,1)S(1)}, bf16[192,512]{1,0:T(8,128)(2,1)S(1)}, u32[]{:S(2)}, u32[]{:S(2)}) collective-permute-start(bf16[192,512]{1,0:T(8,128)(2,1)S(1)} %fold.1.one), channel_id=1, source_target_pairs={{0,96},{1,97},{2,98},{3,99},{4,100},{5,101},{6,102},{7,103},{8,104... | collective-permute-start | bytes 589832 | tf_op jit(solution)/shard_map/ppermute | solution.py:486
  134.7 7.5 %collective-permute-start.30 = (bf16[192,512]{1,0:T(8,128)(2,1)S(1)}, bf16[192,512]{1,0:T(8,128)(2,1)S(1)}, u32[]{:S(2)}, u32[]{:S(2)}) collective-permute-start(bf16[192,512]{1,0:T(8,128)(2,1)S(1)} %fold.1.one), channel_id=1, source_target_pairs={{0,64},{1,65},{2,66},{3,67},{4,68},{5,69},{6,70},{7,71},{8,72},{9,... | collective-permute-start | bytes 589832 | tf_op jit(solution)/shard_map/ppermute | solution.py:486
  142.3 9.0 %collective-permute-start.32 = (bf16[128,1536]{1,0:T(8,128)(2,1)S(1)}, bf16[128,1536]{1,0:T(8,128)(2,1)S(1)}, u32[]{:S(2)}, u32[]{:S(2)}) collective-permute-start(bf16[128,1536]{1,0:T(8,128)(2,1)S(1)} %get-tuple-element.63.refs_0_), channel_id=1, source_target_pairs={{0,1},{1,0},{2,3},{3,2},{4,5},{5,4},{6,7},{7,6},{8,9},{9,8},{10,11... | collective-permute-start | bytes 1179656 | tf_op jit(solution)/shard_map/ppermute | solution.py:486
  145.7 5.6 %collective-permute-start.33 = (bf16[128,1536]{1,0:T(8,128)(2,1)S(1)}, bf16[128,1536]{1,0:T(8,128)(2,1)}, u32[]{:S(2)}, u32[]{:S(2)}) collective-permute-start(bf16[128,1536]{1,0:T(8,128)(2,1)S(1)} %collective-permute-done.26.refs_1_), channel_id=1, source_target_pairs={{0,1},{1,0},{2,3},{3,2},{4,5},{5,4},{6,7},{7,6},{8,9},{9,8},{10,11... | collective-permute-start | bytes 1179656 | tf_op jit(solution)/shard_map/ppermute | solution.py:486
  145.7 5.6 %collective-permute-start.34 = (bf16[128,1536]{1,0:T(8,128)(2,1)S(1)}, bf16[128,1536]{1,0:T(8,128)(2,1)}, u32[]{:S(2)}, u32[]{:S(2)}) collective-permute-start(bf16[128,1536]{1,0:T(8,128)(2,1)S(1)} %collective-permute-done.27.refs_2_), channel_id=1, source_target_pairs={{0,1},{1,0},{2,3},{3,2},{4,5},{5,4},{6,7},{7,6},{8,9},{9,8},{10,11... | collective-permute-start | bytes 1179656 | tf_op jit(solution)/shard_map/ppermute | solution.py:486
  147.3 3.9 %collective-permute-start.35 = (bf16[128,1536]{1,0:T(8,128)(2,1)S(1)}, bf16[128,1536]{1,0:T(8,128)(2,1)}, u32[]{:S(2)}, u32[]{:S(2)}) collective-permute-start(bf16[128,1536]{1,0:T(8,128)(2,1)S(1)} %collective-permute-done.31.refs_3_), channel_id=1, source_target_pairs={{0,1},{1,0},{2,3},{3,2},{4,5},{5,4},{6,7},{7,6},{8,9},{9,8},{10,11... | collective-permute-start | bytes 1179656 | tf_op jit(solution)/shard_map/ppermute | solution.py:486
  147.3 9.6 %all-to-all-start = ((bf16[8,64,128]{2,1,0:T(8,128)(2,1)}), bf16[8,64,128]{2,1,0:T(8,128)(2,1)S(1)}, u32[]{:S(2)}, u32[]{:S(2)}) async-start(bf16[8,64,128]{2,1,0:T(8,128)(2,1)} %get-tuple-element.64), calls=%async_computation | async-start | bytes 262144 | tf_op jit(solution)/shard_map/all_to_all | solution.py:528
  151.2 5.7 %copy-start.5 = (f32[64,512]{1,0:T(8,128)S(1)}, f32[64,512]{1,0:T(8,128)}, u32[]{:S(2)}) copy-start(f32[64,512]{1,0:T(8,128)} %base.2) | copy-start | bytes 393220

commit v7 on v6

--- a/solution.py
+++ b/solution.py
@@ -65,26 +65,19 @@
     return pl.BlockSpec(shape, lambda *_: (0,) * len(shape))
 
 
-def find_slot(rows, counts, owner, block):
-    slot = jnp.int32(0)
-    live = jnp.int32(0)
-    for k in range(NB):
-        hit = (rows[owner, k] == block) & (k < counts[owner])
-        slot = jnp.where(hit, k, slot)
-        live = jnp.where(hit, 1, live)
-    return slot, live
-
-
 def half_of(value, upper):
     return jnp.where(upper > 0, value[PART:], value[:PART])
 
 
 def prep_a_body(place, rows_a, counts_a, part_a, out_a):
-    for block in range(NB):
-        slot, live = find_slot(rows_a, counts_a, place[0], block)
-        at = pl.ds(pl.multiple_of(slot * BS, BS), BS)
-        piece = half_of(part_a[at, :].T, place[1] % 2)
-        out_a[block] = jnp.where(live > 0, piece, jnp.zeros_like(piece))
+    owner = place[0]
+    out_a[...] = jnp.zeros_like(out_a)
+    for k in range(NB):
+        piece = half_of(part_a[k * BS : (k + 1) * BS, :].T, place[1] % 2)
+
+        @pl.when(k < counts_a[owner])
+        def _():
+            out_a[rows_a[owner, k]] = piece
 
 
 def width_slice(rows):
@@ -107,21 +100,28 @@
     )(place, *lists[:2], factor_a)
 
 
-def prep_b_body(place, rows_a, counts_a, rows_b, counts_b, fa, part_b, top, out_b, fix):
+def prep_b_body(place, rows_a, counts_a, rows_b, counts_b, fa, part_b, top, out_b, mixed):
     owner = place[0]
     upper = place[1] % 2
-    fix[...] = lax.dot_general(
-        top[...], fa[...], (((0,), (1,)), ((), ())), preferred_element_type=F32
+    moved = half_of(
+        lax.dot_general(top[...], fa[...], (((0,), (1,)), ((), ())), preferred_element_type=F32),
+        upper,
     )
-    for block in range(NB):
-        slot_a, live_a = find_slot(rows_a, counts_a, owner, block)
-        slot_b, live_b = find_slot(rows_b, counts_b, owner, block)
-        at_a = pl.ds(pl.multiple_of(slot_a * BS, BS), BS)
-        at_b = pl.ds(pl.multiple_of(slot_b * BS, BS), BS)
-        moved = half_of(fix[:, at_a], upper)
-        piece = half_of(part_b[at_b, :].T, upper).astype(F32)
-        piece = jnp.where(live_b > 0, piece, jnp.zeros_like(piece))
-        out_b[block] = (piece - jnp.where(live_a > 0, moved, jnp.zeros_like(moved))).astype(BF)
+    mixed[...] = jnp.zeros_like(mixed)
+    for k in range(NB):
+
+        @pl.when(k < counts_a[owner])
+        def _():
+            mixed[rows_a[owner, k]] = -moved[:, k * BS : (k + 1) * BS]
+
+    for k in range(NB):
+        piece = half_of(part_b[k * BS : (k + 1) * BS, :].T, upper).astype(F32)
+
+        @pl.when(k < counts_b[owner])
+        def _():
+            mixed[rows_b[owner, k]] += piece
+
+    out_b[...] = mixed[...].astype(BF)
 
 
 def prep_b(place, lists, factor_a, factor_b, factor_top):
@@ -133,7 +133,7 @@
             grid=(1,),
             in_specs=[whole((ROWS, W)), width_slice(ROWS), width_slice(W)],
             out_specs=whole((NB, PART, BS)),
-            scratch_shapes=[pltpu.VMEM((BS, ROWS), F32)],
+            scratch_shapes=[pltpu.VMEM((NB, PART, BS), F32)],
         ),
         out_shape=jax.ShapeDtypeStruct((NB, PART, BS), BF),
         compiler_params=params(56),
@@ -304,51 +304,40 @@
     )(place, *bufs, trailing, before)
 
 
-def pair_body(joined, place, mine, taken, *refs):
-    before, outs = refs[: joined], refs[joined:]
+def pair_body(place, mine, taken, *outs):
     x = place[1] // 2
     for i in range(SIDE):
         at = (x + i) % SIDE
-        total = (mine[at].astype(F32) + taken[at].astype(F32)).astype(BF)
-        if joined and i == 2:
-            outs[i][0] = before[0][...]
-            outs[i][1] = total
-        else:
-            outs[i][...] = total
-
-
-def pair_sum(place, mine, taken, *before):
+        outs[i][...] = (mine[at].astype(F32) + taken[at].astype(F32)).astype(BF)
+
+
+def pair_sum(place, mine, taken):
     lanes = 3 * BS
     width = mine.shape[2]
     spec = pl.BlockSpec((SIDE, PAIR, lanes), lambda i, *_: (0, 0, i))
-    one = pl.BlockSpec((PAIR, lanes), lambda i, *_: (0, i))
-    two = pl.BlockSpec((2, PAIR, lanes), lambda i, *_: (0, 0, i))
-    shape = jax.ShapeDtypeStruct((PAIR, width), BF)
-    double = jax.ShapeDtypeStruct((2, PAIR, width), BF)
-    joined = len(before)
-    return pl.pallas_call(
-        functools.partial(pair_body, joined),
+    return pl.pallas_call(
+        pair_body,
         name="pair_sum",
         grid_spec=pltpu.PrefetchScalarGridSpec(
             num_scalar_prefetch=1,
             grid=(width // lanes,),
-            in_specs=[spec, spec] + [one] * joined,
-            out_specs=[one, one, two if joined else one, one],
-        ),
-        out_shape=[shape, shape, double if joined else shape, shape],
+            in_specs=[spec, spec],
+            out_specs=[pl.BlockSpec((PAIR, lanes), lambda i, *_: (0, i))] * SIDE,
+        ),
+        out_shape=[jax.ShapeDtypeStruct((PAIR, width), BF)] * SIDE,
         compiler_params=params(dimension_semantics=("arbitrary",)),
         cost_estimate=cost(W * width, 6 * W * width),
-    )(place, mine, taken, *before)
+    )(place, mine, taken)
 
 
 def slots_body(
     place, rows_a, counts_a, rows_b, counts_b, *refs
 ):
-    slabs, far, (fa, fb, columns, pieces, natural, left) = refs[:6], refs[6], refs[7:]
+    slabs, (fa, fb, columns, pieces, natural, left) = refs[:8], refs[8:]
     owner = place[0]
     width = ROWS // 2
     for half in range(2):
-        total = total_of((*slabs[half * 3 : half * 3 + 3], far.at[half]), slice(None))
+        total = total_of(slabs[half * SIDE : (half + 1) * SIDE], slice(None))
         natural[:, half * width : (half + 1) * width] = (-total).astype(BF)
     for k in range(NB):
         at = slice(k * BS, (k + 1) * BS)
@@ -371,9 +360,7 @@
         grid_spec=pltpu.PrefetchScalarGridSpec(
             num_scalar_prefetch=5,
             grid=(1,),
-            in_specs=[whole((PAIR, ROWS // 2))] * 6
-            + [whole((2, PAIR, ROWS // 2))]
-            + [whole((ROWS, W))] * 2,
+            in_specs=[whole((PAIR, ROWS // 2))] * 8 + [whole((ROWS, W))] * 2,
             out_specs=[whole((PAIR, ROWS)), whole((3 * PART, W))],
             scratch_shapes=[pltpu.VMEM((PAIR, ROWS), BF)] * 2,
         ),
@@ -397,7 +384,7 @@
 
 
 def whole_columns(place, slabs):
-    lanes = 2 * BS
+    lanes = 4 * BS
     out = jax.ShapeDtypeStruct((ROWS, W), BF)
     return pl.pallas_call(
         column_body,
@@ -507,14 +494,13 @@
     a_far, b_far = send(a_next[:2], dz=1), send(b_next[:2], dy=1)
     a_far_more, b_far_more = send(a_up[2:], dz=-1), send(b_up[2:], dy=-1)
     before = early_product(place, (a_down, a_up, b_own, b_down, b_up), trailing)
-    slabs, far = [], ()
+    slabs = []
     for half in range(2):
         keep, give = late_product(
             half, place, (a_own, a_far, a_far_more, b_far, b_far_more), trailing, before
         )
-        own, one, *far, three = pair_sum(place, keep, send(give, dc=1), *far)
-        slabs += [own, send(one, dx=1), send(three, dx=-1)]
-    slabs.append(send(far[0], dx=2))
+        own, one, two, three = pair_sum(place, keep, send(give, dc=1))
+        slabs += [own, send(one, dx=1), send(two, dx=2), send(three, dx=-1)]
     columns, pieces = slots(place, lists, slabs, (factor_a, factor_b))
     near, other = send(columns, dx=1), send(columns, dx=-1)
     first, near, other = lax.optimization_barrier((around(pieces, "dy"), near, other))

time: 159 us -> 157 us (0.987)
  waiting for transfers between devices: 56.2 us -> 49.4 us
  starting transfers between devices: 59.1 us -> 64.5 us
    ppermute x1, waiting for transfers between devices: 5.6 us -> 0.01 us  [on_device(): part_b = lax.ppermute(part_b, BOTH, spread_pairs())]
    ppermute x34 -> x35, starting transfers between devices: 45.4 us -> 50.6 us  [send(): return lax.ppermute(value, BOTH, shifted(**by))]
    ppermute x34 -> x35, waiting for transfers between devices: 47.9 us -> 46.6 us  [send(): return lax.ppermute(value, BOTH, shifted(**by))]
  transfers between devices with their start and end apart: 37 -> 38, of which waited for: 16 -> 18; matrix products, arithmetic and copies ran while one was open for 0% -> 0% of each run, Pallas kernels for 16% -> 17%
where the time goes in v7:
time: 157 us; the launch traced here: 156 us
  starting transfers between devices  64.5 us (41%)
  waiting for transfers between devices  49.4 us (31%)
  Pallas kernels  36.7 us (23%)
  local copies, waits for them, and re-layouts  3.85 us (2%)
    ppermute x35, starting transfers between devices, send(): return lax.ppermute(value, BOTH, shifted(**by))  50.6 us
    ppermute x35, waiting for transfers between devices, send(): return lax.ppermute(value, BOTH, shifted(**by))  46.6 us
    pallas_call x1, Pallas kernels, early_product(): pl.pallas_call(early_body, name='early_product', grid_spec=pltpu.Prefetch...  9.17 us
    pallas_call x2, Pallas kernels, late_product(): pl.pallas_call(functools.partial(late_body, half), name='late_product', g...  8.02 us
    ppermute x1, starting transfers between devices, on_device(): part_a = lax.ppermute(prep_a(place, lists, factor_a), BOTH, spread_pairs())  4.92 us
    ppermute x1, starting transfers between devices, on_device(): part_b = lax.ppermute(part_b, BOTH, spread_pairs())  4.91 us
    pallas_call x1, Pallas kernels, prep_b(): pl.pallas_call(prep_b_body, name='prep_b', grid_spec=pltpu.PrefetchScalar...  4.77 us
    pallas_call x1, Pallas kernels, whole_columns(): pl.pallas_call(column_body, name='whole_columns', grid_spec=pltpu.Prefetc...  4.69 us
  transfers between devices with their start and end apart: 38, of which 18 were waited for; matrix products, arithmetic and copies ran while one was open for 0% of the time, Pallas kernels for 17%

profile of v7, /device:TPU:1, one launch (start us, length us, event | category | flops | bytes accessed | tf_op | source)
XLA Modules:
  0.0 156.3 jit_solution(3294663239147408677)
XLA Ops:
  0.6 0.6 pad_add_fusion.place
  1.2 3.3 %prep_a.1 = bf16[12,64,128]{2,1,0:T(8,128)(2,1)} custom-call(s32[2]{0:T(128)} %pad_add_fusion.place, s32[16,12]{1,0:T(8,128)} %rows_a.5, s32[16]{0:T(128)} %counts_a.5, bf16[1536,512]{1,0:T(8,128)(2,1)} %refs_8_.1), custom_call_target="tpu_custom_call" | custom-call | bytes 786432 | tf_op jit(solution)/shard_map/prep_a/pallas_call | solution.py:88
  4.6 4.9 %collective-permute-start = (bf16[12,64,128]{2,1,0:T(8,128)(2,1)}, bf16[12,64,128]{2,1,0:T(8,128)(2,1)S(1)}, u32[]{:S(2)}, u32[]{:S(2)}) collective-permute-start(bf16[12,64,128]{2,1,0:T(8,128)(2,1)} %prep_a.1), channel_id=1, source_target_pairs={{0,0},{1,32},{2,8},{3,40},{4,16},{5,48},{6,24},{7,56},{8,9},{9,41}... | collective-permute-start | bytes 589832 | tf_op jit(solution)/shard_map/ppermute | solution.py:485
  9.5 4.8 %prep_b.1 = bf16[12,64,128]{2,1,0:T(8,128)(2,1)} custom-call(s32[2]{0:T(128)} %pad_add_fusion.place, s32[16,12]{1,0:T(8,128)} %rows_a.5, s32[16]{0:T(128)} %counts_a.5, s32[16,12]{1,0:T(8,128)} %rows_b.3, s32[16]{0:T(128)} %counts_b.3, bf16[1536,512]{1,0:T(8,128)(2,1)} %refs_8_.1, bf16[1536,512]{1,0:T(8,128)(2,1)} %refs_9_.1, bf16[512,512]{1,0:T(8,128)(2,1)} %top.5), custom_call_target="tpu_custom_call" | custom-call | flops 201326592 | bytes 3145728 | tf_op jit(solution)/shard_map/prep_b/pallas_call | solution.py:128
  14.3 4.9 %collective-permute-start.5 = (bf16[12,64,128]{2,1,0:T(8,128)(2,1)}, bf16[12,64,128]{2,1,0:T(8,128)(2,1)S(1)}, u32[]{:S(2)}, u32[]{:S(2)}) collective-permute-start(bf16[12,64,128]{2,1,0:T(8,128)(2,1)} %prep_b.1), channel_id=1, source_target_pairs={{0,0},{1,32},{2,8},{3,40},{4,16},{5,48},{6,24},{7,56},{8,9},{9,41}... | collective-permute-start | bytes 589832 | tf_op jit(solution)/shard_map/ppermute | solution.py:487
  19.2 2.3 %collective-permute-done = bf16[12,64,128]{2,1,0:T(8,128)(2,1)S(1)} collective-permute-done((bf16[12,64,128]{2,1,0:T(8,128)(2,1)}, bf16[12,64,128]{2,1,0:T(8,128)(2,1)S(1)}, u32[]{:S(2)}, u32[]{:S(2)}) %collective-permute-start) | collective-permute-done | bytes 196640 | tf_op jit(solution)/shard_map/ppermute | solution.py:485
  21.4 2.7 %collective-permute-start.2 = (bf16[12,64,128]{2,1,0:T(8,128)(2,1)S(1)}, bf16[12,64,128]{2,1,0:T(8,128)(2,1)S(1)}, u32[]{:S(2)}, u32[]{:S(2)}) collective-permute-start(bf16[12,64,128]{2,1,0:T(8,128)(2,1)S(1)} %collective-permute-done), channel_id=1, source_target_pairs={{0,24},{1,25},{2,26},{3,27},{4,28},{5,29},{6,30},{7,31},{8,0},{9,1... | collective-permute-start | bytes 589832 | tf_op jit(solution)/shard_map/ppermute | solution.py:473
  24.1 0.3 collective-permute-start.3
  24.4 8.3 %collective-permute-start.6 = (bf16[12,64,128]{2,1,0:T(8,128)(2,1)S(1)}, bf16[12,64,128]{2,1,0:T(8,128)(2,1)S(1)}, u32[]{:S(2)}, u32[]{:S(2)}) collective-permute-start(bf16[12,64,128]{2,1,0:T(8,128)(2,1)S(1)} %collective-permute-done.5), channel_id=1, source_target_pairs={{0,32},{1,33},{2,34},{3,35},{4,36},{5,37},{6,38},{7,39},{8,40},{9,... | collective-permute-start | bytes 589832 | tf_op jit(solution)/shard_map/ppermute | solution.py:473
  32.7 2.1 %collective-permute-start.7 = (bf16[12,64,128]{2,1,0:T(8,128)(2,1)S(1)}, bf16[12,64,128]{2,1,0:T(8,128)(2,1)S(1)}, u32[]{:S(2)}, u32[]{:S(2)}) collective-permute-start(bf16[12,64,128]{2,1,0:T(8,128)(2,1)S(1)} %collective-permute-done.5), channel_id=1, source_target_pairs={{0,96},{1,97},{2,98},{3,99},{4,100},{5,101},{6,102},{7,103},{8,104... | collective-permute-start | bytes 589832 | tf_op jit(solution)/shard_map/ppermute | solution.py:473
  34.8 1.3 collective-permute-start.8
  36.1 3.8 %collective-permute-done.2 = bf16[12,64,128]{2,1,0:T(8,128)(2,1)S(1)} collective-permute-done((bf16[12,64,128]{2,1,0:T(8,128)(2,1)S(1)}, bf16[12,64,128]{2,1,0:T(8,128)(2,1)S(1)}, u32[]{:S(2)}, u32[]{:S(2)}) %collective-permute-start.2) | collective-permute-done | bytes 196640 | tf_op jit(solution)/shard_map/ppermute | solution.py:473
  39.9 0.1 pad_maximum_fusion._.a_own
  40.0 0.1 collective-permute-start.4
  40.2 3.1 %collective-permute-done.7 = bf16[12,64,128]{2,1,0:T(8,128)(2,1)S(1)} collective-permute-done((bf16[12,64,128]{2,1,0:T(8,128)(2,1)S(1)}, bf16[12,64,128]{2,1,0:T(8,128)(2,1)S(1)}, u32[]{:S(2)}, u32[]{:S(2)}) %collective-permute-start.7) | collective-permute-done | bytes 196640 | tf_op jit(solution)/shard_map/ppermute | solution.py:473
  43.3 2.1 %collective-permute-done.8 = bf16[12,64,128]{2,1,0:T(8,128)(2,1)S(1)} collective-permute-done((bf16[12,64,128]{2,1,0:T(8,128)(2,1)S(1)}, bf16[12,64,128]{2,1,0:T(8,128)(2,1)S(1)}, u32[]{:S(2)}, u32[]{:S(2)}) %collective-permute-start.8) | collective-permute-done | bytes 196640 | tf_op jit(solution)/shard_map/ppermute | solution.py:473
  45.3 0.1 pad_maximum_fusion.1.b_own
  45.5 1.1 collective-permute-start.9
  46.6 0.5 collective-permute-start.11
  47.1 2.6 %collective-permute-start.14 = (bf16[4,12,64,128]{3,2,1,0:T(8,128)(2,1)S(1)}, bf16[4,12,64,128]{3,2,1,0:T(8,128)(2,1)S(1)}, u32[]{:S(2)}, u32[]{:S(2)}) collective-permute-start(bf16[4,12,64,128]{3,2,1,0:T(8,128)(2,1)S(1)} %pad_maximum_fusion.1.b_own), channel_id=1, source_target_pairs={{0,24},{1,25},{2,26},{3,27},{4,28},{5,29},{6,30},{7,31},{8,0},{9,1... | collective-permute-start | bytes 2359304 | tf_op jit(solution)/shard_map/ppermute | solution.py:473
  49.7 3.7 %copy-done.1 = bf16[1536,3072]{1,0:T(8,128)(2,1)S(1)} copy-done((bf16[1536,3072]{1,0:T(8,128)(2,1)S(1)}, bf16[1536,3072]{1,0:T(8,128)(2,1)}, u32[]{:S(2)}) %copy-start.1) | copy-done | bytes 9437208
  53.4 0.6 hold.1.tile
  54.0 8.3 %collective-permute-done.4.a_down = bf16[4,12,64,128]{3,2,1,0:T(8,128)(2,1)S(1)} collective-permute-done((bf16[4,12,64,128]{3,2,1,0:T(8,128)(2,1)S(1)}, bf16[4,12,64,128]{3,2,1,0:T(8,128)(2,1)S(1)}, u32[]{:S(2)}, u32[]{:S(2)}) %collective-permute-start.4) | collective-permute-done | bytes 786464 | tf_op jit(solution)/shard_map/ppermute | solution.py:473
  62.4 2.5 %collective-permute-done.9.b_down = bf16[4,12,64,128]{3,2,1,0:T(8,128)(2,1)S(1)} collective-permute-done((bf16[4,12,64,128]{3,2,1,0:T(8,128)(2,1)S(1)}, bf16[4,12,64,128]{3,2,1,0:T(8,128)(2,1)S(1)}, u32[]{:S(2)}, u32[]{:S(2)}) %collective-permute-start.9) | collective-permute-done | bytes 786464 | tf_op jit(solution)/shard_map/ppermute | solution.py:473
  64.9 0.8 collective-permute-start.10
  65.7 0.1 collective-permute-start.13
  65.9 2.0 %collective-permute-start.12 = (bf16[2,12,64,128]{3,2,1,0:T(8,128)(2,1)S(1)}, bf16[2,12,64,128]{3,2,1,0:T(8,128)(2,1)S(1)}, u32[]{:S(2)}, u32[]{:S(2)}) collective-permute-start(bf16[2,12,64,128]{3,2,1,0:T(8,128)(2,1)S(1)} %slice.16), channel_id=1, source_target_pairs={{0,96},{1,97},{2,98},{3,99},{4,100},{5,101},{6,102},{7,103},{8,104... | collective-permute-start | bytes 1179656 | tf_op jit(solution)/shard_map/ppermute | solution.py:473
  67.9 2.7 %collective-permute-start.15 = (bf16[2,12,64,128]{3,2,1,0:T(8,128)(2,1)S(1)}, bf16[2,12,64,128]{3,2,1,0:T(8,128)(2,1)S(1)}, u32[]{:S(2)}, u32[]{:S(2)}) collective-permute-start(bf16[2,12,64,128]{3,2,1,0:T(8,128)(2,1)S(1)} %slice.17), channel_id=1, source_target_pairs={{0,24},{1,25},{2,26},{3,27},{4,28},{5,29},{6,30},{7,31},{8,0},{9,1... | collective-permute-start | bytes 1179656 | tf_op jit(solution)/shard_map/ppermute | solution.py:473
  70.6 9.2 %early_product.1.before = bf16[8,128,1536]{2,1,0:T(8,128)(2,1)S(1)} custom-call(s32[2]{0:T(128)S(1)} %copy-done.8, bf16[4,12,64,128]{3,2,1,0:T(8,128)(2,1)S(1)} %collective-permute-done.4.a_down, bf16[4,12,64,128]{3,2,1,0:T(8,128)(2,1)S(1)} %collective-permute-done.11.a_up, bf16[4,12,64,128]{3,2,1,0:T(8,128)(2,1)S(1)} %pad_maximum_fusion.1.b_own, ...), custom_call_target="tpu_custom_call" | custom-call | flops 6039797760 | bytes 7077888 | tf_op jit(solution)/shard_map/early_product/pallas_call | solution.py:228
  79.9 4.0 %late_product.3 = (bf16[4,128,768]{2,1,0:T(8,128)(2,1)S(1)}, bf16[4,128,768]{2,1,0:T(8,128)(2,1)S(1)}) custom-call(s32[2]{0:T(128)S(1)} %copy-done.8, bf16[4,12,64,128]{3,2,1,0:T(8,128)(2,1)S(1)} %pad_maximum_fusion._.a_own, bf16[2,12,64,128]{3,2,1,0:T(8,128)(2,1)S(1)} %collective-permute-done.10.a_far, ...), custom_call_target="tpu_custom_call" | custom-call | flops 1811939328 | bytes 5505024 | tf_op jit(solution)/shard_map/late_product/pallas_call | solution.py:283
  83.9 3.0 %collective-permute-start.20 = (bf16[4,128,768]{2,1,0:T(8,128)(2,1)S(1)}, bf16[4,128,768]{2,1,0:T(8,128)(2,1)S(1)}, u32[]{:S(2)}, u32[]{:S(2)}) collective-permute-start(bf16[4,128,768]{2,1,0:T(8,128)(2,1)S(1)} %get-tuple-element.47), channel_id=1, source_target_pairs={{0,1},{1,0},{2,3},{3,2},{4,5},{5,4},{6,7},{7,6},{8,9},{9,8},{10,11... | collective-permute-start | bytes 2359304 | tf_op jit(solution)/shard_map/ppermute | solution.py:473
  86.9 4.0 %late_product.2 = (bf16[4,128,768]{2,1,0:T(8,128)(2,1)S(1)}, bf16[4,128,768]{2,1,0:T(8,128)(2,1)S(1)}) custom-call(s32[2]{0:T(128)S(1)} %copy-done.8, bf16[4,12,64,128]{3,2,1,0:T(8,128)(2,1)S(1)} %pad_maximum_fusion._.a_own, bf16[2,12,64,128]{3,2,1,0:T(8,128)(2,1)S(1)} %collective-permute-done.10.a_far, ...), custom_call_target="tpu_custom_call" | custom-call | flops 1811939328 | bytes 5505024 | tf_op jit(solution)/shard_map/late_product/pallas_call | solution.py:283
  90.9 0.1 collective-permute-start.16
  91.1 1.1 pair_sum.3
  92.2 5.4 %collective-permute-start.22 = (bf16[128,768]{1,0:T(8,128)(2,1)S(1)}, bf16[128,768]{1,0:T(8,128)(2,1)S(1)}, u32[]{:S(2)}, u32[]{:S(2)}) collective-permute-start(bf16[128,768]{1,0:T(8,128)(2,1)S(1)} %get-tuple-element.50), channel_id=1, source_target_pairs={{0,4},{1,5},{2,6},{3,7},{4,0},{5,1},{6,2},{7,3},{8,12},{9,13},{10,... | collective-permute-start | bytes 589832 | tf_op jit(solution)/shard_map/ppermute | solution.py:473
  97.7 1.1 pair_sum.2
  98.7 1.7 %collective-permute-start.17 = (bf16[128,768]{1,0:T(8,128)(2,1)S(1)}, bf16[128,768]{1,0:T(8,128)(2,1)S(1)}, u32[]{:S(2)}, u32[]{:S(2)}) collective-permute-start(bf16[128,768]{1,0:T(8,128)(2,1)S(1)} %get-tuple-element.43), channel_id=1, source_target_pairs={{0,2},{1,3},{2,4},{3,5},{4,6},{5,7},{6,0},{7,1},{8,10},{9,11},{10,... | collective-permute-start | bytes 589832 | tf_op jit(solution)/shard_map/ppermute | solution.py:473
  100.4 0.9 collective-permute-done.21.refs_5_
  101.3 1.6 %collective-permute-start.19 = (bf16[128,768]{1,0:T(8,128)(2,1)S(1)}, bf16[128,768]{1,0:T(8,128)(2,1)S(1)}, u32[]{:S(2)}, u32[]{:S(2)}) collective-permute-start(bf16[128,768]{1,0:T(8,128)(2,1)S(1)} %get-tuple-element.45), channel_id=1, source_target_pairs={{0,6},{1,7},{2,0},{3,1},{4,2},{5,3},{6,4},{7,5},{8,14},{9,15},{10,... | collective-permute-start | bytes 589832 | tf_op jit(solution)/shard_map/ppermute | solution.py:473
  102.9 3.5 %collective-permute-done.22.refs_6_ = bf16[128,768]{1,0:T(8,128)(2,1)S(1)} collective-permute-done((bf16[128,768]{1,0:T(8,128)(2,1)S(1)}, bf16[128,768]{1,0:T(8,128)(2,1)S(1)}, u32[]{:S(2)}, u32[]{:S(2)}) %collective-permute-start.22) | collective-permute-done | bytes 196640 | tf_op jit(solution)/shard_map/ppermute | solution.py:473
  106.5 3.8 %collective-permute-done.17.refs_1_ = bf16[128,768]{1,0:T(8,128)(2,1)S(1)} collective-permute-done((bf16[128,768]{1,0:T(8,128)(2,1)S(1)}, bf16[128,768]{1,0:T(8,128)(2,1)S(1)}, u32[]{:S(2)}, u32[]{:S(2)}) %collective-permute-start.17) | collective-permute-done | bytes 196640 | tf_op jit(solution)/shard_map/ppermute | solution.py:473
  110.2 4.6 %collective-permute-done.18.refs_2_ = bf16[128,768]{1,0:T(8,128)(2,1)S(1)} collective-permute-done((bf16[128,768]{1,0:T(8,128)(2,1)S(1)}, bf16[128,768]{1,0:T(8,128)(2,1)S(1)}, u32[]{:S(2)}, u32[]{:S(2)}) %collective-permute-start.18) | collective-permute-done | bytes 196640 | tf_op jit(solution)/shard_map/ppermute | solution.py:473
  114.9 1.9 %slots.1 = (bf16[128,1536]{1,0:T(8,128)(2,1)S(1)}, bf16[192,512]{1,0:T(8,128)(2,1)S(1)}) custom-call(s32[2]{0:T(128)S(1)} %copy-done.8, s32[16,12]{1,0:T(8,128)S(1)} %copy-done.6, s32[16]{0:T(128)S(1)} %copy-done.9, s32[16,12]{1,0:T(8,128)S(1)} %copy-done.7, s32[16]{0:T(128)S(1)} %copy-done.10, bf16[128,768]{1,0:T(8,128)(2,1)S(1)} %get-tuple-element.42.refs_0_, ...), custom_call_target="tpu_custom_call" | custom-call | flops 301989888 | bytes 5111808 | tf_op jit(solution)/shard_map/slots/pallas_call | solution.py:357
  116.8 0.3 collective-permute-start.27
  117.1 2.5 %collective-permute-start.28 = (bf16[128,1536]{1,0:T(8,128)(2,1)S(1)}, bf16[128,1536]{1,0:T(8,128)(2,1)S(1)}, u32[]{:S(2)}, u32[]{:S(2)}) collective-permute-start(bf16[128,1536]{1,0:T(8,128)(2,1)S(1)} %get-tuple-element.63.refs_0_), channel_id=1, source_target_pairs={{0,6},{1,7},{2,0},{3,1},{4,2},{5,3},{6,4},{7,5},{8,14},{9,15},{10,... | collective-permute-start | bytes 1179656 | tf_op jit(solution)/shard_map/ppermute | solution.py:473
  119.6 2.7 %collective-permute-start.25 = (bf16[192,512]{1,0:T(8,128)(2,1)S(1)}, bf16[192,512]{1,0:T(8,128)(2,1)S(1)}, u32[]{:S(2)}, u32[]{:S(2)}) collective-permute-start(bf16[192,512]{1,0:T(8,128)(2,1)S(1)} %get-tuple-element.54.one), channel_id=1, source_target_pairs={{0,24},{1,25},{2,26},{3,27},{4,28},{5,29},{6,30},{7,31},{8,0},{9,1... | collective-permute-start | bytes 589832 | tf_op jit(solution)/shard_map/ppermute | solution.py:473
  122.3 3.3 %collective-permute-done.24.two = bf16[192,512]{1,0:T(8,128)(2,1)S(1)} collective-permute-done((bf16[192,512]{1,0:T(8,128)(2,1)S(1)}, bf16[192,512]{1,0:T(8,128)(2,1)S(1)}, u32[]{:S(2)}, u32[]{:S(2)}) %collective-permute-start.24) | collective-permute-done | bytes 196640 | tf_op jit(solution)/shard_map/ppermute | solution.py:473
  125.6 1.6 %collective-permute-done.25.three = bf16[192,512]{1,0:T(8,128)(2,1)S(1)} collective-permute-done((bf16[192,512]{1,0:T(8,128)(2,1)S(1)}, bf16[192,512]{1,0:T(8,128)(2,1)S(1)}, u32[]{:S(2)}, u32[]{:S(2)}) %collective-permute-start.25) | collective-permute-done | bytes 196640 | tf_op jit(solution)/shard_map/ppermute | solution.py:473
  127.3 1.5 collective-permute-done.26.four
  128.8 0.1 fold.1.one
  128.9 1.9 %collective-permute-start.32 = (bf16[128,1536]{1,0:T(8,128)(2,1)S(1)}, bf16[128,1536]{1,0:T(8,128)(2,1)S(1)}, u32[]{:S(2)}, u32[]{:S(2)}) collective-permute-start(bf16[128,1536]{1,0:T(8,128)(2,1)S(1)} %get-tuple-element.63.refs_0_), channel_id=1, source_target_pairs={{0,4},{1,5},{2,6},{3,7},{4,0},{5,1},{6,2},{7,3},{8,12},{9,13},{10,... | collective-permute-start | bytes 1179656 | tf_op jit(solution)/shard_map/ppermute | solution.py:473
  130.8 0.4 collective-permute-start.29
  131.1 2.3 %collective-permute-start.30 = (bf16[192,512]{1,0:T(8,128)(2,1)S(1)}, bf16[192,512]{1,0:T(8,128)(2,1)S(1)}, u32[]{:S(2)}, u32[]{:S(2)}) collective-permute-start(bf16[192,512]{1,0:T(8,128)(2,1)S(1)} %fold.1.one), channel_id=1, source_target_pairs={{0,96},{1,97},{2,98},{3,99},{4,100},{5,101},{6,102},{7,103},{8,104... | collective-permute-start | bytes 589832 | tf_op jit(solution)/shard_map/ppermute | solution.py:473
  133.4 0.2 collective-permute-start.31
  133.7 2.8 %collective-permute-done.29.two = bf16[192,512]{1,0:T(8,128)(2,1)S(1)} collective-permute-done((bf16[192,512]{1,0:T(8,128)(2,1)S(1)}, bf16[192,512]{1,0:T(8,128)(2,1)S(1)}, u32[]{:S(2)}, u32[]{:S(2)}) %collective-permute-start.29) | collective-permute-done | bytes 196640 | tf_op jit(solution)/shard_map/ppermute | solution.py:473
  136.5 1.7 %collective-permute-done.30.three = bf16[192,512]{1,0:T(8,128)(2,1)S(1)} collective-permute-done((bf16[192,512]{1,0:T(8,128)(2,1)S(1)}, bf16[192,512]{1,0:T(8,128)(2,1)S(1)}, u32[]{:S(2)}, u32[]{:S(2)}) %collective-permute-start.30) | collective-permute-done | bytes 196640 | tf_op jit(solution)/shard_map/ppermute | solution.py:473
  138.2 2.7 %collective-permute-done.31.four = bf16[192,512]{1,0:T(8,128)(2,1)S(1)} collective-permute-done((bf16[192,512]{1,0:T(8,128)(2,1)S(1)}, bf16[192,512]{1,0:T(8,128)(2,1)S(1)}, u32[]{:S(2)}, u32[]{:S(2)}) %collective-permute-start.31) | collective-permute-done | bytes 196640 | tf_op jit(solution)/shard_map/ppermute | solution.py:473
  141.0 3.4 %collective-permute-start.33 = (bf16[128,1536]{1,0:T(8,128)(2,1)S(1)}, bf16[128,1536]{1,0:T(8,128)(2,1)S(1)}, u32[]{:S(2)}, u32[]{:S(2)}) collective-permute-start(bf16[128,1536]{1,0:T(8,128)(2,1)S(1)} %get-tuple-element.63.refs_0_), channel_id=1, source_target_pairs={{0,1},{1,0},{2,3},{3,2},{4,5},{5,4},{6,7},{7,6},{8,9},{9,8},{10,11... | collective-permute-start | bytes 1179656 | tf_op jit(solution)/shard_map/ppermute | solution.py:473
  144.4 0.5 collective-permute-start.35
  144.9 1.1 top_part.1
  146.0 4.1 %all-to-all-start = ((bf16[8,64,128]{2,1,0:T(8,128)(2,1)}), bf16[8,64,128]{2,1,0:T(8,128)(2,1)S(1)}, u32[]{:S(2)}, u32[]{:S(2)}) async-start(bf16[8,64,128]{2,1,0:T(8,128)(2,1)} %get-tuple-element.64), calls=%async_computation | async-start | bytes 262144 | tf_op jit(solution)/shard_map/all_to_all | solution.py:514
  150.2 4.7 %whole_columns.1 = (bf16[1536,512]{1,0:T(8,128)(2,1)}, bf16[1536,512]{1,0:T(8,128)(2,1)}) custom-call(s32[2]{0:T(128)S(1)} %copy-done.8, bf16[128,1536]{1,0:T(8,128)(2,1)S(1)} %get-tuple-element.63.refs_0_, bf16[128,1536]{1,0:T(8,128)(2,1)S(1)} %collective-permute-done.27.refs_1_, bf16[128,1536]{1,0:T(8,128)(2,1)S(1)} %collective-permute-done.28.refs_2_, ...), custom_call_target="tpu_custom_call" | custom-call | bytes 6291456 | tf_op jit(solution)/shard_map/whole_columns/pallas_call | solution.py:389
  154.9 0.5 all-to-all-done.taken
  155.4 0.9 last_part.1
  (54 shorter events, 0.4 us)
Async XLA Ops:
  4.6 16.9 %collective-permute-start = (bf16[12,64,128]{2,1,0:T(8,128)(2,1)}, bf16[12,64,128]{2,1,0:T(8,128)(2,1)S(1)}, u32[]{:S(2)}, u32[]{:S(2)}) collective-permute-start(bf16[12,64,128]{2,1,0:T(8,128)(2,1)} %prep_a.1), channel_id=1, source_target_pairs={{0,0},{1,32},{2,8},{3,40},{4,16},{5,48},{6,24},{7,56},{8,9},{9,41}... | collective-permute-start | bytes 589832 | tf_op jit(solution)/shard_map/ppermute | solution.py:485
  14.3 10.1 %collective-permute-start.5 = (bf16[12,64,128]{2,1,0:T(8,128)(2,1)}, bf16[12,64,128]{2,1,0:T(8,128)(2,1)S(1)}, u32[]{:S(2)}, u32[]{:S(2)}) collective-permute-start(bf16[12,64,128]{2,1,0:T(8,128)(2,1)} %prep_b.1), channel_id=1, source_target_pairs={{0,0},{1,32},{2,8},{3,40},{4,16},{5,48},{6,24},{7,56},{8,9},{9,41}... | collective-permute-start | bytes 589832 | tf_op jit(solution)/shard_map/ppermute | solution.py:487
  21.4 13.3 %collective-permute-start.1 = (bf16[12,64,128]{2,1,0:T(8,128)(2,1)S(1)}, bf16[12,64,128]{2,1,0:T(8,128)(2,1)S(1)}, u32[]{:S(2)}, u32[]{:S(2)}) collective-permute-start(bf16[12,64,128]{2,1,0:T(8,128)(2,1)S(1)} %collective-permute-done), channel_id=1, source_target_pairs={{0,8},{1,9},{2,10},{3,11},{4,12},{5,13},{6,14},{7,15},{8,16},{9,17... | collective-permute-start | bytes 589832 | tf_op jit(solution)/shard_map/ppermute | solution.py:473
  21.4 18.5 %collective-permute-start.2 = (bf16[12,64,128]{2,1,0:T(8,128)(2,1)S(1)}, bf16[12,64,128]{2,1,0:T(8,128)(2,1)S(1)}, u32[]{:S(2)}, u32[]{:S(2)}) collective-permute-start(bf16[12,64,128]{2,1,0:T(8,128)(2,1)S(1)} %collective-permute-done), channel_id=1, source_target_pairs={{0,24},{1,25},{2,26},{3,27},{4,28},{5,29},{6,30},{7,31},{8,0},{9,1... | collective-permute-start | bytes 589832 | tf_op jit(solution)/shard_map/ppermute | solution.py:473
  24.1 15.8 %collective-permute-start.3 = (bf16[12,64,128]{2,1,0:T(8,128)(2,1)S(1)}, bf16[12,64,128]{2,1,0:T(8,128)(2,1)S(1)}, u32[]{:S(2)}, u32[]{:S(2)}) collective-permute-start(bf16[12,64,128]{2,1,0:T(8,128)(2,1)S(1)} %collective-permute-done), channel_id=1, source_target_pairs={{0,16},{1,17},{2,18},{3,19},{4,20},{5,21},{6,22},{7,23},{8,24},{9,... | collective-permute-start | bytes 589832 | tf_op jit(solution)/shard_map/ppermute | solution.py:473
  24.4 15.8 %collective-permute-start.6 = (bf16[12,64,128]{2,1,0:T(8,128)(2,1)S(1)}, bf16[12,64,128]{2,1,0:T(8,128)(2,1)S(1)}, u32[]{:S(2)}, u32[]{:S(2)}) collective-permute-start(bf16[12,64,128]{2,1,0:T(8,128)(2,1)S(1)} %collective-permute-done.5), channel_id=1, source_target_pairs={{0,32},{1,33},{2,34},{3,35},{4,36},{5,37},{6,38},{7,39},{8,40},{9,... | collective-permute-start | bytes 589832 | tf_op jit(solution)/shard_map/ppermute | solution.py:473
  32.7 10.6 %collective-permute-start.7 = (bf16[12,64,128]{2,1,0:T(8,128)(2,1)S(1)}, bf16[12,64,128]{2,1,0:T(8,128)(2,1)S(1)}, u32[]{:S(2)}, u32[]{:S(2)}) collective-permute-start(bf16[12,64,128]{2,1,0:T(8,128)(2,1)S(1)} %collective-permute-done.5), channel_id=1, source_target_pairs={{0,96},{1,97},{2,98},{3,99},{4,100},{5,101},{6,102},{7,103},{8,104... | collective-permute-start | bytes 589832 | tf_op jit(solution)/shard_map/ppermute | solution.py:473
  34.8 10.6 %collective-permute-start.8 = (bf16[12,64,128]{2,1,0:T(8,128)(2,1)S(1)}, bf16[12,64,128]{2,1,0:T(8,128)(2,1)S(1)}, u32[]{:S(2)}, u32[]{:S(2)}) collective-permute-start(bf16[12,64,128]{2,1,0:T(8,128)(2,1)S(1)} %collective-permute-done.5), channel_id=1, source_target_pairs={{0,64},{1,65},{2,66},{3,67},{4,68},{5,69},{6,70},{7,71},{8,72},{9,... | collective-permute-start | bytes 589832 | tf_op jit(solution)/shard_map/ppermute | solution.py:473
  40.0 22.3 %collective-permute-start.4 = (bf16[4,12,64,128]{3,2,1,0:T(8,128)(2,1)S(1)}, bf16[4,12,64,128]{3,2,1,0:T(8,128)(2,1)S(1)}, u32[]{:S(2)}, u32[]{:S(2)}) collective-permute-start(bf16[4,12,64,128]{3,2,1,0:T(8,128)(2,1)S(1)} %pad_maximum_fusion._.a_own), channel_id=1, source_target_pairs={{0,32},{1,33},{2,34},{3,35},{4,36},{5,37},{6,38},{7,39},{8,40},{9,... | collective-permute-start | bytes 2359304 | tf_op jit(solution)/shard_map/ppermute | solution.py:473
  45.5 19.4 %collective-permute-start.9 = (bf16[4,12,64,128]{3,2,1,0:T(8,128)(2,1)S(1)}, bf16[4,12,64,128]{3,2,1,0:T(8,128)(2,1)S(1)}, u32[]{:S(2)}, u32[]{:S(2)}) collective-permute-start(bf16[4,12,64,128]{3,2,1,0:T(8,128)(2,1)S(1)} %pad_maximum_fusion.1.b_own), channel_id=1, source_target_pairs={{0,8},{1,9},{2,10},{3,11},{4,12},{5,13},{6,14},{7,15},{8,16},{9,17... | collective-permute-start | bytes 2359304 | tf_op jit(solution)/shard_map/ppermute | solution.py:473
  46.6 19.3 %collective-permute-start.11 = (bf16[4,12,64,128]{3,2,1,0:T(8,128)(2,1)S(1)}, bf16[4,12,64,128]{3,2,1,0:T(8,128)(2,1)S(1)}, u32[]{:S(2)}, u32[]{:S(2)}) collective-permute-start(bf16[4,12,64,128]{3,2,1,0:T(8,128)(2,1)S(1)} %pad_maximum_fusion._.a_own), channel_id=1, source_target_pairs={{0,96},{1,97},{2,98},{3,99},{4,100},{5,101},{6,102},{7,103},{8,104... | collective-permute-start | bytes 2359304 | tf_op jit(solution)/shard_map/ppermute | solution.py:473
  47.1 20.8 %collective-permute-start.14 = (bf16[4,12,64,128]{3,2,1,0:T(8,128)(2,1)S(1)}, bf16[4,12,64,128]{3,2,1,0:T(8,128)(2,1)S(1)}, u32[]{:S(2)}, u32[]{:S(2)}) collective-permute-start(bf16[4,12,64,128]{3,2,1,0:T(8,128)(2,1)S(1)} %pad_maximum_fusion.1.b_own), channel_id=1, source_target_pairs={{0,24},{1,25},{2,26},{3,27},{4,28},{5,29},{6,30},{7,31},{8,0},{9,1... | collective-permute-start | bytes 2359304 | tf_op jit(solution)/shard_map/ppermute | solution.py:473
  49.7 3.7 %copy-start.1 = (bf16[1536,3072]{1,0:T(8,128)(2,1)S(1)}, bf16[1536,3072]{1,0:T(8,128)(2,1)}, u32[]{:S(2)}) copy-start(bf16[1536,3072]{1,0:T(8,128)(2,1)} %source.1) | copy-start | bytes 28311556
  54.0 16.6 %copy-start.8 = (s32[2]{0:T(128)S(1)}, s32[2]{0:T(128)}, u32[]{:S(2)}) copy-start(s32[2]{0:T(128)} %pad_add_fusion.place) | copy-start | bytes 28
  64.9 14.9 %collective-permute-start.10 = (bf16[2,12,64,128]{3,2,1,0:T(8,128)(2,1)S(1)}, bf16[2,12,64,128]{3,2,1,0:T(8,128)(2,1)S(1)}, u32[]{:S(2)}, u32[]{:S(2)}) collective-permute-start(bf16[2,12,64,128]{3,2,1,0:T(8,128)(2,1)S(1)} %slice.12), channel_id=1, source_target_pairs={{0,32},{1,33},{2,34},{3,35},{4,36},{5,37},{6,38},{7,39},{8,40},{9,... | collective-permute-start | bytes 1179656 | tf_op jit(solution)/shard_map/ppermute | solution.py:473
  65.7 14.1 %collective-permute-start.13 = (bf16[2,12,64,128]{3,2,1,0:T(8,128)(2,1)S(1)}, bf16[2,12,64,128]{3,2,1,0:T(8,128)(2,1)S(1)}, u32[]{:S(2)}, u32[]{:S(2)}) collective-permute-start(bf16[2,12,64,128]{3,2,1,0:T(8,128)(2,1)S(1)} %slice.14), channel_id=1, source_target_pairs={{0,8},{1,9},{2,10},{3,11},{4,12},{5,13},{6,14},{7,15},{8,16},{9,17... | collective-permute-start | bytes 1179656 | tf_op jit(solution)/shard_map/ppermute | solution.py:473
  65.9 14.0 %collective-permute-start.12 = (bf16[2,12,64,128]{3,2,1,0:T(8,128)(2,1)S(1)}, bf16[2,12,64,128]{3,2,1,0:T(8,128)(2,1)S(1)}, u32[]{:S(2)}, u32[]{:S(2)}) collective-permute-start(bf16[2,12,64,128]{3,2,1,0:T(8,128)(2,1)S(1)} %slice.16), channel_id=1, source_target_pairs={{0,96},{1,97},{2,98},{3,99},{4,100},{5,101},{6,102},{7,103},{8,104... | collective-permute-start | bytes 1179656 | tf_op jit(solution)/shard_map/ppermute | solution.py:473
  67.9 11.9 %collective-permute-start.15 = (bf16[2,12,64,128]{3,2,1,0:T(8,128)(2,1)S(1)}, bf16[2,12,64,128]{3,2,1,0:T(8,128)(2,1)S(1)}, u32[]{:S(2)}, u32[]{:S(2)}) collective-permute-start(bf16[2,12,64,128]{3,2,1,0:T(8,128)(2,1)S(1)} %slice.17), channel_id=1, source_target_pairs={{0,24},{1,25},{2,26},{3,27},{4,28},{5,29},{6,30},{7,31},{8,0},{9,1... | collective-permute-start | bytes 1179656 | tf_op jit(solution)/shard_map/ppermute | solution.py:473
  83.9 7.1 %collective-permute-start.20 = (bf16[4,128,768]{2,1,0:T(8,128)(2,1)S(1)}, bf16[4,128,768]{2,1,0:T(8,128)(2,1)S(1)}, u32[]{:S(2)}, u32[]{:S(2)}) collective-permute-start(bf16[4,128,768]{2,1,0:T(8,128)(2,1)S(1)} %get-tuple-element.47), channel_id=1, source_target_pairs={{0,1},{1,0},{2,3},{3,2},{4,5},{5,4},{6,7},{7,6},{8,9},{9,8},{10,11... | collective-permute-start | bytes 2359304 | tf_op jit(solution)/shard_map/ppermute | solution.py:473
  90.9 6.8 %collective-permute-start.16 = (bf16[4,128,768]{2,1,0:T(8,128)(2,1)S(1)}, bf16[4,128,768]{2,1,0:T(8,128)(2,1)S(1)}, u32[]{:S(2)}, u32[]{:S(2)}) collective-permute-start(bf16[4,128,768]{2,1,0:T(8,128)(2,1)S(1)} %get-tuple-element.41), channel_id=1, source_target_pairs={{0,1},{1,0},{2,3},{3,2},{4,5},{5,4},{6,7},{7,6},{8,9},{9,8},{10,11... | collective-permute-start | bytes 2359304 | tf_op jit(solution)/shard_map/ppermute | solution.py:473
  91.0 23.9 %copy-start = (bf16[1536,512]{1,0:T(8,128)(2,1)S(1)}, bf16[1536,512]{1,0:T(8,128)(2,1)}, u32[]{:S(2)}) copy-start(bf16[1536,512]{1,0:T(8,128)(2,1)} %refs_8_.1) | copy-start | bytes 4718596
  91.0 23.9 %copy-start.2 = (bf16[1536,512]{1,0:T(8,128)(2,1)S(1)}, bf16[1536,512]{1,0:T(8,128)(2,1)}, u32[]{:S(2)}) copy-start(bf16[1536,512]{1,0:T(8,128)(2,1)} %refs_9_.1) | copy-start | bytes 4718596
  91.0 23.9 %copy-start.6 = (s32[16,12]{1,0:T(8,128)S(1)}, s32[16,12]{1,0:T(8,128)}, u32[]{:S(2)}) copy-start(s32[16,12]{1,0:T(8,128)} %rows_a.5) | copy-start | bytes 2308
  91.0 23.9 %copy-start.7 = (s32[16,12]{1,0:T(8,128)S(1)}, s32[16,12]{1,0:T(8,128)}, u32[]{:S(2)}) copy-start(s32[16,12]{1,0:T(8,128)} %rows_b.3) | copy-start | bytes 2308
  91.0 23.9 %copy-start.9 = (s32[16]{0:T(128)S(1)}, s32[16]{0:T(128)}, u32[]{:S(2)}) copy-start(s32[16]{0:T(128)} %counts_a.5) | copy-start | bytes 196
  91.1 23.9 %copy-start.10 = (s32[16]{0:T(128)S(1)}, s32[16]{0:T(128)}, u32[]{:S(2)}) copy-start(s32[16]{0:T(128)} %counts_b.3) | copy-start | bytes 196
  92.1 9.2 %collective-permute-start.21 = (bf16[128,768]{1,0:T(8,128)(2,1)S(1)}, bf16[128,768]{1,0:T(8,128)(2,1)S(1)}, u32[]{:S(2)}, u32[]{:S(2)}) collective-permute-start(bf16[128,768]{1,0:T(8,128)(2,1)S(1)} %get-tuple-element.49), channel_id=1, source_target_pairs={{0,2},{1,3},{2,4},{3,5},{4,6},{5,7},{6,0},{7,1},{8,10},{9,11},{10,... | collective-permute-start | bytes 589832 | tf_op jit(solution)/shard_map/ppermute | solution.py:473
  92.2 14.2 %collective-permute-start.22 = (bf16[128,768]{1,0:T(8,128)(2,1)S(1)}, bf16[128,768]{1,0:T(8,128)(2,1)S(1)}, u32[]{:S(2)}, u32[]{:S(2)}) collective-permute-start(bf16[128,768]{1,0:T(8,128)(2,1)S(1)} %get-tuple-element.50), channel_id=1, source_target_pairs={{0,4},{1,5},{2,6},{3,7},{4,0},{5,1},{6,2},{7,3},{8,12},{9,13},{10,... | collective-permute-start | bytes 589832 | tf_op jit(solution)/shard_map/ppermute | solution.py:473
  97.7 8.8 %collective-permute-start.23 = (bf16[128,768]{1,0:T(8,128)(2,1)S(1)}, bf16[128,768]{1,0:T(8,128)(2,1)S(1)}, u32[]{:S(2)}, u32[]{:S(2)}) collective-permute-start(bf16[128,768]{1,0:T(8,128)(2,1)S(1)} %get-tuple-element.51), channel_id=1, source_target_pairs={{0,6},{1,7},{2,0},{3,1},{4,2},{5,3},{6,4},{7,5},{8,14},{9,15},{10,... | collective-permute-start | bytes 589832 | tf_op jit(solution)/shard_map/ppermute | solution.py:473
  98.7 11.5 %collective-permute-start.17 = (bf16[128,768]{1,0:T(8,128)(2,1)S(1)}, bf16[128,768]{1,0:T(8,128)(2,1)S(1)}, u32[]{:S(2)}, u32[]{:S(2)}) collective-permute-start(bf16[128,768]{1,0:T(8,128)(2,1)S(1)} %get-tuple-element.43), channel_id=1, source_target_pairs={{0,2},{1,3},{2,4},{3,5},{4,6},{5,7},{6,0},{7,1},{8,10},{9,11},{10,... | collective-permute-start | bytes 589832 | tf_op jit(solution)/shard_map/ppermute | solution.py:473
  100.4 14.4 %collective-permute-start.18 = (bf16[128,768]{1,0:T(8,128)(2,1)S(1)}, bf16[128,768]{1,0:T(8,128)(2,1)S(1)}, u32[]{:S(2)}, u32[]{:S(2)}) collective-permute-start(bf16[128,768]{1,0:T(8,128)(2,1)S(1)} %get-tuple-element.44), channel_id=1, source_target_pairs={{0,4},{1,5},{2,6},{3,7},{4,0},{5,1},{6,2},{7,3},{8,12},{9,13},{10,... | collective-permute-start | bytes 589832 | tf_op jit(solution)/shard_map/ppermute | solution.py:473
  101.3 13.5 %collective-permute-start.19 = (bf16[128,768]{1,0:T(8,128)(2,1)S(1)}, bf16[128,768]{1,0:T(8,128)(2,1)S(1)}, u32[]{:S(2)}, u32[]{:S(2)}) collective-permute-start(bf16[128,768]{1,0:T(8,128)(2,1)S(1)} %get-tuple-element.45), channel_id=1, source_target_pairs={{0,6},{1,7},{2,0},{3,1},{4,2},{5,3},{6,4},{7,5},{8,14},{9,15},{10,... | collective-permute-start | bytes 589832 | tf_op jit(solution)/shard_map/ppermute | solution.py:473
  114.9 30.0 %copy-start.3 = (bf16[512,512]{1,0:T(8,128)(2,1)S(1)}, bf16[512,512]{1,0:T(8,128)(2,1)}, u32[]{:S(2)}) copy-start(bf16[512,512]{1,0:T(8,128)(2,1)} %top.5) | copy-start | bytes 1572868
  114.9 29.9 %copy-start.4 = (f32[64,512]{1,0:T(8,128)S(1)}, f32[64,512]{1,0:T(8,128)}, u32[]{:S(2)}) copy-start(f32[64,512]{1,0:T(8,128)} %base.1) | copy-start | bytes 393220
  116.8 12.0 %collective-permute-start.27 = (bf16[128,1536]{1,0:T(8,128)(2,1)S(1)}, bf16[128,1536]{1,0:T(8,128)(2,1)S(1)}, u32[]{:S(2)}, u32[]{:S(2)}) collective-permute-start(bf16[128,1536]{1,0:T(8,128)(2,1)S(1)} %get-tuple-element.63.refs_0_), channel_id=1, source_target_pairs={{0,2},{1,3},{2,4},{3,5},{4,6},{5,7},{6,0},{7,1},{8,10},{9,11},{10,... | collective-permute-start | bytes 1179656 | tf_op jit(solution)/shard_map/ppermute | solution.py:473
  117.1 11.6 %collective-permute-start.28 = (bf16[128,1536]{1,0:T(8,128)(2,1)S(1)}, bf16[128,1536]{1,0:T(8,128)(2,1)S(1)}, u32[]{:S(2)}, u32[]{:S(2)}) collective-permute-start(bf16[128,1536]{1,0:T(8,128)(2,1)S(1)} %get-tuple-element.63.refs_0_), channel_id=1, source_target_pairs={{0,6},{1,7},{2,0},{3,1},{4,2},{5,3},{6,4},{7,5},{8,14},{9,15},{10,... | collective-permute-start | bytes 1179656 | tf_op jit(solution)/shard_map/ppermute | solution.py:473
  119.6 6.0 %collective-permute-start.24 = (bf16[192,512]{1,0:T(8,128)(2,1)S(1)}, bf16[192,512]{1,0:T(8,128)(2,1)S(1)}, u32[]{:S(2)}, u32[]{:S(2)}) collective-permute-start(bf16[192,512]{1,0:T(8,128)(2,1)S(1)} %get-tuple-element.54.one), channel_id=1, source_target_pairs={{0,8},{1,9},{2,10},{3,11},{4,12},{5,13},{6,14},{7,15},{8,16},{9,17... | collective-permute-start | bytes 589832 | tf_op jit(solution)/shard_map/ppermute | solution.py:473
  119.6 7.7 %collective-permute-start.25 = (bf16[192,512]{1,0:T(8,128)(2,1)S(1)}, bf16[192,512]{1,0:T(8,128)(2,1)S(1)}, u32[]{:S(2)}, u32[]{:S(2)}) collective-permute-start(bf16[192,512]{1,0:T(8,128)(2,1)S(1)} %get-tuple-element.54.one), channel_id=1, source_target_pairs={{0,24},{1,25},{2,26},{3,27},{4,28},{5,29},{6,30},{7,31},{8,0},{9,1... | collective-permute-start | bytes 589832 | tf_op jit(solution)/shard_map/ppermute | solution.py:473
  122.3 6.5 %collective-permute-start.26 = (bf16[192,512]{1,0:T(8,128)(2,1)S(1)}, bf16[192,512]{1,0:T(8,128)(2,1)S(1)}, u32[]{:S(2)}, u32[]{:S(2)}) collective-permute-start(bf16[192,512]{1,0:T(8,128)(2,1)S(1)} %get-tuple-element.54.one), channel_id=1, source_target_pairs={{0,16},{1,17},{2,18},{3,19},{4,20},{5,21},{6,22},{7,23},{8,24},{9,... | collective-permute-start | bytes 589832 | tf_op jit(solution)/shard_map/ppermute | solution.py:473
  128.9 17.1 %collective-permute-start.32 = (bf16[128,1536]{1,0:T(8,128)(2,1)S(1)}, bf16[128,1536]{1,0:T(8,128)(2,1)S(1)}, u32[]{:S(2)}, u32[]{:S(2)}) collective-permute-start(bf16[128,1536]{1,0:T(8,128)(2,1)S(1)} %get-tuple-element.63.refs_0_), channel_id=1, source_target_pairs={{0,4},{1,5},{2,6},{3,7},{4,0},{5,1},{6,2},{7,3},{8,12},{9,13},{10,... | collective-permute-start | bytes 1179656 | tf_op jit(solution)/shard_map/ppermute | solution.py:473
  130.8 5.7 %collective-permute-start.29 = (bf16[192,512]{1,0:T(8,128)(2,1)S(1)}, bf16[192,512]{1,0:T(8,128)(2,1)S(1)}, u32[]{:S(2)}, u32[]{:S(2)}) collective-permute-start(bf16[192,512]{1,0:T(8,128)(2,1)S(1)} %fold.1.one), channel_id=1, source_target_pairs={{0,32},{1,33},{2,34},{3,35},{4,36},{5,37},{6,38},{7,39},{8,40},{9,... | collective-permute-start | bytes 589832 | tf_op jit(solution)/shard_map/ppermute | solution.py:473
  131.1 7.1 %collective-permute-start.30 = (bf16[192,512]{1,0:T(8,128)(2,1)S(1)}, bf16[192,512]{1,0:T(8,128)(2,1)S(1)}, u32[]{:S(2)}, u32[]{:S(2)}) collective-permute-start(bf16[192,512]{1,0:T(8,128)(2,1)S(1)} %fold.1.one), channel_id=1, source_target_pairs={{0,96},{1,97},{2,98},{3,99},{4,100},{5,101},{6,102},{7,103},{8,104... | collective-permute-start | bytes 589832 | tf_op jit(solution)/shard_map/ppermute | solution.py:473
  133.4 7.5 %collective-permute-start.31 = (bf16[192,512]{1,0:T(8,128)(2,1)S(1)}, bf16[192,512]{1,0:T(8,128)(2,1)S(1)}, u32[]{:S(2)}, u32[]{:S(2)}) collective-permute-start(bf16[192,512]{1,0:T(8,128)(2,1)S(1)} %fold.1.one), channel_id=1, source_target_pairs={{0,64},{1,65},{2,66},{3,67},{4,68},{5,69},{6,70},{7,71},{8,72},{9,... | collective-permute-start | bytes 589832 | tf_op jit(solution)/shard_map/ppermute | solution.py:473
  141.0 9.2 %collective-permute-start.33 = (bf16[128,1536]{1,0:T(8,128)(2,1)S(1)}, bf16[128,1536]{1,0:T(8,128)(2,1)S(1)}, u32[]{:S(2)}, u32[]{:S(2)}) collective-permute-start(bf16[128,1536]{1,0:T(8,128)(2,1)S(1)} %get-tuple-element.63.refs_0_), channel_id=1, source_target_pairs={{0,1},{1,0},{2,3},{3,2},{4,5},{5,4},{6,7},{7,6},{8,9},{9,8},{10,11... | collective-permute-start | bytes 1179656 | tf_op jit(solution)/shard_map/ppermute | solution.py:473
  144.4 5.8 %collective-permute-start.34 = (bf16[128,1536]{1,0:T(8,128)(2,1)S(1)}, bf16[128,1536]{1,0:T(8,128)(2,1)}, u32[]{:S(2)}, u32[]{:S(2)}) collective-permute-start(bf16[128,1536]{1,0:T(8,128)(2,1)S(1)} %collective-permute-done.27.refs_1_), channel_id=1, source_target_pairs={{0,1},{1,0},{2,3},{3,2},{4,5},{5,4},{6,7},{7,6},{8,9},{9,8},{10,11... | collective-permute-start | bytes 1179656 | tf_op jit(solution)/shard_map/ppermute | solution.py:473
  144.4 5.8 %collective-permute-start.35 = (bf16[128,1536]{1,0:T(8,128)(2,1)S(1)}, bf16[128,1536]{1,0:T(8,128)(2,1)}, u32[]{:S(2)}, u32[]{:S(2)}) collective-permute-start(bf16[128,1536]{1,0:T(8,128)(2,1)S(1)} %collective-permute-done.28.refs_2_), channel_id=1, source_target_pairs={{0,1},{1,0},{2,3},{3,2},{4,5},{5,4},{6,7},{7,6},{8,9},{9,8},{10,11... | collective-permute-start | bytes 1179656 | tf_op jit(solution)/shard_map/ppermute | solution.py:473
  146.0 4.1 %collective-permute-start.36 = (bf16[128,1536]{1,0:T(8,128)(2,1)S(1)}, bf16[128,1536]{1,0:T(8,128)(2,1)}, u32[]{:S(2)}, u32[]{:S(2)}) collective-permute-start(bf16[128,1536]{1,0:T(8,128)(2,1)S(1)} %collective-permute-done.32.refs_3_), channel_id=1, source_target_pairs={{0,1},{1,0},{2,3},{3,2},{4,5},{5,4},{6,7},{7,6},{8,9},{9,8},{10,11... | collective-permute-start | bytes 1179656 | tf_op jit(solution)/shard_map/ppermute | solution.py:473
  146.0 9.4 %all-to-all-start = ((bf16[8,64,128]{2,1,0:T(8,128)(2,1)}), bf16[8,64,128]{2,1,0:T(8,128)(2,1)S(1)}, u32[]{:S(2)}, u32[]{:S(2)}) async-start(bf16[8,64,128]{2,1,0:T(8,128)(2,1)} %get-tuple-element.64), calls=%async_computation | async-start | bytes 262144 | tf_op jit(solution)/shard_map/all_to_all | solution.py:514
  150.1 5.3 %copy-start.5 = (f32[64,512]{1,0:T(8,128)S(1)}, f32[64,512]{1,0:T(8,128)}, u32[]{:S(2)}) copy-start(f32[64,512]{1,0:T(8,128)} %base.2) | copy-start | bytes 393220

commit v8 on v6

--- a/solution.py
+++ b/solution.py
@@ -202,7 +202,64 @@
     return tile[pl.ds(pl.multiple_of(step * STRIP, STRIP), STRIP), :]
 
 
-def early_body(place, a_down, a_up, b_own, b_down, b_up, tile, out, spread, sems):
+def half_multiply(spread, tile, step, h):
+    rows = pl.ds(pl.multiple_of(step * STRIP, STRIP), STRIP)
+    left = jnp.concatenate([spread[n] for n in range(NB)], axis=1)
+    right = jnp.concatenate(
+        [tile[rows, pl.ds(pl.multiple_of((2 * n + h) * BS, BS), BS)] for n in range(NB)], axis=1
+    )
+    return lax.dot_general(left, right, (((1,), (1,)), ((), ())), preferred_element_type=F32)
+
+
+def load_half(copies, buf, spread, start=0, many=SIDE):
+    for i in range(start, start + many):
+        copies.append((buf.at[i - start], spread.at[:, i * PART : (i + 1) * PART, :]))
+
+
+def own_body(place, a_own, b_own, tile, half_a, whole_b, spread_a, spread_b, sems):
+    u, _ = where(place)
+
+    @pl.when(pl.program_id(0) == 0)
+    def _():
+        copies = []
+        load_half(copies, a_own, spread_a)
+        load_b(copies, b_own, u, 0, spread_b)
+        run_copies(copies, sems)
+
+    half_a[...] = half_multiply(spread_a, tile, pl.program_id(0), u // 2)
+    whole_b[...] = multiply(spread_b, rows_of(tile, pl.program_id(0)))
+
+
+def own_product(place, a_own, b_own, trailing):
+    deep = trailing.shape[1]
+    return pl.pallas_call(
+        own_body,
+        name="own_product",
+        grid_spec=pltpu.PrefetchScalarGridSpec(
+            num_scalar_prefetch=1,
+            grid=(ROWS // STRIP,),
+            in_specs=[pl.BlockSpec(memory_space=pl.ANY)] * 2
+            + [pl.BlockSpec(memory_space=pltpu.VMEM)],
+            out_specs=[
+                pl.BlockSpec((W // 2, STRIP), lambda i, *_: (0, i)),
+                pl.BlockSpec((2 * PART, STRIP), lambda i, *_: (0, i)),
+            ],
+            scratch_shapes=[
+                pltpu.VMEM((NB, W // 2, BS), BF),
+                pltpu.VMEM((NB, 2, 2 * PART, BS), BF),
+                pltpu.SemaphoreType.DMA((8,)),
+            ],
+        ),
+        out_shape=[
+            jax.ShapeDtypeStruct((W // 2, ROWS), F32),
+            jax.ShapeDtypeStruct((2 * PART, ROWS), BF),
+        ],
+        compiler_params=params(20, dimension_semantics=("arbitrary",)),
+        cost_estimate=cost(4 * PART * ROWS * deep + W // 2 * ROWS * deep, 8 * W * ROWS),
+    )(place, a_own, b_own, trailing)
+
+
+def early_body(place, a_down, a_up, b_down, b_up, tile, whole_b, out, spread, sems):
     u, v = where(place)
 
     @pl.when(pl.program_id(0) == 0)
@@ -210,43 +267,48 @@
         copies = []
         load_a(copies, a_down, turn(u, -1), spread)
         load_a(copies, a_up, turn(u, 1), spread)
-        for t, buf in enumerate((b_own, b_down, b_up)):
+        for t, buf in enumerate((b_down, b_up)):
             load_b(copies, buf, u, W // 2 + 2 * t * PART, spread)
         run_copies(copies, sems)
 
     value = multiply(spread, rows_of(tile, pl.program_id(0)))
     for i, step in enumerate(STEPS):
         out[2 * turn(v, -step) + (u + 1) % 2, :PART, :] = value[i * PART : (i + 1) * PART]
-    for j in range(6):
-        to = 2 * turn(v, -STEPS[j // 2]) + j % 2
+    for j in range(4):
+        to = 2 * turn(v, -STEPS[1 + j // 2]) + j % 2
         out[to, PART:, :] = value[W // 2 + j * PART : W // 2 + (j + 1) * PART]
-
-
-def early_product(place, bufs, trailing):
+    for j in range(2):
+        out[2 * v + j, PART:, :] = whole_b[j * PART : (j + 1) * PART, :]
+
+
+def early_product(place, bufs, trailing, whole_b):
     deep = trailing.shape[1]
-    rows = W // 2 + 6 * PART
+    rows = W // 2 + 4 * PART
     return pl.pallas_call(
         early_body,
         name="early_product",
         grid_spec=pltpu.PrefetchScalarGridSpec(
             num_scalar_prefetch=1,
             grid=(ROWS // STRIP,),
-            in_specs=[pl.BlockSpec(memory_space=pl.ANY)] * 5
-            + [pl.BlockSpec(memory_space=pltpu.VMEM)],
+            in_specs=[pl.BlockSpec(memory_space=pl.ANY)] * 4
+            + [
+                pl.BlockSpec(memory_space=pltpu.VMEM),
+                pl.BlockSpec((2 * PART, STRIP), lambda i, *_: (0, i)),
+            ],
             out_specs=pl.BlockSpec((COLS, PAIR, STRIP), lambda i, *_: (0, 0, i)),
             scratch_shapes=[
                 pltpu.VMEM((NB, 2, rows, BS), BF),
-                pltpu.SemaphoreType.DMA((20,)),
+                pltpu.SemaphoreType.DMA((16,)),
             ],
         ),
         out_shape=jax.ShapeDtypeStruct((COLS, PAIR, ROWS), BF),
         compiler_params=params(20, dimension_semantics=("arbitrary",)),
         cost_estimate=cost(2 * rows * ROWS * deep, 2 * rows * deep + 4 * W * ROWS),
-    )(place, *bufs, trailing)
+    )(place, *bufs, trailing, whole_b)
 
 
 def late_body(
-    half, place, a_own, a_far, a_far_more, b_far, b_far_more, tile, before, keep, give, spread, ready, sems
+    half, place, a_far, a_far_more, b_far, b_far_more, tile, before, half_a, keep, give, spread_a, spread_b, ready, sems
 ):
     u, v = where(place)
     core = place[1] % 2
@@ -254,19 +316,21 @@
     @pl.when(pl.program_id(0) == 0)
     def _():
         copies = []
-        load_a(copies, a_own, u, spread)
-        load_a(copies, a_far, turn(u, 2), spread, 0, 2)
-        load_a(copies, a_far_more, turn(u, 2), spread, 2, 2)
-        load_b(copies, b_far, u, W // 2, spread, 0, 2)
-        load_b(copies, b_far_more, u, W // 2, spread, 2, 2)
+        load_half(copies, a_far, spread_a, 0, 2)
+        load_half(copies, a_far_more, spread_a, 2, 2)
+        load_b(copies, b_far, u, 0, spread_b, 0, 2)
+        load_b(copies, b_far_more, u, 0, spread_b, 2, 2)
         run_copies(copies, sems)
 
     ready[...] = before[...]
-    value = multiply(spread, rows_of(tile, half * HALF_STEPS + pl.program_id(0)))
-    for i, step in enumerate(STEPS):
-        ready[2 * turn(v, -step) + u % 2, :PART, :] = value[i * PART : (i + 1) * PART]
+    step = half * HALF_STEPS + pl.program_id(0)
+    value = half_multiply(spread_a, tile, step, turn(u, 2) // 2)
+    value = (value + half_a[...]).astype(BF)
+    for i, far in enumerate(STEPS):
+        ready[2 * turn(v, -far) + u % 2, :PART, :] = value[i * PART : (i + 1) * PART]
+    value = multiply(spread_b, rows_of(tile, step))
     for j in range(2):
-        ready[2 * turn(v, 2) + j, PART:, :] = value[W // 2 + j * PART : W // 2 + (j + 1) * PART]
+        ready[2 * turn(v, 2) + j, PART:, :] = value[j * PART : (j + 1) * PART]
     for x in range(SIDE):
         keep[x] = ready[2 * x + core]
         give[x] = ready[2 * x + 1 - core]
@@ -275,9 +339,9 @@
 HALF_STEPS = ROWS // STRIP // 2
 
 
-def late_product(half, place, bufs, trailing, before):
+def late_product(half, place, bufs, trailing, before, half_a):
     deep = trailing.shape[1]
-    rows = W // 2 + 2 * PART
+    rows = W // 4 + 2 * PART
     out = jax.ShapeDtypeStruct((SIDE, PAIR, ROWS // 2), BF)
     spec = pl.BlockSpec((SIDE, PAIR, STRIP), lambda i, *_: (0, 0, i))
     return pl.pallas_call(
@@ -286,69 +350,60 @@
         grid_spec=pltpu.PrefetchScalarGridSpec(
             num_scalar_prefetch=1,
             grid=(HALF_STEPS,),
-            in_specs=[pl.BlockSpec(memory_space=pl.ANY)] * 5
+            in_specs=[pl.BlockSpec(memory_space=pl.ANY)] * 4
             + [
                 pl.BlockSpec(memory_space=pltpu.VMEM),
                 pl.BlockSpec((COLS, PAIR, STRIP), lambda i, *_: (0, 0, half * HALF_STEPS + i)),
+                pl.BlockSpec((W // 2, STRIP), lambda i, *_: (0, half * HALF_STEPS + i)),
             ],
             out_specs=[spec, spec],
             scratch_shapes=[
-                pltpu.VMEM((NB, 2, rows, BS), BF),
+                pltpu.VMEM((NB, W // 2, BS), BF),
+                pltpu.VMEM((NB, 2, 2 * PART, BS), BF),
                 pltpu.VMEM((COLS, PAIR, STRIP), BF),
-                pltpu.SemaphoreType.DMA((12,)),
+                pltpu.SemaphoreType.DMA((8,)),
             ],
         ),
         out_shape=[out, out],
         compiler_params=params(20, dimension_semantics=("arbitrary",)),
         cost_estimate=cost(rows * ROWS * deep, 2 * rows * deep + 4 * W * ROWS),
-    )(place, *bufs, trailing, before)
-
-
-def pair_body(joined, place, mine, taken, *refs):
-    before, outs = refs[: joined], refs[joined:]
+    )(place, *bufs, trailing, before, half_a)
+
+
+def pair_body(place, mine, taken, *outs):
     x = place[1] // 2
     for i in range(SIDE):
         at = (x + i) % SIDE
-        total = (mine[at].astype(F32) + taken[at].astype(F32)).astype(BF)
-        if joined and i == 2:
-            outs[i][0] = before[0][...]
-            outs[i][1] = total
-        else:
-            outs[i][...] = total
-
-
-def pair_sum(place, mine, taken, *before):
+        outs[i][...] = (mine[at].astype(F32) + taken[at].astype(F32)).astype(BF)
+
+
+def pair_sum(place, mine, taken):
     lanes = 3 * BS
     width = mine.shape[2]
     spec = pl.BlockSpec((SIDE, PAIR, lanes), lambda i, *_: (0, 0, i))
-    one = pl.BlockSpec((PAIR, lanes), lambda i, *_: (0, i))
-    two = pl.BlockSpec((2, PAIR, lanes), lambda i, *_: (0, 0, i))
-    shape = jax.ShapeDtypeStruct((PAIR, width), BF)
-    double = jax.ShapeDtypeStruct((2, PAIR, width), BF)
-    joined = len(before)
-    return pl.pallas_call(
-        functools.partial(pair_body, joined),
+    return pl.pallas_call(
+        pair_body,
         name="pair_sum",
         grid_spec=pltpu.PrefetchScalarGridSpec(
             num_scalar_prefetch=1,
             grid=(width // lanes,),
-            in_specs=[spec, spec] + [one] * joined,
-            out_specs=[one, one, two if joined else one, one],
-        ),
-        out_shape=[shape, shape, double if joined else shape, shape],
+            in_specs=[spec, spec],
+            out_specs=[pl.BlockSpec((PAIR, lanes), lambda i, *_: (0, i))] * SIDE,
+        ),
+        out_shape=[jax.ShapeDtypeStruct((PAIR, width), BF)] * SIDE,
         compiler_params=params(dimension_semantics=("arbitrary",)),
         cost_estimate=cost(W * width, 6 * W * width),
-    )(place, mine, taken, *before)
+    )(place, mine, taken)
 
 
 def slots_body(
     place, rows_a, counts_a, rows_b, counts_b, *refs
 ):
-    slabs, far, (fa, fb, columns, pieces, natural, left) = refs[:6], refs[6], refs[7:]
+    slabs, (fa, fb, columns, pieces, natural, left) = refs[:8], refs[8:]
     owner = place[0]
     width = ROWS // 2
     for half in range(2):
-        total = total_of((*slabs[half * 3 : half * 3 + 3], far.at[half]), slice(None))
+        total = total_of(slabs[half * SIDE : (half + 1) * SIDE], slice(None))
         natural[:, half * width : (half + 1) * width] = (-total).astype(BF)
     for k in range(NB):
         at = slice(k * BS, (k + 1) * BS)
@@ -371,9 +426,7 @@
         grid_spec=pltpu.PrefetchScalarGridSpec(
             num_scalar_prefetch=5,
             grid=(1,),
-            in_specs=[whole((PAIR, ROWS // 2))] * 6
-            + [whole((2, PAIR, ROWS // 2))]
-            + [whole((ROWS, W))] * 2,
+            in_specs=[whole((PAIR, ROWS // 2))] * 8 + [whole((ROWS, W))] * 2,
             out_specs=[whole((PAIR, ROWS)), whole((3 * PART, W))],
             scratch_shapes=[pltpu.VMEM((PAIR, ROWS), BF)] * 2,
         ),
@@ -397,7 +450,7 @@
 
 
 def whole_columns(place, slabs):
-    lanes = 2 * BS
+    lanes = 4 * BS
     out = jax.ShapeDtypeStruct((ROWS, W), BF)
     return pl.pallas_call(
         column_body,
@@ -497,24 +550,25 @@
     lists = (rows_a, counts_a, rows_b, counts_b)
     part_a = lax.ppermute(prep_a(place, lists, factor_a), BOTH, spread_pairs())
     part_b = prep_b(place, lists, factor_a, factor_b, factor_top)
+    part_b, _ = lax.optimization_barrier((part_b, part_a))
     part_b = lax.ppermute(part_b, BOTH, spread_pairs())
     a_own = jnp.stack(around(part_a, "dy"))
     b_own = jnp.stack(around(part_b, "dz"))
     a_down, a_up = send(a_own, dz=1), send(a_own, dz=-1)
     b_down, b_up = send(b_own, dy=1), send(b_own, dy=-1)
     trailing = hold(trailing, a_own)
-    a_next, b_next, _ = lax.optimization_barrier((a_down, b_down, trailing))
+    half_a, whole_b = own_product(place, a_own, b_own, trailing)
+    a_next, b_next, _ = lax.optimization_barrier((a_down, b_down, half_a))
     a_far, b_far = send(a_next[:2], dz=1), send(b_next[:2], dy=1)
     a_far_more, b_far_more = send(a_up[2:], dz=-1), send(b_up[2:], dy=-1)
-    before = early_product(place, (a_down, a_up, b_own, b_down, b_up), trailing)
-    slabs, far = [], ()
+    before = early_product(place, (a_down, a_up, b_down, b_up), trailing, whole_b)
+    slabs = []
     for half in range(2):
         keep, give = late_product(
-            half, place, (a_own, a_far, a_far_more, b_far, b_far_more), trailing, before
+            half, place, (a_far, a_far_more, b_far, b_far_more), trailing, before, half_a
         )
-        own, one, *far, three = pair_sum(place, keep, send(give, dc=1), *far)
-        slabs += [own, send(one, dx=1), send(three, dx=-1)]
-    slabs.append(send(far[0], dx=2))
+        own, one, two, three = pair_sum(place, keep, send(give, dc=1))
+        slabs += [own, send(one, dx=1), send(two, dx=2), send(three, dx=-1)]
     columns, pieces = slots(place, lists, slabs, (factor_a, factor_b))
     near, other = send(columns, dx=1), send(columns, dx=-1)
     first, near, other = lax.optimization_barrier((around(pieces, "dy"), near, other))

time: 159 us -> 157 us (0.987)
  Pallas kernels: 36.9 us -> 40.7 us
  waiting for transfers between devices: 56.2 us -> 52.4 us
    ppermute x34 -> x35, waiting for transfers between devices: 47.9 us -> 33.4 us  [send(): return lax.ppermute(value, BOTH, shifted(**by))]
    pallas_call x2 -> x3, Pallas kernels: 2.17 us -> 8.32 us  [the longest x1 6.19 us: own_product(): pl.pallas_call(own_body, name='own_product', grid_spec=pltpu.PrefetchScal...]
    ppermute x1, waiting for transfers between devices: 5.6 us -> 10.8 us  [on_device(): part_b = lax.ppermute(part_b, BOTH, spread_pairs())]
    ppermute x1, waiting for transfers between devices: 2.72 us -> 7.65 us  [on_device(): part_a = lax.ppermute(prep_a(place, lists, factor_a), BOTH, spread_pairs())]
    ppermute x1, starting transfers between devices: 4.93 us -> 1.91 us  [on_device(): part_b = lax.ppermute(part_b, BOTH, spread_pairs())]
    ppermute x34 -> x35, starting transfers between devices: 45.4 us -> 47.5 us  [send(): return lax.ppermute(value, BOTH, shifted(**by))]
  transfers between devices with their start and end apart: 37 -> 38, of which waited for: 16 -> 16; matrix products, arithmetic and copies ran while one was open for 0% -> 0% of each run, Pallas kernels for 16% -> 20%
where the time goes in v8:
time: 157 us
  starting transfers between devices  58 us (37%)
  waiting for transfers between devices  52.4 us (33%)
  Pallas kernels  40.7 us (26%)
  local copies, waits for them, and re-layouts  3.84 us (2%)
    ppermute x35, starting transfers between devices, send(): return lax.ppermute(value, BOTH, shifted(**by))  47.5 us
    ppermute x35, waiting for transfers between devices, send(): return lax.ppermute(value, BOTH, shifted(**by))  33.4 us
    ppermute x1, waiting for transfers between devices, on_device(): part_b = lax.ppermute(part_b, BOTH, spread_pairs())  10.8 us
    pallas_call x2, Pallas kernels, late_product(): pl.pallas_call(functools.partial(late_body, half), name='late_product', g...  8.01 us
    pallas_call x1, Pallas kernels, early_product(): pl.pallas_call(early_body, name='early_product', grid_spec=pltpu.Prefetch...  7.9 us
    ppermute x1, waiting for transfers between devices, on_device(): part_a = lax.ppermute(prep_a(place, lists, factor_a), BOTH, spread_pairs())  7.65 us
    pallas_call x1, Pallas kernels, own_product(): pl.pallas_call(own_body, name='own_product', grid_spec=pltpu.PrefetchScal...  6.19 us
    ppermute x1, starting transfers between devices, on_device(): part_a = lax.ppermute(prep_a(place, lists, factor_a), BOTH, spread_pairs())  4.92 us
  transfers between devices with their start and end apart: 38, of which 16 were waited for; matrix products, arithmetic and copies ran while one was open for 0% of the time, Pallas kernels for 20%

profile of v8, /device:TPU:1, one launch (start us, length us, event | category | flops | bytes accessed | tf_op | source)
XLA Modules:
  0.0 156.7 jit_solution(1903296180822798008)
XLA Ops:
  0.6 0.6 pad_add_fusion.place
  1.2 2.9 %prep_a.1 = bf16[12,64,128]{2,1,0:T(8,128)(2,1)} custom-call(s32[2]{0:T(128)} %pad_add_fusion.place, s32[16,12]{1,0:T(8,128)} %rows_a.5, s32[16]{0:T(128)} %counts_a.5, bf16[1536,512]{1,0:T(8,128)(2,1)} %refs_8_.1), custom_call_target="tpu_custom_call" | custom-call | bytes 786432 | tf_op jit(solution)/shard_map/prep_a/pallas_call | solution.py:95
  4.1 4.9 %collective-permute-start = (bf16[12,64,128]{2,1,0:T(8,128)(2,1)}, bf16[12,64,128]{2,1,0:T(8,128)(2,1)S(1)}, u32[]{:S(2)}, u32[]{:S(2)}) collective-permute-start(bf16[12,64,128]{2,1,0:T(8,128)(2,1)} %prep_a.1), channel_id=1, source_target_pairs={{0,0},{1,32},{2,8},{3,40},{4,16},{5,48},{6,24},{7,56},{8,9},{9,41}... | collective-permute-start | bytes 589832 | tf_op jit(solution)/shard_map/ppermute | solution.py:551
  9.0 4.3 %prep_b.1 = bf16[12,64,128]{2,1,0:T(8,128)(2,1)} custom-call(s32[2]{0:T(128)} %pad_add_fusion.place, s32[16,12]{1,0:T(8,128)} %rows_a.5, s32[16]{0:T(128)} %counts_a.5, s32[16,12]{1,0:T(8,128)} %rows_b.3, s32[16]{0:T(128)} %counts_b.3, bf16[1536,512]{1,0:T(8,128)(2,1)} %refs_8_.1, bf16[1536,512]{1,0:T(8,128)(2,1)} %refs_9_.1, bf16[512,512]{1,0:T(8,128)(2,1)} %top.5), custom_call_target="tpu_custom_call" | custom-call | flops 201326592 | bytes 3145728 | tf_op jit(solution)/shard_map/prep_b/pallas_call | solution.py:128
  13.3 7.7 %collective-permute-done = bf16[12,64,128]{2,1,0:T(8,128)(2,1)S(1)} collective-permute-done((bf16[12,64,128]{2,1,0:T(8,128)(2,1)}, bf16[12,64,128]{2,1,0:T(8,128)(2,1)S(1)}, u32[]{:S(2)}, u32[]{:S(2)}) %collective-permute-start) | collective-permute-done | bytes 196640 | tf_op jit(solution)/shard_map/ppermute | solution.py:551
  21.0 1.9 %collective-permute-start.5 = (bf16[12,64,128]{2,1,0:T(8,128)(2,1)}, bf16[12,64,128]{2,1,0:T(8,128)(2,1)S(1)}, u32[]{:S(2)}, u32[]{:S(2)}) collective-permute-start(bf16[12,64,128]{2,1,0:T(8,128)(2,1)} %prep_b.1), channel_id=1, source_target_pairs={{0,0},{1,32},{2,8},{3,40},{4,16},{5,48},{6,24},{7,56},{8,9},{9,41}... | collective-permute-start | bytes 589832 | tf_op jit(solution)/shard_map/ppermute | solution.py:554
  23.0 2.7 %collective-permute-start.2 = (bf16[12,64,128]{2,1,0:T(8,128)(2,1)S(1)}, bf16[12,64,128]{2,1,0:T(8,128)(2,1)S(1)}, u32[]{:S(2)}, u32[]{:S(2)}) collective-permute-start(bf16[12,64,128]{2,1,0:T(8,128)(2,1)S(1)} %collective-permute-done), channel_id=1, source_target_pairs={{0,24},{1,25},{2,26},{3,27},{4,28},{5,29},{6,30},{7,31},{8,0},{9,1... | collective-permute-start | bytes 589832 | tf_op jit(solution)/shard_map/ppermute | solution.py:539
  25.7 10.8 %collective-permute-done.5 = bf16[12,64,128]{2,1,0:T(8,128)(2,1)S(1)} collective-permute-done((bf16[12,64,128]{2,1,0:T(8,128)(2,1)}, bf16[12,64,128]{2,1,0:T(8,128)(2,1)S(1)}, u32[]{:S(2)}, u32[]{:S(2)}) %collective-permute-start.5) | collective-permute-done | bytes 196640 | tf_op jit(solution)/shard_map/ppermute | solution.py:554
  36.4 1.6 %collective-permute-start.6 = (bf16[12,64,128]{2,1,0:T(8,128)(2,1)S(1)}, bf16[12,64,128]{2,1,0:T(8,128)(2,1)S(1)}, u32[]{:S(2)}, u32[]{:S(2)}) collective-permute-start(bf16[12,64,128]{2,1,0:T(8,128)(2,1)S(1)} %collective-permute-done.5), channel_id=1, source_target_pairs={{0,32},{1,33},{2,34},{3,35},{4,36},{5,37},{6,38},{7,39},{8,40},{9,... | collective-permute-start | bytes 589832 | tf_op jit(solution)/shard_map/ppermute | solution.py:539
  38.1 2.5 %collective-permute-start.7 = (bf16[12,64,128]{2,1,0:T(8,128)(2,1)S(1)}, bf16[12,64,128]{2,1,0:T(8,128)(2,1)S(1)}, u32[]{:S(2)}, u32[]{:S(2)}) collective-permute-start(bf16[12,64,128]{2,1,0:T(8,128)(2,1)S(1)} %collective-permute-done.5), channel_id=1, source_target_pairs={{0,96},{1,97},{2,98},{3,99},{4,100},{5,101},{6,102},{7,103},{8,104... | collective-permute-start | bytes 589832 | tf_op jit(solution)/shard_map/ppermute | solution.py:539
  40.6 1.3 collective-permute-start.8
  41.9 0.1 pad_maximum_fusion._.a_own
  42.0 0.7 collective-permute-start.11
  42.7 0.9 collective-permute-start.4
  43.5 0.6 collective-permute-done.6
  44.1 1.2 collective-permute-done.7
  45.3 1.7 %collective-permute-done.8 = bf16[12,64,128]{2,1,0:T(8,128)(2,1)S(1)} collective-permute-done((bf16[12,64,128]{2,1,0:T(8,128)(2,1)S(1)}, bf16[12,64,128]{2,1,0:T(8,128)(2,1)S(1)}, u32[]{:S(2)}, u32[]{:S(2)}) %collective-permute-start.8) | collective-permute-done | bytes 196640 | tf_op jit(solution)/shard_map/ppermute | solution.py:539
  47.0 0.1 pad_maximum_fusion.1.b_own
  47.2 2.7 %collective-permute-start.14 = (bf16[4,12,64,128]{3,2,1,0:T(8,128)(2,1)S(1)}, bf16[4,12,64,128]{3,2,1,0:T(8,128)(2,1)S(1)}, u32[]{:S(2)}, u32[]{:S(2)}) collective-permute-start(bf16[4,12,64,128]{3,2,1,0:T(8,128)(2,1)S(1)} %pad_maximum_fusion.1.b_own), channel_id=1, source_target_pairs={{0,24},{1,25},{2,26},{3,27},{4,28},{5,29},{6,30},{7,31},{8,0},{9,1... | collective-permute-start | bytes 2359304 | tf_op jit(solution)/shard_map/ppermute | solution.py:539
  49.8 3.7 %copy-done.1 = bf16[1536,3072]{1,0:T(8,128)(2,1)S(1)} copy-done((bf16[1536,3072]{1,0:T(8,128)(2,1)S(1)}, bf16[1536,3072]{1,0:T(8,128)(2,1)}, u32[]{:S(2)}) %copy-start.1) | copy-done | bytes 9437208
  53.5 0.6 hold.1.tile
  54.2 6.2 %own_product.1 = (f32[256,1536]{1,0:T(8,128)S(1)}, bf16[128,1536]{1,0:T(8,128)(2,1)S(1)}) custom-call(s32[2]{0:T(128)S(1)} %copy-done.7, bf16[4,12,64,128]{3,2,1,0:T(8,128)(2,1)S(1)} %pad_maximum_fusion._.a_own, bf16[4,12,64,128]{3,2,1,0:T(8,128)(2,1)S(1)} %pad_maximum_fusion.1.b_own, bf16[1536,3072]{1,0:T(8,128)(2,1)S(1)} %hold.1.tile), custom_call_target="tpu_custom_call" | custom-call | flops 2415919104 | bytes 6291456 | tf_op jit(solution)/shard_map/own_product/pallas_call | solution.py:235
  60.4 1.8 %collective-permute-done.11.a_up = bf16[4,12,64,128]{3,2,1,0:T(8,128)(2,1)S(1)} collective-permute-done((bf16[4,12,64,128]{3,2,1,0:T(8,128)(2,1)S(1)}, bf16[4,12,64,128]{3,2,1,0:T(8,128)(2,1)S(1)}, u32[]{:S(2)}, u32[]{:S(2)}) %collective-permute-start.11) | collective-permute-done | bytes 786464 | tf_op jit(solution)/shard_map/ppermute | solution.py:539
  62.2 3.4 %collective-permute-start.12 = (bf16[2,12,64,128]{3,2,1,0:T(8,128)(2,1)S(1)}, bf16[2,12,64,128]{3,2,1,0:T(8,128)(2,1)S(1)}, u32[]{:S(2)}, u32[]{:S(2)}) collective-permute-start(bf16[2,12,64,128]{3,2,1,0:T(8,128)(2,1)S(1)} %slice.16), channel_id=1, source_target_pairs={{0,96},{1,97},{2,98},{3,99},{4,100},{5,101},{6,102},{7,103},{8,104... | collective-permute-start | bytes 1179656 | tf_op jit(solution)/shard_map/ppermute | solution.py:539
  65.8 1.8 %collective-permute-start.13 = (bf16[2,12,64,128]{3,2,1,0:T(8,128)(2,1)S(1)}, bf16[2,12,64,128]{3,2,1,0:T(8,128)(2,1)S(1)}, u32[]{:S(2)}, u32[]{:S(2)}) collective-permute-start(bf16[2,12,64,128]{3,2,1,0:T(8,128)(2,1)S(1)} %slice.14), channel_id=1, source_target_pairs={{0,8},{1,9},{2,10},{3,11},{4,12},{5,13},{6,14},{7,15},{8,16},{9,17... | collective-permute-start | bytes 1179656 | tf_op jit(solution)/shard_map/ppermute | solution.py:539
  67.7 1.0 collective-permute-start.15
  68.7 7.9 %early_product.1.before = bf16[8,128,1536]{2,1,0:T(8,128)(2,1)S(1)} custom-call(s32[2]{0:T(128)S(1)} %copy-done.7, bf16[4,12,64,128]{3,2,1,0:T(8,128)(2,1)S(1)} %collective-permute-done.4.a_down, bf16[4,12,64,128]{3,2,1,0:T(8,128)(2,1)S(1)} %collective-permute-done.11.a_up, bf16[4,12,64,128]{3,2,1,0:T(8,128)(2,1)S(1)} %collective-permute-done.9.b_down, ...), custom_call_target="tpu_custom_call" | custom-call | flops 4831838208 | bytes 6291456 | tf_op jit(solution)/shard_map/early_product/pallas_call | solution.py:287
  76.6 4.0 %late_product.3 = (bf16[4,128,768]{2,1,0:T(8,128)(2,1)S(1)}, bf16[4,128,768]{2,1,0:T(8,128)(2,1)S(1)}) custom-call(s32[2]{0:T(128)S(1)} %copy-done.7, bf16[2,12,64,128]{3,2,1,0:T(8,128)(2,1)S(1)} %collective-permute-done.10.a_far, bf16[2,12,64,128]{3,2,1,0:T(8,128)(2,1)S(1)} %collective-permute-done.12.a_far_more, ...), custom_call_target="tpu_custom_call" | custom-call | flops 1207959552 | bytes 4718592 | tf_op jit(solution)/shard_map/late_product/pallas_call | solution.py:347
  80.7 4.5 %collective-permute-start.20 = (bf16[4,128,768]{2,1,0:T(8,128)(2,1)S(1)}, bf16[4,128,768]{2,1,0:T(8,128)(2,1)S(1)}, u32[]{:S(2)}, u32[]{:S(2)}) collective-permute-start(bf16[4,128,768]{2,1,0:T(8,128)(2,1)S(1)} %get-tuple-element.53), channel_id=1, source_target_pairs={{0,1},{1,0},{2,3},{3,2},{4,5},{5,4},{6,7},{7,6},{8,9},{9,8},{10,11... | collective-permute-start | bytes 2359304 | tf_op jit(solution)/shard_map/ppermute | solution.py:539
  85.1 4.0 %late_product.2 = (bf16[4,128,768]{2,1,0:T(8,128)(2,1)S(1)}, bf16[4,128,768]{2,1,0:T(8,128)(2,1)S(1)}) custom-call(s32[2]{0:T(128)S(1)} %copy-done.7, bf16[2,12,64,128]{3,2,1,0:T(8,128)(2,1)S(1)} %collective-permute-done.10.a_far, bf16[2,12,64,128]{3,2,1,0:T(8,128)(2,1)S(1)} %collective-permute-done.12.a_far_more, ...), custom_call_target="tpu_custom_call" | custom-call | flops 1207959552 | bytes 4718592 | tf_op jit(solution)/shard_map/late_product/pallas_call | solution.py:347
  89.1 0.1 collective-permute-start.16
  89.3 1.1 pair_sum.3
  90.3 0.3 collective-permute-start.21
  90.6 5.8 %collective-permute-start.22 = (bf16[128,768]{1,0:T(8,128)(2,1)S(1)}, bf16[128,768]{1,0:T(8,128)(2,1)S(1)}, u32[]{:S(2)}, u32[]{:S(2)}) collective-permute-start(bf16[128,768]{1,0:T(8,128)(2,1)S(1)} %get-tuple-element.56), channel_id=1, source_target_pairs={{0,4},{1,5},{2,6},{3,7},{4,0},{5,1},{6,2},{7,3},{8,12},{9,13},{10,... | collective-permute-start | bytes 589832 | tf_op jit(solution)/shard_map/ppermute | solution.py:539
  96.5 1.1 pair_sum.2
  97.5 1.5 collective-permute-start.17
  99.1 1.1 collective-permute-done.21.refs_5_
  100.1 1.4 collective-permute-start.19
  101.5 3.7 %collective-permute-done.22.refs_6_ = bf16[128,768]{1,0:T(8,128)(2,1)S(1)} collective-permute-done((bf16[128,768]{1,0:T(8,128)(2,1)S(1)}, bf16[128,768]{1,0:T(8,128)(2,1)S(1)}, u32[]{:S(2)}, u32[]{:S(2)}) %collective-permute-start.22) | collective-permute-done | bytes 196640 | tf_op jit(solution)/shard_map/ppermute | solution.py:539
  105.3 3.6 %collective-permute-done.17.refs_1_ = bf16[128,768]{1,0:T(8,128)(2,1)S(1)} collective-permute-done((bf16[128,768]{1,0:T(8,128)(2,1)S(1)}, bf16[128,768]{1,0:T(8,128)(2,1)S(1)}, u32[]{:S(2)}, u32[]{:S(2)}) %collective-permute-start.17) | collective-permute-done | bytes 196640 | tf_op jit(solution)/shard_map/ppermute | solution.py:539
  108.9 4.8 %collective-permute-done.18.refs_2_ = bf16[128,768]{1,0:T(8,128)(2,1)S(1)} collective-permute-done((bf16[128,768]{1,0:T(8,128)(2,1)S(1)}, bf16[128,768]{1,0:T(8,128)(2,1)S(1)}, u32[]{:S(2)}, u32[]{:S(2)}) %collective-permute-start.18) | collective-permute-done | bytes 196640 | tf_op jit(solution)/shard_map/ppermute | solution.py:539
  113.8 1.9 %slots.1 = (bf16[128,1536]{1,0:T(8,128)(2,1)S(1)}, bf16[192,512]{1,0:T(8,128)(2,1)S(1)}) custom-call(s32[2]{0:T(128)S(1)} %copy-done.7, s32[16,12]{1,0:T(8,128)S(1)} %copy-done.6, s32[16]{0:T(128)S(1)} %copy-done.9, s32[16,12]{1,0:T(8,128)S(1)} %copy-done.8, s32[16]{0:T(128)S(1)} %copy-done.10, bf16[128,768]{1,0:T(8,128)(2,1)S(1)} %get-tuple-element.48.refs_0_, ...), custom_call_target="tpu_custom_call" | custom-call | flops 301989888 | bytes 5111808 | tf_op jit(solution)/shard_map/slots/pallas_call | solution.py:423
  115.6 0.3 collective-permute-start.27
  116.0 2.5 %collective-permute-start.28 = (bf16[128,1536]{1,0:T(8,128)(2,1)S(1)}, bf16[128,1536]{1,0:T(8,128)(2,1)S(1)}, u32[]{:S(2)}, u32[]{:S(2)}) collective-permute-start(bf16[128,1536]{1,0:T(8,128)(2,1)S(1)} %get-tuple-element.69.refs_0_), channel_id=1, source_target_pairs={{0,6},{1,7},{2,0},{3,1},{4,2},{5,3},{6,4},{7,5},{8,14},{9,15},{10,... | collective-permute-start | bytes 1179656 | tf_op jit(solution)/shard_map/ppermute | solution.py:539
  118.4 0.4 collective-permute-start.24
  118.8 2.4 %collective-permute-start.25 = (bf16[192,512]{1,0:T(8,128)(2,1)S(1)}, bf16[192,512]{1,0:T(8,128)(2,1)S(1)}, u32[]{:S(2)}, u32[]{:S(2)}) collective-permute-start(bf16[192,512]{1,0:T(8,128)(2,1)S(1)} %get-tuple-element.60.one), channel_id=1, source_target_pairs={{0,24},{1,25},{2,26},{3,27},{4,28},{5,29},{6,30},{7,31},{8,0},{9,1... | collective-permute-start | bytes 589832 | tf_op jit(solution)/shard_map/ppermute | solution.py:539
  121.2 1.2 collective-permute-start.26
  122.4 2.2 %collective-permute-done.24.two = bf16[192,512]{1,0:T(8,128)(2,1)S(1)} collective-permute-done((bf16[192,512]{1,0:T(8,128)(2,1)S(1)}, bf16[192,512]{1,0:T(8,128)(2,1)S(1)}, u32[]{:S(2)}, u32[]{:S(2)}) %collective-permute-start.24) | collective-permute-done | bytes 196640 | tf_op jit(solution)/shard_map/ppermute | solution.py:539
  124.6 4.9 %collective-permute-done.26.four = bf16[192,512]{1,0:T(8,128)(2,1)S(1)} collective-permute-done((bf16[192,512]{1,0:T(8,128)(2,1)S(1)}, bf16[192,512]{1,0:T(8,128)(2,1)S(1)}, u32[]{:S(2)}, u32[]{:S(2)}) %collective-permute-start.26) | collective-permute-done | bytes 196640 | tf_op jit(solution)/shard_map/ppermute | solution.py:539
  129.4 0.1 fold.1.one
  129.5 2.6 %collective-permute-start.32 = (bf16[128,1536]{1,0:T(8,128)(2,1)S(1)}, bf16[128,1536]{1,0:T(8,128)(2,1)S(1)}, u32[]{:S(2)}, u32[]{:S(2)}) collective-permute-start(bf16[128,1536]{1,0:T(8,128)(2,1)S(1)} %get-tuple-element.69.refs_0_), channel_id=1, source_target_pairs={{0,4},{1,5},{2,6},{3,7},{4,0},{5,1},{6,2},{7,3},{8,12},{9,13},{10,... | collective-permute-start | bytes 1179656 | tf_op jit(solution)/shard_map/ppermute | solution.py:539
  132.2 2.6 %collective-permute-start.30 = (bf16[192,512]{1,0:T(8,128)(2,1)S(1)}, bf16[192,512]{1,0:T(8,128)(2,1)S(1)}, u32[]{:S(2)}, u32[]{:S(2)}) collective-permute-start(bf16[192,512]{1,0:T(8,128)(2,1)S(1)} %fold.1.one), channel_id=1, source_target_pairs={{0,96},{1,97},{2,98},{3,99},{4,100},{5,101},{6,102},{7,103},{8,104... | collective-permute-start | bytes 589832 | tf_op jit(solution)/shard_map/ppermute | solution.py:539
  134.8 0.3 collective-permute-start.31
  135.1 3.0 %collective-permute-done.29.two = bf16[192,512]{1,0:T(8,128)(2,1)S(1)} collective-permute-done((bf16[192,512]{1,0:T(8,128)(2,1)S(1)}, bf16[192,512]{1,0:T(8,128)(2,1)S(1)}, u32[]{:S(2)}, u32[]{:S(2)}) %collective-permute-start.29) | collective-permute-done | bytes 196640 | tf_op jit(solution)/shard_map/ppermute | solution.py:539
  138.1 1.9 %collective-permute-done.30.three = bf16[192,512]{1,0:T(8,128)(2,1)S(1)} collective-permute-done((bf16[192,512]{1,0:T(8,128)(2,1)S(1)}, bf16[192,512]{1,0:T(8,128)(2,1)S(1)}, u32[]{:S(2)}, u32[]{:S(2)}) %collective-permute-start.30) | collective-permute-done | bytes 196640 | tf_op jit(solution)/shard_map/ppermute | solution.py:539
  140.0 2.9 %collective-permute-done.31.four = bf16[192,512]{1,0:T(8,128)(2,1)S(1)} collective-permute-done((bf16[192,512]{1,0:T(8,128)(2,1)S(1)}, bf16[192,512]{1,0:T(8,128)(2,1)S(1)}, u32[]{:S(2)}, u32[]{:S(2)}) %collective-permute-start.31) | collective-permute-done | bytes 196640 | tf_op jit(solution)/shard_map/ppermute | solution.py:539
  142.9 2.2 %collective-permute-start.33 = (bf16[128,1536]{1,0:T(8,128)(2,1)S(1)}, bf16[128,1536]{1,0:T(8,128)(2,1)S(1)}, u32[]{:S(2)}, u32[]{:S(2)}) collective-permute-start(bf16[128,1536]{1,0:T(8,128)(2,1)S(1)} %get-tuple-element.69.refs_0_), channel_id=1, source_target_pairs={{0,1},{1,0},{2,3},{3,2},{4,5},{5,4},{6,7},{7,6},{8,9},{9,8},{10,11... | collective-permute-start | bytes 1179656 | tf_op jit(solution)/shard_map/ppermute | solution.py:539
  145.2 0.4 collective-permute-start.35
  145.6 1.1 top_part.1
  146.8 0.1 collective-permute-start.36
  146.9 3.7 %all-to-all-start = ((bf16[8,64,128]{2,1,0:T(8,128)(2,1)}), bf16[8,64,128]{2,1,0:T(8,128)(2,1)S(1)}, u32[]{:S(2)}, u32[]{:S(2)}) async-start(bf16[8,64,128]{2,1,0:T(8,128)(2,1)} %get-tuple-element.70), calls=%async_computation | async-start | bytes 262144 | tf_op jit(solution)/shard_map/all_to_all | solution.py:582
  150.6 4.7 %whole_columns.1 = (bf16[1536,512]{1,0:T(8,128)(2,1)}, bf16[1536,512]{1,0:T(8,128)(2,1)}) custom-call(s32[2]{0:T(128)S(1)} %copy-done.7, bf16[128,1536]{1,0:T(8,128)(2,1)S(1)} %get-tuple-element.69.refs_0_, bf16[128,1536]{1,0:T(8,128)(2,1)S(1)} %collective-permute-done.27.refs_1_, bf16[128,1536]{1,0:T(8,128)(2,1)S(1)} %collective-permute-done.28.refs_2_, ...), custom_call_target="tpu_custom_call" | custom-call | bytes 6291456 | tf_op jit(solution)/shard_map/whole_columns/pallas_call | solution.py:455
  155.3 0.6 all-to-all-done.taken
  155.9 0.9 last_part.1
  (55 shorter events, 0.6 us)
Async XLA Ops:
  4.1 16.9 %collective-permute-start = (bf16[12,64,128]{2,1,0:T(8,128)(2,1)}, bf16[12,64,128]{2,1,0:T(8,128)(2,1)S(1)}, u32[]{:S(2)}, u32[]{:S(2)}) collective-permute-start(bf16[12,64,128]{2,1,0:T(8,128)(2,1)} %prep_a.1), channel_id=1, source_target_pairs={{0,0},{1,32},{2,8},{3,40},{4,16},{5,48},{6,24},{7,56},{8,9},{9,41}... | collective-permute-start | bytes 589832 | tf_op jit(solution)/shard_map/ppermute | solution.py:551
  21.0 15.4 %collective-permute-start.5 = (bf16[12,64,128]{2,1,0:T(8,128)(2,1)}, bf16[12,64,128]{2,1,0:T(8,128)(2,1)S(1)}, u32[]{:S(2)}, u32[]{:S(2)}) collective-permute-start(bf16[12,64,128]{2,1,0:T(8,128)(2,1)} %prep_b.1), channel_id=1, source_target_pairs={{0,0},{1,32},{2,8},{3,40},{4,16},{5,48},{6,24},{7,56},{8,9},{9,41}... | collective-permute-start | bytes 589832 | tf_op jit(solution)/shard_map/ppermute | solution.py:554
  22.9 17.7 %collective-permute-start.1 = (bf16[12,64,128]{2,1,0:T(8,128)(2,1)S(1)}, bf16[12,64,128]{2,1,0:T(8,128)(2,1)S(1)}, u32[]{:S(2)}, u32[]{:S(2)}) collective-permute-start(bf16[12,64,128]{2,1,0:T(8,128)(2,1)S(1)} %collective-permute-done), channel_id=1, source_target_pairs={{0,8},{1,9},{2,10},{3,11},{4,12},{5,13},{6,14},{7,15},{8,16},{9,17... | collective-permute-start | bytes 589832 | tf_op jit(solution)/shard_map/ppermute | solution.py:539
  23.0 18.9 %collective-permute-start.2 = (bf16[12,64,128]{2,1,0:T(8,128)(2,1)S(1)}, bf16[12,64,128]{2,1,0:T(8,128)(2,1)S(1)}, u32[]{:S(2)}, u32[]{:S(2)}) collective-permute-start(bf16[12,64,128]{2,1,0:T(8,128)(2,1)S(1)} %collective-permute-done), channel_id=1, source_target_pairs={{0,24},{1,25},{2,26},{3,27},{4,28},{5,29},{6,30},{7,31},{8,0},{9,1... | collective-permute-start | bytes 589832 | tf_op jit(solution)/shard_map/ppermute | solution.py:539
  25.7 16.2 %collective-permute-start.3 = (bf16[12,64,128]{2,1,0:T(8,128)(2,1)S(1)}, bf16[12,64,128]{2,1,0:T(8,128)(2,1)S(1)}, u32[]{:S(2)}, u32[]{:S(2)}) collective-permute-start(bf16[12,64,128]{2,1,0:T(8,128)(2,1)S(1)} %collective-permute-done), channel_id=1, source_target_pairs={{0,16},{1,17},{2,18},{3,19},{4,20},{5,21},{6,22},{7,23},{8,24},{9,... | collective-permute-start | bytes 589832 | tf_op jit(solution)/shard_map/ppermute | solution.py:539
  36.4 7.6 %collective-permute-start.6 = (bf16[12,64,128]{2,1,0:T(8,128)(2,1)S(1)}, bf16[12,64,128]{2,1,0:T(8,128)(2,1)S(1)}, u32[]{:S(2)}, u32[]{:S(2)}) collective-permute-start(bf16[12,64,128]{2,1,0:T(8,128)(2,1)S(1)} %collective-permute-done.5), channel_id=1, source_target_pairs={{0,32},{1,33},{2,34},{3,35},{4,36},{5,37},{6,38},{7,39},{8,40},{9,... | collective-permute-start | bytes 589832 | tf_op jit(solution)/shard_map/ppermute | solution.py:539
  38.1 7.2 %collective-permute-start.7 = (bf16[12,64,128]{2,1,0:T(8,128)(2,1)S(1)}, bf16[12,64,128]{2,1,0:T(8,128)(2,1)S(1)}, u32[]{:S(2)}, u32[]{:S(2)}) collective-permute-start(bf16[12,64,128]{2,1,0:T(8,128)(2,1)S(1)} %collective-permute-done.5), channel_id=1, source_target_pairs={{0,96},{1,97},{2,98},{3,99},{4,100},{5,101},{6,102},{7,103},{8,104... | collective-permute-start | bytes 589832 | tf_op jit(solution)/shard_map/ppermute | solution.py:539
  40.6 6.4 %collective-permute-start.8 = (bf16[12,64,128]{2,1,0:T(8,128)(2,1)S(1)}, bf16[12,64,128]{2,1,0:T(8,128)(2,1)S(1)}, u32[]{:S(2)}, u32[]{:S(2)}) collective-permute-start(bf16[12,64,128]{2,1,0:T(8,128)(2,1)S(1)} %collective-permute-done.5), channel_id=1, source_target_pairs={{0,64},{1,65},{2,66},{3,67},{4,68},{5,69},{6,70},{7,71},{8,72},{9,... | collective-permute-start | bytes 589832 | tf_op jit(solution)/shard_map/ppermute | solution.py:539
  42.0 20.2 %collective-permute-start.11 = (bf16[4,12,64,128]{3,2,1,0:T(8,128)(2,1)S(1)}, bf16[4,12,64,128]{3,2,1,0:T(8,128)(2,1)S(1)}, u32[]{:S(2)}, u32[]{:S(2)}) collective-permute-start(bf16[4,12,64,128]{3,2,1,0:T(8,128)(2,1)S(1)} %pad_maximum_fusion._.a_own), channel_id=1, source_target_pairs={{0,96},{1,97},{2,98},{3,99},{4,100},{5,101},{6,102},{7,103},{8,104... | collective-permute-start | bytes 2359304 | tf_op jit(solution)/shard_map/ppermute | solution.py:539
  42.7 23.0 %collective-permute-start.4 = (bf16[4,12,64,128]{3,2,1,0:T(8,128)(2,1)S(1)}, bf16[4,12,64,128]{3,2,1,0:T(8,128)(2,1)S(1)}, u32[]{:S(2)}, u32[]{:S(2)}) collective-permute-start(bf16[4,12,64,128]{3,2,1,0:T(8,128)(2,1)S(1)} %pad_maximum_fusion._.a_own), channel_id=1, source_target_pairs={{0,32},{1,33},{2,34},{3,35},{4,36},{5,37},{6,38},{7,39},{8,40},{9,... | collective-permute-start | bytes 2359304 | tf_op jit(solution)/shard_map/ppermute | solution.py:539
  47.0 7.2 %copy-start.7 = (s32[2]{0:T(128)S(1)}, s32[2]{0:T(128)}, u32[]{:S(2)}) copy-start(s32[2]{0:T(128)} %pad_add_fusion.place) | copy-start | bytes 28
  47.1 18.6 %collective-permute-start.9 = (bf16[4,12,64,128]{3,2,1,0:T(8,128)(2,1)S(1)}, bf16[4,12,64,128]{3,2,1,0:T(8,128)(2,1)S(1)}, u32[]{:S(2)}, u32[]{:S(2)}) collective-permute-start(bf16[4,12,64,128]{3,2,1,0:T(8,128)(2,1)S(1)} %pad_maximum_fusion.1.b_own), channel_id=1, source_target_pairs={{0,8},{1,9},{2,10},{3,11},{4,12},{5,13},{6,14},{7,15},{8,16},{9,17... | collective-permute-start | bytes 2359304 | tf_op jit(solution)/shard_map/ppermute | solution.py:539
  47.2 20.5 %collective-permute-start.14 = (bf16[4,12,64,128]{3,2,1,0:T(8,128)(2,1)S(1)}, bf16[4,12,64,128]{3,2,1,0:T(8,128)(2,1)S(1)}, u32[]{:S(2)}, u32[]{:S(2)}) collective-permute-start(bf16[4,12,64,128]{3,2,1,0:T(8,128)(2,1)S(1)} %pad_maximum_fusion.1.b_own), channel_id=1, source_target_pairs={{0,24},{1,25},{2,26},{3,27},{4,28},{5,29},{6,30},{7,31},{8,0},{9,1... | collective-permute-start | bytes 2359304 | tf_op jit(solution)/shard_map/ppermute | solution.py:539
  49.8 3.7 %copy-start.1 = (bf16[1536,3072]{1,0:T(8,128)(2,1)S(1)}, bf16[1536,3072]{1,0:T(8,128)(2,1)}, u32[]{:S(2)}) copy-start(bf16[1536,3072]{1,0:T(8,128)(2,1)} %source.1) | copy-start | bytes 28311556
  62.2 14.4 %collective-permute-start.12 = (bf16[2,12,64,128]{3,2,1,0:T(8,128)(2,1)S(1)}, bf16[2,12,64,128]{3,2,1,0:T(8,128)(2,1)S(1)}, u32[]{:S(2)}, u32[]{:S(2)}) collective-permute-start(bf16[2,12,64,128]{3,2,1,0:T(8,128)(2,1)S(1)} %slice.16), channel_id=1, source_target_pairs={{0,96},{1,97},{2,98},{3,99},{4,100},{5,101},{6,102},{7,103},{8,104... | collective-permute-start | bytes 1179656 | tf_op jit(solution)/shard_map/ppermute | solution.py:539
  65.7 10.9 %collective-permute-start.10 = (bf16[2,12,64,128]{3,2,1,0:T(8,128)(2,1)S(1)}, bf16[2,12,64,128]{3,2,1,0:T(8,128)(2,1)S(1)}, u32[]{:S(2)}, u32[]{:S(2)}) collective-permute-start(bf16[2,12,64,128]{3,2,1,0:T(8,128)(2,1)S(1)} %slice.12), channel_id=1, source_target_pairs={{0,32},{1,33},{2,34},{3,35},{4,36},{5,37},{6,38},{7,39},{8,40},{9,... | collective-permute-start | bytes 1179656 | tf_op jit(solution)/shard_map/ppermute | solution.py:539
  65.8 10.8 %collective-permute-start.13 = (bf16[2,12,64,128]{3,2,1,0:T(8,128)(2,1)S(1)}, bf16[2,12,64,128]{3,2,1,0:T(8,128)(2,1)S(1)}, u32[]{:S(2)}, u32[]{:S(2)}) collective-permute-start(bf16[2,12,64,128]{3,2,1,0:T(8,128)(2,1)S(1)} %slice.14), channel_id=1, source_target_pairs={{0,8},{1,9},{2,10},{3,11},{4,12},{5,13},{6,14},{7,15},{8,16},{9,17... | collective-permute-start | bytes 1179656 | tf_op jit(solution)/shard_map/ppermute | solution.py:539
  67.7 9.0 %collective-permute-start.15 = (bf16[2,12,64,128]{3,2,1,0:T(8,128)(2,1)S(1)}, bf16[2,12,64,128]{3,2,1,0:T(8,128)(2,1)S(1)}, u32[]{:S(2)}, u32[]{:S(2)}) collective-permute-start(bf16[2,12,64,128]{3,2,1,0:T(8,128)(2,1)S(1)} %slice.17), channel_id=1, source_target_pairs={{0,24},{1,25},{2,26},{3,27},{4,28},{5,29},{6,30},{7,31},{8,0},{9,1... | collective-permute-start | bytes 1179656 | tf_op jit(solution)/shard_map/ppermute | solution.py:539
  80.7 8.5 %collective-permute-start.20 = (bf16[4,128,768]{2,1,0:T(8,128)(2,1)S(1)}, bf16[4,128,768]{2,1,0:T(8,128)(2,1)S(1)}, u32[]{:S(2)}, u32[]{:S(2)}) collective-permute-start(bf16[4,128,768]{2,1,0:T(8,128)(2,1)S(1)} %get-tuple-element.53), channel_id=1, source_target_pairs={{0,1},{1,0},{2,3},{3,2},{4,5},{5,4},{6,7},{7,6},{8,9},{9,8},{10,11... | collective-permute-start | bytes 2359304 | tf_op jit(solution)/shard_map/ppermute | solution.py:539
  89.1 7.4 %collective-permute-start.16 = (bf16[4,128,768]{2,1,0:T(8,128)(2,1)S(1)}, bf16[4,128,768]{2,1,0:T(8,128)(2,1)S(1)}, u32[]{:S(2)}, u32[]{:S(2)}) collective-permute-start(bf16[4,128,768]{2,1,0:T(8,128)(2,1)S(1)} %get-tuple-element.47), channel_id=1, source_target_pairs={{0,1},{1,0},{2,3},{3,2},{4,5},{5,4},{6,7},{7,6},{8,9},{9,8},{10,11... | collective-permute-start | bytes 2359304 | tf_op jit(solution)/shard_map/ppermute | solution.py:539
  89.2 24.5 %copy-start = (bf16[1536,512]{1,0:T(8,128)(2,1)S(1)}, bf16[1536,512]{1,0:T(8,128)(2,1)}, u32[]{:S(2)}) copy-start(bf16[1536,512]{1,0:T(8,128)(2,1)} %refs_8_.1) | copy-start | bytes 4718596
  89.2 24.5 %copy-start.2 = (bf16[1536,512]{1,0:T(8,128)(2,1)S(1)}, bf16[1536,512]{1,0:T(8,128)(2,1)}, u32[]{:S(2)}) copy-start(bf16[1536,512]{1,0:T(8,128)(2,1)} %refs_9_.1) | copy-start | bytes 4718596
  89.2 24.5 %copy-start.6 = (s32[16,12]{1,0:T(8,128)S(1)}, s32[16,12]{1,0:T(8,128)}, u32[]{:S(2)}) copy-start(s32[16,12]{1,0:T(8,128)} %rows_a.5) | copy-start | bytes 2308
  89.2 24.5 %copy-start.8 = (s32[16,12]{1,0:T(8,128)S(1)}, s32[16,12]{1,0:T(8,128)}, u32[]{:S(2)}) copy-start(s32[16,12]{1,0:T(8,128)} %rows_b.3) | copy-start | bytes 2308
  89.2 24.5 %copy-start.9 = (s32[16]{0:T(128)S(1)}, s32[16]{0:T(128)}, u32[]{:S(2)}) copy-start(s32[16]{0:T(128)} %counts_a.5) | copy-start | bytes 196
  89.3 24.5 %copy-start.10 = (s32[16]{0:T(128)S(1)}, s32[16]{0:T(128)}, u32[]{:S(2)}) copy-start(s32[16]{0:T(128)} %counts_b.3) | copy-start | bytes 196
  90.3 9.8 %collective-permute-start.21 = (bf16[128,768]{1,0:T(8,128)(2,1)S(1)}, bf16[128,768]{1,0:T(8,128)(2,1)S(1)}, u32[]{:S(2)}, u32[]{:S(2)}) collective-permute-start(bf16[128,768]{1,0:T(8,128)(2,1)S(1)} %get-tuple-element.55), channel_id=1, source_target_pairs={{0,2},{1,3},{2,4},{3,5},{4,6},{5,7},{6,0},{7,1},{8,10},{9,11},{10,... | collective-permute-start | bytes 589832 | tf_op jit(solution)/shard_map/ppermute | solution.py:539
  90.6 14.6 %collective-permute-start.22 = (bf16[128,768]{1,0:T(8,128)(2,1)S(1)}, bf16[128,768]{1,0:T(8,128)(2,1)S(1)}, u32[]{:S(2)}, u32[]{:S(2)}) collective-permute-start(bf16[128,768]{1,0:T(8,128)(2,1)S(1)} %get-tuple-element.56), channel_id=1, source_target_pairs={{0,4},{1,5},{2,6},{3,7},{4,0},{5,1},{6,2},{7,3},{8,12},{9,13},{10,... | collective-permute-start | bytes 589832 | tf_op jit(solution)/shard_map/ppermute | solution.py:539
  96.5 8.8 %collective-permute-start.23 = (bf16[128,768]{1,0:T(8,128)(2,1)S(1)}, bf16[128,768]{1,0:T(8,128)(2,1)S(1)}, u32[]{:S(2)}, u32[]{:S(2)}) collective-permute-start(bf16[128,768]{1,0:T(8,128)(2,1)S(1)} %get-tuple-element.57), channel_id=1, source_target_pairs={{0,6},{1,7},{2,0},{3,1},{4,2},{5,3},{6,4},{7,5},{8,14},{9,15},{10,... | collective-permute-start | bytes 589832 | tf_op jit(solution)/shard_map/ppermute | solution.py:539
  97.5 11.3 %collective-permute-start.17 = (bf16[128,768]{1,0:T(8,128)(2,1)S(1)}, bf16[128,768]{1,0:T(8,128)(2,1)S(1)}, u32[]{:S(2)}, u32[]{:S(2)}) collective-permute-start(bf16[128,768]{1,0:T(8,128)(2,1)S(1)} %get-tuple-element.49), channel_id=1, source_target_pairs={{0,2},{1,3},{2,4},{3,5},{4,6},{5,7},{6,0},{7,1},{8,10},{9,11},{10,... | collective-permute-start | bytes 589832 | tf_op jit(solution)/shard_map/ppermute | solution.py:539
  99.1 14.6 %collective-permute-start.18 = (bf16[128,768]{1,0:T(8,128)(2,1)S(1)}, bf16[128,768]{1,0:T(8,128)(2,1)S(1)}, u32[]{:S(2)}, u32[]{:S(2)}) collective-permute-start(bf16[128,768]{1,0:T(8,128)(2,1)S(1)} %get-tuple-element.50), channel_id=1, source_target_pairs={{0,4},{1,5},{2,6},{3,7},{4,0},{5,1},{6,2},{7,3},{8,12},{9,13},{10,... | collective-permute-start | bytes 589832 | tf_op jit(solution)/shard_map/ppermute | solution.py:539
  100.1 13.5 %collective-permute-start.19 = (bf16[128,768]{1,0:T(8,128)(2,1)S(1)}, bf16[128,768]{1,0:T(8,128)(2,1)S(1)}, u32[]{:S(2)}, u32[]{:S(2)}) collective-permute-start(bf16[128,768]{1,0:T(8,128)(2,1)S(1)} %get-tuple-element.51), channel_id=1, source_target_pairs={{0,6},{1,7},{2,0},{3,1},{4,2},{5,3},{6,4},{7,5},{8,14},{9,15},{10,... | collective-permute-start | bytes 589832 | tf_op jit(solution)/shard_map/ppermute | solution.py:539
  113.7 31.9 %copy-start.3 = (bf16[512,512]{1,0:T(8,128)(2,1)S(1)}, bf16[512,512]{1,0:T(8,128)(2,1)}, u32[]{:S(2)}) copy-start(bf16[512,512]{1,0:T(8,128)(2,1)} %top.5) | copy-start | bytes 1572868
  113.7 31.9 %copy-start.4 = (f32[64,512]{1,0:T(8,128)S(1)}, f32[64,512]{1,0:T(8,128)}, u32[]{:S(2)}) copy-start(f32[64,512]{1,0:T(8,128)} %base.1) | copy-start | bytes 393220
  115.6 13.8 %collective-permute-start.27 = (bf16[128,1536]{1,0:T(8,128)(2,1)S(1)}, bf16[128,1536]{1,0:T(8,128)(2,1)S(1)}, u32[]{:S(2)}, u32[]{:S(2)}) collective-permute-start(bf16[128,1536]{1,0:T(8,128)(2,1)S(1)} %get-tuple-element.69.refs_0_), channel_id=1, source_target_pairs={{0,2},{1,3},{2,4},{3,5},{4,6},{5,7},{6,0},{7,1},{8,10},{9,11},{10,... | collective-permute-start | bytes 1179656 | tf_op jit(solution)/shard_map/ppermute | solution.py:539
  116.0 13.5 %collective-permute-start.28 = (bf16[128,1536]{1,0:T(8,128)(2,1)S(1)}, bf16[128,1536]{1,0:T(8,128)(2,1)S(1)}, u32[]{:S(2)}, u32[]{:S(2)}) collective-permute-start(bf16[128,1536]{1,0:T(8,128)(2,1)S(1)} %get-tuple-element.69.refs_0_), channel_id=1, source_target_pairs={{0,6},{1,7},{2,0},{3,1},{4,2},{5,3},{6,4},{7,5},{8,14},{9,15},{10,... | collective-permute-start | bytes 1179656 | tf_op jit(solution)/shard_map/ppermute | solution.py:539
  118.4 6.1 %collective-permute-start.24 = (bf16[192,512]{1,0:T(8,128)(2,1)S(1)}, bf16[192,512]{1,0:T(8,128)(2,1)S(1)}, u32[]{:S(2)}, u32[]{:S(2)}) collective-permute-start(bf16[192,512]{1,0:T(8,128)(2,1)S(1)} %get-tuple-element.60.one), channel_id=1, source_target_pairs={{0,8},{1,9},{2,10},{3,11},{4,12},{5,13},{6,14},{7,15},{8,16},{9,17... | collective-permute-start | bytes 589832 | tf_op jit(solution)/shard_map/ppermute | solution.py:539
  118.8 5.8 %collective-permute-start.25 = (bf16[192,512]{1,0:T(8,128)(2,1)S(1)}, bf16[192,512]{1,0:T(8,128)(2,1)S(1)}, u32[]{:S(2)}, u32[]{:S(2)}) collective-permute-start(bf16[192,512]{1,0:T(8,128)(2,1)S(1)} %get-tuple-element.60.one), channel_id=1, source_target_pairs={{0,24},{1,25},{2,26},{3,27},{4,28},{5,29},{6,30},{7,31},{8,0},{9,1... | collective-permute-start | bytes 589832 | tf_op jit(solution)/shard_map/ppermute | solution.py:539
  121.2 8.2 %collective-permute-start.26 = (bf16[192,512]{1,0:T(8,128)(2,1)S(1)}, bf16[192,512]{1,0:T(8,128)(2,1)S(1)}, u32[]{:S(2)}, u32[]{:S(2)}) collective-permute-start(bf16[192,512]{1,0:T(8,128)(2,1)S(1)} %get-tuple-element.60.one), channel_id=1, source_target_pairs={{0,16},{1,17},{2,18},{3,19},{4,20},{5,21},{6,22},{7,23},{8,24},{9,... | collective-permute-start | bytes 589832 | tf_op jit(solution)/shard_map/ppermute | solution.py:539
  129.5 17.2 %collective-permute-start.32 = (bf16[128,1536]{1,0:T(8,128)(2,1)S(1)}, bf16[128,1536]{1,0:T(8,128)(2,1)S(1)}, u32[]{:S(2)}, u32[]{:S(2)}) collective-permute-start(bf16[128,1536]{1,0:T(8,128)(2,1)S(1)} %get-tuple-element.69.refs_0_), channel_id=1, source_target_pairs={{0,4},{1,5},{2,6},{3,7},{4,0},{5,1},{6,2},{7,3},{8,12},{9,13},{10,... | collective-permute-start | bytes 1179656 | tf_op jit(solution)/shard_map/ppermute | solution.py:539
  132.1 6.0 %collective-permute-start.29 = (bf16[192,512]{1,0:T(8,128)(2,1)S(1)}, bf16[192,512]{1,0:T(8,128)(2,1)S(1)}, u32[]{:S(2)}, u32[]{:S(2)}) collective-permute-start(bf16[192,512]{1,0:T(8,128)(2,1)S(1)} %fold.1.one), channel_id=1, source_target_pairs={{0,32},{1,33},{2,34},{3,35},{4,36},{5,37},{6,38},{7,39},{8,40},{9,... | collective-permute-start | bytes 589832 | tf_op jit(solution)/shard_map/ppermute | solution.py:539
  132.2 7.8 %collective-permute-start.30 = (bf16[192,512]{1,0:T(8,128)(2,1)S(1)}, bf16[192,512]{1,0:T(8,128)(2,1)S(1)}, u32[]{:S(2)}, u32[]{:S(2)}) collective-permute-start(bf16[192,512]{1,0:T(8,128)(2,1)S(1)} %fold.1.one), channel_id=1, source_target_pairs={{0,96},{1,97},{2,98},{3,99},{4,100},{5,101},{6,102},{7,103},{8,104... | collective-permute-start | bytes 589832 | tf_op jit(solution)/shard_map/ppermute | solution.py:539
  134.8 8.1 %collective-permute-start.31 = (bf16[192,512]{1,0:T(8,128)(2,1)S(1)}, bf16[192,512]{1,0:T(8,128)(2,1)S(1)}, u32[]{:S(2)}, u32[]{:S(2)}) collective-permute-start(bf16[192,512]{1,0:T(8,128)(2,1)S(1)} %fold.1.one), channel_id=1, source_target_pairs={{0,64},{1,65},{2,66},{3,67},{4,68},{5,69},{6,70},{7,71},{8,72},{9,... | collective-permute-start | bytes 589832 | tf_op jit(solution)/shard_map/ppermute | solution.py:539
  142.9 7.7 %collective-permute-start.33 = (bf16[128,1536]{1,0:T(8,128)(2,1)S(1)}, bf16[128,1536]{1,0:T(8,128)(2,1)S(1)}, u32[]{:S(2)}, u32[]{:S(2)}) collective-permute-start(bf16[128,1536]{1,0:T(8,128)(2,1)S(1)} %get-tuple-element.69.refs_0_), channel_id=1, source_target_pairs={{0,1},{1,0},{2,3},{3,2},{4,5},{5,4},{6,7},{7,6},{8,9},{9,8},{10,11... | collective-permute-start | bytes 1179656 | tf_op jit(solution)/shard_map/ppermute | solution.py:539
  145.1 5.4 %collective-permute-start.34 = (bf16[128,1536]{1,0:T(8,128)(2,1)S(1)}, bf16[128,1536]{1,0:T(8,128)(2,1)}, u32[]{:S(2)}, u32[]{:S(2)}) collective-permute-start(bf16[128,1536]{1,0:T(8,128)(2,1)S(1)} %collective-permute-done.27.refs_1_), channel_id=1, source_target_pairs={{0,1},{1,0},{2,3},{3,2},{4,5},{5,4},{6,7},{7,6},{8,9},{9,8},{10,11... | collective-permute-start | bytes 1179656 | tf_op jit(solution)/shard_map/ppermute | solution.py:539
  145.2 5.4 %collective-permute-start.35 = (bf16[128,1536]{1,0:T(8,128)(2,1)S(1)}, bf16[128,1536]{1,0:T(8,128)(2,1)}, u32[]{:S(2)}, u32[]{:S(2)}) collective-permute-start(bf16[128,1536]{1,0:T(8,128)(2,1)S(1)} %collective-permute-done.28.refs_2_), channel_id=1, source_target_pairs={{0,1},{1,0},{2,3},{3,2},{4,5},{5,4},{6,7},{7,6},{8,9},{9,8},{10,11... | collective-permute-start | bytes 1179656 | tf_op jit(solution)/shard_map/ppermute | solution.py:539
  146.8 3.8 %collective-permute-start.36 = (bf16[128,1536]{1,0:T(8,128)(2,1)S(1)}, bf16[128,1536]{1,0:T(8,128)(2,1)}, u32[]{:S(2)}, u32[]{:S(2)}) collective-permute-start(bf16[128,1536]{1,0:T(8,128)(2,1)S(1)} %collective-permute-done.32.refs_3_), channel_id=1, source_target_pairs={{0,1},{1,0},{2,3},{3,2},{4,5},{5,4},{6,7},{7,6},{8,9},{9,8},{10,11... | collective-permute-start | bytes 1179656 | tf_op jit(solution)/shard_map/ppermute | solution.py:539
  146.9 9.0 %all-to-all-start = ((bf16[8,64,128]{2,1,0:T(8,128)(2,1)}), bf16[8,64,128]{2,1,0:T(8,128)(2,1)S(1)}, u32[]{:S(2)}, u32[]{:S(2)}) async-start(bf16[8,64,128]{2,1,0:T(8,128)(2,1)} %get-tuple-element.70), calls=%async_computation | async-start | bytes 262144 | tf_op jit(solution)/shard_map/all_to_all | solution.py:582
  150.6 5.3 %copy-start.5 = (f32[64,512]{1,0:T(8,128)S(1)}, f32[64,512]{1,0:T(8,128)}, u32[]{:S(2)}) copy-start(f32[64,512]{1,0:T(8,128)} %base.2) | copy-start | bytes 393220

commit v9 on v8

--- a/solution.py
+++ b/solution.py
@@ -15,7 +15,6 @@
 PART = 64
 COLS = 8
 STEPS = (0, 1, -1, 2)
-STRIP = 2 * BS
 PAIR = 2 * PART
 BOTH = ("row", "col")
 MIB = 1024 * 1024
@@ -152,11 +151,6 @@
     return (value + by + SIDE) % SIDE
 
 
-def load_a(copies, buf, u, spread, start=0, many=SIDE):
-    for i in range(start, start + many):
-        copies.append((buf.at[i - start], spread.at[:, u // 2, i * PART : (i + 1) * PART, :]))
-
-
 def load_b(copies, buf, u, first, spread, start=0, many=SIDE):
     for i in range(start, start + many):
         ui = turn(u, -STEPS[i])
@@ -164,12 +158,8 @@
         copies.append((buf.at[i - start], spread.at[:, ui // 2, at, :]))
 
 
-def run_copies(copies, sems):
-    started = [pltpu.make_async_copy(a, b, sems.at[i]) for i, (a, b) in enumerate(copies)]
-    for copy in started:
-        copy.start()
-    for copy in started:
-        copy.wait()
+def copies_of(copies, sems):
+    return [pltpu.make_async_copy(a, b, sems.at[i]) for i, (a, b) in enumerate(copies)]
 
 
 def multiply(spread, tile):
@@ -198,36 +188,56 @@
     )(trailing, after)
 
 
-def rows_of(tile, step):
-    return tile[pl.ds(pl.multiple_of(step * STRIP, STRIP), STRIP), :]
-
-
-def half_multiply(spread, tile, step, h):
-    rows = pl.ds(pl.multiple_of(step * STRIP, STRIP), STRIP)
-    left = jnp.concatenate([spread[n] for n in range(NB)], axis=1)
+def multiply_half(members, tile, strip, step, h):
+    rows = pl.ds(pl.multiple_of(step * strip, strip), strip)
+    left = jnp.concatenate(
+        [jnp.concatenate([member[n] for member in members], axis=0) for n in range(NB)], axis=1
+    )
     right = jnp.concatenate(
         [tile[rows, pl.ds(pl.multiple_of((2 * n + h) * BS, BS), BS)] for n in range(NB)], axis=1
     )
     return lax.dot_general(left, right, (((1,), (1,)), ((), ())), preferred_element_type=F32)
 
 
-def load_half(copies, buf, spread, start=0, many=SIDE):
-    for i in range(start, start + many):
-        copies.append((buf.at[i - start], spread.at[:, i * PART : (i + 1) * PART, :]))
-
-
-def own_body(place, a_own, b_own, tile, half_a, whole_b, spread_a, spread_b, sems):
+def members_of(*lists):
+    return [part.at[i] for part in lists for i in range(part.shape[0])]
+
+
+def on_first(action):
+    pl.when(pl.program_id(0) == 0)(action)
+
+
+def start_all(copies):
+    for copy in copies:
+        copy.start()
+
+
+def wait_all(copies):
+    for copy in copies:
+        copy.wait()
+
+
+def rows_of(tile, strip, step):
+    return tile[pl.ds(pl.multiple_of(step * strip, strip), strip), :]
+
+
+IN_VMEM = pl.BlockSpec(memory_space=pltpu.VMEM)
+ANYWHERE = pl.BlockSpec(memory_space=pl.ANY)
+WIDE = 4 * BS
+NARROW = 3 * BS
+HALF_STEPS = ROWS // NARROW // 2
+
+
+def own_body(place, a_own, b_own, tile, half_a, whole_b, spread, sems):
     u, _ = where(place)
-
-    @pl.when(pl.program_id(0) == 0)
-    def _():
-        copies = []
-        load_half(copies, a_own, spread_a)
-        load_b(copies, b_own, u, 0, spread_b)
-        run_copies(copies, sems)
-
-    half_a[...] = half_multiply(spread_a, tile, pl.program_id(0), u // 2)
-    whole_b[...] = multiply(spread_b, rows_of(tile, pl.program_id(0)))
+    step = pl.program_id(0)
+    pairs = []
+    load_b(pairs, b_own, u, 0, spread)
+    copies = copies_of(pairs, sems)
+    on_first(lambda: start_all(copies))
+    half_a[...] = multiply_half(members_of(a_own), tile, WIDE, step, u // 2)
+    on_first(lambda: wait_all(copies))
+    whole_b[...] = multiply(spread, rows_of(tile, WIDE, step))
 
 
 def own_product(place, a_own, b_own, trailing):
@@ -237,17 +247,15 @@
         name="own_product",
         grid_spec=pltpu.PrefetchScalarGridSpec(
             num_scalar_prefetch=1,
-            grid=(ROWS // STRIP,),
-            in_specs=[pl.BlockSpec(memory_space=pl.ANY)] * 2
-            + [pl.BlockSpec(memory_space=pltpu.VMEM)],
+            grid=(ROWS // WIDE,),
+            in_specs=[IN_VMEM, ANYWHERE, IN_VMEM],
             out_specs=[
-                pl.BlockSpec((W // 2, STRIP), lambda i, *_: (0, i)),
-                pl.BlockSpec((2 * PART, STRIP), lambda i, *_: (0, i)),
+                pl.BlockSpec((W // 2, WIDE), lambda i, *_: (0, i)),
+                pl.BlockSpec((2 * PART, WIDE), lambda i, *_: (0, i)),
             ],
             scratch_shapes=[
-                pltpu.VMEM((NB, W // 2, BS), BF),
                 pltpu.VMEM((NB, 2, 2 * PART, BS), BF),
-                pltpu.SemaphoreType.DMA((8,)),
+                pltpu.SemaphoreType.DMA((4,)),
             ],
         ),
         out_shape=[
@@ -261,22 +269,22 @@
 
 def early_body(place, a_down, a_up, b_down, b_up, tile, whole_b, out, spread, sems):
     u, v = where(place)
-
-    @pl.when(pl.program_id(0) == 0)
-    def _():
-        copies = []
-        load_a(copies, a_down, turn(u, -1), spread)
-        load_a(copies, a_up, turn(u, 1), spread)
-        for t, buf in enumerate((b_down, b_up)):
-            load_b(copies, buf, u, W // 2 + 2 * t * PART, spread)
-        run_copies(copies, sems)
-
-    value = multiply(spread, rows_of(tile, pl.program_id(0)))
-    for i, step in enumerate(STEPS):
-        out[2 * turn(v, -step) + (u + 1) % 2, :PART, :] = value[i * PART : (i + 1) * PART]
+    step = pl.program_id(0)
+    pairs = []
+    load_b(pairs, b_down, u, 0, spread)
+    load_b(pairs, b_up, u, 2 * PART, spread)
+    copies = copies_of(pairs, sems)
+    on_first(lambda: start_all(copies))
+    value = multiply_half(members_of(a_down), tile, WIDE, step, turn(u, -1) // 2)
+    value = value + multiply_half(members_of(a_up), tile, WIDE, step, turn(u, 1) // 2)
+    value = value.astype(BF)
+    for i, far in enumerate(STEPS):
+        out[2 * turn(v, -far) + (u + 1) % 2, :PART, :] = value[i * PART : (i + 1) * PART]
+    on_first(lambda: wait_all(copies))
+    value = multiply(spread, rows_of(tile, WIDE, step))
     for j in range(4):
         to = 2 * turn(v, -STEPS[1 + j // 2]) + j % 2
-        out[to, PART:, :] = value[W // 2 + j * PART : W // 2 + (j + 1) * PART]
+        out[to, PART:, :] = value[j * PART : (j + 1) * PART]
     for j in range(2):
         out[2 * v + j, PART:, :] = whole_b[j * PART : (j + 1) * PART, :]
 
@@ -289,16 +297,14 @@
         name="early_product",
         grid_spec=pltpu.PrefetchScalarGridSpec(
             num_scalar_prefetch=1,
-            grid=(ROWS // STRIP,),
-            in_specs=[pl.BlockSpec(memory_space=pl.ANY)] * 4
-            + [
-                pl.BlockSpec(memory_space=pltpu.VMEM),
-                pl.BlockSpec((2 * PART, STRIP), lambda i, *_: (0, i)),
-            ],
-            out_specs=pl.BlockSpec((COLS, PAIR, STRIP), lambda i, *_: (0, 0, i)),
+            grid=(ROWS // WIDE,),
+            in_specs=[IN_VMEM] * 2
+            + [ANYWHERE] * 2
+            + [IN_VMEM, pl.BlockSpec((2 * PART, WIDE), lambda i, *_: (0, i))],
+            out_specs=pl.BlockSpec((COLS, PAIR, WIDE), lambda i, *_: (0, 0, i)),
             scratch_shapes=[
-                pltpu.VMEM((NB, 2, rows, BS), BF),
-                pltpu.SemaphoreType.DMA((16,)),
+                pltpu.VMEM((NB, 2, 4 * PART, BS), BF),
+                pltpu.SemaphoreType.DMA((8,)),
             ],
         ),
         out_shape=jax.ShapeDtypeStruct((COLS, PAIR, ROWS), BF),
@@ -308,27 +314,23 @@
 
 
 def late_body(
-    half, place, a_far, a_far_more, b_far, b_far_more, tile, before, half_a, keep, give, spread_a, spread_b, ready, sems
+    half, place, a_far, a_more, b_far, b_more, tile, before, half_a, keep, give, spread, ready, sems
 ):
     u, v = where(place)
     core = place[1] % 2
-
-    @pl.when(pl.program_id(0) == 0)
-    def _():
-        copies = []
-        load_half(copies, a_far, spread_a, 0, 2)
-        load_half(copies, a_far_more, spread_a, 2, 2)
-        load_b(copies, b_far, u, 0, spread_b, 0, 2)
-        load_b(copies, b_far_more, u, 0, spread_b, 2, 2)
-        run_copies(copies, sems)
-
+    step = half * HALF_STEPS + pl.program_id(0)
+    pairs = []
+    load_b(pairs, b_far, u, 0, spread, 0, 2)
+    load_b(pairs, b_more, u, 0, spread, 2, 2)
+    copies = copies_of(pairs, sems)
+    on_first(lambda: start_all(copies))
     ready[...] = before[...]
-    step = half * HALF_STEPS + pl.program_id(0)
-    value = half_multiply(spread_a, tile, step, turn(u, 2) // 2)
+    value = multiply_half(members_of(a_far, a_more), tile, NARROW, step, turn(u, 2) // 2)
     value = (value + half_a[...]).astype(BF)
     for i, far in enumerate(STEPS):
         ready[2 * turn(v, -far) + u % 2, :PART, :] = value[i * PART : (i + 1) * PART]
-    value = multiply(spread_b, rows_of(tile, step))
+    on_first(lambda: wait_all(copies))
+    value = multiply(spread, rows_of(tile, NARROW, step))
     for j in range(2):
         ready[2 * turn(v, 2) + j, PART:, :] = value[j * PART : (j + 1) * PART]
     for x in range(SIDE):
@@ -336,32 +338,29 @@
         give[x] = ready[2 * x + 1 - core]
 
 
-HALF_STEPS = ROWS // STRIP // 2
-
-
 def late_product(half, place, bufs, trailing, before, half_a):
     deep = trailing.shape[1]
     rows = W // 4 + 2 * PART
     out = jax.ShapeDtypeStruct((SIDE, PAIR, ROWS // 2), BF)
-    spec = pl.BlockSpec((SIDE, PAIR, STRIP), lambda i, *_: (0, 0, i))
+    spec = pl.BlockSpec((SIDE, PAIR, NARROW), lambda i, *_: (0, 0, i))
     return pl.pallas_call(
         functools.partial(late_body, half),
         name="late_product",
         grid_spec=pltpu.PrefetchScalarGridSpec(
             num_scalar_prefetch=1,
             grid=(HALF_STEPS,),
-            in_specs=[pl.BlockSpec(memory_space=pl.ANY)] * 4
+            in_specs=[IN_VMEM] * 2
+            + [ANYWHERE] * 2
             + [
-                pl.BlockSpec(memory_space=pltpu.VMEM),
-                pl.BlockSpec((COLS, PAIR, STRIP), lambda i, *_: (0, 0, half * HALF_STEPS + i)),
-                pl.BlockSpec((W // 2, STRIP), lambda i, *_: (0, half * HALF_STEPS + i)),
+                IN_VMEM,
+                pl.BlockSpec((COLS, PAIR, NARROW), lambda i, *_: (0, 0, half * HALF_STEPS + i)),
+                pl.BlockSpec((W // 2, NARROW), lambda i, *_: (0, half * HALF_STEPS + i)),
             ],
             out_specs=[spec, spec],
             scratch_shapes=[
-                pltpu.VMEM((NB, W // 2, BS), BF),
                 pltpu.VMEM((NB, 2, 2 * PART, BS), BF),
-                pltpu.VMEM((COLS, PAIR, STRIP), BF),
-                pltpu.SemaphoreType.DMA((8,)),
+                pltpu.VMEM((COLS, PAIR, NARROW), BF),
+                pltpu.SemaphoreType.DMA((4,)),
             ],
         ),
         out_shape=[out, out],
@@ -550,7 +549,6 @@
     lists = (rows_a, counts_a, rows_b, counts_b)
     part_a = lax.ppermute(prep_a(place, lists, factor_a), BOTH, spread_pairs())
     part_b = prep_b(place, lists, factor_a, factor_b, factor_top)
-    part_b, _ = lax.optimization_barrier((part_b, part_a))
     part_b = lax.ppermute(part_b, BOTH, spread_pairs())
     a_own = jnp.stack(around(part_a, "dy"))
     b_own = jnp.stack(around(part_b, "dz"))

time: 157 us -> 158 us (level)
  Pallas kernels: 40.7 us -> 43.1 us
  waiting for transfers between devices: 52.4 us -> 50.1 us
    ppermute x35, waiting for transfers between devices: 33.4 us -> 41.3 us  [send(): return lax.ppermute(value, BOTH, shifted(**by))]
    ppermute x1, waiting for transfers between devices: 10.8 us -> 5.6 us  [on_device(): part_b = lax.ppermute(part_b, BOTH, spread_pairs())]
    ppermute x1, waiting for transfers between devices: 7.65 us -> 2.72 us  [on_device(): part_a = lax.ppermute(prep_a(place, lists, factor_a), BOTH, spread_pairs())]
    ppermute x35, starting transfers between devices: 47.5 us -> 44.4 us  [send(): return lax.ppermute(value, BOTH, shifted(**by))]
    ppermute x1, starting transfers between devices: 1.91 us -> 4.92 us  [on_device(): part_b = lax.ppermute(part_b, BOTH, spread_pairs())]
    pallas_call x2, Pallas kernels: 8.01 us -> 10.1 us  [late_product(): pl.pallas_call(functools.partial(late_body, half), name='late_product', g...]
  transfers between devices with their start and end apart: 38 -> 38, of which waited for: 16 -> 16; matrix products, arithmetic and copies ran while one was open for 0% -> 0% of each run, Pallas kernels for 20% -> 21%
where the time goes in v9:
time: 158 us; the launch traced here: 157 us
  starting transfers between devices  58.3 us (37%)
  waiting for transfers between devices  50.1 us (32%)
  Pallas kernels  43.1 us (27%)
  local copies, waits for them, and re-layouts  3.84 us (2%)
    ppermute x35, starting transfers between devices, send(): return lax.ppermute(value, BOTH, shifted(**by))  44.4 us
    ppermute x35, waiting for transfers between devices, send(): return lax.ppermute(value, BOTH, shifted(**by))  41.3 us
    pallas_call x2, Pallas kernels, late_product(): pl.pallas_call(functools.partial(late_body, half), name='late_product', g...  10.1 us
    pallas_call x1, Pallas kernels, early_product(): pl.pallas_call(early_body, name='early_product', grid_spec=pltpu.Prefetch...  7.82 us
    pallas_call x1, Pallas kernels, own_product(): pl.pallas_call(own_body, name='own_product', grid_spec=pltpu.PrefetchScal...  6.57 us
    ppermute x1, waiting for transfers between devices, on_device(): part_b = lax.ppermute(part_b, BOTH, spread_pairs())  5.6 us
    ppermute x1, starting transfers between devices, on_device(): part_a = lax.ppermute(prep_a(place, lists, factor_a), BOTH, spread_pairs())  4.92 us
    ppermute x1, starting transfers between devices, on_device(): part_b = lax.ppermute(part_b, BOTH, spread_pairs())  4.92 us
  transfers between devices with their start and end apart: 38, of which 16 were waited for; matrix products, arithmetic and copies ran while one was open for 0% of the time, Pallas kernels for 21%

profile of v9, /device:TPU:1, one launch (start us, length us, event | category | flops | bytes accessed | tf_op | source)
XLA Modules:
  0.0 157.2 jit_solution(14701271103353747888)
XLA Ops:
  0.6 0.6 pad_add_fusion.place
  1.2 2.9 %prep_a.1 = bf16[12,64,128]{2,1,0:T(8,128)(2,1)} custom-call(s32[2]{0:T(128)} %pad_add_fusion.place, s32[16,12]{1,0:T(8,128)} %rows_a.5, s32[16]{0:T(128)} %counts_a.5, bf16[1536,512]{1,0:T(8,128)(2,1)} %refs_8_.1), custom_call_target="tpu_custom_call" | custom-call | bytes 786432 | tf_op jit(solution)/shard_map/prep_a/pallas_call | solution.py:94
  4.1 4.9 %collective-permute-start = (bf16[12,64,128]{2,1,0:T(8,128)(2,1)}, bf16[12,64,128]{2,1,0:T(8,128)(2,1)S(1)}, u32[]{:S(2)}, u32[]{:S(2)}) collective-permute-start(bf16[12,64,128]{2,1,0:T(8,128)(2,1)} %prep_a.1), channel_id=1, source_target_pairs={{0,0},{1,32},{2,8},{3,40},{4,16},{5,48},{6,24},{7,56},{8,9},{9,41}... | collective-permute-start | bytes 589832 | tf_op jit(solution)/shard_map/ppermute | solution.py:550
  9.0 4.3 %prep_b.1 = bf16[12,64,128]{2,1,0:T(8,128)(2,1)} custom-call(s32[2]{0:T(128)} %pad_add_fusion.place, s32[16,12]{1,0:T(8,128)} %rows_a.5, s32[16]{0:T(128)} %counts_a.5, s32[16,12]{1,0:T(8,128)} %rows_b.3, s32[16]{0:T(128)} %counts_b.3, bf16[1536,512]{1,0:T(8,128)(2,1)} %refs_8_.1, bf16[1536,512]{1,0:T(8,128)(2,1)} %refs_9_.1, bf16[512,512]{1,0:T(8,128)(2,1)} %top.5), custom_call_target="tpu_custom_call" | custom-call | flops 201326592 | bytes 3145728 | tf_op jit(solution)/shard_map/prep_b/pallas_call | solution.py:127
  13.3 4.9 %collective-permute-start.5 = (bf16[12,64,128]{2,1,0:T(8,128)(2,1)}, bf16[12,64,128]{2,1,0:T(8,128)(2,1)S(1)}, u32[]{:S(2)}, u32[]{:S(2)}) collective-permute-start(bf16[12,64,128]{2,1,0:T(8,128)(2,1)} %prep_b.1), channel_id=1, source_target_pairs={{0,0},{1,32},{2,8},{3,40},{4,16},{5,48},{6,24},{7,56},{8,9},{9,41}... | collective-permute-start | bytes 589832 | tf_op jit(solution)/shard_map/ppermute | solution.py:552
  18.3 2.7 %collective-permute-done = bf16[12,64,128]{2,1,0:T(8,128)(2,1)S(1)} collective-permute-done((bf16[12,64,128]{2,1,0:T(8,128)(2,1)}, bf16[12,64,128]{2,1,0:T(8,128)(2,1)S(1)}, u32[]{:S(2)}, u32[]{:S(2)}) %collective-permute-start) | collective-permute-done | bytes 196640 | tf_op jit(solution)/shard_map/ppermute | solution.py:550
  21.0 2.7 %collective-permute-start.2 = (bf16[12,64,128]{2,1,0:T(8,128)(2,1)S(1)}, bf16[12,64,128]{2,1,0:T(8,128)(2,1)S(1)}, u32[]{:S(2)}, u32[]{:S(2)}) collective-permute-start(bf16[12,64,128]{2,1,0:T(8,128)(2,1)S(1)} %collective-permute-done), channel_id=1, source_target_pairs={{0,24},{1,25},{2,26},{3,27},{4,28},{5,29},{6,30},{7,31},{8,0},{9,1... | collective-permute-start | bytes 589832 | tf_op jit(solution)/shard_map/ppermute | solution.py:538
  23.7 5.6 %collective-permute-done.5 = bf16[12,64,128]{2,1,0:T(8,128)(2,1)S(1)} collective-permute-done((bf16[12,64,128]{2,1,0:T(8,128)(2,1)}, bf16[12,64,128]{2,1,0:T(8,128)(2,1)S(1)}, u32[]{:S(2)}, u32[]{:S(2)}) %collective-permute-start.5) | collective-permute-done | bytes 196640 | tf_op jit(solution)/shard_map/ppermute | solution.py:552
  29.3 2.9 %collective-permute-start.6 = (bf16[12,64,128]{2,1,0:T(8,128)(2,1)S(1)}, bf16[12,64,128]{2,1,0:T(8,128)(2,1)S(1)}, u32[]{:S(2)}, u32[]{:S(2)}) collective-permute-start(bf16[12,64,128]{2,1,0:T(8,128)(2,1)S(1)} %collective-permute-done.5), channel_id=1, source_target_pairs={{0,32},{1,33},{2,34},{3,35},{4,36},{5,37},{6,38},{7,39},{8,40},{9,... | collective-permute-start | bytes 589832 | tf_op jit(solution)/shard_map/ppermute | solution.py:538
  32.2 2.1 %collective-permute-start.7 = (bf16[12,64,128]{2,1,0:T(8,128)(2,1)S(1)}, bf16[12,64,128]{2,1,0:T(8,128)(2,1)S(1)}, u32[]{:S(2)}, u32[]{:S(2)}) collective-permute-start(bf16[12,64,128]{2,1,0:T(8,128)(2,1)S(1)} %collective-permute-done.5), channel_id=1, source_target_pairs={{0,96},{1,97},{2,98},{3,99},{4,100},{5,101},{6,102},{7,103},{8,104... | collective-permute-start | bytes 589832 | tf_op jit(solution)/shard_map/ppermute | solution.py:538
  34.4 1.3 collective-permute-start.8
  35.6 3.9 %collective-permute-done.2 = bf16[12,64,128]{2,1,0:T(8,128)(2,1)S(1)} collective-permute-done((bf16[12,64,128]{2,1,0:T(8,128)(2,1)S(1)}, bf16[12,64,128]{2,1,0:T(8,128)(2,1)S(1)}, u32[]{:S(2)}, u32[]{:S(2)}) %collective-permute-start.2) | collective-permute-done | bytes 196640 | tf_op jit(solution)/shard_map/ppermute | solution.py:538
  39.5 0.1 pad_maximum_fusion._.a_own
  39.6 0.1 collective-permute-start.4
  39.7 4.2 %collective-permute-done.8 = bf16[12,64,128]{2,1,0:T(8,128)(2,1)S(1)} collective-permute-done((bf16[12,64,128]{2,1,0:T(8,128)(2,1)S(1)}, bf16[12,64,128]{2,1,0:T(8,128)(2,1)S(1)}, u32[]{:S(2)}, u32[]{:S(2)}) %collective-permute-start.8) | collective-permute-done | bytes 196640 | tf_op jit(solution)/shard_map/ppermute | solution.py:538
  43.9 0.1 pad_maximum_fusion.1.b_own
  44.0 1.9 %collective-permute-start.9 = (bf16[4,12,64,128]{3,2,1,0:T(8,128)(2,1)S(1)}, bf16[4,12,64,128]{3,2,1,0:T(8,128)(2,1)S(1)}, u32[]{:S(2)}, u32[]{:S(2)}) collective-permute-start(bf16[4,12,64,128]{3,2,1,0:T(8,128)(2,1)S(1)} %pad_maximum_fusion.1.b_own), channel_id=1, source_target_pairs={{0,8},{1,9},{2,10},{3,11},{4,12},{5,13},{6,14},{7,15},{8,16},{9,17... | collective-permute-start | bytes 2359304 | tf_op jit(solution)/shard_map/ppermute | solution.py:538
  46.0 1.3 collective-permute-start.14
  47.2 3.7 %copy-done.1 = bf16[1536,3072]{1,0:T(8,128)(2,1)S(1)} copy-done((bf16[1536,3072]{1,0:T(8,128)(2,1)S(1)}, bf16[1536,3072]{1,0:T(8,128)(2,1)}, u32[]{:S(2)}) %copy-start.1) | copy-done | bytes 9437208
  50.9 0.6 hold.1.tile
  51.6 6.6 %own_product.1 = (f32[256,1536]{1,0:T(8,128)S(1)}, bf16[128,1536]{1,0:T(8,128)(2,1)S(1)}) custom-call(s32[2]{0:T(128)S(1)} %copy-done.7, bf16[4,12,64,128]{3,2,1,0:T(8,128)(2,1)S(1)} %pad_maximum_fusion._.a_own, bf16[4,12,64,128]{3,2,1,0:T(8,128)(2,1)S(1)} %pad_maximum_fusion.1.b_own, bf16[1536,3072]{1,0:T(8,128)(2,1)S(1)} %hold.1.tile), custom_call_target="tpu_custom_call" | custom-call | flops 2415919104 | bytes 6291456 | tf_op jit(solution)/shard_map/own_product/pallas_call | solution.py:245
  58.1 3.6 %collective-permute-done.4.a_down = bf16[4,12,64,128]{3,2,1,0:T(8,128)(2,1)S(1)} collective-permute-done((bf16[4,12,64,128]{3,2,1,0:T(8,128)(2,1)S(1)}, bf16[4,12,64,128]{3,2,1,0:T(8,128)(2,1)S(1)}, u32[]{:S(2)}, u32[]{:S(2)}) %collective-permute-start.4) | collective-permute-done | bytes 786464 | tf_op jit(solution)/shard_map/ppermute | solution.py:538
  61.8 1.2 collective-permute-start.10
  63.0 1.1 collective-permute-start.13
  64.2 2.1 %collective-permute-start.12 = (bf16[2,12,64,128]{3,2,1,0:T(8,128)(2,1)S(1)}, bf16[2,12,64,128]{3,2,1,0:T(8,128)(2,1)S(1)}, u32[]{:S(2)}, u32[]{:S(2)}) collective-permute-start(bf16[2,12,64,128]{3,2,1,0:T(8,128)(2,1)S(1)} %slice.16), channel_id=1, source_target_pairs={{0,96},{1,97},{2,98},{3,99},{4,100},{5,101},{6,102},{7,103},{8,104... | collective-permute-start | bytes 1179656 | tf_op jit(solution)/shard_map/ppermute | solution.py:538
  66.3 1.9 %collective-permute-start.15 = (bf16[2,12,64,128]{3,2,1,0:T(8,128)(2,1)S(1)}, bf16[2,12,64,128]{3,2,1,0:T(8,128)(2,1)S(1)}, u32[]{:S(2)}, u32[]{:S(2)}) collective-permute-start(bf16[2,12,64,128]{3,2,1,0:T(8,128)(2,1)S(1)} %slice.17), channel_id=1, source_target_pairs={{0,24},{1,25},{2,26},{3,27},{4,28},{5,29},{6,30},{7,31},{8,0},{9,1... | collective-permute-start | bytes 1179656 | tf_op jit(solution)/shard_map/ppermute | solution.py:538
  68.2 7.8 %early_product.1.before = bf16[8,128,1536]{2,1,0:T(8,128)(2,1)S(1)} custom-call(s32[2]{0:T(128)S(1)} %copy-done.7, bf16[4,12,64,128]{3,2,1,0:T(8,128)(2,1)S(1)} %collective-permute-done.4.a_down, bf16[4,12,64,128]{3,2,1,0:T(8,128)(2,1)S(1)} %collective-permute-done.11.a_up, bf16[4,12,64,128]{3,2,1,0:T(8,128)(2,1)S(1)} %collective-permute-done.9.b_down, ...), custom_call_target="tpu_custom_call" | custom-call | flops 4831838208 | bytes 6291456 | tf_op jit(solution)/shard_map/early_product/pallas_call | solution.py:295
  76.1 5.0 %late_product.3 = (bf16[4,128,768]{2,1,0:T(8,128)(2,1)S(1)}, bf16[4,128,768]{2,1,0:T(8,128)(2,1)S(1)}) custom-call(s32[2]{0:T(128)S(1)} %copy-done.7, bf16[2,12,64,128]{3,2,1,0:T(8,128)(2,1)S(1)} %collective-permute-done.10.a_far, bf16[2,12,64,128]{3,2,1,0:T(8,128)(2,1)S(1)} %collective-permute-done.12.a_more, ...), custom_call_target="tpu_custom_call" | custom-call | flops 1207959552 | bytes 4718592 | tf_op jit(solution)/shard_map/late_product/pallas_call | solution.py:346
  81.1 4.2 %collective-permute-start.20 = (bf16[4,128,768]{2,1,0:T(8,128)(2,1)S(1)}, bf16[4,128,768]{2,1,0:T(8,128)(2,1)S(1)}, u32[]{:S(2)}, u32[]{:S(2)}) collective-permute-start(bf16[4,128,768]{2,1,0:T(8,128)(2,1)S(1)} %get-tuple-element.51), channel_id=1, source_target_pairs={{0,1},{1,0},{2,3},{3,2},{4,5},{5,4},{6,7},{7,6},{8,9},{9,8},{10,11... | collective-permute-start | bytes 2359304 | tf_op jit(solution)/shard_map/ppermute | solution.py:538
  85.3 5.0 %late_product.2 = (bf16[4,128,768]{2,1,0:T(8,128)(2,1)S(1)}, bf16[4,128,768]{2,1,0:T(8,128)(2,1)S(1)}) custom-call(s32[2]{0:T(128)S(1)} %copy-done.7, bf16[2,12,64,128]{3,2,1,0:T(8,128)(2,1)S(1)} %collective-permute-done.10.a_far, bf16[2,12,64,128]{3,2,1,0:T(8,128)(2,1)S(1)} %collective-permute-done.12.a_more, ...), custom_call_target="tpu_custom_call" | custom-call | flops 1207959552 | bytes 4718592 | tf_op jit(solution)/shard_map/late_product/pallas_call | solution.py:346
  90.3 0.1 collective-permute-start.16
  90.5 1.1 pair_sum.3
  91.6 1.6 %collective-permute-start.21 = (bf16[128,768]{1,0:T(8,128)(2,1)S(1)}, bf16[128,768]{1,0:T(8,128)(2,1)S(1)}, u32[]{:S(2)}, u32[]{:S(2)}) collective-permute-start(bf16[128,768]{1,0:T(8,128)(2,1)S(1)} %get-tuple-element.53), channel_id=1, source_target_pairs={{0,2},{1,3},{2,4},{3,5},{4,6},{5,7},{6,0},{7,1},{8,10},{9,11},{10,... | collective-permute-start | bytes 589832 | tf_op jit(solution)/shard_map/ppermute | solution.py:538
  93.2 4.4 %collective-permute-start.22 = (bf16[128,768]{1,0:T(8,128)(2,1)S(1)}, bf16[128,768]{1,0:T(8,128)(2,1)S(1)}, u32[]{:S(2)}, u32[]{:S(2)}) collective-permute-start(bf16[128,768]{1,0:T(8,128)(2,1)S(1)} %get-tuple-element.54), channel_id=1, source_target_pairs={{0,4},{1,5},{2,6},{3,7},{4,0},{5,1},{6,2},{7,3},{8,12},{9,13},{10,... | collective-permute-start | bytes 589832 | tf_op jit(solution)/shard_map/ppermute | solution.py:538
  97.6 1.1 pair_sum.2
  98.7 1.5 collective-permute-start.17
  100.2 1.1 collective-permute-done.21.refs_5_
  101.3 1.4 collective-permute-start.19
  102.7 3.7 %collective-permute-done.22.refs_6_ = bf16[128,768]{1,0:T(8,128)(2,1)S(1)} collective-permute-done((bf16[128,768]{1,0:T(8,128)(2,1)S(1)}, bf16[128,768]{1,0:T(8,128)(2,1)S(1)}, u32[]{:S(2)}, u32[]{:S(2)}) %collective-permute-start.22) | collective-permute-done | bytes 196640 | tf_op jit(solution)/shard_map/ppermute | solution.py:538
  106.4 3.6 %collective-permute-done.17.refs_1_ = bf16[128,768]{1,0:T(8,128)(2,1)S(1)} collective-permute-done((bf16[128,768]{1,0:T(8,128)(2,1)S(1)}, bf16[128,768]{1,0:T(8,128)(2,1)S(1)}, u32[]{:S(2)}, u32[]{:S(2)}) %collective-permute-start.17) | collective-permute-done | bytes 196640 | tf_op jit(solution)/shard_map/ppermute | solution.py:538
  110.0 4.8 %collective-permute-done.18.refs_2_ = bf16[128,768]{1,0:T(8,128)(2,1)S(1)} collective-permute-done((bf16[128,768]{1,0:T(8,128)(2,1)S(1)}, bf16[128,768]{1,0:T(8,128)(2,1)S(1)}, u32[]{:S(2)}, u32[]{:S(2)}) %collective-permute-start.18) | collective-permute-done | bytes 196640 | tf_op jit(solution)/shard_map/ppermute | solution.py:538
  114.9 1.9 %slots.1 = (bf16[128,1536]{1,0:T(8,128)(2,1)S(1)}, bf16[192,512]{1,0:T(8,128)(2,1)S(1)}) custom-call(s32[2]{0:T(128)S(1)} %copy-done.7, s32[16,12]{1,0:T(8,128)S(1)} %copy-done.6, s32[16]{0:T(128)S(1)} %copy-done.9, s32[16,12]{1,0:T(8,128)S(1)} %copy-done.8, s32[16]{0:T(128)S(1)} %copy-done.10, bf16[128,768]{1,0:T(8,128)(2,1)S(1)} %get-tuple-element.46.refs_0_, ...), custom_call_target="tpu_custom_call" | custom-call | flops 301989888 | bytes 5111808 | tf_op jit(solution)/shard_map/slots/pallas_call | solution.py:422
  116.8 0.4 collective-permute-start.27
  117.2 2.4 %collective-permute-start.28 = (bf16[128,1536]{1,0:T(8,128)(2,1)S(1)}, bf16[128,1536]{1,0:T(8,128)(2,1)S(1)}, u32[]{:S(2)}, u32[]{:S(2)}) collective-permute-start(bf16[128,1536]{1,0:T(8,128)(2,1)S(1)} %get-tuple-element.67.refs_0_), channel_id=1, source_target_pairs={{0,6},{1,7},{2,0},{3,1},{4,2},{5,3},{6,4},{7,5},{8,14},{9,15},{10,... | collective-permute-start | bytes 1179656 | tf_op jit(solution)/shard_map/ppermute | solution.py:538
  119.6 2.7 %collective-permute-start.25 = (bf16[192,512]{1,0:T(8,128)(2,1)S(1)}, bf16[192,512]{1,0:T(8,128)(2,1)S(1)}, u32[]{:S(2)}, u32[]{:S(2)}) collective-permute-start(bf16[192,512]{1,0:T(8,128)(2,1)S(1)} %get-tuple-element.58.one), channel_id=1, source_target_pairs={{0,24},{1,25},{2,26},{3,27},{4,28},{5,29},{6,30},{7,31},{8,0},{9,1... | collective-permute-start | bytes 589832 | tf_op jit(solution)/shard_map/ppermute | solution.py:538
  122.2 0.3 collective-permute-start.26
  122.5 3.1 %collective-permute-done.24.two = bf16[192,512]{1,0:T(8,128)(2,1)S(1)} collective-permute-done((bf16[192,512]{1,0:T(8,128)(2,1)S(1)}, bf16[192,512]{1,0:T(8,128)(2,1)S(1)}, u32[]{:S(2)}, u32[]{:S(2)}) %collective-permute-start.24) | collective-permute-done | bytes 196640 | tf_op jit(solution)/shard_map/ppermute | solution.py:538
  125.6 0.7 collective-permute-done.25.three
  126.3 4.3 %collective-permute-done.26.four = bf16[192,512]{1,0:T(8,128)(2,1)S(1)} collective-permute-done((bf16[192,512]{1,0:T(8,128)(2,1)S(1)}, bf16[192,512]{1,0:T(8,128)(2,1)S(1)}, u32[]{:S(2)}, u32[]{:S(2)}) %collective-permute-start.26) | collective-permute-done | bytes 196640 | tf_op jit(solution)/shard_map/ppermute | solution.py:538
  130.6 0.1 fold.1.one
  130.7 1.5 collective-permute-start.32
  132.2 2.7 %collective-permute-start.30 = (bf16[192,512]{1,0:T(8,128)(2,1)S(1)}, bf16[192,512]{1,0:T(8,128)(2,1)S(1)}, u32[]{:S(2)}, u32[]{:S(2)}) collective-permute-start(bf16[192,512]{1,0:T(8,128)(2,1)S(1)} %fold.1.one), channel_id=1, source_target_pairs={{0,96},{1,97},{2,98},{3,99},{4,100},{5,101},{6,102},{7,103},{8,104... | collective-permute-start | bytes 589832 | tf_op jit(solution)/shard_map/ppermute | solution.py:538
  134.9 0.1 collective-permute-start.31
  135.0 3.3 %collective-permute-done.29.two = bf16[192,512]{1,0:T(8,128)(2,1)S(1)} collective-permute-done((bf16[192,512]{1,0:T(8,128)(2,1)S(1)}, bf16[192,512]{1,0:T(8,128)(2,1)S(1)}, u32[]{:S(2)}, u32[]{:S(2)}) %collective-permute-start.29) | collective-permute-done | bytes 196640 | tf_op jit(solution)/shard_map/ppermute | solution.py:538
  138.2 2.0 %collective-permute-done.30.three = bf16[192,512]{1,0:T(8,128)(2,1)S(1)} collective-permute-done((bf16[192,512]{1,0:T(8,128)(2,1)S(1)}, bf16[192,512]{1,0:T(8,128)(2,1)S(1)}, u32[]{:S(2)}, u32[]{:S(2)}) %collective-permute-start.30) | collective-permute-done | bytes 196640 | tf_op jit(solution)/shard_map/ppermute | solution.py:538
  140.2 3.0 %collective-permute-done.31.four = bf16[192,512]{1,0:T(8,128)(2,1)S(1)} collective-permute-done((bf16[192,512]{1,0:T(8,128)(2,1)S(1)}, bf16[192,512]{1,0:T(8,128)(2,1)S(1)}, u32[]{:S(2)}, u32[]{:S(2)}) %collective-permute-start.31) | collective-permute-done | bytes 196640 | tf_op jit(solution)/shard_map/ppermute | solution.py:538
  143.2 2.0 %collective-permute-start.33 = (bf16[128,1536]{1,0:T(8,128)(2,1)S(1)}, bf16[128,1536]{1,0:T(8,128)(2,1)S(1)}, u32[]{:S(2)}, u32[]{:S(2)}) collective-permute-start(bf16[128,1536]{1,0:T(8,128)(2,1)S(1)} %get-tuple-element.67.refs_0_), channel_id=1, source_target_pairs={{0,1},{1,0},{2,3},{3,2},{4,5},{5,4},{6,7},{7,6},{8,9},{9,8},{10,11... | collective-permute-start | bytes 1179656 | tf_op jit(solution)/shard_map/ppermute | solution.py:538
  145.3 0.5 collective-permute-start.35
  145.8 1.1 top_part.1
  146.9 0.0 collective-permute-start.36
  146.9 4.1 %all-to-all-start = ((bf16[8,64,128]{2,1,0:T(8,128)(2,1)}), bf16[8,64,128]{2,1,0:T(8,128)(2,1)S(1)}, u32[]{:S(2)}, u32[]{:S(2)}) async-start(bf16[8,64,128]{2,1,0:T(8,128)(2,1)} %get-tuple-element.68), calls=%async_computation | async-start | bytes 262144 | tf_op jit(solution)/shard_map/all_to_all | solution.py:580
  151.0 4.7 %whole_columns.1 = (bf16[1536,512]{1,0:T(8,128)(2,1)}, bf16[1536,512]{1,0:T(8,128)(2,1)}) custom-call(s32[2]{0:T(128)S(1)} %copy-done.7, bf16[128,1536]{1,0:T(8,128)(2,1)S(1)} %get-tuple-element.67.refs_0_, bf16[128,1536]{1,0:T(8,128)(2,1)S(1)} %collective-permute-done.27.refs_1_, bf16[128,1536]{1,0:T(8,128)(2,1)S(1)} %collective-permute-done.28.refs_2_, ...), custom_call_target="tpu_custom_call" | custom-call | bytes 6291456 | tf_op jit(solution)/shard_map/whole_columns/pallas_call | solution.py:454
  155.7 0.5 all-to-all-done.taken
  156.3 0.9 last_part.1
  (55 shorter events, 0.2 us)
Async XLA Ops:
  4.1 16.9 %collective-permute-start = (bf16[12,64,128]{2,1,0:T(8,128)(2,1)}, bf16[12,64,128]{2,1,0:T(8,128)(2,1)S(1)}, u32[]{:S(2)}, u32[]{:S(2)}) collective-permute-start(bf16[12,64,128]{2,1,0:T(8,128)(2,1)} %prep_a.1), channel_id=1, source_target_pairs={{0,0},{1,32},{2,8},{3,40},{4,16},{5,48},{6,24},{7,56},{8,9},{9,41}... | collective-permute-start | bytes 589832 | tf_op jit(solution)/shard_map/ppermute | solution.py:550
  13.3 15.9 %collective-permute-start.5 = (bf16[12,64,128]{2,1,0:T(8,128)(2,1)}, bf16[12,64,128]{2,1,0:T(8,128)(2,1)S(1)}, u32[]{:S(2)}, u32[]{:S(2)}) collective-permute-start(bf16[12,64,128]{2,1,0:T(8,128)(2,1)} %prep_b.1), channel_id=1, source_target_pairs={{0,0},{1,32},{2,8},{3,40},{4,16},{5,48},{6,24},{7,56},{8,9},{9,41}... | collective-permute-start | bytes 589832 | tf_op jit(solution)/shard_map/ppermute | solution.py:552
  21.0 13.4 %collective-permute-start.1 = (bf16[12,64,128]{2,1,0:T(8,128)(2,1)S(1)}, bf16[12,64,128]{2,1,0:T(8,128)(2,1)S(1)}, u32[]{:S(2)}, u32[]{:S(2)}) collective-permute-start(bf16[12,64,128]{2,1,0:T(8,128)(2,1)S(1)} %collective-permute-done), channel_id=1, source_target_pairs={{0,8},{1,9},{2,10},{3,11},{4,12},{5,13},{6,14},{7,15},{8,16},{9,17... | collective-permute-start | bytes 589832 | tf_op jit(solution)/shard_map/ppermute | solution.py:538
  21.0 18.5 %collective-permute-start.2 = (bf16[12,64,128]{2,1,0:T(8,128)(2,1)S(1)}, bf16[12,64,128]{2,1,0:T(8,128)(2,1)S(1)}, u32[]{:S(2)}, u32[]{:S(2)}) collective-permute-start(bf16[12,64,128]{2,1,0:T(8,128)(2,1)S(1)} %collective-permute-done), channel_id=1, source_target_pairs={{0,24},{1,25},{2,26},{3,27},{4,28},{5,29},{6,30},{7,31},{8,0},{9,1... | collective-permute-start | bytes 589832 | tf_op jit(solution)/shard_map/ppermute | solution.py:538
  23.7 15.8 %collective-permute-start.3 = (bf16[12,64,128]{2,1,0:T(8,128)(2,1)S(1)}, bf16[12,64,128]{2,1,0:T(8,128)(2,1)S(1)}, u32[]{:S(2)}, u32[]{:S(2)}) collective-permute-start(bf16[12,64,128]{2,1,0:T(8,128)(2,1)S(1)} %collective-permute-done), channel_id=1, source_target_pairs={{0,16},{1,17},{2,18},{3,19},{4,20},{5,21},{6,22},{7,23},{8,24},{9,... | collective-permute-start | bytes 589832 | tf_op jit(solution)/shard_map/ppermute | solution.py:538
  29.3 10.4 %collective-permute-start.6 = (bf16[12,64,128]{2,1,0:T(8,128)(2,1)S(1)}, bf16[12,64,128]{2,1,0:T(8,128)(2,1)S(1)}, u32[]{:S(2)}, u32[]{:S(2)}) collective-permute-start(bf16[12,64,128]{2,1,0:T(8,128)(2,1)S(1)} %collective-permute-done.5), channel_id=1, source_target_pairs={{0,32},{1,33},{2,34},{3,35},{4,36},{5,37},{6,38},{7,39},{8,40},{9,... | collective-permute-start | bytes 589832 | tf_op jit(solution)/shard_map/ppermute | solution.py:538
  32.2 7.5 %collective-permute-start.7 = (bf16[12,64,128]{2,1,0:T(8,128)(2,1)S(1)}, bf16[12,64,128]{2,1,0:T(8,128)(2,1)S(1)}, u32[]{:S(2)}, u32[]{:S(2)}) collective-permute-start(bf16[12,64,128]{2,1,0:T(8,128)(2,1)S(1)} %collective-permute-done.5), channel_id=1, source_target_pairs={{0,96},{1,97},{2,98},{3,99},{4,100},{5,101},{6,102},{7,103},{8,104... | collective-permute-start | bytes 589832 | tf_op jit(solution)/shard_map/ppermute | solution.py:538
  34.4 9.6 %collective-permute-start.8 = (bf16[12,64,128]{2,1,0:T(8,128)(2,1)S(1)}, bf16[12,64,128]{2,1,0:T(8,128)(2,1)S(1)}, u32[]{:S(2)}, u32[]{:S(2)}) collective-permute-start(bf16[12,64,128]{2,1,0:T(8,128)(2,1)S(1)} %collective-permute-done.5), channel_id=1, source_target_pairs={{0,64},{1,65},{2,66},{3,67},{4,68},{5,69},{6,70},{7,71},{8,72},{9,... | collective-permute-start | bytes 589832 | tf_op jit(solution)/shard_map/ppermute | solution.py:538
  39.6 22.1 %collective-permute-start.4 = (bf16[4,12,64,128]{3,2,1,0:T(8,128)(2,1)S(1)}, bf16[4,12,64,128]{3,2,1,0:T(8,128)(2,1)S(1)}, u32[]{:S(2)}, u32[]{:S(2)}) collective-permute-start(bf16[4,12,64,128]{3,2,1,0:T(8,128)(2,1)S(1)} %pad_maximum_fusion._.a_own), channel_id=1, source_target_pairs={{0,32},{1,33},{2,34},{3,35},{4,36},{5,37},{6,38},{7,39},{8,40},{9,... | collective-permute-start | bytes 2359304 | tf_op jit(solution)/shard_map/ppermute | solution.py:538
  43.9 7.6 %copy-start.7 = (s32[2]{0:T(128)S(1)}, s32[2]{0:T(128)}, u32[]{:S(2)}) copy-start(s32[2]{0:T(128)} %pad_add_fusion.place) | copy-start | bytes 28
  44.0 17.7 %collective-permute-start.9 = (bf16[4,12,64,128]{3,2,1,0:T(8,128)(2,1)S(1)}, bf16[4,12,64,128]{3,2,1,0:T(8,128)(2,1)S(1)}, u32[]{:S(2)}, u32[]{:S(2)}) collective-permute-start(bf16[4,12,64,128]{3,2,1,0:T(8,128)(2,1)S(1)} %pad_maximum_fusion.1.b_own), channel_id=1, source_target_pairs={{0,8},{1,9},{2,10},{3,11},{4,12},{5,13},{6,14},{7,15},{8,16},{9,17... | collective-permute-start | bytes 2359304 | tf_op jit(solution)/shard_map/ppermute | solution.py:538
  45.9 18.2 %collective-permute-start.11 = (bf16[4,12,64,128]{3,2,1,0:T(8,128)(2,1)S(1)}, bf16[4,12,64,128]{3,2,1,0:T(8,128)(2,1)S(1)}, u32[]{:S(2)}, u32[]{:S(2)}) collective-permute-start(bf16[4,12,64,128]{3,2,1,0:T(8,128)(2,1)S(1)} %pad_maximum_fusion._.a_own), channel_id=1, source_target_pairs={{0,96},{1,97},{2,98},{3,99},{4,100},{5,101},{6,102},{7,103},{8,104... | collective-permute-start | bytes 2359304 | tf_op jit(solution)/shard_map/ppermute | solution.py:538
  46.0 20.3 %collective-permute-start.14 = (bf16[4,12,64,128]{3,2,1,0:T(8,128)(2,1)S(1)}, bf16[4,12,64,128]{3,2,1,0:T(8,128)(2,1)S(1)}, u32[]{:S(2)}, u32[]{:S(2)}) collective-permute-start(bf16[4,12,64,128]{3,2,1,0:T(8,128)(2,1)S(1)} %pad_maximum_fusion.1.b_own), channel_id=1, source_target_pairs={{0,24},{1,25},{2,26},{3,27},{4,28},{5,29},{6,30},{7,31},{8,0},{9,1... | collective-permute-start | bytes 2359304 | tf_op jit(solution)/shard_map/ppermute | solution.py:538
  47.2 3.7 %copy-start.1 = (bf16[1536,3072]{1,0:T(8,128)(2,1)S(1)}, bf16[1536,3072]{1,0:T(8,128)(2,1)}, u32[]{:S(2)}) copy-start(bf16[1536,3072]{1,0:T(8,128)(2,1)} %source.1) | copy-start | bytes 28311556
  61.8 14.3 %collective-permute-start.10 = (bf16[2,12,64,128]{3,2,1,0:T(8,128)(2,1)S(1)}, bf16[2,12,64,128]{3,2,1,0:T(8,128)(2,1)S(1)}, u32[]{:S(2)}, u32[]{:S(2)}) collective-permute-start(bf16[2,12,64,128]{3,2,1,0:T(8,128)(2,1)S(1)} %slice.12), channel_id=1, source_target_pairs={{0,32},{1,33},{2,34},{3,35},{4,36},{5,37},{6,38},{7,39},{8,40},{9,... | collective-permute-start | bytes 1179656 | tf_op jit(solution)/shard_map/ppermute | solution.py:538
  63.0 13.0 %collective-permute-start.13 = (bf16[2,12,64,128]{3,2,1,0:T(8,128)(2,1)S(1)}, bf16[2,12,64,128]{3,2,1,0:T(8,128)(2,1)S(1)}, u32[]{:S(2)}, u32[]{:S(2)}) collective-permute-start(bf16[2,12,64,128]{3,2,1,0:T(8,128)(2,1)S(1)} %slice.14), channel_id=1, source_target_pairs={{0,8},{1,9},{2,10},{3,11},{4,12},{5,13},{6,14},{7,15},{8,16},{9,17... | collective-permute-start | bytes 1179656 | tf_op jit(solution)/shard_map/ppermute | solution.py:538
  64.2 11.9 %collective-permute-start.12 = (bf16[2,12,64,128]{3,2,1,0:T(8,128)(2,1)S(1)}, bf16[2,12,64,128]{3,2,1,0:T(8,128)(2,1)S(1)}, u32[]{:S(2)}, u32[]{:S(2)}) collective-permute-start(bf16[2,12,64,128]{3,2,1,0:T(8,128)(2,1)S(1)} %slice.16), channel_id=1, source_target_pairs={{0,96},{1,97},{2,98},{3,99},{4,100},{5,101},{6,102},{7,103},{8,104... | collective-permute-start | bytes 1179656 | tf_op jit(solution)/shard_map/ppermute | solution.py:538
  66.3 9.8 %collective-permute-start.15 = (bf16[2,12,64,128]{3,2,1,0:T(8,128)(2,1)S(1)}, bf16[2,12,64,128]{3,2,1,0:T(8,128)(2,1)S(1)}, u32[]{:S(2)}, u32[]{:S(2)}) collective-permute-start(bf16[2,12,64,128]{3,2,1,0:T(8,128)(2,1)S(1)} %slice.17), channel_id=1, source_target_pairs={{0,24},{1,25},{2,26},{3,27},{4,28},{5,29},{6,30},{7,31},{8,0},{9,1... | collective-permute-start | bytes 1179656 | tf_op jit(solution)/shard_map/ppermute | solution.py:538
  81.1 9.3 %collective-permute-start.20 = (bf16[4,128,768]{2,1,0:T(8,128)(2,1)S(1)}, bf16[4,128,768]{2,1,0:T(8,128)(2,1)S(1)}, u32[]{:S(2)}, u32[]{:S(2)}) collective-permute-start(bf16[4,128,768]{2,1,0:T(8,128)(2,1)S(1)} %get-tuple-element.51), channel_id=1, source_target_pairs={{0,1},{1,0},{2,3},{3,2},{4,5},{5,4},{6,7},{7,6},{8,9},{9,8},{10,11... | collective-permute-start | bytes 2359304 | tf_op jit(solution)/shard_map/ppermute | solution.py:538
  90.3 7.3 %collective-permute-start.16 = (bf16[4,128,768]{2,1,0:T(8,128)(2,1)S(1)}, bf16[4,128,768]{2,1,0:T(8,128)(2,1)S(1)}, u32[]{:S(2)}, u32[]{:S(2)}) collective-permute-start(bf16[4,128,768]{2,1,0:T(8,128)(2,1)S(1)} %get-tuple-element.45), channel_id=1, source_target_pairs={{0,1},{1,0},{2,3},{3,2},{4,5},{5,4},{6,7},{7,6},{8,9},{9,8},{10,11... | collective-permute-start | bytes 2359304 | tf_op jit(solution)/shard_map/ppermute | solution.py:538
  90.4 24.4 %copy-start = (bf16[1536,512]{1,0:T(8,128)(2,1)S(1)}, bf16[1536,512]{1,0:T(8,128)(2,1)}, u32[]{:S(2)}) copy-start(bf16[1536,512]{1,0:T(8,128)(2,1)} %refs_8_.1) | copy-start | bytes 4718596
  90.5 24.4 %copy-start.2 = (bf16[1536,512]{1,0:T(8,128)(2,1)S(1)}, bf16[1536,512]{1,0:T(8,128)(2,1)}, u32[]{:S(2)}) copy-start(bf16[1536,512]{1,0:T(8,128)(2,1)} %refs_9_.1) | copy-start | bytes 4718596
  90.5 24.4 %copy-start.6 = (s32[16,12]{1,0:T(8,128)S(1)}, s32[16,12]{1,0:T(8,128)}, u32[]{:S(2)}) copy-start(s32[16,12]{1,0:T(8,128)} %rows_a.5) | copy-start | bytes 2308
  90.5 24.4 %copy-start.8 = (s32[16,12]{1,0:T(8,128)S(1)}, s32[16,12]{1,0:T(8,128)}, u32[]{:S(2)}) copy-start(s32[16,12]{1,0:T(8,128)} %rows_b.3) | copy-start | bytes 2308
  90.5 24.4 %copy-start.9 = (s32[16]{0:T(128)S(1)}, s32[16]{0:T(128)}, u32[]{:S(2)}) copy-start(s32[16]{0:T(128)} %counts_a.5) | copy-start | bytes 196
  90.5 24.4 %copy-start.10 = (s32[16]{0:T(128)S(1)}, s32[16]{0:T(128)}, u32[]{:S(2)}) copy-start(s32[16]{0:T(128)} %counts_b.3) | copy-start | bytes 196
  91.6 9.7 %collective-permute-start.21 = (bf16[128,768]{1,0:T(8,128)(2,1)S(1)}, bf16[128,768]{1,0:T(8,128)(2,1)S(1)}, u32[]{:S(2)}, u32[]{:S(2)}) collective-permute-start(bf16[128,768]{1,0:T(8,128)(2,1)S(1)} %get-tuple-element.53), channel_id=1, source_target_pairs={{0,2},{1,3},{2,4},{3,5},{4,6},{5,7},{6,0},{7,1},{8,10},{9,11},{10,... | collective-permute-start | bytes 589832 | tf_op jit(solution)/shard_map/ppermute | solution.py:538
  93.2 13.2 %collective-permute-start.22 = (bf16[128,768]{1,0:T(8,128)(2,1)S(1)}, bf16[128,768]{1,0:T(8,128)(2,1)S(1)}, u32[]{:S(2)}, u32[]{:S(2)}) collective-permute-start(bf16[128,768]{1,0:T(8,128)(2,1)S(1)} %get-tuple-element.54), channel_id=1, source_target_pairs={{0,4},{1,5},{2,6},{3,7},{4,0},{5,1},{6,2},{7,3},{8,12},{9,13},{10,... | collective-permute-start | bytes 589832 | tf_op jit(solution)/shard_map/ppermute | solution.py:538
  97.6 8.8 %collective-permute-start.23 = (bf16[128,768]{1,0:T(8,128)(2,1)S(1)}, bf16[128,768]{1,0:T(8,128)(2,1)S(1)}, u32[]{:S(2)}, u32[]{:S(2)}) collective-permute-start(bf16[128,768]{1,0:T(8,128)(2,1)S(1)} %get-tuple-element.55), channel_id=1, source_target_pairs={{0,6},{1,7},{2,0},{3,1},{4,2},{5,3},{6,4},{7,5},{8,14},{9,15},{10,... | collective-permute-start | bytes 589832 | tf_op jit(solution)/shard_map/ppermute | solution.py:538
  98.7 11.3 %collective-permute-start.17 = (bf16[128,768]{1,0:T(8,128)(2,1)S(1)}, bf16[128,768]{1,0:T(8,128)(2,1)S(1)}, u32[]{:S(2)}, u32[]{:S(2)}) collective-permute-start(bf16[128,768]{1,0:T(8,128)(2,1)S(1)} %get-tuple-element.47), channel_id=1, source_target_pairs={{0,2},{1,3},{2,4},{3,5},{4,6},{5,7},{6,0},{7,1},{8,10},{9,11},{10,... | collective-permute-start | bytes 589832 | tf_op jit(solution)/shard_map/ppermute | solution.py:538
  100.2 14.6 %collective-permute-start.18 = (bf16[128,768]{1,0:T(8,128)(2,1)S(1)}, bf16[128,768]{1,0:T(8,128)(2,1)S(1)}, u32[]{:S(2)}, u32[]{:S(2)}) collective-permute-start(bf16[128,768]{1,0:T(8,128)(2,1)S(1)} %get-tuple-element.48), channel_id=1, source_target_pairs={{0,4},{1,5},{2,6},{3,7},{4,0},{5,1},{6,2},{7,3},{8,12},{9,13},{10,... | collective-permute-start | bytes 589832 | tf_op jit(solution)/shard_map/ppermute | solution.py:538
  101.3 13.5 %collective-permute-start.19 = (bf16[128,768]{1,0:T(8,128)(2,1)S(1)}, bf16[128,768]{1,0:T(8,128)(2,1)S(1)}, u32[]{:S(2)}, u32[]{:S(2)}) collective-permute-start(bf16[128,768]{1,0:T(8,128)(2,1)S(1)} %get-tuple-element.49), channel_id=1, source_target_pairs={{0,6},{1,7},{2,0},{3,1},{4,2},{5,3},{6,4},{7,5},{8,14},{9,15},{10,... | collective-permute-start | bytes 589832 | tf_op jit(solution)/shard_map/ppermute | solution.py:538
  114.9 30.9 %copy-start.3 = (bf16[512,512]{1,0:T(8,128)(2,1)S(1)}, bf16[512,512]{1,0:T(8,128)(2,1)}, u32[]{:S(2)}) copy-start(bf16[512,512]{1,0:T(8,128)(2,1)} %top.5) | copy-start | bytes 1572868
  114.9 30.9 %copy-start.4 = (f32[64,512]{1,0:T(8,128)S(1)}, f32[64,512]{1,0:T(8,128)}, u32[]{:S(2)}) copy-start(f32[64,512]{1,0:T(8,128)} %base.1) | copy-start | bytes 393220
  116.8 13.8 %collective-permute-start.27 = (bf16[128,1536]{1,0:T(8,128)(2,1)S(1)}, bf16[128,1536]{1,0:T(8,128)(2,1)S(1)}, u32[]{:S(2)}, u32[]{:S(2)}) collective-permute-start(bf16[128,1536]{1,0:T(8,128)(2,1)S(1)} %get-tuple-element.67.refs_0_), channel_id=1, source_target_pairs={{0,2},{1,3},{2,4},{3,5},{4,6},{5,7},{6,0},{7,1},{8,10},{9,11},{10,... | collective-permute-start | bytes 1179656 | tf_op jit(solution)/shard_map/ppermute | solution.py:538
  117.2 13.4 %collective-permute-start.28 = (bf16[128,1536]{1,0:T(8,128)(2,1)S(1)}, bf16[128,1536]{1,0:T(8,128)(2,1)S(1)}, u32[]{:S(2)}, u32[]{:S(2)}) collective-permute-start(bf16[128,1536]{1,0:T(8,128)(2,1)S(1)} %get-tuple-element.67.refs_0_), channel_id=1, source_target_pairs={{0,6},{1,7},{2,0},{3,1},{4,2},{5,3},{6,4},{7,5},{8,14},{9,15},{10,... | collective-permute-start | bytes 1179656 | tf_op jit(solution)/shard_map/ppermute | solution.py:538
  119.6 6.0 %collective-permute-start.24 = (bf16[192,512]{1,0:T(8,128)(2,1)S(1)}, bf16[192,512]{1,0:T(8,128)(2,1)S(1)}, u32[]{:S(2)}, u32[]{:S(2)}) collective-permute-start(bf16[192,512]{1,0:T(8,128)(2,1)S(1)} %get-tuple-element.58.one), channel_id=1, source_target_pairs={{0,8},{1,9},{2,10},{3,11},{4,12},{5,13},{6,14},{7,15},{8,16},{9,17... | collective-permute-start | bytes 589832 | tf_op jit(solution)/shard_map/ppermute | solution.py:538
  119.6 6.7 %collective-permute-start.25 = (bf16[192,512]{1,0:T(8,128)(2,1)S(1)}, bf16[192,512]{1,0:T(8,128)(2,1)S(1)}, u32[]{:S(2)}, u32[]{:S(2)}) collective-permute-start(bf16[192,512]{1,0:T(8,128)(2,1)S(1)} %get-tuple-element.58.one), channel_id=1, source_target_pairs={{0,24},{1,25},{2,26},{3,27},{4,28},{5,29},{6,30},{7,31},{8,0},{9,1... | collective-permute-start | bytes 589832 | tf_op jit(solution)/shard_map/ppermute | solution.py:538
  122.2 8.3 %collective-permute-start.26 = (bf16[192,512]{1,0:T(8,128)(2,1)S(1)}, bf16[192,512]{1,0:T(8,128)(2,1)S(1)}, u32[]{:S(2)}, u32[]{:S(2)}) collective-permute-start(bf16[192,512]{1,0:T(8,128)(2,1)S(1)} %get-tuple-element.58.one), channel_id=1, source_target_pairs={{0,16},{1,17},{2,18},{3,19},{4,20},{5,21},{6,22},{7,23},{8,24},{9,... | collective-permute-start | bytes 589832 | tf_op jit(solution)/shard_map/ppermute | solution.py:538
  130.7 16.2 %collective-permute-start.32 = (bf16[128,1536]{1,0:T(8,128)(2,1)S(1)}, bf16[128,1536]{1,0:T(8,128)(2,1)S(1)}, u32[]{:S(2)}, u32[]{:S(2)}) collective-permute-start(bf16[128,1536]{1,0:T(8,128)(2,1)S(1)} %get-tuple-element.67.refs_0_), channel_id=1, source_target_pairs={{0,4},{1,5},{2,6},{3,7},{4,0},{5,1},{6,2},{7,3},{8,12},{9,13},{10,... | collective-permute-start | bytes 1179656 | tf_op jit(solution)/shard_map/ppermute | solution.py:538
  132.2 6.0 %collective-permute-start.29 = (bf16[192,512]{1,0:T(8,128)(2,1)S(1)}, bf16[192,512]{1,0:T(8,128)(2,1)S(1)}, u32[]{:S(2)}, u32[]{:S(2)}) collective-permute-start(bf16[192,512]{1,0:T(8,128)(2,1)S(1)} %fold.1.one), channel_id=1, source_target_pairs={{0,32},{1,33},{2,34},{3,35},{4,36},{5,37},{6,38},{7,39},{8,40},{9,... | collective-permute-start | bytes 589832 | tf_op jit(solution)/shard_map/ppermute | solution.py:538
  132.2 8.0 %collective-permute-start.30 = (bf16[192,512]{1,0:T(8,128)(2,1)S(1)}, bf16[192,512]{1,0:T(8,128)(2,1)S(1)}, u32[]{:S(2)}, u32[]{:S(2)}) collective-permute-start(bf16[192,512]{1,0:T(8,128)(2,1)S(1)} %fold.1.one), channel_id=1, source_target_pairs={{0,96},{1,97},{2,98},{3,99},{4,100},{5,101},{6,102},{7,103},{8,104... | collective-permute-start | bytes 589832 | tf_op jit(solution)/shard_map/ppermute | solution.py:538
  134.9 8.4 %collective-permute-start.31 = (bf16[192,512]{1,0:T(8,128)(2,1)S(1)}, bf16[192,512]{1,0:T(8,128)(2,1)S(1)}, u32[]{:S(2)}, u32[]{:S(2)}) collective-permute-start(bf16[192,512]{1,0:T(8,128)(2,1)S(1)} %fold.1.one), channel_id=1, source_target_pairs={{0,64},{1,65},{2,66},{3,67},{4,68},{5,69},{6,70},{7,71},{8,72},{9,... | collective-permute-start | bytes 589832 | tf_op jit(solution)/shard_map/ppermute | solution.py:538
  143.2 7.8 %collective-permute-start.33 = (bf16[128,1536]{1,0:T(8,128)(2,1)S(1)}, bf16[128,1536]{1,0:T(8,128)(2,1)S(1)}, u32[]{:S(2)}, u32[]{:S(2)}) collective-permute-start(bf16[128,1536]{1,0:T(8,128)(2,1)S(1)} %get-tuple-element.67.refs_0_), channel_id=1, source_target_pairs={{0,1},{1,0},{2,3},{3,2},{4,5},{5,4},{6,7},{7,6},{8,9},{9,8},{10,11... | collective-permute-start | bytes 1179656 | tf_op jit(solution)/shard_map/ppermute | solution.py:538
  145.2 5.8 %collective-permute-start.34 = (bf16[128,1536]{1,0:T(8,128)(2,1)S(1)}, bf16[128,1536]{1,0:T(8,128)(2,1)}, u32[]{:S(2)}, u32[]{:S(2)}) collective-permute-start(bf16[128,1536]{1,0:T(8,128)(2,1)S(1)} %collective-permute-done.27.refs_1_), channel_id=1, source_target_pairs={{0,1},{1,0},{2,3},{3,2},{4,5},{5,4},{6,7},{7,6},{8,9},{9,8},{10,11... | collective-permute-start | bytes 1179656 | tf_op jit(solution)/shard_map/ppermute | solution.py:538
  145.3 5.8 %collective-permute-start.35 = (bf16[128,1536]{1,0:T(8,128)(2,1)S(1)}, bf16[128,1536]{1,0:T(8,128)(2,1)}, u32[]{:S(2)}, u32[]{:S(2)}) collective-permute-start(bf16[128,1536]{1,0:T(8,128)(2,1)S(1)} %collective-permute-done.28.refs_2_), channel_id=1, source_target_pairs={{0,1},{1,0},{2,3},{3,2},{4,5},{5,4},{6,7},{7,6},{8,9},{9,8},{10,11... | collective-permute-start | bytes 1179656 | tf_op jit(solution)/shard_map/ppermute | solution.py:538
  146.9 4.1 %collective-permute-start.36 = (bf16[128,1536]{1,0:T(8,128)(2,1)S(1)}, bf16[128,1536]{1,0:T(8,128)(2,1)}, u32[]{:S(2)}, u32[]{:S(2)}) collective-permute-start(bf16[128,1536]{1,0:T(8,128)(2,1)S(1)} %collective-permute-done.32.refs_3_), channel_id=1, source_target_pairs={{0,1},{1,0},{2,3},{3,2},{4,5},{5,4},{6,7},{7,6},{8,9},{9,8},{10,11... | collective-permute-start | bytes 1179656 | tf_op jit(solution)/shard_map/ppermute | solution.py:538
  146.9 9.4 %all-to-all-start = ((bf16[8,64,128]{2,1,0:T(8,128)(2,1)}), bf16[8,64,128]{2,1,0:T(8,128)(2,1)S(1)}, u32[]{:S(2)}, u32[]{:S(2)}) async-start(bf16[8,64,128]{2,1,0:T(8,128)(2,1)} %get-tuple-element.68), calls=%async_computation | async-start | bytes 262144 | tf_op jit(solution)/shard_map/all_to_all | solution.py:580
  151.0 5.3 %copy-start.5 = (f32[64,512]{1,0:T(8,128)S(1)}, f32[64,512]{1,0:T(8,128)}, u32[]{:S(2)}) copy-start(f32[64,512]{1,0:T(8,128)} %base.2) | copy-start | bytes 393220

commit v10 on v8

--- a/solution.py
+++ b/solution.py
@@ -14,7 +14,7 @@
 SIDE = 4
 PART = 64
 COLS = 8
-STEPS = (0, 1, -1, 2)
+STEPS = (0, 2, 1, -1)
 STRIP = 2 * BS
 PAIR = 2 * PART
 BOTH = ("row", "col")
@@ -275,7 +275,7 @@
     for i, step in enumerate(STEPS):
         out[2 * turn(v, -step) + (u + 1) % 2, :PART, :] = value[i * PART : (i + 1) * PART]
     for j in range(4):
-        to = 2 * turn(v, -STEPS[1 + j // 2]) + j % 2
+        to = 2 * turn(v, (-1, 1)[j // 2]) + j % 2
         out[to, PART:, :] = value[W // 2 + j * PART : W // 2 + (j + 1) * PART]
     for j in range(2):
         out[2 * v + j, PART:, :] = whole_b[j * PART : (j + 1) * PART, :]
@@ -550,7 +550,6 @@
     lists = (rows_a, counts_a, rows_b, counts_b)
     part_a = lax.ppermute(prep_a(place, lists, factor_a), BOTH, spread_pairs())
     part_b = prep_b(place, lists, factor_a, factor_b, factor_top)
-    part_b, _ = lax.optimization_barrier((part_b, part_a))
     part_b = lax.ppermute(part_b, BOTH, spread_pairs())
     a_own = jnp.stack(around(part_a, "dy"))
     b_own = jnp.stack(around(part_b, "dz"))
@@ -568,7 +567,7 @@
             half, place, (a_far, a_far_more, b_far, b_far_more), trailing, before, half_a
         )
         own, one, two, three = pair_sum(place, keep, send(give, dc=1))
-        slabs += [own, send(one, dx=1), send(two, dx=2), send(three, dx=-1)]
+        slabs += [own, send(two, dx=2), send(one, dx=1), send(three, dx=-1)]
     columns, pieces = slots(place, lists, slabs, (factor_a, factor_b))
     near, other = send(columns, dx=1), send(columns, dx=-1)
     first, near, other = lax.optimization_barrier((around(pieces, "dy"), near, other))
@@ -576,11 +575,14 @@
     got = around(folded, "dz")
     far = send(lax.optimization_barrier((columns, folded))[0], dx=2)
     _, (own, near, other) = lax.optimization_barrier((got, (columns, near, other)))
-    mates = [send(slab, dc=1) for slab in (own, near, other)]
+    mates = [send(slab, dc=1) for slab in (near, other)]
+    mate = send(own, dc=1)
     diag_a, top_b, sent = top_part(got, base_a, factor_top)
     far, _ = lax.optimization_barrier((far, sent))
     taken = lax.all_to_all(sent, "col", 0, 0)
-    column_a, column_b = whole_columns(place, [own, near, other, far, *mates, send(far, dc=1)])
+    column_a, column_b = whole_columns(
+        place, [own, far, near, other, mate, send(far, dc=1), *mates]
+    )
     base_b, _ = lax.optimization_barrier((base_b, column_a))
     diag_b = last_part(got, base_b, taken, factor_top)
     return (column_a, diag_a, column_b, top_b, diag_b)

time: 157 us -> 155 us (0.987)
  waiting for transfers between devices: 52.4 us -> 47.5 us
  starting transfers between devices: 58 us -> 60.4 us
    ppermute x35, waiting for transfers between devices: 33.4 us -> 39.7 us  [send(): return lax.ppermute(value, BOTH, shifted(**by))]
    ppermute x1, waiting for transfers between devices: 10.8 us -> 4.62 us  [on_device(): part_b = lax.ppermute(part_b, BOTH, spread_pairs())]
    ppermute x1, waiting for transfers between devices: 7.65 us -> 2.72 us  [on_device(): part_a = lax.ppermute(prep_a(place, lists, factor_a), BOTH, spread_pairs())]
    ppermute x1, starting transfers between devices: 1.91 us -> 4.92 us  [on_device(): part_b = lax.ppermute(part_b, BOTH, spread_pairs())]
where the time goes in v10:
time: 155 us; the launch traced here: 154 us
  starting transfers between devices  60.4 us (39%)
  waiting for transfers between devices  47.5 us (31%)
  Pallas kernels  40.8 us (26%)
  local copies, waits for them, and re-layouts  3.84 us (2%)
    ppermute x35, starting transfers between devices, send(): return lax.ppermute(value, BOTH, shifted(**by))  46.1 us
    ppermute x35, waiting for transfers between devices, send(): return lax.ppermute(value, BOTH, shifted(**by))  39.7 us
    pallas_call x2, Pallas kernels, late_product(): pl.pallas_call(functools.partial(late_body, half), name='late_product', g...  8.02 us
    pallas_call x1, Pallas kernels, early_product(): pl.pallas_call(early_body, name='early_product', grid_spec=pltpu.Prefetch...  7.9 us
    pallas_call x1, Pallas kernels, own_product(): pl.pallas_call(own_body, name='own_product', grid_spec=pltpu.PrefetchScal...  6.2 us
    ppermute x1, starting transfers between devices, on_device(): part_a = lax.ppermute(prep_a(place, lists, factor_a), BOTH, spread_pairs())  4.92 us
    ppermute x1, starting transfers between devices, on_device(): part_b = lax.ppermute(part_b, BOTH, spread_pairs())  4.92 us
    pallas_call x1, Pallas kernels, whole_columns(): pl.pallas_call(column_body, name='whole_columns', grid_spec=pltpu.Prefetc...  4.69 us
  transfers between devices with their start and end apart: 38, of which 16 were waited for; matrix products, arithmetic and copies ran while one was open for 0% of the time, Pallas kernels for 20%

profile of v10, /device:TPU:1, one launch (start us, length us, event | category | flops | bytes accessed | tf_op | source)
XLA Modules:
  0.0 154.3 jit_solution(6084391481873079774)
XLA Ops:
  0.6 0.6 pad_add_fusion.place
  1.2 2.9 %prep_a.1 = bf16[12,64,128]{2,1,0:T(8,128)(2,1)} custom-call(s32[2]{0:T(128)} %pad_add_fusion.place, s32[16,12]{1,0:T(8,128)} %rows_a.5, s32[16]{0:T(128)} %counts_a.5, bf16[1536,512]{1,0:T(8,128)(2,1)} %refs_8_.1), custom_call_target="tpu_custom_call" | custom-call | bytes 786432 | tf_op jit(solution)/shard_map/prep_a/pallas_call | solution.py:95
  4.1 4.9 %collective-permute-start = (bf16[12,64,128]{2,1,0:T(8,128)(2,1)}, bf16[12,64,128]{2,1,0:T(8,128)(2,1)S(1)}, u32[]{:S(2)}, u32[]{:S(2)}) collective-permute-start(bf16[12,64,128]{2,1,0:T(8,128)(2,1)} %prep_a.1), channel_id=1, source_target_pairs={{0,0},{1,32},{2,8},{3,40},{4,16},{5,48},{6,24},{7,56},{8,9},{9,41}... | collective-permute-start | bytes 589832 | tf_op jit(solution)/shard_map/ppermute | solution.py:551
  9.0 4.3 %prep_b.1 = bf16[12,64,128]{2,1,0:T(8,128)(2,1)} custom-call(s32[2]{0:T(128)} %pad_add_fusion.place, s32[16,12]{1,0:T(8,128)} %rows_a.5, s32[16]{0:T(128)} %counts_a.5, s32[16,12]{1,0:T(8,128)} %rows_b.3, s32[16]{0:T(128)} %counts_b.3, bf16[1536,512]{1,0:T(8,128)(2,1)} %refs_8_.1, bf16[1536,512]{1,0:T(8,128)(2,1)} %refs_9_.1, bf16[512,512]{1,0:T(8,128)(2,1)} %top.5), custom_call_target="tpu_custom_call" | custom-call | flops 201326592 | bytes 3145728 | tf_op jit(solution)/shard_map/prep_b/pallas_call | solution.py:128
  13.3 4.9 %collective-permute-start.5 = (bf16[12,64,128]{2,1,0:T(8,128)(2,1)}, bf16[12,64,128]{2,1,0:T(8,128)(2,1)S(1)}, u32[]{:S(2)}, u32[]{:S(2)}) collective-permute-start(bf16[12,64,128]{2,1,0:T(8,128)(2,1)} %prep_b.1), channel_id=1, source_target_pairs={{0,0},{1,32},{2,8},{3,40},{4,16},{5,48},{6,24},{7,56},{8,9},{9,41}... | collective-permute-start | bytes 589832 | tf_op jit(solution)/shard_map/ppermute | solution.py:553
  18.3 2.7 %collective-permute-done = bf16[12,64,128]{2,1,0:T(8,128)(2,1)S(1)} collective-permute-done((bf16[12,64,128]{2,1,0:T(8,128)(2,1)}, bf16[12,64,128]{2,1,0:T(8,128)(2,1)S(1)}, u32[]{:S(2)}, u32[]{:S(2)}) %collective-permute-start) | collective-permute-done | bytes 196640 | tf_op jit(solution)/shard_map/ppermute | solution.py:551
  21.0 1.0 collective-permute-start.1
  22.0 2.7 %collective-permute-start.3 = (bf16[12,64,128]{2,1,0:T(8,128)(2,1)S(1)}, bf16[12,64,128]{2,1,0:T(8,128)(2,1)S(1)}, u32[]{:S(2)}, u32[]{:S(2)}) collective-permute-start(bf16[12,64,128]{2,1,0:T(8,128)(2,1)S(1)} %collective-permute-done), channel_id=1, source_target_pairs={{0,24},{1,25},{2,26},{3,27},{4,28},{5,29},{6,30},{7,31},{8,0},{9,1... | collective-permute-start | bytes 589832 | tf_op jit(solution)/shard_map/ppermute | solution.py:539
  24.7 4.6 %collective-permute-done.5 = bf16[12,64,128]{2,1,0:T(8,128)(2,1)S(1)} collective-permute-done((bf16[12,64,128]{2,1,0:T(8,128)(2,1)}, bf16[12,64,128]{2,1,0:T(8,128)(2,1)S(1)}, u32[]{:S(2)}, u32[]{:S(2)}) %collective-permute-start.5) | collective-permute-done | bytes 196640 | tf_op jit(solution)/shard_map/ppermute | solution.py:553
  29.3 4.8 %collective-permute-start.6 = (bf16[12,64,128]{2,1,0:T(8,128)(2,1)S(1)}, bf16[12,64,128]{2,1,0:T(8,128)(2,1)S(1)}, u32[]{:S(2)}, u32[]{:S(2)}) collective-permute-start(bf16[12,64,128]{2,1,0:T(8,128)(2,1)S(1)} %collective-permute-done.5), channel_id=1, source_target_pairs={{0,64},{1,65},{2,66},{3,67},{4,68},{5,69},{6,70},{7,71},{8,72},{9,... | collective-permute-start | bytes 589832 | tf_op jit(solution)/shard_map/ppermute | solution.py:539
  34.1 1.0 collective-permute-start.7
  35.1 1.7 %collective-permute-start.8 = (bf16[12,64,128]{2,1,0:T(8,128)(2,1)S(1)}, bf16[12,64,128]{2,1,0:T(8,128)(2,1)S(1)}, u32[]{:S(2)}, u32[]{:S(2)}) collective-permute-start(bf16[12,64,128]{2,1,0:T(8,128)(2,1)S(1)} %collective-permute-done.5), channel_id=1, source_target_pairs={{0,96},{1,97},{2,98},{3,99},{4,100},{5,101},{6,102},{7,103},{8,104... | collective-permute-start | bytes 589832 | tf_op jit(solution)/shard_map/ppermute | solution.py:539
  36.8 0.3 collective-permute-done.2
  37.1 3.4 %collective-permute-done.3 = bf16[12,64,128]{2,1,0:T(8,128)(2,1)S(1)} collective-permute-done((bf16[12,64,128]{2,1,0:T(8,128)(2,1)S(1)}, bf16[12,64,128]{2,1,0:T(8,128)(2,1)S(1)}, u32[]{:S(2)}, u32[]{:S(2)}) %collective-permute-start.3) | collective-permute-done | bytes 196640 | tf_op jit(solution)/shard_map/ppermute | solution.py:539
  40.5 0.1 pad_maximum_fusion._.a_own
  40.6 1.1 collective-permute-done.7
  41.8 2.6 %collective-permute-done.8 = bf16[12,64,128]{2,1,0:T(8,128)(2,1)S(1)} collective-permute-done((bf16[12,64,128]{2,1,0:T(8,128)(2,1)S(1)}, bf16[12,64,128]{2,1,0:T(8,128)(2,1)S(1)}, u32[]{:S(2)}, u32[]{:S(2)}) %collective-permute-start.8) | collective-permute-done | bytes 196640 | tf_op jit(solution)/shard_map/ppermute | solution.py:539
  44.6 2.7 %collective-permute-start.11 = (bf16[4,12,64,128]{3,2,1,0:T(8,128)(2,1)S(1)}, bf16[4,12,64,128]{3,2,1,0:T(8,128)(2,1)S(1)}, u32[]{:S(2)}, u32[]{:S(2)}) collective-permute-start(bf16[4,12,64,128]{3,2,1,0:T(8,128)(2,1)S(1)} %pad_maximum_fusion._.a_own), channel_id=1, source_target_pairs={{0,96},{1,97},{2,98},{3,99},{4,100},{5,101},{6,102},{7,103},{8,104... | collective-permute-start | bytes 2359304 | tf_op jit(solution)/shard_map/ppermute | solution.py:539
  47.3 2.6 %collective-permute-start.14 = (bf16[4,12,64,128]{3,2,1,0:T(8,128)(2,1)S(1)}, bf16[4,12,64,128]{3,2,1,0:T(8,128)(2,1)S(1)}, u32[]{:S(2)}, u32[]{:S(2)}) collective-permute-start(bf16[4,12,64,128]{3,2,1,0:T(8,128)(2,1)S(1)} %pad_maximum_fusion.1.b_own), channel_id=1, source_target_pairs={{0,24},{1,25},{2,26},{3,27},{4,28},{5,29},{6,30},{7,31},{8,0},{9,1... | collective-permute-start | bytes 2359304 | tf_op jit(solution)/shard_map/ppermute | solution.py:539
  49.9 3.7 %copy-done.1 = bf16[1536,3072]{1,0:T(8,128)(2,1)S(1)} copy-done((bf16[1536,3072]{1,0:T(8,128)(2,1)S(1)}, bf16[1536,3072]{1,0:T(8,128)(2,1)}, u32[]{:S(2)}) %copy-start.1) | copy-done | bytes 9437208
  53.6 0.6 hold.1.tile
  54.2 6.2 %own_product.1 = (f32[256,1536]{1,0:T(8,128)S(1)}, bf16[128,1536]{1,0:T(8,128)(2,1)S(1)}) custom-call(s32[2]{0:T(128)S(1)} %copy-done.7, bf16[4,12,64,128]{3,2,1,0:T(8,128)(2,1)S(1)} %pad_maximum_fusion._.a_own, bf16[4,12,64,128]{3,2,1,0:T(8,128)(2,1)S(1)} %pad_maximum_fusion.1.b_own, bf16[1536,3072]{1,0:T(8,128)(2,1)S(1)} %hold.1.tile), custom_call_target="tpu_custom_call" | custom-call | flops 2415919104 | bytes 6291456 | tf_op jit(solution)/shard_map/own_product/pallas_call | solution.py:235
  60.5 3.6 %collective-permute-done.9.b_down = bf16[4,12,64,128]{3,2,1,0:T(8,128)(2,1)S(1)} collective-permute-done((bf16[4,12,64,128]{3,2,1,0:T(8,128)(2,1)S(1)}, bf16[4,12,64,128]{3,2,1,0:T(8,128)(2,1)S(1)}, u32[]{:S(2)}, u32[]{:S(2)}) %collective-permute-start.9) | collective-permute-done | bytes 786464 | tf_op jit(solution)/shard_map/ppermute | solution.py:539
  64.1 1.7 %collective-permute-start.10 = (bf16[2,12,64,128]{3,2,1,0:T(8,128)(2,1)S(1)}, bf16[2,12,64,128]{3,2,1,0:T(8,128)(2,1)S(1)}, u32[]{:S(2)}, u32[]{:S(2)}) collective-permute-start(bf16[2,12,64,128]{3,2,1,0:T(8,128)(2,1)S(1)} %slice.12), channel_id=1, source_target_pairs={{0,32},{1,33},{2,34},{3,35},{4,36},{5,37},{6,38},{7,39},{8,40},{9,... | collective-permute-start | bytes 1179656 | tf_op jit(solution)/shard_map/ppermute | solution.py:539
  65.9 1.6 %collective-permute-start.12 = (bf16[2,12,64,128]{3,2,1,0:T(8,128)(2,1)S(1)}, bf16[2,12,64,128]{3,2,1,0:T(8,128)(2,1)S(1)}, u32[]{:S(2)}, u32[]{:S(2)}) collective-permute-start(bf16[2,12,64,128]{3,2,1,0:T(8,128)(2,1)S(1)} %slice.16), channel_id=1, source_target_pairs={{0,96},{1,97},{2,98},{3,99},{4,100},{5,101},{6,102},{7,103},{8,104... | collective-permute-start | bytes 1179656 | tf_op jit(solution)/shard_map/ppermute | solution.py:539
  67.5 2.7 %collective-permute-start.15 = (bf16[2,12,64,128]{3,2,1,0:T(8,128)(2,1)S(1)}, bf16[2,12,64,128]{3,2,1,0:T(8,128)(2,1)S(1)}, u32[]{:S(2)}, u32[]{:S(2)}) collective-permute-start(bf16[2,12,64,128]{3,2,1,0:T(8,128)(2,1)S(1)} %slice.17), channel_id=1, source_target_pairs={{0,24},{1,25},{2,26},{3,27},{4,28},{5,29},{6,30},{7,31},{8,0},{9,1... | collective-permute-start | bytes 1179656 | tf_op jit(solution)/shard_map/ppermute | solution.py:539
  70.3 7.9 %early_product.1.before = bf16[8,128,1536]{2,1,0:T(8,128)(2,1)S(1)} custom-call(s32[2]{0:T(128)S(1)} %copy-done.7, bf16[4,12,64,128]{3,2,1,0:T(8,128)(2,1)S(1)} %collective-permute-done.4.a_down, bf16[4,12,64,128]{3,2,1,0:T(8,128)(2,1)S(1)} %collective-permute-done.11.a_up, bf16[4,12,64,128]{3,2,1,0:T(8,128)(2,1)S(1)} %collective-permute-done.9.b_down, ...), custom_call_target="tpu_custom_call" | custom-call | flops 4831838208 | bytes 6291456 | tf_op jit(solution)/shard_map/early_product/pallas_call | solution.py:287
  78.2 4.0 %late_product.3 = (bf16[4,128,768]{2,1,0:T(8,128)(2,1)S(1)}, bf16[4,128,768]{2,1,0:T(8,128)(2,1)S(1)}) custom-call(s32[2]{0:T(128)S(1)} %copy-done.7, bf16[2,12,64,128]{3,2,1,0:T(8,128)(2,1)S(1)} %collective-permute-done.10.a_far, bf16[2,12,64,128]{3,2,1,0:T(8,128)(2,1)S(1)} %collective-permute-done.12.a_far_more, ...), custom_call_target="tpu_custom_call" | custom-call | flops 1207959552 | bytes 4718592 | tf_op jit(solution)/shard_map/late_product/pallas_call | solution.py:347
  82.2 2.5 %collective-permute-start.20 = (bf16[4,128,768]{2,1,0:T(8,128)(2,1)S(1)}, bf16[4,128,768]{2,1,0:T(8,128)(2,1)S(1)}, u32[]{:S(2)}, u32[]{:S(2)}) collective-permute-start(bf16[4,128,768]{2,1,0:T(8,128)(2,1)S(1)} %get-tuple-element.51), channel_id=1, source_target_pairs={{0,1},{1,0},{2,3},{3,2},{4,5},{5,4},{6,7},{7,6},{8,9},{9,8},{10,11... | collective-permute-start | bytes 2359304 | tf_op jit(solution)/shard_map/ppermute | solution.py:539
  84.7 4.0 %late_product.2 = (bf16[4,128,768]{2,1,0:T(8,128)(2,1)S(1)}, bf16[4,128,768]{2,1,0:T(8,128)(2,1)S(1)}) custom-call(s32[2]{0:T(128)S(1)} %copy-done.7, bf16[2,12,64,128]{3,2,1,0:T(8,128)(2,1)S(1)} %collective-permute-done.10.a_far, bf16[2,12,64,128]{3,2,1,0:T(8,128)(2,1)S(1)} %collective-permute-done.12.a_far_more, ...), custom_call_target="tpu_custom_call" | custom-call | flops 1207959552 | bytes 4718592 | tf_op jit(solution)/shard_map/late_product/pallas_call | solution.py:347
  88.9 1.1 pair_sum.3
  89.9 0.6 collective-permute-start.21
  90.5 2.2 %collective-permute-start.22 = (bf16[128,768]{1,0:T(8,128)(2,1)S(1)}, bf16[128,768]{1,0:T(8,128)(2,1)S(1)}, u32[]{:S(2)}, u32[]{:S(2)}) collective-permute-start(bf16[128,768]{1,0:T(8,128)(2,1)S(1)} %get-tuple-element.54), channel_id=1, source_target_pairs={{0,2},{1,3},{2,4},{3,5},{4,6},{5,7},{6,0},{7,1},{8,10},{9,11},{10,... | collective-permute-start | bytes 589832 | tf_op jit(solution)/shard_map/ppermute | solution.py:539
  92.7 1.5 collective-permute-start.23
  94.2 1.1 pair_sum.2
  95.3 1.3 collective-permute-start.17
  96.5 0.9 collective-permute-start.18
  97.4 0.2 collective-permute-done.21.refs_5_
  97.6 2.1 %collective-permute-start.19 = (bf16[128,768]{1,0:T(8,128)(2,1)S(1)}, bf16[128,768]{1,0:T(8,128)(2,1)S(1)}, u32[]{:S(2)}, u32[]{:S(2)}) collective-permute-start(bf16[128,768]{1,0:T(8,128)(2,1)S(1)} %get-tuple-element.49), channel_id=1, source_target_pairs={{0,6},{1,7},{2,0},{3,1},{4,2},{5,3},{6,4},{7,5},{8,14},{9,15},{10,... | collective-permute-start | bytes 589832 | tf_op jit(solution)/shard_map/ppermute | solution.py:539
  99.7 3.7 %collective-permute-done.22.refs_6_ = bf16[128,768]{1,0:T(8,128)(2,1)S(1)} collective-permute-done((bf16[128,768]{1,0:T(8,128)(2,1)S(1)}, bf16[128,768]{1,0:T(8,128)(2,1)S(1)}, u32[]{:S(2)}, u32[]{:S(2)}) %collective-permute-start.22) | collective-permute-done | bytes 196640 | tf_op jit(solution)/shard_map/ppermute | solution.py:539
  103.4 2.7 %collective-permute-done.17.refs_1_ = bf16[128,768]{1,0:T(8,128)(2,1)S(1)} collective-permute-done((bf16[128,768]{1,0:T(8,128)(2,1)S(1)}, bf16[128,768]{1,0:T(8,128)(2,1)S(1)}, u32[]{:S(2)}, u32[]{:S(2)}) %collective-permute-start.17) | collective-permute-done | bytes 196640 | tf_op jit(solution)/shard_map/ppermute | solution.py:539
  106.0 5.0 %collective-permute-done.18.refs_2_ = bf16[128,768]{1,0:T(8,128)(2,1)S(1)} collective-permute-done((bf16[128,768]{1,0:T(8,128)(2,1)S(1)}, bf16[128,768]{1,0:T(8,128)(2,1)S(1)}, u32[]{:S(2)}, u32[]{:S(2)}) %collective-permute-start.18) | collective-permute-done | bytes 196640 | tf_op jit(solution)/shard_map/ppermute | solution.py:539
  111.1 1.9 %slots.1 = (bf16[128,1536]{1,0:T(8,128)(2,1)S(1)}, bf16[192,512]{1,0:T(8,128)(2,1)S(1)}) custom-call(s32[2]{0:T(128)S(1)} %copy-done.7, s32[16,12]{1,0:T(8,128)S(1)} %copy-done.6, s32[16]{0:T(128)S(1)} %copy-done.9, s32[16,12]{1,0:T(8,128)S(1)} %copy-done.8, s32[16]{0:T(128)S(1)} %copy-done.10, bf16[128,768]{1,0:T(8,128)(2,1)S(1)} %get-tuple-element.46.refs_0_, ...), custom_call_target="tpu_custom_call" | custom-call | flops 301989888 | bytes 5111808 | tf_op jit(solution)/shard_map/slots/pallas_call | solution.py:423
  113.0 1.8 %collective-permute-start.27 = (bf16[128,1536]{1,0:T(8,128)(2,1)S(1)}, bf16[128,1536]{1,0:T(8,128)(2,1)S(1)}, u32[]{:S(2)}, u32[]{:S(2)}) collective-permute-start(bf16[128,1536]{1,0:T(8,128)(2,1)S(1)} %get-tuple-element.65.refs_0_), channel_id=1, source_target_pairs={{0,2},{1,3},{2,4},{3,5},{4,6},{5,7},{6,0},{7,1},{8,10},{9,11},{10,... | collective-permute-start | bytes 1179656 | tf_op jit(solution)/shard_map/ppermute | solution.py:539
  114.8 0.9 collective-permute-start.28
  115.7 1.0 collective-permute-start.24
  116.7 2.1 %collective-permute-start.25 = (bf16[192,512]{1,0:T(8,128)(2,1)S(1)}, bf16[192,512]{1,0:T(8,128)(2,1)S(1)}, u32[]{:S(2)}, u32[]{:S(2)}) collective-permute-start(bf16[192,512]{1,0:T(8,128)(2,1)S(1)} %get-tuple-element.58.one), channel_id=1, source_target_pairs={{0,8},{1,9},{2,10},{3,11},{4,12},{5,13},{6,14},{7,15},{8,16},{9,17... | collective-permute-start | bytes 589832 | tf_op jit(solution)/shard_map/ppermute | solution.py:539
  118.8 0.6 collective-permute-start.26
  119.4 3.2 %collective-permute-done.24.two = bf16[192,512]{1,0:T(8,128)(2,1)S(1)} collective-permute-done((bf16[192,512]{1,0:T(8,128)(2,1)S(1)}, bf16[192,512]{1,0:T(8,128)(2,1)S(1)}, u32[]{:S(2)}, u32[]{:S(2)}) %collective-permute-start.24) | collective-permute-done | bytes 196640 | tf_op jit(solution)/shard_map/ppermute | solution.py:539
  122.6 5.6 %collective-permute-done.25.three = bf16[192,512]{1,0:T(8,128)(2,1)S(1)} collective-permute-done((bf16[192,512]{1,0:T(8,128)(2,1)S(1)}, bf16[192,512]{1,0:T(8,128)(2,1)S(1)}, u32[]{:S(2)}, u32[]{:S(2)}) %collective-permute-start.25) | collective-permute-done | bytes 196640 | tf_op jit(solution)/shard_map/ppermute | solution.py:539
  128.3 0.1 fold.1.one
  128.4 0.6 collective-permute-start.32
  129.0 0.9 collective-permute-start.29
  129.9 0.7 collective-permute-start.30
  130.5 2.0 %collective-permute-start.31 = (bf16[192,512]{1,0:T(8,128)(2,1)S(1)}, bf16[192,512]{1,0:T(8,128)(2,1)S(1)}, u32[]{:S(2)}, u32[]{:S(2)}) collective-permute-start(bf16[192,512]{1,0:T(8,128)(2,1)S(1)} %fold.1.one), channel_id=1, source_target_pairs={{0,96},{1,97},{2,98},{3,99},{4,100},{5,101},{6,102},{7,103},{8,104... | collective-permute-start | bytes 589832 | tf_op jit(solution)/shard_map/ppermute | solution.py:539
  132.5 2.8 %collective-permute-done.29.two = bf16[192,512]{1,0:T(8,128)(2,1)S(1)} collective-permute-done((bf16[192,512]{1,0:T(8,128)(2,1)S(1)}, bf16[192,512]{1,0:T(8,128)(2,1)S(1)}, u32[]{:S(2)}, u32[]{:S(2)}) %collective-permute-start.29) | collective-permute-done | bytes 196640 | tf_op jit(solution)/shard_map/ppermute | solution.py:539
  135.3 5.4 %collective-permute-done.30.three = bf16[192,512]{1,0:T(8,128)(2,1)S(1)} collective-permute-done((bf16[192,512]{1,0:T(8,128)(2,1)S(1)}, bf16[192,512]{1,0:T(8,128)(2,1)S(1)}, u32[]{:S(2)}, u32[]{:S(2)}) %collective-permute-start.30) | collective-permute-done | bytes 196640 | tf_op jit(solution)/shard_map/ppermute | solution.py:539
  140.7 1.3 collective-permute-start.33
  142.0 0.5 collective-permute-start.36
  142.5 1.1 top_part.1
  143.7 4.5 %all-to-all-start = ((bf16[8,64,128]{2,1,0:T(8,128)(2,1)}), bf16[8,64,128]{2,1,0:T(8,128)(2,1)S(1)}, u32[]{:S(2)}, u32[]{:S(2)}) async-start(bf16[8,64,128]{2,1,0:T(8,128)(2,1)} %get-tuple-element.66), calls=%async_computation | async-start | bytes 262144 | tf_op jit(solution)/shard_map/all_to_all | solution.py:582
  148.2 4.7 %whole_columns.1 = (bf16[1536,512]{1,0:T(8,128)(2,1)}, bf16[1536,512]{1,0:T(8,128)(2,1)}) custom-call(s32[2]{0:T(128)S(1)} %copy-done.7, bf16[128,1536]{1,0:T(8,128)(2,1)S(1)} %get-tuple-element.65.refs_0_, bf16[128,1536]{1,0:T(8,128)(2,1)S(1)} %collective-permute-done.32.refs_1_, bf16[128,1536]{1,0:T(8,128)(2,1)S(1)} %collective-permute-done.27.refs_2_, ...), custom_call_target="tpu_custom_call" | custom-call | bytes 6291456 | tf_op jit(solution)/shard_map/whole_columns/pallas_call | solution.py:455
  152.9 0.5 all-to-all-done.taken
  153.4 0.9 last_part.1
  (55 shorter events, 0.7 us)
Async XLA Ops:
  4.1 16.9 %collective-permute-start = (bf16[12,64,128]{2,1,0:T(8,128)(2,1)}, bf16[12,64,128]{2,1,0:T(8,128)(2,1)S(1)}, u32[]{:S(2)}, u32[]{:S(2)}) collective-permute-start(bf16[12,64,128]{2,1,0:T(8,128)(2,1)} %prep_a.1), channel_id=1, source_target_pairs={{0,0},{1,32},{2,8},{3,40},{4,16},{5,48},{6,24},{7,56},{8,9},{9,41}... | collective-permute-start | bytes 589832 | tf_op jit(solution)/shard_map/ppermute | solution.py:551
  13.3 16.0 %collective-permute-start.5 = (bf16[12,64,128]{2,1,0:T(8,128)(2,1)}, bf16[12,64,128]{2,1,0:T(8,128)(2,1)S(1)}, u32[]{:S(2)}, u32[]{:S(2)}) collective-permute-start(bf16[12,64,128]{2,1,0:T(8,128)(2,1)} %prep_b.1), channel_id=1, source_target_pairs={{0,0},{1,32},{2,8},{3,40},{4,16},{5,48},{6,24},{7,56},{8,9},{9,41}... | collective-permute-start | bytes 589832 | tf_op jit(solution)/shard_map/ppermute | solution.py:553
  21.0 14.1 %collective-permute-start.1 = (bf16[12,64,128]{2,1,0:T(8,128)(2,1)S(1)}, bf16[12,64,128]{2,1,0:T(8,128)(2,1)S(1)}, u32[]{:S(2)}, u32[]{:S(2)}) collective-permute-start(bf16[12,64,128]{2,1,0:T(8,128)(2,1)S(1)} %collective-permute-done), channel_id=1, source_target_pairs={{0,16},{1,17},{2,18},{3,19},{4,20},{5,21},{6,22},{7,23},{8,24},{9,... | collective-permute-start | bytes 589832 | tf_op jit(solution)/shard_map/ppermute | solution.py:539
  22.0 15.0 %collective-permute-start.2 = (bf16[12,64,128]{2,1,0:T(8,128)(2,1)S(1)}, bf16[12,64,128]{2,1,0:T(8,128)(2,1)S(1)}, u32[]{:S(2)}, u32[]{:S(2)}) collective-permute-start(bf16[12,64,128]{2,1,0:T(8,128)(2,1)S(1)} %collective-permute-done), channel_id=1, source_target_pairs={{0,8},{1,9},{2,10},{3,11},{4,12},{5,13},{6,14},{7,15},{8,16},{9,17... | collective-permute-start | bytes 589832 | tf_op jit(solution)/shard_map/ppermute | solution.py:539
  22.0 18.4 %collective-permute-start.3 = (bf16[12,64,128]{2,1,0:T(8,128)(2,1)S(1)}, bf16[12,64,128]{2,1,0:T(8,128)(2,1)S(1)}, u32[]{:S(2)}, u32[]{:S(2)}) collective-permute-start(bf16[12,64,128]{2,1,0:T(8,128)(2,1)S(1)} %collective-permute-done), channel_id=1, source_target_pairs={{0,24},{1,25},{2,26},{3,27},{4,28},{5,29},{6,30},{7,31},{8,0},{9,1... | collective-permute-start | bytes 589832 | tf_op jit(solution)/shard_map/ppermute | solution.py:539
  29.3 11.3 %collective-permute-start.6 = (bf16[12,64,128]{2,1,0:T(8,128)(2,1)S(1)}, bf16[12,64,128]{2,1,0:T(8,128)(2,1)S(1)}, u32[]{:S(2)}, u32[]{:S(2)}) collective-permute-start(bf16[12,64,128]{2,1,0:T(8,128)(2,1)S(1)} %collective-permute-done.5), channel_id=1, source_target_pairs={{0,64},{1,65},{2,66},{3,67},{4,68},{5,69},{6,70},{7,71},{8,72},{9,... | collective-permute-start | bytes 589832 | tf_op jit(solution)/shard_map/ppermute | solution.py:539
  34.1 7.7 %collective-permute-start.7 = (bf16[12,64,128]{2,1,0:T(8,128)(2,1)S(1)}, bf16[12,64,128]{2,1,0:T(8,128)(2,1)S(1)}, u32[]{:S(2)}, u32[]{:S(2)}) collective-permute-start(bf16[12,64,128]{2,1,0:T(8,128)(2,1)S(1)} %collective-permute-done.5), channel_id=1, source_target_pairs={{0,32},{1,33},{2,34},{3,35},{4,36},{5,37},{6,38},{7,39},{8,40},{9,... | collective-permute-start | bytes 589832 | tf_op jit(solution)/shard_map/ppermute | solution.py:539
  35.1 9.3 %collective-permute-start.8 = (bf16[12,64,128]{2,1,0:T(8,128)(2,1)S(1)}, bf16[12,64,128]{2,1,0:T(8,128)(2,1)S(1)}, u32[]{:S(2)}, u32[]{:S(2)}) collective-permute-start(bf16[12,64,128]{2,1,0:T(8,128)(2,1)S(1)} %collective-permute-done.5), channel_id=1, source_target_pairs={{0,96},{1,97},{2,98},{3,99},{4,100},{5,101},{6,102},{7,103},{8,104... | collective-permute-start | bytes 589832 | tf_op jit(solution)/shard_map/ppermute | solution.py:539
  40.6 19.9 %collective-permute-start.4 = (bf16[4,12,64,128]{3,2,1,0:T(8,128)(2,1)S(1)}, bf16[4,12,64,128]{3,2,1,0:T(8,128)(2,1)S(1)}, u32[]{:S(2)}, u32[]{:S(2)}) collective-permute-start(bf16[4,12,64,128]{3,2,1,0:T(8,128)(2,1)S(1)} %pad_maximum_fusion._.a_own), channel_id=1, source_target_pairs={{0,32},{1,33},{2,34},{3,35},{4,36},{5,37},{6,38},{7,39},{8,40},{9,... | collective-permute-start | bytes 2359304 | tf_op jit(solution)/shard_map/ppermute | solution.py:539
  44.4 9.8 %copy-start.7 = (s32[2]{0:T(128)S(1)}, s32[2]{0:T(128)}, u32[]{:S(2)}) copy-start(s32[2]{0:T(128)} %pad_add_fusion.place) | copy-start | bytes 28
  44.5 19.6 %collective-permute-start.9 = (bf16[4,12,64,128]{3,2,1,0:T(8,128)(2,1)S(1)}, bf16[4,12,64,128]{3,2,1,0:T(8,128)(2,1)S(1)}, u32[]{:S(2)}, u32[]{:S(2)}) collective-permute-start(bf16[4,12,64,128]{3,2,1,0:T(8,128)(2,1)S(1)} %pad_maximum_fusion.1.b_own), channel_id=1, source_target_pairs={{0,8},{1,9},{2,10},{3,11},{4,12},{5,13},{6,14},{7,15},{8,16},{9,17... | collective-permute-start | bytes 2359304 | tf_op jit(solution)/shard_map/ppermute | solution.py:539
  44.6 21.3 %collective-permute-start.11 = (bf16[4,12,64,128]{3,2,1,0:T(8,128)(2,1)S(1)}, bf16[4,12,64,128]{3,2,1,0:T(8,128)(2,1)S(1)}, u32[]{:S(2)}, u32[]{:S(2)}) collective-permute-start(bf16[4,12,64,128]{3,2,1,0:T(8,128)(2,1)S(1)} %pad_maximum_fusion._.a_own), channel_id=1, source_target_pairs={{0,96},{1,97},{2,98},{3,99},{4,100},{5,101},{6,102},{7,103},{8,104... | collective-permute-start | bytes 2359304 | tf_op jit(solution)/shard_map/ppermute | solution.py:539
  47.3 20.2 %collective-permute-start.14 = (bf16[4,12,64,128]{3,2,1,0:T(8,128)(2,1)S(1)}, bf16[4,12,64,128]{3,2,1,0:T(8,128)(2,1)S(1)}, u32[]{:S(2)}, u32[]{:S(2)}) collective-permute-start(bf16[4,12,64,128]{3,2,1,0:T(8,128)(2,1)S(1)} %pad_maximum_fusion.1.b_own), channel_id=1, source_target_pairs={{0,24},{1,25},{2,26},{3,27},{4,28},{5,29},{6,30},{7,31},{8,0},{9,1... | collective-permute-start | bytes 2359304 | tf_op jit(solution)/shard_map/ppermute | solution.py:539
  49.9 3.7 %copy-start.1 = (bf16[1536,3072]{1,0:T(8,128)(2,1)S(1)}, bf16[1536,3072]{1,0:T(8,128)(2,1)}, u32[]{:S(2)}) copy-start(bf16[1536,3072]{1,0:T(8,128)(2,1)} %source.1) | copy-start | bytes 28311556
  64.1 14.0 %collective-permute-start.10 = (bf16[2,12,64,128]{3,2,1,0:T(8,128)(2,1)S(1)}, bf16[2,12,64,128]{3,2,1,0:T(8,128)(2,1)S(1)}, u32[]{:S(2)}, u32[]{:S(2)}) collective-permute-start(bf16[2,12,64,128]{3,2,1,0:T(8,128)(2,1)S(1)} %slice.12), channel_id=1, source_target_pairs={{0,32},{1,33},{2,34},{3,35},{4,36},{5,37},{6,38},{7,39},{8,40},{9,... | collective-permute-start | bytes 1179656 | tf_op jit(solution)/shard_map/ppermute | solution.py:539
  65.8 12.4 %collective-permute-start.13 = (bf16[2,12,64,128]{3,2,1,0:T(8,128)(2,1)S(1)}, bf16[2,12,64,128]{3,2,1,0:T(8,128)(2,1)S(1)}, u32[]{:S(2)}, u32[]{:S(2)}) collective-permute-start(bf16[2,12,64,128]{3,2,1,0:T(8,128)(2,1)S(1)} %slice.14), channel_id=1, source_target_pairs={{0,8},{1,9},{2,10},{3,11},{4,12},{5,13},{6,14},{7,15},{8,16},{9,17... | collective-permute-start | bytes 1179656 | tf_op jit(solution)/shard_map/ppermute | solution.py:539
  65.9 12.2 %collective-permute-start.12 = (bf16[2,12,64,128]{3,2,1,0:T(8,128)(2,1)S(1)}, bf16[2,12,64,128]{3,2,1,0:T(8,128)(2,1)S(1)}, u32[]{:S(2)}, u32[]{:S(2)}) collective-permute-start(bf16[2,12,64,128]{3,2,1,0:T(8,128)(2,1)S(1)} %slice.16), channel_id=1, source_target_pairs={{0,96},{1,97},{2,98},{3,99},{4,100},{5,101},{6,102},{7,103},{8,104... | collective-permute-start | bytes 1179656 | tf_op jit(solution)/shard_map/ppermute | solution.py:539
  67.5 10.7 %collective-permute-start.15 = (bf16[2,12,64,128]{3,2,1,0:T(8,128)(2,1)S(1)}, bf16[2,12,64,128]{3,2,1,0:T(8,128)(2,1)S(1)}, u32[]{:S(2)}, u32[]{:S(2)}) collective-permute-start(bf16[2,12,64,128]{3,2,1,0:T(8,128)(2,1)S(1)} %slice.17), channel_id=1, source_target_pairs={{0,24},{1,25},{2,26},{3,27},{4,28},{5,29},{6,30},{7,31},{8,0},{9,1... | collective-permute-start | bytes 1179656 | tf_op jit(solution)/shard_map/ppermute | solution.py:539
  82.2 6.5 %collective-permute-start.20 = (bf16[4,128,768]{2,1,0:T(8,128)(2,1)S(1)}, bf16[4,128,768]{2,1,0:T(8,128)(2,1)S(1)}, u32[]{:S(2)}, u32[]{:S(2)}) collective-permute-start(bf16[4,128,768]{2,1,0:T(8,128)(2,1)S(1)} %get-tuple-element.51), channel_id=1, source_target_pairs={{0,1},{1,0},{2,3},{3,2},{4,5},{5,4},{6,7},{7,6},{8,9},{9,8},{10,11... | collective-permute-start | bytes 2359304 | tf_op jit(solution)/shard_map/ppermute | solution.py:539
  88.7 5.5 %collective-permute-start.16 = (bf16[4,128,768]{2,1,0:T(8,128)(2,1)S(1)}, bf16[4,128,768]{2,1,0:T(8,128)(2,1)S(1)}, u32[]{:S(2)}, u32[]{:S(2)}) collective-permute-start(bf16[4,128,768]{2,1,0:T(8,128)(2,1)S(1)} %get-tuple-element.45), channel_id=1, source_target_pairs={{0,1},{1,0},{2,3},{3,2},{4,5},{5,4},{6,7},{7,6},{8,9},{9,8},{10,11... | collective-permute-start | bytes 2359304 | tf_op jit(solution)/shard_map/ppermute | solution.py:539
  88.8 22.2 %copy-start = (bf16[1536,512]{1,0:T(8,128)(2,1)S(1)}, bf16[1536,512]{1,0:T(8,128)(2,1)}, u32[]{:S(2)}) copy-start(bf16[1536,512]{1,0:T(8,128)(2,1)} %refs_8_.1) | copy-start | bytes 4718596
  88.8 22.2 %copy-start.2 = (bf16[1536,512]{1,0:T(8,128)(2,1)S(1)}, bf16[1536,512]{1,0:T(8,128)(2,1)}, u32[]{:S(2)}) copy-start(bf16[1536,512]{1,0:T(8,128)(2,1)} %refs_9_.1) | copy-start | bytes 4718596
  88.8 22.2 %copy-start.6 = (s32[16,12]{1,0:T(8,128)S(1)}, s32[16,12]{1,0:T(8,128)}, u32[]{:S(2)}) copy-start(s32[16,12]{1,0:T(8,128)} %rows_a.5) | copy-start | bytes 2308
  88.8 22.2 %copy-start.8 = (s32[16,12]{1,0:T(8,128)S(1)}, s32[16,12]{1,0:T(8,128)}, u32[]{:S(2)}) copy-start(s32[16,12]{1,0:T(8,128)} %rows_b.3) | copy-start | bytes 2308
  88.8 22.2 %copy-start.9 = (s32[16]{0:T(128)S(1)}, s32[16]{0:T(128)}, u32[]{:S(2)}) copy-start(s32[16]{0:T(128)} %counts_a.5) | copy-start | bytes 196
  88.9 22.2 %copy-start.10 = (s32[16]{0:T(128)S(1)}, s32[16]{0:T(128)}, u32[]{:S(2)}) copy-start(s32[16]{0:T(128)} %counts_b.3) | copy-start | bytes 196
  89.9 7.6 %collective-permute-start.21 = (bf16[128,768]{1,0:T(8,128)(2,1)S(1)}, bf16[128,768]{1,0:T(8,128)(2,1)S(1)}, u32[]{:S(2)}, u32[]{:S(2)}) collective-permute-start(bf16[128,768]{1,0:T(8,128)(2,1)S(1)} %get-tuple-element.53), channel_id=1, source_target_pairs={{0,4},{1,5},{2,6},{3,7},{4,0},{5,1},{6,2},{7,3},{8,12},{9,13},{10,... | collective-permute-start | bytes 589832 | tf_op jit(solution)/shard_map/ppermute | solution.py:539
  90.5 12.8 %collective-permute-start.22 = (bf16[128,768]{1,0:T(8,128)(2,1)S(1)}, bf16[128,768]{1,0:T(8,128)(2,1)S(1)}, u32[]{:S(2)}, u32[]{:S(2)}) collective-permute-start(bf16[128,768]{1,0:T(8,128)(2,1)S(1)} %get-tuple-element.54), channel_id=1, source_target_pairs={{0,2},{1,3},{2,4},{3,5},{4,6},{5,7},{6,0},{7,1},{8,10},{9,11},{10,... | collective-permute-start | bytes 589832 | tf_op jit(solution)/shard_map/ppermute | solution.py:539
  92.7 10.6 %collective-permute-start.23 = (bf16[128,768]{1,0:T(8,128)(2,1)S(1)}, bf16[128,768]{1,0:T(8,128)(2,1)S(1)}, u32[]{:S(2)}, u32[]{:S(2)}) collective-permute-start(bf16[128,768]{1,0:T(8,128)(2,1)S(1)} %get-tuple-element.55), channel_id=1, source_target_pairs={{0,6},{1,7},{2,0},{3,1},{4,2},{5,3},{6,4},{7,5},{8,14},{9,15},{10,... | collective-permute-start | bytes 589832 | tf_op jit(solution)/shard_map/ppermute | solution.py:539
  95.3 10.8 %collective-permute-start.17 = (bf16[128,768]{1,0:T(8,128)(2,1)S(1)}, bf16[128,768]{1,0:T(8,128)(2,1)S(1)}, u32[]{:S(2)}, u32[]{:S(2)}) collective-permute-start(bf16[128,768]{1,0:T(8,128)(2,1)S(1)} %get-tuple-element.47), channel_id=1, source_target_pairs={{0,4},{1,5},{2,6},{3,7},{4,0},{5,1},{6,2},{7,3},{8,12},{9,13},{10,... | collective-permute-start | bytes 589832 | tf_op jit(solution)/shard_map/ppermute | solution.py:539
  96.5 14.5 %collective-permute-start.18 = (bf16[128,768]{1,0:T(8,128)(2,1)S(1)}, bf16[128,768]{1,0:T(8,128)(2,1)S(1)}, u32[]{:S(2)}, u32[]{:S(2)}) collective-permute-start(bf16[128,768]{1,0:T(8,128)(2,1)S(1)} %get-tuple-element.48), channel_id=1, source_target_pairs={{0,2},{1,3},{2,4},{3,5},{4,6},{5,7},{6,0},{7,1},{8,10},{9,11},{10,... | collective-permute-start | bytes 589832 | tf_op jit(solution)/shard_map/ppermute | solution.py:539
  97.6 13.4 %collective-permute-start.19 = (bf16[128,768]{1,0:T(8,128)(2,1)S(1)}, bf16[128,768]{1,0:T(8,128)(2,1)S(1)}, u32[]{:S(2)}, u32[]{:S(2)}) collective-permute-start(bf16[128,768]{1,0:T(8,128)(2,1)S(1)} %get-tuple-element.49), channel_id=1, source_target_pairs={{0,6},{1,7},{2,0},{3,1},{4,2},{5,3},{6,4},{7,5},{8,14},{9,15},{10,... | collective-permute-start | bytes 589832 | tf_op jit(solution)/shard_map/ppermute | solution.py:539
  111.0 31.5 %copy-start.3 = (bf16[512,512]{1,0:T(8,128)(2,1)S(1)}, bf16[512,512]{1,0:T(8,128)(2,1)}, u32[]{:S(2)}) copy-start(bf16[512,512]{1,0:T(8,128)(2,1)} %top.5) | copy-start | bytes 1572868
  111.1 31.5 %copy-start.4 = (f32[64,512]{1,0:T(8,128)S(1)}, f32[64,512]{1,0:T(8,128)}, u32[]{:S(2)}) copy-start(f32[64,512]{1,0:T(8,128)} %base.1) | copy-start | bytes 393220
  113.0 15.3 %collective-permute-start.27 = (bf16[128,1536]{1,0:T(8,128)(2,1)S(1)}, bf16[128,1536]{1,0:T(8,128)(2,1)S(1)}, u32[]{:S(2)}, u32[]{:S(2)}) collective-permute-start(bf16[128,1536]{1,0:T(8,128)(2,1)S(1)} %get-tuple-element.65.refs_0_), channel_id=1, source_target_pairs={{0,2},{1,3},{2,4},{3,5},{4,6},{5,7},{6,0},{7,1},{8,10},{9,11},{10,... | collective-permute-start | bytes 1179656 | tf_op jit(solution)/shard_map/ppermute | solution.py:539
  114.8 13.5 %collective-permute-start.28 = (bf16[128,1536]{1,0:T(8,128)(2,1)S(1)}, bf16[128,1536]{1,0:T(8,128)(2,1)S(1)}, u32[]{:S(2)}, u32[]{:S(2)}) collective-permute-start(bf16[128,1536]{1,0:T(8,128)(2,1)S(1)} %get-tuple-element.65.refs_0_), channel_id=1, source_target_pairs={{0,6},{1,7},{2,0},{3,1},{4,2},{5,3},{6,4},{7,5},{8,14},{9,15},{10,... | collective-permute-start | bytes 1179656 | tf_op jit(solution)/shard_map/ppermute | solution.py:539
  115.7 6.9 %collective-permute-start.24 = (bf16[192,512]{1,0:T(8,128)(2,1)S(1)}, bf16[192,512]{1,0:T(8,128)(2,1)S(1)}, u32[]{:S(2)}, u32[]{:S(2)}) collective-permute-start(bf16[192,512]{1,0:T(8,128)(2,1)S(1)} %get-tuple-element.58.one), channel_id=1, source_target_pairs={{0,16},{1,17},{2,18},{3,19},{4,20},{5,21},{6,22},{7,23},{8,24},{9,... | collective-permute-start | bytes 589832 | tf_op jit(solution)/shard_map/ppermute | solution.py:539
  116.7 11.5 %collective-permute-start.25 = (bf16[192,512]{1,0:T(8,128)(2,1)S(1)}, bf16[192,512]{1,0:T(8,128)(2,1)S(1)}, u32[]{:S(2)}, u32[]{:S(2)}) collective-permute-start(bf16[192,512]{1,0:T(8,128)(2,1)S(1)} %get-tuple-element.58.one), channel_id=1, source_target_pairs={{0,8},{1,9},{2,10},{3,11},{4,12},{5,13},{6,14},{7,15},{8,16},{9,17... | collective-permute-start | bytes 589832 | tf_op jit(solution)/shard_map/ppermute | solution.py:539
  118.8 9.5 %collective-permute-start.26 = (bf16[192,512]{1,0:T(8,128)(2,1)S(1)}, bf16[192,512]{1,0:T(8,128)(2,1)S(1)}, u32[]{:S(2)}, u32[]{:S(2)}) collective-permute-start(bf16[192,512]{1,0:T(8,128)(2,1)S(1)} %get-tuple-element.58.one), channel_id=1, source_target_pairs={{0,24},{1,25},{2,26},{3,27},{4,28},{5,29},{6,30},{7,31},{8,0},{9,1... | collective-permute-start | bytes 589832 | tf_op jit(solution)/shard_map/ppermute | solution.py:539
  128.4 15.3 %collective-permute-start.32 = (bf16[128,1536]{1,0:T(8,128)(2,1)S(1)}, bf16[128,1536]{1,0:T(8,128)(2,1)S(1)}, u32[]{:S(2)}, u32[]{:S(2)}) collective-permute-start(bf16[128,1536]{1,0:T(8,128)(2,1)S(1)} %get-tuple-element.65.refs_0_), channel_id=1, source_target_pairs={{0,4},{1,5},{2,6},{3,7},{4,0},{5,1},{6,2},{7,3},{8,12},{9,13},{10,... | collective-permute-start | bytes 1179656 | tf_op jit(solution)/shard_map/ppermute | solution.py:539
  129.0 6.3 %collective-permute-start.29 = (bf16[192,512]{1,0:T(8,128)(2,1)S(1)}, bf16[192,512]{1,0:T(8,128)(2,1)S(1)}, u32[]{:S(2)}, u32[]{:S(2)}) collective-permute-start(bf16[192,512]{1,0:T(8,128)(2,1)S(1)} %fold.1.one), channel_id=1, source_target_pairs={{0,64},{1,65},{2,66},{3,67},{4,68},{5,69},{6,70},{7,71},{8,72},{9,... | collective-permute-start | bytes 589832 | tf_op jit(solution)/shard_map/ppermute | solution.py:539
  129.9 10.9 %collective-permute-start.30 = (bf16[192,512]{1,0:T(8,128)(2,1)S(1)}, bf16[192,512]{1,0:T(8,128)(2,1)S(1)}, u32[]{:S(2)}, u32[]{:S(2)}) collective-permute-start(bf16[192,512]{1,0:T(8,128)(2,1)S(1)} %fold.1.one), channel_id=1, source_target_pairs={{0,32},{1,33},{2,34},{3,35},{4,36},{5,37},{6,38},{7,39},{8,40},{9,... | collective-permute-start | bytes 589832 | tf_op jit(solution)/shard_map/ppermute | solution.py:539
  130.5 10.2 %collective-permute-start.31 = (bf16[192,512]{1,0:T(8,128)(2,1)S(1)}, bf16[192,512]{1,0:T(8,128)(2,1)S(1)}, u32[]{:S(2)}, u32[]{:S(2)}) collective-permute-start(bf16[192,512]{1,0:T(8,128)(2,1)S(1)} %fold.1.one), channel_id=1, source_target_pairs={{0,96},{1,97},{2,98},{3,99},{4,100},{5,101},{6,102},{7,103},{8,104... | collective-permute-start | bytes 589832 | tf_op jit(solution)/shard_map/ppermute | solution.py:539
  140.7 7.4 %collective-permute-start.33 = (bf16[128,1536]{1,0:T(8,128)(2,1)S(1)}, bf16[128,1536]{1,0:T(8,128)(2,1)S(1)}, u32[]{:S(2)}, u32[]{:S(2)}) collective-permute-start(bf16[128,1536]{1,0:T(8,128)(2,1)S(1)} %get-tuple-element.65.refs_0_), channel_id=1, source_target_pairs={{0,1},{1,0},{2,3},{3,2},{4,5},{5,4},{6,7},{7,6},{8,9},{9,8},{10,11... | collective-permute-start | bytes 1179656 | tf_op jit(solution)/shard_map/ppermute | solution.py:539
  142.0 6.2 %collective-permute-start.35 = (bf16[128,1536]{1,0:T(8,128)(2,1)S(1)}, bf16[128,1536]{1,0:T(8,128)(2,1)}, u32[]{:S(2)}, u32[]{:S(2)}) collective-permute-start(bf16[128,1536]{1,0:T(8,128)(2,1)S(1)} %collective-permute-done.27.refs_2_), channel_id=1, source_target_pairs={{0,1},{1,0},{2,3},{3,2},{4,5},{5,4},{6,7},{7,6},{8,9},{9,8},{10,11... | collective-permute-start | bytes 1179656 | tf_op jit(solution)/shard_map/ppermute | solution.py:539
  142.0 6.2 %collective-permute-start.36 = (bf16[128,1536]{1,0:T(8,128)(2,1)S(1)}, bf16[128,1536]{1,0:T(8,128)(2,1)}, u32[]{:S(2)}, u32[]{:S(2)}) collective-permute-start(bf16[128,1536]{1,0:T(8,128)(2,1)S(1)} %collective-permute-done.28.refs_3_), channel_id=1, source_target_pairs={{0,1},{1,0},{2,3},{3,2},{4,5},{5,4},{6,7},{7,6},{8,9},{9,8},{10,11... | collective-permute-start | bytes 1179656 | tf_op jit(solution)/shard_map/ppermute | solution.py:539
  143.7 4.5 %collective-permute-start.34 = (bf16[128,1536]{1,0:T(8,128)(2,1)S(1)}, bf16[128,1536]{1,0:T(8,128)(2,1)}, u32[]{:S(2)}, u32[]{:S(2)}) collective-permute-start(bf16[128,1536]{1,0:T(8,128)(2,1)S(1)} %collective-permute-done.32.refs_1_), channel_id=1, source_target_pairs={{0,1},{1,0},{2,3},{3,2},{4,5},{5,4},{6,7},{7,6},{8,9},{9,8},{10,11... | collective-permute-start | bytes 1179656 | tf_op jit(solution)/shard_map/ppermute | solution.py:539
  143.7 9.8 %all-to-all-start = ((bf16[8,64,128]{2,1,0:T(8,128)(2,1)}), bf16[8,64,128]{2,1,0:T(8,128)(2,1)S(1)}, u32[]{:S(2)}, u32[]{:S(2)}) async-start(bf16[8,64,128]{2,1,0:T(8,128)(2,1)} %get-tuple-element.66), calls=%async_computation | async-start | bytes 262144 | tf_op jit(solution)/shard_map/all_to_all | solution.py:582
  148.2 5.3 %copy-start.5 = (f32[64,512]{1,0:T(8,128)S(1)}, f32[64,512]{1,0:T(8,128)}, u32[]{:S(2)}) copy-start(f32[64,512]{1,0:T(8,128)} %base.2) | copy-start | bytes 393220

commit v11 on v10

--- a/solution.py
+++ b/solution.py
@@ -48,7 +48,8 @@
     pairs = []
     for z, y, x, core in all_places():
         plane = (z * SIDE + y) % 8
-        to = device(z + core, y + x, plane // 2, plane % 2)
+        far = 2 - (x - plane // 2)
+        to = device(z + core, y + far, plane // 2, plane % 2)
         pairs.append((device(z, y, x, core), to))
     return pairs
 
@@ -148,6 +149,10 @@
     return u, v
 
 
+def slice_of(place, v):
+    return (place[1] // 2 + 2 - v + SIDE) % SIDE
+
+
 def turn(value, by):
     return (value + by + SIDE) % SIDE
 
@@ -273,12 +278,12 @@
 
     value = multiply(spread, rows_of(tile, pl.program_id(0)))
     for i, step in enumerate(STEPS):
-        out[2 * turn(v, -step) + (u + 1) % 2, :PART, :] = value[i * PART : (i + 1) * PART]
+        out[2 * slice_of(place, turn(v, -step)) + (u + 1) % 2, :PART, :] = value[i * PART : (i + 1) * PART]
     for j in range(4):
-        to = 2 * turn(v, (-1, 1)[j // 2]) + j % 2
+        to = 2 * slice_of(place, turn(v, (-1, 1)[j // 2])) + j % 2
         out[to, PART:, :] = value[W // 2 + j * PART : W // 2 + (j + 1) * PART]
     for j in range(2):
-        out[2 * v + j, PART:, :] = whole_b[j * PART : (j + 1) * PART, :]
+        out[2 * slice_of(place, v) + j, PART:, :] = whole_b[j * PART : (j + 1) * PART, :]
 
 
 def early_product(place, bufs, trailing, whole_b):
@@ -327,10 +332,10 @@
     value = half_multiply(spread_a, tile, step, turn(u, 2) // 2)
     value = (value + half_a[...]).astype(BF)
     for i, far in enumerate(STEPS):
-        ready[2 * turn(v, -far) + u % 2, :PART, :] = value[i * PART : (i + 1) * PART]
+        ready[2 * slice_of(place, turn(v, -far)) + u % 2, :PART, :] = value[i * PART : (i + 1) * PART]
     value = multiply(spread_b, rows_of(tile, step))
     for j in range(2):
-        ready[2 * turn(v, 2) + j, PART:, :] = value[j * PART : (j + 1) * PART]
+        ready[2 * slice_of(place, turn(v, 2)) + j, PART:, :] = value[j * PART : (j + 1) * PART]
     for x in range(SIDE):
         keep[x] = ready[2 * x + core]
         give[x] = ready[2 * x + 1 - core]

time: 155 us -> 153 us (0.987)
  waiting for transfers between devices: 47.5 us -> 44 us
  starting transfers between devices: 60.4 us -> 62 us
    ppermute x35, waiting for transfers between devices: 39.7 us -> 36.2 us  [send(): return lax.ppermute(value, BOTH, shifted(**by))]
    ppermute x1, waiting for transfers between devices: 4.62 us -> 1.67 us  [on_device(): part_b = lax.ppermute(part_b, BOTH, spread_pairs())]
    ppermute x35, starting transfers between devices: 46.1 us -> 49 us  [send(): return lax.ppermute(value, BOTH, shifted(**by))]
    ppermute x1, waiting for transfers between devices: 2.72 us -> 5.61 us  [on_device(): part_a = lax.ppermute(prep_a(place, lists, factor_a), BOTH, spread_pairs())]
  transfers between devices with their start and end apart: 38 -> 38, of which waited for: 16 -> 15; matrix products, arithmetic and copies ran while one was open for 0% -> 0% of each run, Pallas kernels for 20% -> 20%
where the time goes in v11:
time: 153 us; the launch traced here: 152 us
  starting transfers between devices  62 us (41%)
  waiting for transfers between devices  44 us (29%)
  Pallas kernels  40.7 us (27%)
  local copies, waits for them, and re-layouts  3.84 us (3%)
    ppermute x35, starting transfers between devices, send(): return lax.ppermute(value, BOTH, shifted(**by))  49 us
    ppermute x35, waiting for transfers between devices, send(): return lax.ppermute(value, BOTH, shifted(**by))  36.2 us
    pallas_call x2, Pallas kernels, late_product(): pl.pallas_call(functools.partial(late_body, half), name='late_product', g...  8.01 us
    pallas_call x1, Pallas kernels, early_product(): pl.pallas_call(early_body, name='early_product', grid_spec=pltpu.Prefetch...  7.9 us
    pallas_call x1, Pallas kernels, own_product(): pl.pallas_call(own_body, name='own_product', grid_spec=pltpu.PrefetchScal...  6.2 us
    ppermute x1, starting transfers between devices, on_device(): part_a = lax.ppermute(prep_a(place, lists, factor_a), BOTH, spread_pairs())  5.66 us
    ppermute x1, waiting for transfers between devices, on_device(): part_a = lax.ppermute(prep_a(place, lists, factor_a), BOTH, spread_pairs())  5.61 us
    pallas_call x1, Pallas kernels, whole_columns(): pl.pallas_call(column_body, name='whole_columns', grid_spec=pltpu.Prefetc...  4.69 us
  transfers between devices with their start and end apart: 38, of which 15 were waited for; matrix products, arithmetic and copies ran while one was open for 0% of the time, Pallas kernels for 20%

profile of v11, /device:TPU:1, one launch (start us, length us, event | category | flops | bytes accessed | tf_op | source)
XLA Modules:
  0.0 152.4 jit_solution(4381519684903787297)
XLA Ops:
  0.6 0.6 pad_add_fusion.place
  1.2 2.9 %prep_a.1 = bf16[12,64,128]{2,1,0:T(8,128)(2,1)} custom-call(s32[2]{0:T(128)} %pad_add_fusion.place, s32[16,12]{1,0:T(8,128)} %rows_a.5, s32[16]{0:T(128)} %counts_a.5, bf16[1536,512]{1,0:T(8,128)(2,1)} %refs_8_.1), custom_call_target="tpu_custom_call" | custom-call | bytes 786432 | tf_op jit(solution)/shard_map/prep_a/pallas_call | solution.py:96
  4.1 5.7 %collective-permute-start = (bf16[12,64,128]{2,1,0:T(8,128)(2,1)}, bf16[12,64,128]{2,1,0:T(8,128)(2,1)S(1)}, u32[]{:S(2)}, u32[]{:S(2)}) collective-permute-start(bf16[12,64,128]{2,1,0:T(8,128)(2,1)} %prep_a.1), channel_id=1, source_target_pairs={{0,16},{1,48},{2,8},{3,40},{4,0},{5,32},{6,24},{7,56},{8,25},{9,57... | collective-permute-start | bytes 589832 | tf_op jit(solution)/shard_map/ppermute | solution.py:556
  9.8 4.3 %prep_b.1 = bf16[12,64,128]{2,1,0:T(8,128)(2,1)} custom-call(s32[2]{0:T(128)} %pad_add_fusion.place, s32[16,12]{1,0:T(8,128)} %rows_a.5, s32[16]{0:T(128)} %counts_a.5, s32[16,12]{1,0:T(8,128)} %rows_b.3, s32[16]{0:T(128)} %counts_b.3, bf16[1536,512]{1,0:T(8,128)(2,1)} %refs_8_.1, bf16[1536,512]{1,0:T(8,128)(2,1)} %refs_9_.1, bf16[512,512]{1,0:T(8,128)(2,1)} %top.5), custom_call_target="tpu_custom_call" | custom-call | flops 201326592 | bytes 3145728 | tf_op jit(solution)/shard_map/prep_b/pallas_call | solution.py:129
  14.1 3.5 %collective-permute-start.5 = (bf16[12,64,128]{2,1,0:T(8,128)(2,1)}, bf16[12,64,128]{2,1,0:T(8,128)(2,1)S(1)}, u32[]{:S(2)}, u32[]{:S(2)}) collective-permute-start(bf16[12,64,128]{2,1,0:T(8,128)(2,1)} %prep_b.1), channel_id=1, source_target_pairs={{0,16},{1,48},{2,8},{3,40},{4,0},{5,32},{6,24},{7,56},{8,25},{9,57... | collective-permute-start | bytes 589832 | tf_op jit(solution)/shard_map/ppermute | solution.py:558
  17.5 5.6 %collective-permute-done = bf16[12,64,128]{2,1,0:T(8,128)(2,1)S(1)} collective-permute-done((bf16[12,64,128]{2,1,0:T(8,128)(2,1)}, bf16[12,64,128]{2,1,0:T(8,128)(2,1)S(1)}, u32[]{:S(2)}, u32[]{:S(2)}) %collective-permute-start) | collective-permute-done | bytes 196640 | tf_op jit(solution)/shard_map/ppermute | solution.py:556
  23.2 2.7 %collective-permute-start.3 = (bf16[12,64,128]{2,1,0:T(8,128)(2,1)S(1)}, bf16[12,64,128]{2,1,0:T(8,128)(2,1)S(1)}, u32[]{:S(2)}, u32[]{:S(2)}) collective-permute-start(bf16[12,64,128]{2,1,0:T(8,128)(2,1)S(1)} %collective-permute-done), channel_id=1, source_target_pairs={{0,24},{1,25},{2,26},{3,27},{4,28},{5,29},{6,30},{7,31},{8,0},{9,1... | collective-permute-start | bytes 589832 | tf_op jit(solution)/shard_map/ppermute | solution.py:544
  25.8 1.7 %collective-permute-done.5 = bf16[12,64,128]{2,1,0:T(8,128)(2,1)S(1)} collective-permute-done((bf16[12,64,128]{2,1,0:T(8,128)(2,1)}, bf16[12,64,128]{2,1,0:T(8,128)(2,1)S(1)}, u32[]{:S(2)}, u32[]{:S(2)}) %collective-permute-start.5) | collective-permute-done | bytes 196640 | tf_op jit(solution)/shard_map/ppermute | solution.py:558
  27.5 3.2 %collective-permute-start.6 = (bf16[12,64,128]{2,1,0:T(8,128)(2,1)S(1)}, bf16[12,64,128]{2,1,0:T(8,128)(2,1)S(1)}, u32[]{:S(2)}, u32[]{:S(2)}) collective-permute-start(bf16[12,64,128]{2,1,0:T(8,128)(2,1)S(1)} %collective-permute-done.5), channel_id=1, source_target_pairs={{0,64},{1,65},{2,66},{3,67},{4,68},{5,69},{6,70},{7,71},{8,72},{9,... | collective-permute-start | bytes 589832 | tf_op jit(solution)/shard_map/ppermute | solution.py:544
  30.7 0.9 collective-permute-start.7
  31.6 3.9 %collective-permute-start.8 = (bf16[12,64,128]{2,1,0:T(8,128)(2,1)S(1)}, bf16[12,64,128]{2,1,0:T(8,128)(2,1)S(1)}, u32[]{:S(2)}, u32[]{:S(2)}) collective-permute-start(bf16[12,64,128]{2,1,0:T(8,128)(2,1)S(1)} %collective-permute-done.5), channel_id=1, source_target_pairs={{0,96},{1,97},{2,98},{3,99},{4,100},{5,101},{6,102},{7,103},{8,104... | collective-permute-start | bytes 589832 | tf_op jit(solution)/shard_map/ppermute | solution.py:544
  35.4 0.1 pad_maximum_fusion._.a_own
  35.6 1.3 collective-permute-start.4
  36.9 2.1 %collective-permute-done.7 = bf16[12,64,128]{2,1,0:T(8,128)(2,1)S(1)} collective-permute-done((bf16[12,64,128]{2,1,0:T(8,128)(2,1)S(1)}, bf16[12,64,128]{2,1,0:T(8,128)(2,1)S(1)}, u32[]{:S(2)}, u32[]{:S(2)}) %collective-permute-start.7) | collective-permute-done | bytes 196640 | tf_op jit(solution)/shard_map/ppermute | solution.py:544
  38.9 1.8 %collective-permute-done.8 = bf16[12,64,128]{2,1,0:T(8,128)(2,1)S(1)} collective-permute-done((bf16[12,64,128]{2,1,0:T(8,128)(2,1)S(1)}, bf16[12,64,128]{2,1,0:T(8,128)(2,1)S(1)}, u32[]{:S(2)}, u32[]{:S(2)}) %collective-permute-start.8) | collective-permute-done | bytes 196640 | tf_op jit(solution)/shard_map/ppermute | solution.py:544
  40.8 0.1 pad_maximum_fusion.1.b_own
  40.9 0.1 collective-permute-start.9
  41.0 3.5 %collective-permute-start.11 = (bf16[4,12,64,128]{3,2,1,0:T(8,128)(2,1)S(1)}, bf16[4,12,64,128]{3,2,1,0:T(8,128)(2,1)S(1)}, u32[]{:S(2)}, u32[]{:S(2)}) collective-permute-start(bf16[4,12,64,128]{3,2,1,0:T(8,128)(2,1)S(1)} %pad_maximum_fusion._.a_own), channel_id=1, source_target_pairs={{0,96},{1,97},{2,98},{3,99},{4,100},{5,101},{6,102},{7,103},{8,104... | collective-permute-start | bytes 2359304 | tf_op jit(solution)/shard_map/ppermute | solution.py:544
  44.4 2.6 %collective-permute-start.14 = (bf16[4,12,64,128]{3,2,1,0:T(8,128)(2,1)S(1)}, bf16[4,12,64,128]{3,2,1,0:T(8,128)(2,1)S(1)}, u32[]{:S(2)}, u32[]{:S(2)}) collective-permute-start(bf16[4,12,64,128]{3,2,1,0:T(8,128)(2,1)S(1)} %pad_maximum_fusion.1.b_own), channel_id=1, source_target_pairs={{0,24},{1,25},{2,26},{3,27},{4,28},{5,29},{6,30},{7,31},{8,0},{9,1... | collective-permute-start | bytes 2359304 | tf_op jit(solution)/shard_map/ppermute | solution.py:544
  47.0 3.7 %copy-done.1 = bf16[1536,3072]{1,0:T(8,128)(2,1)S(1)} copy-done((bf16[1536,3072]{1,0:T(8,128)(2,1)S(1)}, bf16[1536,3072]{1,0:T(8,128)(2,1)}, u32[]{:S(2)}) %copy-start.1) | copy-done | bytes 9437208
  50.7 0.6 hold.1.tile
  51.4 6.2 %own_product.1 = (f32[256,1536]{1,0:T(8,128)S(1)}, bf16[128,1536]{1,0:T(8,128)(2,1)S(1)}) custom-call(s32[2]{0:T(128)S(1)} %copy-done.7, bf16[4,12,64,128]{3,2,1,0:T(8,128)(2,1)S(1)} %pad_maximum_fusion._.a_own, bf16[4,12,64,128]{3,2,1,0:T(8,128)(2,1)S(1)} %pad_maximum_fusion.1.b_own, bf16[1536,3072]{1,0:T(8,128)(2,1)S(1)} %hold.1.tile), custom_call_target="tpu_custom_call" | custom-call | flops 2415919104 | bytes 6291456 | tf_op jit(solution)/shard_map/own_product/pallas_call | solution.py:240
  57.6 3.6 %collective-permute-done.9.b_down = bf16[4,12,64,128]{3,2,1,0:T(8,128)(2,1)S(1)} collective-permute-done((bf16[4,12,64,128]{3,2,1,0:T(8,128)(2,1)S(1)}, bf16[4,12,64,128]{3,2,1,0:T(8,128)(2,1)S(1)}, u32[]{:S(2)}, u32[]{:S(2)}) %collective-permute-start.9) | collective-permute-done | bytes 786464 | tf_op jit(solution)/shard_map/ppermute | solution.py:544
  61.2 0.5 collective-permute-start.10
  61.7 0.1 collective-permute-start.13
  61.8 2.3 %collective-permute-start.12 = (bf16[2,12,64,128]{3,2,1,0:T(8,128)(2,1)S(1)}, bf16[2,12,64,128]{3,2,1,0:T(8,128)(2,1)S(1)}, u32[]{:S(2)}, u32[]{:S(2)}) collective-permute-start(bf16[2,12,64,128]{3,2,1,0:T(8,128)(2,1)S(1)} %slice.16), channel_id=1, source_target_pairs={{0,96},{1,97},{2,98},{3,99},{4,100},{5,101},{6,102},{7,103},{8,104... | collective-permute-start | bytes 1179656 | tf_op jit(solution)/shard_map/ppermute | solution.py:544
  64.2 2.7 %collective-permute-start.15 = (bf16[2,12,64,128]{3,2,1,0:T(8,128)(2,1)S(1)}, bf16[2,12,64,128]{3,2,1,0:T(8,128)(2,1)S(1)}, u32[]{:S(2)}, u32[]{:S(2)}) collective-permute-start(bf16[2,12,64,128]{3,2,1,0:T(8,128)(2,1)S(1)} %slice.17), channel_id=1, source_target_pairs={{0,24},{1,25},{2,26},{3,27},{4,28},{5,29},{6,30},{7,31},{8,0},{9,1... | collective-permute-start | bytes 1179656 | tf_op jit(solution)/shard_map/ppermute | solution.py:544
  66.9 7.9 %early_product.1.before = bf16[8,128,1536]{2,1,0:T(8,128)(2,1)S(1)} custom-call(s32[2]{0:T(128)S(1)} %copy-done.7, bf16[4,12,64,128]{3,2,1,0:T(8,128)(2,1)S(1)} %collective-permute-done.4.a_down, bf16[4,12,64,128]{3,2,1,0:T(8,128)(2,1)S(1)} %collective-permute-done.11.a_up, bf16[4,12,64,128]{3,2,1,0:T(8,128)(2,1)S(1)} %collective-permute-done.9.b_down, ...), custom_call_target="tpu_custom_call" | custom-call | flops 4831838208 | bytes 6291456 | tf_op jit(solution)/shard_map/early_product/pallas_call | solution.py:292
  74.8 4.0 %late_product.3 = (bf16[4,128,768]{2,1,0:T(8,128)(2,1)S(1)}, bf16[4,128,768]{2,1,0:T(8,128)(2,1)S(1)}) custom-call(s32[2]{0:T(128)S(1)} %copy-done.7, bf16[2,12,64,128]{3,2,1,0:T(8,128)(2,1)S(1)} %collective-permute-done.10.a_far, bf16[2,12,64,128]{3,2,1,0:T(8,128)(2,1)S(1)} %collective-permute-done.12.a_far_more, ...), custom_call_target="tpu_custom_call" | custom-call | flops 1207959552 | bytes 4718592 | tf_op jit(solution)/shard_map/late_product/pallas_call | solution.py:352
  78.9 2.9 %collective-permute-start.20 = (bf16[4,128,768]{2,1,0:T(8,128)(2,1)S(1)}, bf16[4,128,768]{2,1,0:T(8,128)(2,1)S(1)}, u32[]{:S(2)}, u32[]{:S(2)}) collective-permute-start(bf16[4,128,768]{2,1,0:T(8,128)(2,1)S(1)} %get-tuple-element.51), channel_id=1, source_target_pairs={{0,1},{1,0},{2,3},{3,2},{4,5},{5,4},{6,7},{7,6},{8,9},{9,8},{10,11... | collective-permute-start | bytes 2359304 | tf_op jit(solution)/shard_map/ppermute | solution.py:544
  81.8 4.0 %late_product.2 = (bf16[4,128,768]{2,1,0:T(8,128)(2,1)S(1)}, bf16[4,128,768]{2,1,0:T(8,128)(2,1)S(1)}) custom-call(s32[2]{0:T(128)S(1)} %copy-done.7, bf16[2,12,64,128]{3,2,1,0:T(8,128)(2,1)S(1)} %collective-permute-done.10.a_far, bf16[2,12,64,128]{3,2,1,0:T(8,128)(2,1)S(1)} %collective-permute-done.12.a_far_more, ...), custom_call_target="tpu_custom_call" | custom-call | flops 1207959552 | bytes 4718592 | tf_op jit(solution)/shard_map/late_product/pallas_call | solution.py:352
  85.8 0.3 collective-permute-start.16
  86.1 1.1 pair_sum.3
  87.2 1.6 %collective-permute-start.21 = (bf16[128,768]{1,0:T(8,128)(2,1)S(1)}, bf16[128,768]{1,0:T(8,128)(2,1)S(1)}, u32[]{:S(2)}, u32[]{:S(2)}) collective-permute-start(bf16[128,768]{1,0:T(8,128)(2,1)S(1)} %get-tuple-element.53), channel_id=1, source_target_pairs={{0,4},{1,5},{2,6},{3,7},{4,0},{5,1},{6,2},{7,3},{8,12},{9,13},{10,... | collective-permute-start | bytes 589832 | tf_op jit(solution)/shard_map/ppermute | solution.py:544
  88.9 3.4 %collective-permute-start.22 = (bf16[128,768]{1,0:T(8,128)(2,1)S(1)}, bf16[128,768]{1,0:T(8,128)(2,1)S(1)}, u32[]{:S(2)}, u32[]{:S(2)}) collective-permute-start(bf16[128,768]{1,0:T(8,128)(2,1)S(1)} %get-tuple-element.54), channel_id=1, source_target_pairs={{0,2},{1,3},{2,4},{3,5},{4,6},{5,7},{6,0},{7,1},{8,10},{9,11},{10,... | collective-permute-start | bytes 589832 | tf_op jit(solution)/shard_map/ppermute | solution.py:544
  92.3 1.1 pair_sum.2
  93.4 1.9 %collective-permute-start.17 = (bf16[128,768]{1,0:T(8,128)(2,1)S(1)}, bf16[128,768]{1,0:T(8,128)(2,1)S(1)}, u32[]{:S(2)}, u32[]{:S(2)}) collective-permute-start(bf16[128,768]{1,0:T(8,128)(2,1)S(1)} %get-tuple-element.47), channel_id=1, source_target_pairs={{0,4},{1,5},{2,6},{3,7},{4,0},{5,1},{6,2},{7,3},{8,12},{9,13},{10,... | collective-permute-start | bytes 589832 | tf_op jit(solution)/shard_map/ppermute | solution.py:544
  95.2 4.0 %collective-permute-start.19 = (bf16[128,768]{1,0:T(8,128)(2,1)S(1)}, bf16[128,768]{1,0:T(8,128)(2,1)S(1)}, u32[]{:S(2)}, u32[]{:S(2)}) collective-permute-start(bf16[128,768]{1,0:T(8,128)(2,1)S(1)} %get-tuple-element.49), channel_id=1, source_target_pairs={{0,6},{1,7},{2,0},{3,1},{4,2},{5,3},{6,4},{7,5},{8,14},{9,15},{10,... | collective-permute-start | bytes 589832 | tf_op jit(solution)/shard_map/ppermute | solution.py:544
  99.3 1.4 collective-permute-done.22.refs_6_
  100.6 0.5 collective-permute-done.23.refs_7_
  101.1 2.2 %collective-permute-done.17.refs_1_ = bf16[128,768]{1,0:T(8,128)(2,1)S(1)} collective-permute-done((bf16[128,768]{1,0:T(8,128)(2,1)S(1)}, bf16[128,768]{1,0:T(8,128)(2,1)S(1)}, u32[]{:S(2)}, u32[]{:S(2)}) %collective-permute-start.17) | collective-permute-done | bytes 196640 | tf_op jit(solution)/shard_map/ppermute | solution.py:544
  103.3 5.0 %collective-permute-done.18.refs_2_ = bf16[128,768]{1,0:T(8,128)(2,1)S(1)} collective-permute-done((bf16[128,768]{1,0:T(8,128)(2,1)S(1)}, bf16[128,768]{1,0:T(8,128)(2,1)S(1)}, u32[]{:S(2)}, u32[]{:S(2)}) %collective-permute-start.18) | collective-permute-done | bytes 196640 | tf_op jit(solution)/shard_map/ppermute | solution.py:544
  108.3 1.3 collective-permute-done.19.refs_3_
  109.6 1.9 %slots.1 = (bf16[128,1536]{1,0:T(8,128)(2,1)S(1)}, bf16[192,512]{1,0:T(8,128)(2,1)S(1)}) custom-call(s32[2]{0:T(128)S(1)} %copy-done.7, s32[16,12]{1,0:T(8,128)S(1)} %copy-done.6, s32[16]{0:T(128)S(1)} %copy-done.9, s32[16,12]{1,0:T(8,128)S(1)} %copy-done.8, s32[16]{0:T(128)S(1)} %copy-done.10, bf16[128,768]{1,0:T(8,128)(2,1)S(1)} %get-tuple-element.46.refs_0_, ...), custom_call_target="tpu_custom_call" | custom-call | flops 301989888 | bytes 5111808 | tf_op jit(solution)/shard_map/slots/pallas_call | solution.py:428
  111.5 0.8 collective-permute-start.27
  112.3 2.4 %collective-permute-start.28 = (bf16[128,1536]{1,0:T(8,128)(2,1)S(1)}, bf16[128,1536]{1,0:T(8,128)(2,1)S(1)}, u32[]{:S(2)}, u32[]{:S(2)}) collective-permute-start(bf16[128,1536]{1,0:T(8,128)(2,1)S(1)} %get-tuple-element.65.refs_0_), channel_id=1, source_target_pairs={{0,6},{1,7},{2,0},{3,1},{4,2},{5,3},{6,4},{7,5},{8,14},{9,15},{10,... | collective-permute-start | bytes 1179656 | tf_op jit(solution)/shard_map/ppermute | solution.py:544
  114.7 1.3 collective-permute-start.25
  116.0 1.3 collective-permute-start.26
  117.4 3.9 %collective-permute-done.24.two = bf16[192,512]{1,0:T(8,128)(2,1)S(1)} collective-permute-done((bf16[192,512]{1,0:T(8,128)(2,1)S(1)}, bf16[192,512]{1,0:T(8,128)(2,1)S(1)}, u32[]{:S(2)}, u32[]{:S(2)}) %collective-permute-start.24) | collective-permute-done | bytes 196640 | tf_op jit(solution)/shard_map/ppermute | solution.py:544
  121.2 5.4 %collective-permute-done.25.three = bf16[192,512]{1,0:T(8,128)(2,1)S(1)} collective-permute-done((bf16[192,512]{1,0:T(8,128)(2,1)S(1)}, bf16[192,512]{1,0:T(8,128)(2,1)S(1)}, u32[]{:S(2)}, u32[]{:S(2)}) %collective-permute-start.25) | collective-permute-done | bytes 196640 | tf_op jit(solution)/shard_map/ppermute | solution.py:544
  126.6 0.1 fold.1.one
  126.7 1.2 collective-permute-start.32
  127.9 0.9 collective-permute-start.30
  128.8 1.7 %collective-permute-start.31 = (bf16[192,512]{1,0:T(8,128)(2,1)S(1)}, bf16[192,512]{1,0:T(8,128)(2,1)S(1)}, u32[]{:S(2)}, u32[]{:S(2)}) collective-permute-start(bf16[192,512]{1,0:T(8,128)(2,1)S(1)} %fold.1.one), channel_id=1, source_target_pairs={{0,96},{1,97},{2,98},{3,99},{4,100},{5,101},{6,102},{7,103},{8,104... | collective-permute-start | bytes 589832 | tf_op jit(solution)/shard_map/ppermute | solution.py:544
  130.6 4.2 %collective-permute-done.29.two = bf16[192,512]{1,0:T(8,128)(2,1)S(1)} collective-permute-done((bf16[192,512]{1,0:T(8,128)(2,1)S(1)}, bf16[192,512]{1,0:T(8,128)(2,1)S(1)}, u32[]{:S(2)}, u32[]{:S(2)}) %collective-permute-start.29) | collective-permute-done | bytes 196640 | tf_op jit(solution)/shard_map/ppermute | solution.py:544
  134.8 5.0 %collective-permute-done.30.three = bf16[192,512]{1,0:T(8,128)(2,1)S(1)} collective-permute-done((bf16[192,512]{1,0:T(8,128)(2,1)S(1)}, bf16[192,512]{1,0:T(8,128)(2,1)S(1)}, u32[]{:S(2)}, u32[]{:S(2)}) %collective-permute-start.30) | collective-permute-done | bytes 196640 | tf_op jit(solution)/shard_map/ppermute | solution.py:544
  139.8 0.9 collective-permute-start.33
  140.6 0.5 collective-permute-start.36
  141.2 1.1 top_part.1
  142.3 0.0 collective-permute-start.34
  142.3 3.9 %all-to-all-start = ((bf16[8,64,128]{2,1,0:T(8,128)(2,1)}), bf16[8,64,128]{2,1,0:T(8,128)(2,1)S(1)}, u32[]{:S(2)}, u32[]{:S(2)}) async-start(bf16[8,64,128]{2,1,0:T(8,128)(2,1)} %get-tuple-element.66), calls=%async_computation | async-start | bytes 262144 | tf_op jit(solution)/shard_map/all_to_all | solution.py:587
  146.2 4.7 %whole_columns.1 = (bf16[1536,512]{1,0:T(8,128)(2,1)}, bf16[1536,512]{1,0:T(8,128)(2,1)}) custom-call(s32[2]{0:T(128)S(1)} %copy-done.7, bf16[128,1536]{1,0:T(8,128)(2,1)S(1)} %get-tuple-element.65.refs_0_, bf16[128,1536]{1,0:T(8,128)(2,1)S(1)} %collective-permute-done.32.refs_1_, bf16[128,1536]{1,0:T(8,128)(2,1)S(1)} %collective-permute-done.27.refs_2_, ...), custom_call_target="tpu_custom_call" | custom-call | bytes 6291456 | tf_op jit(solution)/shard_map/whole_columns/pallas_call | solution.py:460
  150.9 0.5 all-to-all-done.taken
  151.5 0.9 last_part.1
  (55 shorter events, 0.2 us)
Async XLA Ops:
  4.1 19.0 %collective-permute-start = (bf16[12,64,128]{2,1,0:T(8,128)(2,1)}, bf16[12,64,128]{2,1,0:T(8,128)(2,1)S(1)}, u32[]{:S(2)}, u32[]{:S(2)}) collective-permute-start(bf16[12,64,128]{2,1,0:T(8,128)(2,1)} %prep_a.1), channel_id=1, source_target_pairs={{0,16},{1,48},{2,8},{3,40},{4,0},{5,32},{6,24},{7,56},{8,25},{9,57... | collective-permute-start | bytes 589832 | tf_op jit(solution)/shard_map/ppermute | solution.py:556
  14.1 13.4 %collective-permute-start.5 = (bf16[12,64,128]{2,1,0:T(8,128)(2,1)}, bf16[12,64,128]{2,1,0:T(8,128)(2,1)S(1)}, u32[]{:S(2)}, u32[]{:S(2)}) collective-permute-start(bf16[12,64,128]{2,1,0:T(8,128)(2,1)} %prep_b.1), channel_id=1, source_target_pairs={{0,16},{1,48},{2,8},{3,40},{4,0},{5,32},{6,24},{7,56},{8,25},{9,57... | collective-permute-start | bytes 589832 | tf_op jit(solution)/shard_map/ppermute | solution.py:558
  23.2 8.4 %collective-permute-start.1 = (bf16[12,64,128]{2,1,0:T(8,128)(2,1)S(1)}, bf16[12,64,128]{2,1,0:T(8,128)(2,1)S(1)}, u32[]{:S(2)}, u32[]{:S(2)}) collective-permute-start(bf16[12,64,128]{2,1,0:T(8,128)(2,1)S(1)} %collective-permute-done), channel_id=1, source_target_pairs={{0,16},{1,17},{2,18},{3,19},{4,20},{5,21},{6,22},{7,23},{8,24},{9,... | collective-permute-start | bytes 589832 | tf_op jit(solution)/shard_map/ppermute | solution.py:544
  23.2 12.3 %collective-permute-start.2 = (bf16[12,64,128]{2,1,0:T(8,128)(2,1)S(1)}, bf16[12,64,128]{2,1,0:T(8,128)(2,1)S(1)}, u32[]{:S(2)}, u32[]{:S(2)}) collective-permute-start(bf16[12,64,128]{2,1,0:T(8,128)(2,1)S(1)} %collective-permute-done), channel_id=1, source_target_pairs={{0,8},{1,9},{2,10},{3,11},{4,12},{5,13},{6,14},{7,15},{8,16},{9,17... | collective-permute-start | bytes 589832 | tf_op jit(solution)/shard_map/ppermute | solution.py:544
  23.2 12.3 %collective-permute-start.3 = (bf16[12,64,128]{2,1,0:T(8,128)(2,1)S(1)}, bf16[12,64,128]{2,1,0:T(8,128)(2,1)S(1)}, u32[]{:S(2)}, u32[]{:S(2)}) collective-permute-start(bf16[12,64,128]{2,1,0:T(8,128)(2,1)S(1)} %collective-permute-done), channel_id=1, source_target_pairs={{0,24},{1,25},{2,26},{3,27},{4,28},{5,29},{6,30},{7,31},{8,0},{9,1... | collective-permute-start | bytes 589832 | tf_op jit(solution)/shard_map/ppermute | solution.py:544
  27.5 9.4 %collective-permute-start.6 = (bf16[12,64,128]{2,1,0:T(8,128)(2,1)S(1)}, bf16[12,64,128]{2,1,0:T(8,128)(2,1)S(1)}, u32[]{:S(2)}, u32[]{:S(2)}) collective-permute-start(bf16[12,64,128]{2,1,0:T(8,128)(2,1)S(1)} %collective-permute-done.5), channel_id=1, source_target_pairs={{0,64},{1,65},{2,66},{3,67},{4,68},{5,69},{6,70},{7,71},{8,72},{9,... | collective-permute-start | bytes 589832 | tf_op jit(solution)/shard_map/ppermute | solution.py:544
  30.7 8.2 %collective-permute-start.7 = (bf16[12,64,128]{2,1,0:T(8,128)(2,1)S(1)}, bf16[12,64,128]{2,1,0:T(8,128)(2,1)S(1)}, u32[]{:S(2)}, u32[]{:S(2)}) collective-permute-start(bf16[12,64,128]{2,1,0:T(8,128)(2,1)S(1)} %collective-permute-done.5), channel_id=1, source_target_pairs={{0,32},{1,33},{2,34},{3,35},{4,36},{5,37},{6,38},{7,39},{8,40},{9,... | collective-permute-start | bytes 589832 | tf_op jit(solution)/shard_map/ppermute | solution.py:544
  31.6 9.2 %collective-permute-start.8 = (bf16[12,64,128]{2,1,0:T(8,128)(2,1)S(1)}, bf16[12,64,128]{2,1,0:T(8,128)(2,1)S(1)}, u32[]{:S(2)}, u32[]{:S(2)}) collective-permute-start(bf16[12,64,128]{2,1,0:T(8,128)(2,1)S(1)} %collective-permute-done.5), channel_id=1, source_target_pairs={{0,96},{1,97},{2,98},{3,99},{4,100},{5,101},{6,102},{7,103},{8,104... | collective-permute-start | bytes 589832 | tf_op jit(solution)/shard_map/ppermute | solution.py:544
  35.6 22.0 %collective-permute-start.4 = (bf16[4,12,64,128]{3,2,1,0:T(8,128)(2,1)S(1)}, bf16[4,12,64,128]{3,2,1,0:T(8,128)(2,1)S(1)}, u32[]{:S(2)}, u32[]{:S(2)}) collective-permute-start(bf16[4,12,64,128]{3,2,1,0:T(8,128)(2,1)S(1)} %pad_maximum_fusion._.a_own), channel_id=1, source_target_pairs={{0,32},{1,33},{2,34},{3,35},{4,36},{5,37},{6,38},{7,39},{8,40},{9,... | collective-permute-start | bytes 2359304 | tf_op jit(solution)/shard_map/ppermute | solution.py:544
  40.8 10.6 %copy-start.7 = (s32[2]{0:T(128)S(1)}, s32[2]{0:T(128)}, u32[]{:S(2)}) copy-start(s32[2]{0:T(128)} %pad_add_fusion.place) | copy-start | bytes 28
  40.9 20.3 %collective-permute-start.9 = (bf16[4,12,64,128]{3,2,1,0:T(8,128)(2,1)S(1)}, bf16[4,12,64,128]{3,2,1,0:T(8,128)(2,1)S(1)}, u32[]{:S(2)}, u32[]{:S(2)}) collective-permute-start(bf16[4,12,64,128]{3,2,1,0:T(8,128)(2,1)S(1)} %pad_maximum_fusion.1.b_own), channel_id=1, source_target_pairs={{0,8},{1,9},{2,10},{3,11},{4,12},{5,13},{6,14},{7,15},{8,16},{9,17... | collective-permute-start | bytes 2359304 | tf_op jit(solution)/shard_map/ppermute | solution.py:544
  41.0 20.8 %collective-permute-start.11 = (bf16[4,12,64,128]{3,2,1,0:T(8,128)(2,1)S(1)}, bf16[4,12,64,128]{3,2,1,0:T(8,128)(2,1)S(1)}, u32[]{:S(2)}, u32[]{:S(2)}) collective-permute-start(bf16[4,12,64,128]{3,2,1,0:T(8,128)(2,1)S(1)} %pad_maximum_fusion._.a_own), channel_id=1, source_target_pairs={{0,96},{1,97},{2,98},{3,99},{4,100},{5,101},{6,102},{7,103},{8,104... | collective-permute-start | bytes 2359304 | tf_op jit(solution)/shard_map/ppermute | solution.py:544
  44.4 19.7 %collective-permute-start.14 = (bf16[4,12,64,128]{3,2,1,0:T(8,128)(2,1)S(1)}, bf16[4,12,64,128]{3,2,1,0:T(8,128)(2,1)S(1)}, u32[]{:S(2)}, u32[]{:S(2)}) collective-permute-start(bf16[4,12,64,128]{3,2,1,0:T(8,128)(2,1)S(1)} %pad_maximum_fusion.1.b_own), channel_id=1, source_target_pairs={{0,24},{1,25},{2,26},{3,27},{4,28},{5,29},{6,30},{7,31},{8,0},{9,1... | collective-permute-start | bytes 2359304 | tf_op jit(solution)/shard_map/ppermute | solution.py:544
  47.0 3.7 %copy-start.1 = (bf16[1536,3072]{1,0:T(8,128)(2,1)S(1)}, bf16[1536,3072]{1,0:T(8,128)(2,1)}, u32[]{:S(2)}) copy-start(bf16[1536,3072]{1,0:T(8,128)(2,1)} %source.1) | copy-start | bytes 28311556
  61.2 13.6 %collective-permute-start.10 = (bf16[2,12,64,128]{3,2,1,0:T(8,128)(2,1)S(1)}, bf16[2,12,64,128]{3,2,1,0:T(8,128)(2,1)S(1)}, u32[]{:S(2)}, u32[]{:S(2)}) collective-permute-start(bf16[2,12,64,128]{3,2,1,0:T(8,128)(2,1)S(1)} %slice.12), channel_id=1, source_target_pairs={{0,32},{1,33},{2,34},{3,35},{4,36},{5,37},{6,38},{7,39},{8,40},{9,... | collective-permute-start | bytes 1179656 | tf_op jit(solution)/shard_map/ppermute | solution.py:544
  61.7 13.1 %collective-permute-start.13 = (bf16[2,12,64,128]{3,2,1,0:T(8,128)(2,1)S(1)}, bf16[2,12,64,128]{3,2,1,0:T(8,128)(2,1)S(1)}, u32[]{:S(2)}, u32[]{:S(2)}) collective-permute-start(bf16[2,12,64,128]{3,2,1,0:T(8,128)(2,1)S(1)} %slice.14), channel_id=1, source_target_pairs={{0,8},{1,9},{2,10},{3,11},{4,12},{5,13},{6,14},{7,15},{8,16},{9,17... | collective-permute-start | bytes 1179656 | tf_op jit(solution)/shard_map/ppermute | solution.py:544
  61.8 13.0 %collective-permute-start.12 = (bf16[2,12,64,128]{3,2,1,0:T(8,128)(2,1)S(1)}, bf16[2,12,64,128]{3,2,1,0:T(8,128)(2,1)S(1)}, u32[]{:S(2)}, u32[]{:S(2)}) collective-permute-start(bf16[2,12,64,128]{3,2,1,0:T(8,128)(2,1)S(1)} %slice.16), channel_id=1, source_target_pairs={{0,96},{1,97},{2,98},{3,99},{4,100},{5,101},{6,102},{7,103},{8,104... | collective-permute-start | bytes 1179656 | tf_op jit(solution)/shard_map/ppermute | solution.py:544
  64.2 10.7 %collective-permute-start.15 = (bf16[2,12,64,128]{3,2,1,0:T(8,128)(2,1)S(1)}, bf16[2,12,64,128]{3,2,1,0:T(8,128)(2,1)S(1)}, u32[]{:S(2)}, u32[]{:S(2)}) collective-permute-start(bf16[2,12,64,128]{3,2,1,0:T(8,128)(2,1)S(1)} %slice.17), channel_id=1, source_target_pairs={{0,24},{1,25},{2,26},{3,27},{4,28},{5,29},{6,30},{7,31},{8,0},{9,1... | collective-permute-start | bytes 1179656 | tf_op jit(solution)/shard_map/ppermute | solution.py:544
  78.9 7.2 %collective-permute-start.20 = (bf16[4,128,768]{2,1,0:T(8,128)(2,1)S(1)}, bf16[4,128,768]{2,1,0:T(8,128)(2,1)S(1)}, u32[]{:S(2)}, u32[]{:S(2)}) collective-permute-start(bf16[4,128,768]{2,1,0:T(8,128)(2,1)S(1)} %get-tuple-element.51), channel_id=1, source_target_pairs={{0,1},{1,0},{2,3},{3,2},{4,5},{5,4},{6,7},{7,6},{8,9},{9,8},{10,11... | collective-permute-start | bytes 2359304 | tf_op jit(solution)/shard_map/ppermute | solution.py:544
  85.8 6.5 %collective-permute-start.16 = (bf16[4,128,768]{2,1,0:T(8,128)(2,1)S(1)}, bf16[4,128,768]{2,1,0:T(8,128)(2,1)S(1)}, u32[]{:S(2)}, u32[]{:S(2)}) collective-permute-start(bf16[4,128,768]{2,1,0:T(8,128)(2,1)S(1)} %get-tuple-element.45), channel_id=1, source_target_pairs={{0,1},{1,0},{2,3},{3,2},{4,5},{5,4},{6,7},{7,6},{8,9},{9,8},{10,11... | collective-permute-start | bytes 2359304 | tf_op jit(solution)/shard_map/ppermute | solution.py:544
  86.1 23.5 %copy-start = (bf16[1536,512]{1,0:T(8,128)(2,1)S(1)}, bf16[1536,512]{1,0:T(8,128)(2,1)}, u32[]{:S(2)}) copy-start(bf16[1536,512]{1,0:T(8,128)(2,1)} %refs_8_.1) | copy-start | bytes 4718596
  86.1 23.5 %copy-start.2 = (bf16[1536,512]{1,0:T(8,128)(2,1)S(1)}, bf16[1536,512]{1,0:T(8,128)(2,1)}, u32[]{:S(2)}) copy-start(bf16[1536,512]{1,0:T(8,128)(2,1)} %refs_9_.1) | copy-start | bytes 4718596
  86.1 23.5 %copy-start.6 = (s32[16,12]{1,0:T(8,128)S(1)}, s32[16,12]{1,0:T(8,128)}, u32[]{:S(2)}) copy-start(s32[16,12]{1,0:T(8,128)} %rows_a.5) | copy-start | bytes 2308
  86.1 23.5 %copy-start.8 = (s32[16,12]{1,0:T(8,128)S(1)}, s32[16,12]{1,0:T(8,128)}, u32[]{:S(2)}) copy-start(s32[16,12]{1,0:T(8,128)} %rows_b.3) | copy-start | bytes 2308
  86.1 23.5 %copy-start.9 = (s32[16]{0:T(128)S(1)}, s32[16]{0:T(128)}, u32[]{:S(2)}) copy-start(s32[16]{0:T(128)} %counts_a.5) | copy-start | bytes 196
  86.1 23.5 %copy-start.10 = (s32[16]{0:T(128)S(1)}, s32[16]{0:T(128)}, u32[]{:S(2)}) copy-start(s32[16]{0:T(128)} %counts_b.3) | copy-start | bytes 196
  87.2 8.0 %collective-permute-start.21 = (bf16[128,768]{1,0:T(8,128)(2,1)S(1)}, bf16[128,768]{1,0:T(8,128)(2,1)S(1)}, u32[]{:S(2)}, u32[]{:S(2)}) collective-permute-start(bf16[128,768]{1,0:T(8,128)(2,1)S(1)} %get-tuple-element.53), channel_id=1, source_target_pairs={{0,4},{1,5},{2,6},{3,7},{4,0},{5,1},{6,2},{7,3},{8,12},{9,13},{10,... | collective-permute-start | bytes 589832 | tf_op jit(solution)/shard_map/ppermute | solution.py:544
  88.9 11.8 %collective-permute-start.22 = (bf16[128,768]{1,0:T(8,128)(2,1)S(1)}, bf16[128,768]{1,0:T(8,128)(2,1)S(1)}, u32[]{:S(2)}, u32[]{:S(2)}) collective-permute-start(bf16[128,768]{1,0:T(8,128)(2,1)S(1)} %get-tuple-element.54), channel_id=1, source_target_pairs={{0,2},{1,3},{2,4},{3,5},{4,6},{5,7},{6,0},{7,1},{8,10},{9,11},{10,... | collective-permute-start | bytes 589832 | tf_op jit(solution)/shard_map/ppermute | solution.py:544
  92.3 8.8 %collective-permute-start.23 = (bf16[128,768]{1,0:T(8,128)(2,1)S(1)}, bf16[128,768]{1,0:T(8,128)(2,1)S(1)}, u32[]{:S(2)}, u32[]{:S(2)}) collective-permute-start(bf16[128,768]{1,0:T(8,128)(2,1)S(1)} %get-tuple-element.55), channel_id=1, source_target_pairs={{0,6},{1,7},{2,0},{3,1},{4,2},{5,3},{6,4},{7,5},{8,14},{9,15},{10,... | collective-permute-start | bytes 589832 | tf_op jit(solution)/shard_map/ppermute | solution.py:544
  93.4 9.9 %collective-permute-start.17 = (bf16[128,768]{1,0:T(8,128)(2,1)S(1)}, bf16[128,768]{1,0:T(8,128)(2,1)S(1)}, u32[]{:S(2)}, u32[]{:S(2)}) collective-permute-start(bf16[128,768]{1,0:T(8,128)(2,1)S(1)} %get-tuple-element.47), channel_id=1, source_target_pairs={{0,4},{1,5},{2,6},{3,7},{4,0},{5,1},{6,2},{7,3},{8,12},{9,13},{10,... | collective-permute-start | bytes 589832 | tf_op jit(solution)/shard_map/ppermute | solution.py:544
  95.2 13.0 %collective-permute-start.18 = (bf16[128,768]{1,0:T(8,128)(2,1)S(1)}, bf16[128,768]{1,0:T(8,128)(2,1)S(1)}, u32[]{:S(2)}, u32[]{:S(2)}) collective-permute-start(bf16[128,768]{1,0:T(8,128)(2,1)S(1)} %get-tuple-element.48), channel_id=1, source_target_pairs={{0,2},{1,3},{2,4},{3,5},{4,6},{5,7},{6,0},{7,1},{8,10},{9,11},{10,... | collective-permute-start | bytes 589832 | tf_op jit(solution)/shard_map/ppermute | solution.py:544
  95.2 14.3 %collective-permute-start.19 = (bf16[128,768]{1,0:T(8,128)(2,1)S(1)}, bf16[128,768]{1,0:T(8,128)(2,1)S(1)}, u32[]{:S(2)}, u32[]{:S(2)}) collective-permute-start(bf16[128,768]{1,0:T(8,128)(2,1)S(1)} %get-tuple-element.49), channel_id=1, source_target_pairs={{0,6},{1,7},{2,0},{3,1},{4,2},{5,3},{6,4},{7,5},{8,14},{9,15},{10,... | collective-permute-start | bytes 589832 | tf_op jit(solution)/shard_map/ppermute | solution.py:544
  109.6 31.6 %copy-start.3 = (bf16[512,512]{1,0:T(8,128)(2,1)S(1)}, bf16[512,512]{1,0:T(8,128)(2,1)}, u32[]{:S(2)}) copy-start(bf16[512,512]{1,0:T(8,128)(2,1)} %top.5) | copy-start | bytes 1572868
  109.6 31.5 %copy-start.4 = (f32[64,512]{1,0:T(8,128)S(1)}, f32[64,512]{1,0:T(8,128)}, u32[]{:S(2)}) copy-start(f32[64,512]{1,0:T(8,128)} %base.1) | copy-start | bytes 393220
  111.5 15.1 %collective-permute-start.27 = (bf16[128,1536]{1,0:T(8,128)(2,1)S(1)}, bf16[128,1536]{1,0:T(8,128)(2,1)S(1)}, u32[]{:S(2)}, u32[]{:S(2)}) collective-permute-start(bf16[128,1536]{1,0:T(8,128)(2,1)S(1)} %get-tuple-element.65.refs_0_), channel_id=1, source_target_pairs={{0,2},{1,3},{2,4},{3,5},{4,6},{5,7},{6,0},{7,1},{8,10},{9,11},{10,... | collective-permute-start | bytes 1179656 | tf_op jit(solution)/shard_map/ppermute | solution.py:544
  112.3 14.3 %collective-permute-start.28 = (bf16[128,1536]{1,0:T(8,128)(2,1)S(1)}, bf16[128,1536]{1,0:T(8,128)(2,1)S(1)}, u32[]{:S(2)}, u32[]{:S(2)}) collective-permute-start(bf16[128,1536]{1,0:T(8,128)(2,1)S(1)} %get-tuple-element.65.refs_0_), channel_id=1, source_target_pairs={{0,6},{1,7},{2,0},{3,1},{4,2},{5,3},{6,4},{7,5},{8,14},{9,15},{10,... | collective-permute-start | bytes 1179656 | tf_op jit(solution)/shard_map/ppermute | solution.py:544
  114.7 6.5 %collective-permute-start.24 = (bf16[192,512]{1,0:T(8,128)(2,1)S(1)}, bf16[192,512]{1,0:T(8,128)(2,1)S(1)}, u32[]{:S(2)}, u32[]{:S(2)}) collective-permute-start(bf16[192,512]{1,0:T(8,128)(2,1)S(1)} %get-tuple-element.58.one), channel_id=1, source_target_pairs={{0,16},{1,17},{2,18},{3,19},{4,20},{5,21},{6,22},{7,23},{8,24},{9,... | collective-permute-start | bytes 589832 | tf_op jit(solution)/shard_map/ppermute | solution.py:544
  114.7 11.9 %collective-permute-start.25 = (bf16[192,512]{1,0:T(8,128)(2,1)S(1)}, bf16[192,512]{1,0:T(8,128)(2,1)S(1)}, u32[]{:S(2)}, u32[]{:S(2)}) collective-permute-start(bf16[192,512]{1,0:T(8,128)(2,1)S(1)} %get-tuple-element.58.one), channel_id=1, source_target_pairs={{0,8},{1,9},{2,10},{3,11},{4,12},{5,13},{6,14},{7,15},{8,16},{9,17... | collective-permute-start | bytes 589832 | tf_op jit(solution)/shard_map/ppermute | solution.py:544
  116.0 10.5 %collective-permute-start.26 = (bf16[192,512]{1,0:T(8,128)(2,1)S(1)}, bf16[192,512]{1,0:T(8,128)(2,1)S(1)}, u32[]{:S(2)}, u32[]{:S(2)}) collective-permute-start(bf16[192,512]{1,0:T(8,128)(2,1)S(1)} %get-tuple-element.58.one), channel_id=1, source_target_pairs={{0,24},{1,25},{2,26},{3,27},{4,28},{5,29},{6,30},{7,31},{8,0},{9,1... | collective-permute-start | bytes 589832 | tf_op jit(solution)/shard_map/ppermute | solution.py:544
  126.7 15.6 %collective-permute-start.32 = (bf16[128,1536]{1,0:T(8,128)(2,1)S(1)}, bf16[128,1536]{1,0:T(8,128)(2,1)S(1)}, u32[]{:S(2)}, u32[]{:S(2)}) collective-permute-start(bf16[128,1536]{1,0:T(8,128)(2,1)S(1)} %get-tuple-element.65.refs_0_), channel_id=1, source_target_pairs={{0,4},{1,5},{2,6},{3,7},{4,0},{5,1},{6,2},{7,3},{8,12},{9,13},{10,... | collective-permute-start | bytes 1179656 | tf_op jit(solution)/shard_map/ppermute | solution.py:544
  127.9 6.9 %collective-permute-start.29 = (bf16[192,512]{1,0:T(8,128)(2,1)S(1)}, bf16[192,512]{1,0:T(8,128)(2,1)S(1)}, u32[]{:S(2)}, u32[]{:S(2)}) collective-permute-start(bf16[192,512]{1,0:T(8,128)(2,1)S(1)} %fold.1.one), channel_id=1, source_target_pairs={{0,64},{1,65},{2,66},{3,67},{4,68},{5,69},{6,70},{7,71},{8,72},{9,... | collective-permute-start | bytes 589832 | tf_op jit(solution)/shard_map/ppermute | solution.py:544
  127.9 11.9 %collective-permute-start.30 = (bf16[192,512]{1,0:T(8,128)(2,1)S(1)}, bf16[192,512]{1,0:T(8,128)(2,1)S(1)}, u32[]{:S(2)}, u32[]{:S(2)}) collective-permute-start(bf16[192,512]{1,0:T(8,128)(2,1)S(1)} %fold.1.one), channel_id=1, source_target_pairs={{0,32},{1,33},{2,34},{3,35},{4,36},{5,37},{6,38},{7,39},{8,40},{9,... | collective-permute-start | bytes 589832 | tf_op jit(solution)/shard_map/ppermute | solution.py:544
  128.8 11.0 %collective-permute-start.31 = (bf16[192,512]{1,0:T(8,128)(2,1)S(1)}, bf16[192,512]{1,0:T(8,128)(2,1)S(1)}, u32[]{:S(2)}, u32[]{:S(2)}) collective-permute-start(bf16[192,512]{1,0:T(8,128)(2,1)S(1)} %fold.1.one), channel_id=1, source_target_pairs={{0,96},{1,97},{2,98},{3,99},{4,100},{5,101},{6,102},{7,103},{8,104... | collective-permute-start | bytes 589832 | tf_op jit(solution)/shard_map/ppermute | solution.py:544
  139.8 6.4 %collective-permute-start.33 = (bf16[128,1536]{1,0:T(8,128)(2,1)S(1)}, bf16[128,1536]{1,0:T(8,128)(2,1)S(1)}, u32[]{:S(2)}, u32[]{:S(2)}) collective-permute-start(bf16[128,1536]{1,0:T(8,128)(2,1)S(1)} %get-tuple-element.65.refs_0_), channel_id=1, source_target_pairs={{0,1},{1,0},{2,3},{3,2},{4,5},{5,4},{6,7},{7,6},{8,9},{9,8},{10,11... | collective-permute-start | bytes 1179656 | tf_op jit(solution)/shard_map/ppermute | solution.py:544
  140.6 5.6 %collective-permute-start.35 = (bf16[128,1536]{1,0:T(8,128)(2,1)S(1)}, bf16[128,1536]{1,0:T(8,128)(2,1)}, u32[]{:S(2)}, u32[]{:S(2)}) collective-permute-start(bf16[128,1536]{1,0:T(8,128)(2,1)S(1)} %collective-permute-done.27.refs_2_), channel_id=1, source_target_pairs={{0,1},{1,0},{2,3},{3,2},{4,5},{5,4},{6,7},{7,6},{8,9},{9,8},{10,11... | collective-permute-start | bytes 1179656 | tf_op jit(solution)/shard_map/ppermute | solution.py:544
  140.6 5.6 %collective-permute-start.36 = (bf16[128,1536]{1,0:T(8,128)(2,1)S(1)}, bf16[128,1536]{1,0:T(8,128)(2,1)}, u32[]{:S(2)}, u32[]{:S(2)}) collective-permute-start(bf16[128,1536]{1,0:T(8,128)(2,1)S(1)} %collective-permute-done.28.refs_3_), channel_id=1, source_target_pairs={{0,1},{1,0},{2,3},{3,2},{4,5},{5,4},{6,7},{7,6},{8,9},{9,8},{10,11... | collective-permute-start | bytes 1179656 | tf_op jit(solution)/shard_map/ppermute | solution.py:544
  142.3 3.9 %collective-permute-start.34 = (bf16[128,1536]{1,0:T(8,128)(2,1)S(1)}, bf16[128,1536]{1,0:T(8,128)(2,1)}, u32[]{:S(2)}, u32[]{:S(2)}) collective-permute-start(bf16[128,1536]{1,0:T(8,128)(2,1)S(1)} %collective-permute-done.32.refs_1_), channel_id=1, source_target_pairs={{0,1},{1,0},{2,3},{3,2},{4,5},{5,4},{6,7},{7,6},{8,9},{9,8},{10,11... | collective-permute-start | bytes 1179656 | tf_op jit(solution)/shard_map/ppermute | solution.py:544
  142.3 9.2 %all-to-all-start = ((bf16[8,64,128]{2,1,0:T(8,128)(2,1)}), bf16[8,64,128]{2,1,0:T(8,128)(2,1)S(1)}, u32[]{:S(2)}, u32[]{:S(2)}) async-start(bf16[8,64,128]{2,1,0:T(8,128)(2,1)} %get-tuple-element.66), calls=%async_computation | async-start | bytes 262144 | tf_op jit(solution)/shard_map/all_to_all | solution.py:587
  146.2 5.3 %copy-start.5 = (f32[64,512]{1,0:T(8,128)S(1)}, f32[64,512]{1,0:T(8,128)}, u32[]{:S(2)}) copy-start(f32[64,512]{1,0:T(8,128)} %base.2) | copy-start | bytes 393220
